TPU v7x, 768 devices: a whole 4x8x12 slice. The times are simulated.
768 devices in a mesh: ctx: 12 (over z), head: 64 (over y, x, core).
Axes of the slice: x: 4, y: 8, z: 12, core: 2. Of those that a mesh axis runs over, the one named last changes fastest.
Arguments:
- incoming_signals: bfloat16 [6144, 4096], P('ctx'), may hold values from -6 to 6
- receptor_linear_map: bfloat16 [4096, 4096], P(None, 'head'), may hold values from -0.09375 to 0.09375
- lock_linear_map: bfloat16 [4096, 4096], P(None, 'head'), may hold values from -0.09375 to 0.09375
- worth_linear_map: bfloat16 [4096, 4096], P(None, 'head'), may hold values from -0.09375 to 0.09375
- outbound_linear_map: bfloat16 [4096, 4096], P('head'), may hold values from -0.25 to 0.25
- selfward_extra: float32 [4096], P('head'), may hold values from 2 to 32
- cluster_amplify_level: float32 [4096], P('head'), may hold values from 0.25 to 1.75
- dwindle_powers: int32 [4096], P('head'), may hold values from 0 to 63
- bisect_indicators: int32 [6144], P('ctx'), may hold values 0 or 1
- tutor_aggregated: bfloat16 [6144, 4096], P('ctx', 'head'), may hold values from -6 to 6
Outputs:
- mixed: bfloat16 [6144, 4096], P('ctx', 'head')
- receptor_sensitivity: bfloat16 [6144, 4096], P('ctx', 'head')
- grad_keys: bfloat16 [6144, 4096], P('ctx', 'head')
- value_gradients: bfloat16 [6144, 4096], P('ctx', 'head')
All inputs are finite; a program needn't handle non-finite values. No bound on the sum of `bisect_indicators` on one device may be relied on, other than what follows from the above.
Results may differ from a plain program's by a relative error of at most 0.014.
Values may be sent and summed in bfloat16 or wider, within the bound.
No kernel may reach another device: no remote copies, remote signals or barrier semaphores. Data moves between devices by JAX's collectives and lax.ppermute only.
A program may use at most 64 MiB of HBM per device.

v0:
```python
import jax
import jax.numpy as jnp
from jax import lax
from jax.sharding import PartitionSpec as P

LANES_EACH_HEAD = 64
CODES = 64


numeric_fidelity = lax.Precision.HIGHEST
epsilon = 1e-05
log_half = -0.6931471805599453
rate_span = 1.2


def prefix(value, axis, join, neutral, backward):
    count, mine = (lax.axis_size(axis), lax.axis_index(axis))
    pieces = jax.tree.map(lambda part: lax.all_gather(part, axis), value)
    if backward:
        pieces = jax.tree.map(lambda part: part[::-1], pieces)
        mine = count - 1 - mine
    running = jax.tree.map(
        lambda part, zero: jnp.full_like(part, 0) + jnp.asarray(zero, part.dtype), value, neutral
    )

    def turn(position, running):
        longer = join(running, jax.tree.map(lambda part: part[position], pieces))
        return jax.tree.map(lambda new, old: jnp.where(position < mine, new, old), longer, running)

    return lax.fori_loop(0, count - 1, turn, running)


def key_norm(keys_raw):
    scale = lax.rsqrt(jnp.mean(keys_raw * keys_raw, axis=-1, keepdims=True) + epsilon)
    return (keys_raw * scale * 0.125, scale)


def key_norm_back(keys_raw, scale, sensitivity_whitened_guess):
    inner = jnp.mean(keys_raw * sensitivity_whitened_guess, axis=-1, keepdims=True)
    return 0.125 * scale * (sensitivity_whitened_guess - scale * scale * keys_raw * inner)


def head_norm(generated_elements):
    centred = generated_elements - jnp.mean(generated_elements, axis=-1, keepdims=True)
    inverse = lax.rsqrt(jnp.mean(centred * centred, axis=-1, keepdims=True) + epsilon)
    return (centred * inverse, inverse)


def head_norm_back(unit, inverse, gain, grad_normed):
    scaled = grad_normed * gain
    return inverse * (
        scaled
        - jnp.mean(scaled, axis=-1, keepdims=True)
        - unit * jnp.mean(scaled * unit, axis=-1, keepdims=True)
    )


def piece_summands(receptor_linear_coeffs, lock_linear_coeffs, prefix_logarithm):
    length = prefix_logarithm.shape[1]
    last = prefix_logarithm[:, length - 1 :, :]
    enlarging_quotient = jnp.exp(prefix_logarithm)
    dwindling_quotient = jnp.exp(-prefix_logarithm)
    inquiry_this_moment = receptor_linear_coeffs * enlarging_quotient
    lock_this_moment = lock_linear_coeffs * dwindling_quotient
    closing_addition = jnp.exp(last - prefix_logarithm)
    forgetting_rate = jnp.exp(last[:, 0, :])
    triangular_mask = jnp.arange(length)[:, None] >= jnp.arange(length)[None, :]
    affinity_logits = jnp.where(
        triangular_mask[None],
        jnp.einsum(
            "htk,hsk->hts", inquiry_this_moment, lock_this_moment, precision=numeric_fidelity
        ),
        0.0,
    )
    return (
        enlarging_quotient,
        dwindling_quotient,
        inquiry_this_moment,
        lock_this_moment,
        closing_addition,
        forgetting_rate,
        triangular_mask,
        affinity_logits,
    )


def slice_yields(
    receptor_linear_coeffs,
    lock_linear_coeffs,
    worth_linear_coeffs,
    selfward_extra,
    collated_additions,
    beginning_hidden_carryover,
):
    instant_portion_amount = jnp.sum(
        receptor_linear_coeffs * selfward_extra * lock_linear_coeffs, axis=-1, keepdims=True
    )
    return (
        jnp.einsum(
            "how,hwr->hor", collated_additions[7], worth_linear_coeffs, precision=numeric_fidelity
        )
        + jnp.einsum(
            "kdo,kom->kdm",
            collated_additions[2],
            beginning_hidden_carryover,
            precision=numeric_fidelity,
        )
        + instant_portion_amount * worth_linear_coeffs
    )


def slice_sensitivities(
    receptor_linear_coeffs,
    lock_linear_coeffs,
    worth_linear_coeffs,
    selfward_extra,
    collated_additions,
    beginning_hidden_carryover,
    walking_hidden_carryover,
    outcome_sensitivity,
):
    (
        enlarging_quotient,
        dwindling_quotient,
        inquiry_this_moment,
        lock_this_moment,
        closing_addition,
        forgetting_rate,
        triangular_mask,
        affinity_logits,
    ) = collated_additions
    twofold_contracted_mul = jnp.where(
        triangular_mask[None],
        jnp.einsum(
            "htv,hsv->hts", outcome_sensitivity, worth_linear_coeffs, precision=numeric_fidelity
        ),
        0.0,
    )
    progressive_totals = jnp.sum(outcome_sensitivity * worth_linear_coeffs, axis=-1, keepdims=True)
    instant_portion_amount = jnp.sum(
        receptor_linear_coeffs * selfward_extra * lock_linear_coeffs, axis=-1, keepdims=True
    )
    receptor_sensitivity = (
        enlarging_quotient
        * (
            jnp.einsum(
                "kvn,kgn->kvg",
                outcome_sensitivity,
                beginning_hidden_carryover,
                precision=numeric_fidelity,
            )
            + jnp.einsum(
                "bnd,bdf->bnf", twofold_contracted_mul, lock_this_moment, precision=numeric_fidelity
            )
        )
        + progressive_totals * selfward_extra * lock_linear_coeffs
    )
    sensitivity_whitened_guess = (
        dwindling_quotient
        * jnp.einsum(
            "zwh,zws->zhs", twofold_contracted_mul, inquiry_this_moment, precision=numeric_fidelity
        )
        + closing_addition
        * jnp.einsum(
            "kop,kup->kou",
            worth_linear_coeffs,
            walking_hidden_carryover,
            precision=numeric_fidelity,
        )
        + progressive_totals * selfward_extra * receptor_linear_coeffs
    )
    value_gradients = (
        jnp.einsum("ljp,lje->lpe", affinity_logits, outcome_sensitivity, precision=numeric_fidelity)
        + jnp.einsum(
            "ely,eyc->elc",
            lock_linear_coeffs * closing_addition,
            walking_hidden_carryover,
            precision=numeric_fidelity,
        )
        + instant_portion_amount * outcome_sensitivity
    )
    return (receptor_sensitivity, sensitivity_whitened_guess, value_gradients)


def assemble_outputs(earlier, later):
    return (earlier[0] * later[0], later[0][..., None] * earlier[1] + later[1])


def on_device(
    incoming_signals,
    receptor_linear_map,
    lock_linear_map,
    worth_linear_map,
    outbound_linear_map,
    selfward_extra,
    cluster_amplify_level,
    dwindle_powers,
    bisect_indicators,
    tutor_aggregated,
):
    length = incoming_signals.shape[0]
    width = receptor_linear_map.shape[1]
    cluster_number_series = width // LANES_EACH_HEAD
    all_frames = length * lax.axis_size("ctx")

    def by_head(array):
        return array.reshape(length, cluster_number_series, LANES_EACH_HEAD).transpose(1, 0, 2)

    def by_frame(array):
        return array.transpose(1, 0, 2).reshape(length, width)

    receptor_linear_coeffs = by_head(
        jnp.dot(incoming_signals, receptor_linear_map, preferred_element_type=jnp.float32)
    )
    keys_raw = by_head(
        jnp.dot(incoming_signals, lock_linear_map, preferred_element_type=jnp.float32)
    )
    worth_linear_coeffs = by_head(
        jnp.dot(incoming_signals, worth_linear_map, preferred_element_type=jnp.float32)
    )
    lock_linear_coeffs, scale = key_norm(keys_raw)
    rate = -rate_span * (dwindle_powers.astype(jnp.float32) + 1.0) / float(CODES * all_frames)
    log_steps = rate.reshape(cluster_number_series, 1, LANES_EACH_HEAD) + (
        bisect_indicators.astype(jnp.float32) * log_half
    ).reshape(1, length, 1)
    prefix_logarithm = jnp.cumsum(log_steps, axis=1)
    stacked_selfward_extras = selfward_extra.reshape(cluster_number_series, 1, LANES_EACH_HEAD)
    gain_heads = cluster_amplify_level.reshape(cluster_number_series, 1, LANES_EACH_HEAD)
    collated_additions = piece_summands(
        receptor_linear_coeffs, lock_linear_coeffs, prefix_logarithm
    )
    within_piece_share = jnp.einsum(
        "atn,ato->ano",
        lock_linear_coeffs * collated_additions[4],
        worth_linear_coeffs,
        precision=numeric_fidelity,
    )
    unit_diagonal = (
        jnp.ones((cluster_number_series, LANES_EACH_HEAD), jnp.float32),
        jnp.zeros((cluster_number_series, LANES_EACH_HEAD, LANES_EACH_HEAD), jnp.float32),
    )
    unused, beginning_hidden_carryover = prefix(
        (collated_additions[5], within_piece_share), "ctx", assemble_outputs, unit_diagonal, False
    )
    generated_elements = slice_yields(
        receptor_linear_coeffs,
        lock_linear_coeffs,
        worth_linear_coeffs,
        stacked_selfward_extras,
        collated_additions,
        beginning_hidden_carryover,
    )
    unit, inverse = head_norm(generated_elements)
    normed = by_frame(unit * gain_heads).astype(jnp.bfloat16)
    mixed_sum = lax.psum_scatter(
        lax.dot_general(
            outbound_linear_map,
            normed,
            (((0,), (1,)), ((), ())),
            preferred_element_type=jnp.float32,
        ),
        "head",
        scatter_dimension=0,
        tiled=True,
    ).T
    mixed = mixed_sum.astype(jnp.bfloat16)
    diff = (mixed.astype(jnp.float32) - tutor_aggregated.astype(jnp.float32)).astype(jnp.bfloat16)
    grad_normed = lax.dot_general(
        lax.all_gather(diff, "head", axis=1, tiled=True),
        outbound_linear_map,
        (((1,), (1,)), ((), ())),
        preferred_element_type=jnp.float32,
    )
    outcome_sensitivity = head_norm_back(unit, inverse, gain_heads, by_head(grad_normed))
    reverse_sweeping = jnp.einsum(
        "atn,ato->ano", collated_additions[2], outcome_sensitivity, precision=numeric_fidelity
    )
    unused_decay, walking_hidden_carryover = prefix(
        (collated_additions[5], reverse_sweeping), "ctx", assemble_outputs, unit_diagonal, True
    )
    receptor_sensitivity, sensitivity_whitened_guess, value_gradients = slice_sensitivities(
        receptor_linear_coeffs,
        lock_linear_coeffs,
        worth_linear_coeffs,
        stacked_selfward_extras,
        collated_additions,
        beginning_hidden_carryover,
        walking_hidden_carryover,
        outcome_sensitivity,
    )
    grad_keys = key_norm_back(keys_raw, scale, sensitivity_whitened_guess)
    return (
        mixed,
        by_frame(receptor_sensitivity).astype(jnp.bfloat16),
        by_frame(grad_keys).astype(jnp.bfloat16),
        by_frame(value_gradients).astype(jnp.bfloat16),
    )


def solution(mesh):
    in_specs = (
        P("ctx", None),
        P(None, "head"),
        P(None, "head"),
        P(None, "head"),
        P("head", None),
        P("head"),
        P("head"),
        P("head"),
        P("ctx"),
        P("ctx", "head"),
    )
    out_specs = (P("ctx", "head"), P("ctx", "head"), P("ctx", "head"), P("ctx", "head"))
    return jax.shard_map(
        on_device, mesh=mesh, in_specs=in_specs, out_specs=out_specs, check_vma=False
    )
```

profile of v0, /device:TPU:16, one launch (start us, length us, event | category | flops | bytes accessed | tf_op | source)
XLA Modules:
  0.0 406.4 jit_solution(418142689368829318)
XLA Ops:
  7.2 0.0 reduce-scatter.4.cloned.1.call-start
  7.2 0.8 convert_multiply_fusion
  8.0 0.7 add_multiply_fusion
  8.7 0.1 broadcast_add_fusion
  8.8 1.2 reduce-window.6
  10.0 0.1 copy.42
  10.2 0.2 slice_reduce_fusion
  10.5 3.7 multiply_reduce_fusion.4
  14.2 0.1 copy.43
  14.3 3.6 fusion.43
  17.9 0.7 fusion.21
  18.6 34.4 %all-gather = f32[768,64]{1,0:T(8,128)S(1)} all-gather(f32[64,64]{1,0:T(8,128)S(1)} %fusion.21), channel_id=2, replica_groups=mesh['ctx'=12,'head'=64] {'ctx'}, dimensions={0}, use_global_device_ids=true | all-gather | bytes 212992 | tf_op jit(solution)/shard_map/all_gather | solution.py:18
  53.0 19.4 %all_gather.21 = f32[12,1,64]{2,1,0:T(1,128)S(1)} all-gather(f32[1,1,64]{2,1,0:T(1,128)S(1)} %get-tuple-element.303), channel_id=1, replica_groups=mesh['ctx'=12,'head'=64] {'ctx'}, dimensions={0}, use_global_device_ids=true | all-gather | bytes 3328 | tf_op jit(solution)/shard_map/all_gather | solution.py:18
  72.4 1.0 while.28
  72.4 0.1 fusion.67
  72.5 0.1 fusion.67
  72.6 0.1 fusion.67
  72.7 0.1 fusion.67
  72.8 0.1 fusion.67
  72.9 0.1 fusion.67
  73.0 0.1 fusion.67
  73.1 0.1 fusion.67
  73.2 0.1 fusion.67
  73.2 0.1 fusion.67
  73.3 0.1 fusion.67
  73.4 3.5 multiply_reduce_fusion
  77.0 1.1 convolution_select_fusion
  78.1 0.5 fusion.29
  78.5 1.2 fusion.42
  79.8 4.6 %convolution_bitcast_fusion = f32[4096,512]{0,1:T(8,128)} fusion(bf16[64,4096]{1,0:T(8,128)(2,1)S(1)} %copy-done, f32[512,64]{0,1:T(8,128)S(1)} %get-tuple-element.312, f32[64]{0:T(128)S(1)} %copy-done.3, f32[512]{0:T(512)S(1)} %add_rsqrt_fusion, f32[512]{0:T(512)S(1)} %broadcast_multiply_fusion.4), kind=kOutput, calls=%fused_computation.6 | convolution fusion | flops 268566528 | bytes 9048320 | tf_op jit(solution)/shard_map/dot_general | solution.py:256
  84.3 9.0 %copy.62 = f32[4096,512]{1,0:T(8,128)} copy(f32[4096,512]{0,1:T(8,128)} %convolution_bitcast_fusion) | data formatting | bytes 16777216
  93.3 0.0 reduce-scatter.4.cloned.1.call-update
  93.3 0.0 all-gather.4.cloned.1.call-start
  93.4 163.0 %reduce-scatter.4.cloned.1.call-done = f32[64,512]{1,0:T(8,128)} async-done(((f32[4096,512]{1,0:T(8,128)}), f32[64,512]{1,0:T(8,128)}) %reduce-scatter.4.cloned.1.call-update) | async-done | bytes 131088 | tf_op jit(solution)/shard_map/reduce_scatter | solution.py:255
  256.4 1.6 subtract_convert_fusion
  258.0 0.0 all-gather.4.cloned.1.call-update
  258.0 91.9 %all-gather.4.cloned.1.call-done = bf16[512,4096]{0,1:T(8,128)(2,1)} async-done(((bf16[512,64]{0,1:T(8,128)(2,1)}), bf16[512,4096]{0,1:T(8,128)(2,1)}) %all-gather.4.cloned.1.call-update) | async-done | bytes 4194320 | tf_op jit(solution)/shard_map/all_gather | solution.py:269
  350.0 3.0 fusion.41
  353.0 0.1 multiply_reduce_fusion.1
  353.1 0.6 fusion.26
  353.7 26.8 %all-gather.1 = f32[768,64]{1,0:T(8,128)S(1)} all-gather(f32[64,64]{1,0:T(8,128)S(1)} %fusion.26), channel_id=3, replica_groups=mesh['ctx'=12,'head'=64] {'ctx'}, dimensions={0}, use_global_device_ids=true | all-gather | bytes 212992 | tf_op jit(solution)/shard_map/all_gather | solution.py:18
  380.4 0.8 rev.7
  381.2 9.4 %while.29 = (s32[]{:T(128)}, f32[1,64,64]{2,1,0:T(8,128)S(1)}, s32[]{:T(128)}, f32[12,1,64]{2,1,0:T(1,128)S(1)}, f32[12,1,64,64]{3,2,1,0:T(8,128)}, /*index=5*/s32[]{:T(128)}, s32[]{:T(128)}) while((s32[]{:T(128)}, f32[1,64,64]{2,1,0:T(8,128)S(1)}, s32[]{:T(128)}, f32[12,1,64]{2,1,0:T(1,128)S(1)}, f32[12,1,64,64]{3,2,1,0:T(8,128)}, ...), condition=%wide.region_13.14_spmd.clone, body=%wide.region_12.13_spmd.clone.sunk | while | flops 16388 | bytes 50025 | solution.py:30
  381.2 0.8 fusion.68
  382.1 0.8 fusion.68
  382.9 0.8 fusion.68
  383.8 0.8 fusion.68
  384.6 0.8 fusion.68
  385.5 0.8 fusion.68
  386.3 0.8 fusion.68
  387.2 0.8 fusion.68
  388.1 0.8 fusion.68
  388.9 0.8 fusion.68
  389.8 0.8 fusion.68
  390.6 0.5 fusion.19
  391.1 0.6 fusion.6
  391.7 1.0 convolution_select_fusion.1
  392.8 1.4 fusion.13
  394.2 1.1 fusion.23
  395.3 1.9 fusion.18
  397.2 0.3 fusion.32
  397.4 0.7 copy.56
  398.2 0.6 fusion.10
  398.8 0.7 copy.55
  (48 shorter events, 0.2 us)
Async XLA Ops:
  7.2 72.6 %copy-start = (bf16[64,4096]{1,0:T(8,128)(2,1)S(1)}, bf16[64,4096]{1,0:T(8,128)(2,1)}, u32[]{:S(2)}) copy-start(bf16[64,4096]{1,0:T(8,128)(2,1)} %param.18) | copy-start | bytes 1572868
  7.2 7.2 %copy-start.1 = (bf16[4096,64]{0,1:T(8,128)(2,1)S(1)}, bf16[4096,64]{0,1:T(8,128)(2,1)}, u32[]{:S(2)}) copy-start(bf16[4096,64]{0,1:T(8,128)(2,1)} %param.17) | copy-start | bytes 1572868
  7.2 249.2 %reduce-scatter.4.cloned.1.call-start = ((), (), s32[]{:S(2)}) async-start(), calls=%async_computation.2 | async-start | bytes 8519680 | tf_op jit(solution)/shard_map/reduce_scatter | solution.py:255
  14.2 59.2 %copy-start.4 = (f32[64]{0:T(128)S(1)}, f32[64]{0:T(128)}, u32[]{:S(2)}) copy-start(f32[64]{0:T(128)} %param.19) | copy-start | bytes 772
  14.2 59.2 %copy-start.5 = (bf16[4096,64]{0,1:T(8,128)(2,1)S(1)}, bf16[4096,64]{0,1:T(8,128)(2,1)}, u32[]{:S(2)}) copy-start(bf16[4096,64]{0,1:T(8,128)(2,1)} %param.15) | copy-start | bytes 1572868
  73.4 6.3 %copy-start.3 = (f32[64]{0:T(128)S(1)}, f32[64]{0:T(128)}, u32[]{:S(2)}) copy-start(f32[64]{0:T(128)} %param.20) | copy-start | bytes 772
  93.3 163.1 %copy-start.2 = (bf16[512,64]{0,1:T(8,128)(2,1)S(1)}, bf16[512,64]{0,1:T(8,128)(2,1)}, u32[]{:S(2)}) copy-start(bf16[512,64]{0,1:T(8,128)(2,1)} %param.23) | copy-start | bytes 196612
  93.3 256.6 %all-gather.4.cloned.1.call-start = ((), (), s32[]{:S(2)}) async-start(), calls=%async_computation.1 | async-start | bytes 4259840 | tf_op jit(solution)/shard_map/all_gather | solution.py:269
Sparse Core Ops, SparseCore 0:
  93.5 162.9 reduce-scatter.3
  261.6 88.3 all-gather.3
where the time goes:
time: 408 us; the launch traced here: 406 us
  waiting for transfers between devices  255 us (62%)
  blocking collectives  80.6 us (20%)
  matrix products  29.5 us (7%)
  other arithmetic  14.9 us (4%)
  between operations  14.3 us (4%)
  local copies, waits for them, and re-layouts  11.8 us (3%)
    reduce_scatter x1, waiting for transfers between devices, on_device(): lax.psum_scatter(lax.dot_general(outbound_linear_map, normed, (((0,), (1,...  163 us
    all_gather x1, waiting for transfers between devices, on_device(): lax.all_gather(diff, 'head', axis=1, tiled=True)  91.9 us
    all_gather x3, blocking collectives, prefix(): pieces = jax.tree.map(lambda part: lax.all_gather(part, axis), value)  80.6 us
    unnamed x15, local copies, waits for them, and re-layouts  10.5 us
    select_n x22, other arithmetic, turn(): jnp.where(position < mine, new, old)  10.1 us
  transfers between devices with their start and end apart: 2, of which 2 were waited for; matrix products, arithmetic and copies ran while one was open for 0% of the time, Pallas kernels for 0%

commit v1 on v0

--- a/solution.py
+++ b/solution.py
@@ -1,7 +1,7 @@
 import jax
 import jax.numpy as jnp
 from jax import lax
-from jax.sharding import PartitionSpec as P
+from jax.sharding import Mesh, PartitionSpec as P
 
 LANES_EACH_HEAD = 64
 CODES = 64
@@ -11,23 +11,6 @@
 epsilon = 1e-05
 log_half = -0.6931471805599453
 rate_span = 1.2
-
-
-def prefix(value, axis, join, neutral, backward):
-    count, mine = (lax.axis_size(axis), lax.axis_index(axis))
-    pieces = jax.tree.map(lambda part: lax.all_gather(part, axis), value)
-    if backward:
-        pieces = jax.tree.map(lambda part: part[::-1], pieces)
-        mine = count - 1 - mine
-    running = jax.tree.map(
-        lambda part, zero: jnp.full_like(part, 0) + jnp.asarray(zero, part.dtype), value, neutral
-    )
-
-    def turn(position, running):
-        longer = join(running, jax.tree.map(lambda part: part[position], pieces))
-        return jax.tree.map(lambda new, old: jnp.where(position < mine, new, old), longer, running)
-
-    return lax.fori_loop(0, count - 1, turn, running)
 
 
 def key_norm(keys_raw):
@@ -182,8 +165,38 @@
     return (receptor_sensitivity, sensitivity_whitened_guess, value_gradients)
 
 
-def assemble_outputs(earlier, later):
-    return (earlier[0] * later[0], later[0][..., None] * earlier[1] + later[1])
+GRID = {"y": 8, "x": 4, "core": 2}
+TILE = ("x", "core")
+
+
+def exchange(array, axis):
+    return lax.all_to_all(array, axis, 0, 0)
+
+
+def to_all(array, axis, count):
+    return exchange(jnp.broadcast_to(array[None], (count,) + array.shape), axis)
+
+
+def gather_rows(local):
+    n = GRID["x"]
+    parts = [local]
+    for step in (1, 3, 2):
+        parts.append(lax.ppermute(local, "x", [(i, (i + step) % n) for i in range(n)]))
+    mine = jnp.concatenate([parts[0], parts[1], parts[3], parts[2]], axis=0)
+    return mine, lax.ppermute(mine, "core", [(0, 1), (1, 0)])
+
+
+def weights_between(log_totals, mine, backward):
+    count = log_totals.shape[0]
+    at = jnp.arange(count)
+    if backward:
+        between = (at[None, :] > mine) & (at[None, :] < at[:, None])
+        counts = at > mine
+    else:
+        between = (at[None, :] < mine) & (at[None, :] > at[:, None])
+        counts = at < mine
+    span = jnp.sum(jnp.where(between[:, :, None], log_totals[None], 0.0), axis=1)
+    return jnp.where(counts[:, None], jnp.exp(span), 0.0)
 
 
 def on_device(
@@ -199,33 +212,32 @@
     tutor_aggregated,
 ):
     length = incoming_signals.shape[0]
-    width = receptor_linear_map.shape[1]
-    cluster_number_series = width // LANES_EACH_HEAD
-    all_frames = length * lax.axis_size("ctx")
-
-    def by_head(array):
-        return array.reshape(length, cluster_number_series, LANES_EACH_HEAD).transpose(1, 0, 2)
-
-    def by_frame(array):
-        return array.transpose(1, 0, 2).reshape(length, width)
-
-    receptor_linear_coeffs = by_head(
-        jnp.dot(incoming_signals, receptor_linear_map, preferred_element_type=jnp.float32)
-    )
-    keys_raw = by_head(
-        jnp.dot(incoming_signals, lock_linear_map, preferred_element_type=jnp.float32)
-    )
-    worth_linear_coeffs = by_head(
-        jnp.dot(incoming_signals, worth_linear_map, preferred_element_type=jnp.float32)
-    )
+    lanes = LANES_EACH_HEAD
+    blocks = lax.axis_size("ctx")
+    mine = lax.axis_index("ctx")
+    x_at, core_at = lax.axis_index("x"), lax.axis_index("core")
+    tiles = GRID["x"] * GRID["core"]
+    rows = GRID["y"]
+    part = length // tiles
+    all_frames = length * blocks
+
+    w_mine, w_other = gather_rows(outbound_linear_map)
+
+    receptor_linear_coeffs = jnp.dot(
+        incoming_signals, receptor_linear_map, preferred_element_type=jnp.float32
+    )[None]
+    keys_raw = jnp.dot(incoming_signals, lock_linear_map, preferred_element_type=jnp.float32)[None]
+    worth_linear_coeffs = jnp.dot(
+        incoming_signals, worth_linear_map, preferred_element_type=jnp.float32
+    )[None]
     lock_linear_coeffs, scale = key_norm(keys_raw)
     rate = -rate_span * (dwindle_powers.astype(jnp.float32) + 1.0) / float(CODES * all_frames)
-    log_steps = rate.reshape(cluster_number_series, 1, LANES_EACH_HEAD) + (
+    log_steps = rate.reshape(1, 1, lanes) + (
         bisect_indicators.astype(jnp.float32) * log_half
     ).reshape(1, length, 1)
     prefix_logarithm = jnp.cumsum(log_steps, axis=1)
-    stacked_selfward_extras = selfward_extra.reshape(cluster_number_series, 1, LANES_EACH_HEAD)
-    gain_heads = cluster_amplify_level.reshape(cluster_number_series, 1, LANES_EACH_HEAD)
+    stacked_selfward_extras = selfward_extra.reshape(1, 1, lanes)
+    gain_heads = cluster_amplify_level.reshape(1, 1, lanes)
     collated_additions = piece_summands(
         receptor_linear_coeffs, lock_linear_coeffs, prefix_logarithm
     )
@@ -234,14 +246,22 @@
         lock_linear_coeffs * collated_additions[4],
         worth_linear_coeffs,
         precision=numeric_fidelity,
-    )
-    unit_diagonal = (
-        jnp.ones((cluster_number_series, LANES_EACH_HEAD), jnp.float32),
-        jnp.zeros((cluster_number_series, LANES_EACH_HEAD, LANES_EACH_HEAD), jnp.float32),
-    )
-    unused, beginning_hidden_carryover = prefix(
-        (collated_additions[5], within_piece_share), "ctx", assemble_outputs, unit_diagonal, False
-    )
+    )[0]
+    last = prefix_logarithm[0, length - 1, :]
+    half = lanes // 2
+    packed = jnp.concatenate(
+        [
+            jnp.concatenate([within_piece_share[:half], within_piece_share[half:]], axis=1),
+            jnp.broadcast_to(jnp.concatenate([last, last])[None], (8, 2 * lanes)),
+        ],
+        axis=0,
+    )
+    everyone = to_all(packed, "ctx", blocks)
+    shares = jnp.concatenate([everyone[:, :half, :lanes], everyone[:, :half, lanes:]], axis=1)
+    log_totals = everyone[:, half, :lanes]
+    beginning_hidden_carryover = jnp.sum(
+        weights_between(log_totals, mine, False)[:, :, None] * shares, axis=0
+    )[None]
     generated_elements = slice_yields(
         receptor_linear_coeffs,
         lock_linear_coeffs,
@@ -251,33 +271,63 @@
         beginning_hidden_carryover,
     )
     unit, inverse = head_norm(generated_elements)
-    normed = by_frame(unit * gain_heads).astype(jnp.bfloat16)
-    mixed_sum = lax.psum_scatter(
-        lax.dot_general(
-            outbound_linear_map,
-            normed,
-            (((0,), (1,)), ((), ())),
-            preferred_element_type=jnp.float32,
+    normed = (unit * gain_heads).astype(jnp.bfloat16)
+
+    sent = jnp.concatenate(
+        [
+            normed.reshape(tiles, part, lanes),
+            tutor_aggregated.reshape(tiles, part, lanes),
+        ],
+        axis=2,
+    )
+    got = exchange(sent, TILE)
+    order_x = (x_at - jnp.arange(GRID["x"])) % GRID["x"]
+    order = jnp.concatenate([order_x * 2 + core_at, order_x * 2 + 1 - core_at])
+    ordered = jnp.take(got[:, :, :lanes], order, axis=0).transpose(1, 0, 2).reshape(part, tiles * lanes)
+    cut = tiles * lanes // 2
+    partial_mixed = jnp.dot(
+        ordered[:, :cut], w_mine, preferred_element_type=jnp.float32
+    ) + jnp.dot(ordered[:, cut:], w_other, preferred_element_type=jnp.float32)
+    pieces = partial_mixed.reshape(part, rows, tiles * lanes).transpose(1, 0, 2).astype(jnp.bfloat16)
+    mixed = jnp.sum(exchange(pieces, "y").astype(jnp.float32), axis=0).astype(jnp.bfloat16)
+    tutor = got[:, :, lanes:].transpose(1, 0, 2).reshape(part, tiles * lanes)
+    diff = (mixed.astype(jnp.float32) - tutor.astype(jnp.float32)).astype(jnp.bfloat16)
+    diff_all = to_all(diff, "y", rows).transpose(1, 0, 2).reshape(part, rows * tiles * lanes)
+    over_columns = (((1,), (1,)), ((), ()))
+    grads = jnp.concatenate(
+        [
+            lax.dot_general(diff_all, w_mine, over_columns, preferred_element_type=jnp.float32),
+            lax.dot_general(diff_all, w_other, over_columns, preferred_element_type=jnp.float32),
+        ],
+        axis=1,
+    )
+    source = jnp.arange(tiles)
+    place = (x_at - source // 2) % GRID["x"] + jnp.where(source % 2 == core_at, 0, GRID["x"])
+    grads = jnp.take(grads.reshape(part, tiles, lanes).transpose(1, 0, 2), place, axis=0)
+    back = exchange(
+        jnp.concatenate(
+            [
+                grads.astype(jnp.bfloat16),
+                mixed.reshape(part, tiles, lanes).transpose(1, 0, 2),
+            ],
+            axis=2,
         ),
-        "head",
-        scatter_dimension=0,
-        tiled=True,
-    ).T
-    mixed = mixed_sum.astype(jnp.bfloat16)
-    diff = (mixed.astype(jnp.float32) - tutor_aggregated.astype(jnp.float32)).astype(jnp.bfloat16)
-    grad_normed = lax.dot_general(
-        lax.all_gather(diff, "head", axis=1, tiled=True),
-        outbound_linear_map,
-        (((1,), (1,)), ((), ())),
-        preferred_element_type=jnp.float32,
-    )
-    outcome_sensitivity = head_norm_back(unit, inverse, gain_heads, by_head(grad_normed))
+        TILE,
+    ).reshape(length, 2 * lanes)
+    mixed_out = back[:, lanes:]
+    grad_normed = back[:, :lanes].astype(jnp.float32)[None]
+
+    outcome_sensitivity = head_norm_back(unit, inverse, gain_heads, grad_normed)
     reverse_sweeping = jnp.einsum(
         "atn,ato->ano", collated_additions[2], outcome_sensitivity, precision=numeric_fidelity
-    )
-    unused_decay, walking_hidden_carryover = prefix(
-        (collated_additions[5], reverse_sweeping), "ctx", assemble_outputs, unit_diagonal, True
-    )
+    )[0]
+    later = to_all(
+        jnp.concatenate([reverse_sweeping[:half], reverse_sweeping[half:]], axis=1), "ctx", blocks
+    )
+    later = jnp.concatenate([later[:, :, :lanes], later[:, :, lanes:]], axis=1)
+    walking_hidden_carryover = jnp.sum(
+        weights_between(log_totals, mine, True)[:, :, None] * later, axis=0
+    )[None]
     receptor_sensitivity, sensitivity_whitened_guess, value_gradients = slice_sensitivities(
         receptor_linear_coeffs,
         lock_linear_coeffs,
@@ -290,27 +340,30 @@
     )
     grad_keys = key_norm_back(keys_raw, scale, sensitivity_whitened_guess)
     return (
-        mixed,
-        by_frame(receptor_sensitivity).astype(jnp.bfloat16),
-        by_frame(grad_keys).astype(jnp.bfloat16),
-        by_frame(value_gradients).astype(jnp.bfloat16),
+        mixed_out,
+        receptor_sensitivity[0].astype(jnp.bfloat16),
+        grad_keys[0].astype(jnp.bfloat16),
+        value_gradients[0].astype(jnp.bfloat16),
     )
 
 
 def solution(mesh):
+    blocks = mesh.shape["ctx"]
+    grid = Mesh(mesh.devices.reshape((blocks,) + tuple(GRID.values())), ("ctx",) + tuple(GRID))
+    head = tuple(GRID)
     in_specs = (
         P("ctx", None),
-        P(None, "head"),
-        P(None, "head"),
-        P(None, "head"),
-        P("head", None),
-        P("head"),
-        P("head"),
-        P("head"),
+        P(None, head),
+        P(None, head),
+        P(None, head),
+        P(head, None),
+        P(head),
+        P(head),
+        P(head),
         P("ctx"),
-        P("ctx", "head"),
-    )
-    out_specs = (P("ctx", "head"), P("ctx", "head"), P("ctx", "head"), P("ctx", "head"))
+        P("ctx", head),
+    )
+    out_specs = (P("ctx", head), P("ctx", head), P("ctx", head), P("ctx", head))
     return jax.shard_map(
-        on_device, mesh=mesh, in_specs=in_specs, out_specs=out_specs, check_vma=False
-    )
+        on_device, mesh=grid, in_specs=in_specs, out_specs=out_specs, check_vma=False
+    )

time: 408 us -> 169 us (0.41)
  the two profiles are of different devices: /device:TPU:16 before, /device:TPU:64 now
where the time goes in v1:
time: 169 us; the launch traced here: 168 us
  starting transfers between devices  55.7 us (33%)
  waiting for transfers between devices  52.8 us (31%)
  matrix products  28.1 us (17%)
  other arithmetic  15.2 us (9%)
  local copies, waits for them, and re-layouts  14.7 us (9%)
    all_to_all x6, waiting for transfers between devices, exchange(): return lax.all_to_all(array, axis, 0, 0)  52.7 us
    all_to_all x6, starting transfers between devices, exchange(): return lax.all_to_all(array, axis, 0, 0)  41.6 us
    ppermute x3, starting transfers between devices, gather_rows(): lax.ppermute(local, 'x', [(i, (i + step) % n) for i in range(n)])  12.1 us
    unnamed x63, local copies, waits for them, and re-layouts  4.53 us
    dot_general x1, matrix products, on_device(): jnp.dot(incoming_signals, worth_linear_map, preferred_element_type=jnp.fl...  3.84 us
    dot_general x1, matrix products, on_device(): jnp.dot(incoming_signals, receptor_linear_map, preferred_element_type=jnp...  3.59 us
  transfers between devices with their start and end apart: 10, of which 6 were waited for; matrix products, arithmetic and copies ran while one was open for 22% of the time, Pallas kernels for 0%

profile of v1, /device:TPU:64, one launch (start us, length us, event | category | flops | bytes accessed | tf_op | source)
XLA Modules:
  0.0 167.9 jit_solution(962634137552586712)
XLA Ops:
  0.6 5.1 %collective-permute-start.1 = (bf16[64,4096]{1,0:T(8,128)(2,1)}, bf16[64,4096]{1,0:T(8,128)(2,1)}, u32[]{:S(2)}, u32[]{:S(2)}) collective-permute-start(bf16[64,4096]{1,0:T(8,128)(2,1)} %param.14), channel_id=1, source_target_pairs={{0,4},{2,6},{4,0},{6,2},{1,5},{3,7},{5,1},{7,3},{8,12},{10,14},{12... | collective-permute-start | bytes 1572872 | tf_op jit(solution)/shard_map/ppermute | solution.py:184
  5.7 2.5 %collective-permute-start = (bf16[64,4096]{1,0:T(8,128)(2,1)}, bf16[64,4096]{1,0:T(8,128)(2,1)}, u32[]{:S(2)}, u32[]{:S(2)}) collective-permute-start(bf16[64,4096]{1,0:T(8,128)(2,1)} %param.14), channel_id=1, source_target_pairs={{0,2},{2,4},{4,6},{6,0},{1,3},{3,5},{5,7},{7,1},{8,10},{10,12},{12... | collective-permute-start | bytes 1572872 | tf_op jit(solution)/shard_map/ppermute | solution.py:184
  8.2 4.6 %collective-permute-start.2 = (bf16[64,4096]{1,0:T(8,128)(2,1)}, bf16[64,4096]{1,0:T(8,128)(2,1)}, u32[]{:S(2)}, u32[]{:S(2)}) collective-permute-start(bf16[64,4096]{1,0:T(8,128)(2,1)} %param.14), channel_id=1, source_target_pairs={{0,6},{2,0},{4,2},{6,4},{1,7},{3,1},{5,3},{7,5},{8,14},{10,8},{12,... | collective-permute-start | bytes 1572872 | tf_op jit(solution)/shard_map/ppermute | solution.py:184
  12.8 0.7 add_multiply_fusion
  13.5 0.7 convert_multiply_fusion.1
  14.3 1.2 reduce-window.6
  16.3 3.8 %fusion.61 = f32[512,64]{0,1:T(8,128)S(1)} fusion(bf16[512,4096]{1,0:T(8,128)(2,1)} %param.10, bf16[4096,64]{0,1:T(8,128)(2,1)} %param.13), kind=kOutput, calls=%fused_computation.164 | convolution fusion | flops 268435456 | bytes 4849664 | tf_op jit(solution)/shard_map/dot_general | solution.py:230
  20.2 1.4 multiply_reduce_fusion.4
  21.6 0.6 broadcast_multiply_fusion
  22.7 0.7 broadcast_in_dim.144
  23.4 14.8 %all-to-all-start = ((f32[12,40,128]{2,1,0:T(8,128)}), f32[12,40,128]{2,1,0:T(8,128)S(1)}, u32[]{:S(2)}, u32[]{:S(2)}) async-start(f32[12,40,128]{2,1,0:T(8,128)} %broadcast_in_dim.144), calls=%async_computation | async-start | bytes 491520 | tf_op jit(solution)/shard_map/all_to_all | solution.py:173
  38.2 0.8 copy.45
  39.0 3.6 %multiply_reduce_fusion.3 = (f32[512]{0:T(512)S(1)}, f32[512,64]{0,1:T(8,128)S(1)}) fusion(f32[512,64]{0,1:T(8,128)S(1)} %get-tuple-element.38, f32[64]{0:T(128)S(1)} %copy-done.14, f32[512]{0:T(512)S(1)} %get-tuple-element.36, bf16[512,4096]{1,0:T(8,128)(2,1)} %param.10, bf16[4096,64]{0,1:T(8,128)(2,1)S(1)} %copy-done.5), kind=kOutput, calls=%fused_computation.70 | convolution fusion | flops 268598784 | bytes 4985088 | tf_op jit(solution)/shard_map/dot_general | solution.py:226
  42.6 1.0 convolution_select_fusion.1
  43.6 1.8 %fusion.62 = f32[512,64]{0,1:T(8,128)} fusion(f32[512,512]{1,0:T(8,128)S(1)} %convolution_select_fusion.1, f32[512,64]{0,1:T(8,128)S(1)} %fusion.61), kind=kOutput, calls=%fused_computation.165 | convolution fusion | flops 201326592 | bytes 1310720 | tf_op jit(solution)/shard_map/how,hwr->hor/dot_general | solution.py:82
  45.5 0.6 compare_and_fusion
  46.1 1.1 constant_dynamic-update-slice_fusion.2
  47.2 1.1 constant_dynamic-update-slice_fusion.1
  48.3 1.1 constant_dynamic-update-slice_fusion
  49.4 1.9 %collective-permute-start.3 = (bf16[256,4096]{1,0:T(8,128)(2,1)S(1)}, bf16[256,4096]{1,0:T(8,128)(2,1)}, u32[]{:S(2)}, u32[]{:S(2)}) collective-permute-start(bf16[256,4096]{1,0:T(8,128)(2,1)S(1)} %constant_dynamic-update-slice_fusion), channel_id=1, source_target_pairs={{0,1},{1,0},{2,3},{3,2},{4,5},{5,4},{6,7},{7,6},{8,9},{9,8},{10,11... | collective-permute-start | bytes 6291464 | tf_op jit(solution)/shard_map/ppermute | solution.py:186
  51.4 1.1 all-to-all-done
  52.4 0.7 select_reduce_fusion
  53.5 1.2 fusion.60
  54.9 0.7 multiply_convert_fusion
  55.7 1.7 pad_maximum_fusion
  57.4 3.4 %all-to-all-start.1 = ((bf16[8,64,128]{2,1,0:T(8,128)(2,1)}), bf16[8,64,128]{2,1,0:T(8,128)(2,1)S(1)}, u32[]{:S(2)}, u32[]{:S(2)}) async-start(bf16[8,64,128]{2,1,0:T(8,128)(2,1)} %pad_maximum_fusion), calls=%async_computation.1 | async-start | bytes 262144 | tf_op jit(solution)/shard_map/all_to_all | solution.py:173
  60.9 0.6 pad_clamp_fusion.1
  61.5 5.4 %all-to-all-done.1 = bf16[8,64,128]{2,1,0:T(8,128)(2,1)S(1)} async-done(((bf16[8,64,128]{2,1,0:T(8,128)(2,1)}), bf16[8,64,128]{2,1,0:T(8,128)(2,1)S(1)}, u32[]{:S(2)}, u32[]{:S(2)}) %all-to-all-start.1) | async-done | bytes 131104 | tf_op jit(solution)/shard_map/all_to_all | solution.py:173
  66.8 0.8 convert_bitcast_fusion
  67.6 0.7 gather_fusion
  68.3 0.7 select_bitcast_fusion
  69.3 0.6 copy-done.9
  69.9 2.1 %fusion.37 = f32[64,4096]{1,0:T(8,128)S(1)} fusion(bf16[256,4096]{1,0:T(8,128)(2,1)} %collective-permute-done.3, bf16[64,512]{1,0:T(8,128)(2,1)S(1)} %reshape.611), kind=kOutput, calls=%fused_computation.84 | convolution fusion | flops 134217728 | bytes 3178496 | tf_op jit(solution)/shard_map/dot_general | solution.py:290
  72.0 1.3 fusion
  73.3 0.8 copy.66
  74.1 7.1 %all-to-all-start.2 = ((bf16[8,64,512]{2,1,0:T(8,128)(2,1)}), bf16[8,64,512]{2,1,0:T(8,128)(2,1)}, u32[]{:S(2)}, u32[]{:S(2)}) async-start(bf16[8,64,512]{2,1,0:T(8,128)(2,1)} %bitcast.180), calls=%async_computation.2 | async-start | bytes 1048576 | tf_op jit(solution)/shard_map/all_to_all | solution.py:173
  81.2 0.9 copy.49
  82.1 1.1 reshape.616
  83.1 15.5 %all-to-all-done.2 = bf16[8,64,512]{2,1,0:T(8,128)(2,1)} async-done(((bf16[8,64,512]{2,1,0:T(8,128)(2,1)}), bf16[8,64,512]{2,1,0:T(8,128)(2,1)}, u32[]{:S(2)}, u32[]{:S(2)}) %all-to-all-start.2) | async-done | bytes 524320 | tf_op jit(solution)/shard_map/all_to_all | solution.py:173
  98.6 1.1 reduce_sum.130
  99.8 0.8 broadcast_in_dim.150
  100.6 4.1 %all-to-all-start.3 = ((bf16[8,64,512]{2,1,0:T(8,128)(2,1)}), bf16[8,64,512]{2,1,0:T(8,128)(2,1)}, u32[]{:S(2)}, u32[]{:S(2)}) async-start(bf16[8,64,512]{2,1,0:T(8,128)(2,1)} %broadcast_in_dim.150), calls=%async_computation.3 | async-start | bytes 1048576 | tf_op jit(solution)/shard_map/all_to_all | solution.py:173
  104.8 0.5 compare_and_fusion.1
  105.3 0.6 pad_clamp_fusion
  106.0 16.5 %all-to-all-done.3 = bf16[8,64,512]{2,1,0:T(8,128)(2,1)} async-done(((bf16[8,64,512]{2,1,0:T(8,128)(2,1)}), bf16[8,64,512]{2,1,0:T(8,128)(2,1)}, u32[]{:S(2)}, u32[]{:S(2)}) %all-to-all-start.3) | async-done | bytes 524320 | tf_op jit(solution)/shard_map/all_to_all | solution.py:173
  122.6 1.1 copy.60
  123.6 0.8 fusion.63
  124.5 2.4 %fusion.64 = bf16[64,256]{1,0:T(8,128)(2,1)S(1)} fusion(bf16[64,4096]{1,0:T(8,128)(2,1)S(1)} %bitcast.178, bf16[256,4096]{1,0:T(8,128)(2,1)} %collective-permute-done.3), kind=kOutput, calls=%fused_computation.167 | convolution fusion | flops 134217728 | bytes 2654208 | tf_op jit(solution)/shard_map/dot_general | solution.py:300
  127.0 0.7 gather_fusion.1
  127.8 0.8 pad_maximum_fusion.2
  128.6 3.5 %all-to-all-start.4 = ((bf16[8,64,128]{2,1,0:T(8,128)(2,1)}), bf16[8,64,128]{2,1,0:T(8,128)(2,1)S(1)}, u32[]{:S(2)}, u32[]{:S(2)}) async-start(bf16[8,64,128]{2,1,0:T(8,128)(2,1)} %pad_maximum_fusion.2), calls=%async_computation.4 | async-start | bytes 262144 | tf_op jit(solution)/shard_map/all_to_all | solution.py:173
  132.1 0.7 exponential_select_fusion
  132.8 5.2 %all-to-all-done.4 = bf16[8,64,128]{2,1,0:T(8,128)(2,1)S(1)} async-done(((bf16[8,64,128]{2,1,0:T(8,128)(2,1)}), bf16[8,64,128]{2,1,0:T(8,128)(2,1)S(1)}, u32[]{:S(2)}, u32[]{:S(2)}) %all-to-all-start.4) | async-done | bytes 131104 | tf_op jit(solution)/shard_map/all_to_all | solution.py:173
  138.3 0.7 multiply_reduce_fusion
  139.3 1.0 convolution_select_fusion
  140.4 0.7 copy.54
  141.2 0.7 broadcast_in_dim.154
  141.9 8.7 %all-to-all-start.5 = ((f32[12,32,128]{2,1,0:T(8,128)}), f32[12,32,128]{2,1,0:T(8,128)S(1)}, u32[]{:S(2)}, u32[]{:S(2)}) async-start(f32[12,32,128]{2,1,0:T(8,128)} %broadcast_in_dim.154), calls=%async_computation.5 | async-start | bytes 393216 | tf_op jit(solution)/shard_map/all_to_all | solution.py:173
  150.9 2.4 %fusion.12 = bf16[512,64]{0,1:T(8,128)(2,1)} fusion(f32[512,64]{0,1:T(8,128)S(1)} %fusion.65, f32[512,512]{1,0:T(8,128)S(1)} %convolution_select_fusion, f32[1,512,64]{1,2,0:T(8,128)S(1)} %fusion.17, f32[512,64]{0,1:T(8,128)S(1)} %get-tuple-element.38, f32[512]{0:T(512)S(1)} %copy-done.13, f32[64]{0:T(128)} %param.15, f32[512]{0:T(512)S(1)} %get-tuple-element.36), kind=kOutput, calls=%fused_computation.22 | convolution fusion | flops 201719808 | bytes 1511680 | tf_op jit(solution)/shard_map/bnd,bdf->bnf/dot_general | solution.py:135
  153.3 1.4 fusion.66
  154.7 9.2 %all-to-all-done.5 = f32[12,32,128]{2,1,0:T(8,128)S(1)} async-done(((f32[12,32,128]{2,1,0:T(8,128)}), f32[12,32,128]{2,1,0:T(8,128)S(1)}, u32[]{:S(2)}, u32[]{:S(2)}) %all-to-all-start.5) | async-done | bytes 196640 | tf_op jit(solution)/shard_map/all_to_all | solution.py:173
  164.5 1.9 %fusion.10 = bf16[512,64]{0,1:T(8,128)(2,1)} fusion(f32[512,64]{0,1:T(8,128)} %fusion.66, f32[64,64]{1,0:T(8,128)S(1)} %fusion.14, f32[512,64]{0,1:T(8,128)S(1)} %get-tuple-element.21, f32[512]{0:T(512)S(1)} %get-tuple-element.39, f32[1,512,64]{1,2,0:T(8,128)S(1)} %fusion.17, f32[512,64]{0,1:T(8,128)S(1)} %get-tuple-element.38, f32[64]{0:T(128)S(1)} %copy-done.19, ...), kind=kOutput, calls=%fused_computation.20 | convolution fusion | flops 25427968 | bytes 610560 | tf_op jit(solution)/shard_map/ely,eyc->elc/dot_general | solution.py:157
  166.4 0.8 fusion.20
  167.2 0.7 fusion.32
  (112 shorter events, 4.3 us)
Async XLA Ops:
  0.6 19.5 %copy-start = (bf16[4096,64]{0,1:T(8,128)(2,1)S(1)}, bf16[4096,64]{0,1:T(8,128)(2,1)}, u32[]{:S(2)}) copy-start(bf16[4096,64]{0,1:T(8,128)(2,1)} %param.12) | copy-start | bytes 1572868
  0.6 46.6 %collective-permute-start.1 = (bf16[64,4096]{1,0:T(8,128)(2,1)}, bf16[64,4096]{1,0:T(8,128)(2,1)}, u32[]{:S(2)}, u32[]{:S(2)}) collective-permute-start(bf16[64,4096]{1,0:T(8,128)(2,1)} %param.14), channel_id=1, source_target_pairs={{0,4},{2,6},{4,0},{6,2},{1,5},{3,7},{5,1},{7,3},{8,12},{10,14},{12... | collective-permute-start | bytes 1572872 | tf_op jit(solution)/shard_map/ppermute | solution.py:184
  5.7 40.4 %collective-permute-start = (bf16[64,4096]{1,0:T(8,128)(2,1)}, bf16[64,4096]{1,0:T(8,128)(2,1)}, u32[]{:S(2)}, u32[]{:S(2)}) collective-permute-start(bf16[64,4096]{1,0:T(8,128)(2,1)} %param.14), channel_id=1, source_target_pairs={{0,2},{2,4},{4,6},{6,0},{1,3},{3,5},{5,7},{7,1},{8,10},{10,12},{12... | collective-permute-start | bytes 1572872 | tf_op jit(solution)/shard_map/ppermute | solution.py:184
  8.2 40.1 %collective-permute-start.2 = (bf16[64,4096]{1,0:T(8,128)(2,1)}, bf16[64,4096]{1,0:T(8,128)(2,1)}, u32[]{:S(2)}, u32[]{:S(2)}) collective-permute-start(bf16[64,4096]{1,0:T(8,128)(2,1)} %param.14), channel_id=1, source_target_pairs={{0,6},{2,0},{4,2},{6,4},{1,7},{3,1},{5,3},{7,5},{8,14},{10,8},{12,... | collective-permute-start | bytes 1572872 | tf_op jit(solution)/shard_map/ppermute | solution.py:184
  16.2 6.0 %copy-start.18 = (f32[64]{0:T(128)}, f32[64]{0:T(128)S(1)}, u32[]{:S(2)}) copy-start(f32[64]{0:T(128)S(1)} %slice_reduce_fusion.1) | copy-start | bytes 772
  16.3 3.9 %copy-start.1 = (bf16[512,4096]{1,0:T(8,128)(2,1)S(1)}, bf16[512,4096]{1,0:T(8,128)(2,1)}, u32[]{:S(2)}) copy-start(bf16[512,4096]{1,0:T(8,128)(2,1)} %param.10) | copy-start | bytes 12582916
  20.2 18.0 %copy-start.10 = (bf16[512,64]{0,1:T(8,128)(2,1)S(1)}, bf16[512,64]{0,1:T(8,128)(2,1)}, u32[]{:S(2)}) copy-start(bf16[512,64]{0,1:T(8,128)(2,1)} %param.19) | copy-start | bytes 196612
  20.2 18.8 %copy-start.5 = (bf16[4096,64]{0,1:T(8,128)(2,1)S(1)}, bf16[4096,64]{0,1:T(8,128)(2,1)}, u32[]{:S(2)}) copy-start(bf16[4096,64]{0,1:T(8,128)(2,1)} %param.11) | copy-start | bytes 1572868
  20.2 18.8 %copy-start.14 = (f32[64]{0:T(128)S(1)}, f32[64]{0:T(128)}, u32[]{:S(2)}) copy-start(f32[64]{0:T(128)} %param.15) | copy-start | bytes 772
  23.4 29.0 %all-to-all-start = ((f32[12,40,128]{2,1,0:T(8,128)}), f32[12,40,128]{2,1,0:T(8,128)S(1)}, u32[]{:S(2)}, u32[]{:S(2)}) async-start(f32[12,40,128]{2,1,0:T(8,128)} %broadcast_in_dim.144), calls=%async_computation | async-start | bytes 491520 | tf_op jit(solution)/shard_map/all_to_all | solution.py:173
  38.2 7.3 %copy-start.21 = (pred[12]{0:T(512)(128)(4,1)}, pred[12]{0:T(512)(128)(4,1)S(1)}, u32[]{:S(2)}) copy-start(pred[12]{0:T(512)(128)(4,1)S(1)} %iota_compare_fusion.3) | copy-start | bytes 40
  42.6 2.9 %copy-start.6 = (bf16[64,4096]{1,0:T(8,128)(2,1)S(1)}, bf16[64,4096]{1,0:T(8,128)(2,1)}, u32[]{:S(2)}) copy-start(bf16[64,4096]{1,0:T(8,128)(2,1)} %param.14) | copy-start | bytes 1572868
  43.6 4.7 %copy-start.2 = (f32[512,512]{1,0:T(8,128)}, f32[512,512]{1,0:T(8,128)S(1)}, u32[]{:S(2)}) copy-start(f32[512,512]{1,0:T(8,128)S(1)} %convolution_select_fusion.1) | copy-start | bytes 3145732
  45.5 4.0 %copy-start.24 = (s32[4]{0:T(128)}, s32[4]{0:T(128)S(1)}, u32[]{:S(2)}) copy-start(s32[4]{0:T(128)S(1)} %get-tuple-element.47) | copy-start | bytes 52
  45.5 4.0 %copy-start.26 = (s32[4]{0:T(128)}, s32[4]{0:T(128)S(1)}, u32[]{:S(2)}) copy-start(s32[4]{0:T(128)S(1)} %get-tuple-element.48) | copy-start | bytes 52
  49.4 19.8 %collective-permute-start.3 = (bf16[256,4096]{1,0:T(8,128)(2,1)S(1)}, bf16[256,4096]{1,0:T(8,128)(2,1)}, u32[]{:S(2)}, u32[]{:S(2)}) collective-permute-start(bf16[256,4096]{1,0:T(8,128)(2,1)S(1)} %constant_dynamic-update-slice_fusion), channel_id=1, source_target_pairs={{0,1},{1,0},{2,3},{3,2},{4,5},{5,4},{6,7},{7,6},{8,9},{9,8},{10,11... | collective-permute-start | bytes 6291464 | tf_op jit(solution)/shard_map/ppermute | solution.py:186
  53.2 7.6 %copy-start.25 = (s32[4]{0:T(128)S(1)}, s32[4]{0:T(128)}, u32[]{:S(2)}) copy-start(s32[4]{0:T(128)} %copy-done.24) | copy-start | bytes 52
  53.2 7.6 %copy-start.27 = (s32[4]{0:T(128)S(1)}, s32[4]{0:T(128)}, u32[]{:S(2)}) copy-start(s32[4]{0:T(128)} %copy-done.26) | copy-start | bytes 52
  53.5 1.3 copy-start.7
  57.4 9.4 %all-to-all-start.1 = ((bf16[8,64,128]{2,1,0:T(8,128)(2,1)}), bf16[8,64,128]{2,1,0:T(8,128)(2,1)S(1)}, u32[]{:S(2)}, u32[]{:S(2)}) async-start(bf16[8,64,128]{2,1,0:T(8,128)(2,1)} %pad_maximum_fusion), calls=%async_computation.1 | async-start | bytes 262144 | tf_op jit(solution)/shard_map/all_to_all | solution.py:173
  69.3 0.6 copy-start.9
  72.0 9.2 %copy-start.4 = (f32[64,8,64]{2,0,1:T(8,128)S(1)}, f32[64,8,64]{2,0,1:T(8,128)}, u32[]{:S(2)}) copy-start(f32[64,8,64]{2,0,1:T(8,128)} %get-tuple-element.28) | copy-start | bytes 393220
  74.1 24.5 %all-to-all-start.2 = ((bf16[8,64,512]{2,1,0:T(8,128)(2,1)}), bf16[8,64,512]{2,1,0:T(8,128)(2,1)}, u32[]{:S(2)}, u32[]{:S(2)}) async-start(bf16[8,64,512]{2,1,0:T(8,128)(2,1)} %bitcast.180), calls=%async_computation.2 | async-start | bytes 1048576 | tf_op jit(solution)/shard_map/all_to_all | solution.py:173
  100.6 22.0 %all-to-all-start.3 = ((bf16[8,64,512]{2,1,0:T(8,128)(2,1)}), bf16[8,64,512]{2,1,0:T(8,128)(2,1)}, u32[]{:S(2)}, u32[]{:S(2)}) async-start(bf16[8,64,512]{2,1,0:T(8,128)(2,1)} %broadcast_in_dim.150), calls=%async_computation.3 | async-start | bytes 1048576 | tf_op jit(solution)/shard_map/all_to_all | solution.py:173
  124.4 3.3 %copy-start.23 = (pred[8]{0:T(512)(128)(4,1)S(1)}, pred[8]{0:T(512)(128)(4,1)}, u32[]{:S(2)}) copy-start(pred[8]{0:T(512)(128)(4,1)} %compare_and_fusion.1) | copy-start | bytes 28
  124.4 7.7 %copy-start.11 = (f32[12,64]{1,0:T(8,128)S(1)}, f32[12,64]{1,0:T(8,128)}, u32[]{:S(2)}) copy-start(f32[12,64]{1,0:T(8,128)} %get-tuple-element.18) | copy-start | bytes 9220
  124.4 7.7 %copy-start.22 = (pred[12]{0:T(512)(128)(4,1)S(1)}, pred[12]{0:T(512)(128)(4,1)}, u32[]{:S(2)}) copy-start(pred[12]{0:T(512)(128)(4,1)} %copy-done.21) | copy-start | bytes 40
  124.4 13.8 %copy-start.20 = (f32[64]{0:T(128)S(1)}, f32[64]{0:T(128)}, u32[]{:S(2)}) copy-start(f32[64]{0:T(128)} %param.16) | copy-start | bytes 772
  128.6 9.4 %all-to-all-start.4 = ((bf16[8,64,128]{2,1,0:T(8,128)(2,1)}), bf16[8,64,128]{2,1,0:T(8,128)(2,1)S(1)}, u32[]{:S(2)}, u32[]{:S(2)}) async-start(bf16[8,64,128]{2,1,0:T(8,128)(2,1)} %pad_maximum_fusion.2), calls=%async_computation.4 | async-start | bytes 262144 | tf_op jit(solution)/shard_map/all_to_all | solution.py:173
  132.1 18.4 %copy-start.8 = (f32[64,64]{1,0:T(8,128)S(1)}, f32[64,64]{1,0:T(8,128)}, u32[]{:S(2)}) copy-start(f32[64,64]{1,0:T(8,128)} %copy-done.7) | copy-start | bytes 49156
  139.0 11.8 %copy-start.13 = (f32[512]{0:T(512)S(1)}, f32[512]{0:T(512)}, u32[]{:S(2)}) copy-start(f32[512]{0:T(512)} %get-tuple-element.20) | copy-start | bytes 6148
  139.3 14.0 %copy-start.3 = (f32[512,512]{1,0:T(8,128)S(1)}, f32[512,512]{1,0:T(8,128)}, u32[]{:S(2)}) copy-start(f32[512,512]{1,0:T(8,128)} %copy-done.2) | copy-start | bytes 3145732
  141.9 22.2 %copy-start.12 = (f32[12,64]{1,0:T(8,128)S(1)}, f32[12,64]{1,0:T(8,128)}, u32[]{:S(2)}) copy-start(f32[12,64]{1,0:T(8,128)} %exponential_select_fusion) | copy-start | bytes 9220
  141.9 22.0 %all-to-all-start.5 = ((f32[12,32,128]{2,1,0:T(8,128)}), f32[12,32,128]{2,1,0:T(8,128)S(1)}, u32[]{:S(2)}, u32[]{:S(2)}) async-start(f32[12,32,128]{2,1,0:T(8,128)} %broadcast_in_dim.154), calls=%async_computation.5 | async-start | bytes 393216 | tf_op jit(solution)/shard_map/all_to_all | solution.py:173
  150.8 13.4 %copy-start.19 = (f32[64]{0:T(128)S(1)}, f32[64]{0:T(128)}, u32[]{:S(2)}) copy-start(f32[64]{0:T(128)} %copy-done.18) | copy-start | bytes 772
  153.3 13.1 %copy-start.15 = (f32[64]{0:T(128)S(1)}, f32[64]{0:T(128)}, u32[]{:S(2)}) copy-start(f32[64]{0:T(128)} %param.15) | copy-start | bytes 772
  154.7 12.5 %copy-start.16 = (f32[512]{0:T(512)S(1)}, f32[512]{0:T(512)}, u32[]{:S(2)}) copy-start(f32[512]{0:T(512)} %get-tuple-element.34) | copy-start | bytes 6148
  154.7 12.5 %copy-start.17 = (f32[512]{0:T(512)S(1)}, f32[512]{0:T(512)}, u32[]{:S(2)}) copy-start(f32[512]{0:T(512)} %get-tuple-element.35) | copy-start | bytes 6148

commit v2 on v0

v2 whole, which is shorter than its diff:
```python
import functools

import jax
import jax.numpy as jnp
from jax import lax
from jax.experimental import pallas as pl
from jax.experimental.pallas import tpu as pltpu
from jax.sharding import Mesh, PartitionSpec as P

LANES = 64
CODES = 64
GRID = {"y": 8, "x": 4, "core": 2}
STEPS = 8
COUNT_BASE = 64

epsilon = 1e-05
log_half = -0.6931471805599453
rate_span = 1.2
f32 = jnp.float32
bf16 = jnp.bfloat16


def nn(a, b):
    return lax.dot_general(
        a, b, (((1,), (0,)), ((), ())), precision=lax.Precision.HIGHEST, preferred_element_type=f32
    )


def nt(a, b):
    return lax.dot_general(
        a, b, (((1,), (1,)), ((), ())), precision=lax.Precision.HIGHEST, preferred_element_type=f32
    )


def tn(a, b):
    return nn(a.T, b)


def column(row):
    n = row.shape[1]
    at = lax.broadcasted_iota(jnp.int32, (n, n), 0)
    on = at == lax.broadcasted_iota(jnp.int32, (n, n), 1)
    return jnp.sum(jnp.where(on, row, 0.0), axis=1, keepdims=True)


def rates(codes_row, all_frames):
    return -rate_span * (column(codes_row.astype(f32)) + 1.0) / float(CODES * all_frames)


def over_channels(array):
    return jnp.mean(array, axis=0, keepdims=True)


def key_norm(keys_raw):
    scale = lax.rsqrt(over_channels(keys_raw * keys_raw) + epsilon)
    return keys_raw * scale * 0.125, scale


def fold(square):
    half = square.shape[0] // 2
    return jnp.concatenate([square[:half], square[half:]], axis=1)


def unfold(packed):
    return jnp.concatenate([packed[:, :LANES], packed[:, LANES:]], axis=0)


def causal(length):
    s = lax.broadcasted_iota(jnp.int32, (length, length), 0)
    return s <= lax.broadcasted_iota(jnp.int32, (length, length), 1)


def keys_kernel(all_frames, x, wk, wv, codes, halvings, payload, keys_raw, values, logs, acc):
    step = pl.program_id(0)

    @pl.when(step == 0)
    def _():
        acc[...] = jnp.zeros_like(acc)

    acc[...] += lax.dot_general(
        jnp.concatenate([wk[...], wv[...]], axis=0),
        x[...],
        (((1,), (1,)), ((), ())),
        preferred_element_type=f32,
    )

    @pl.when(step == STEPS - 1)
    def _():
        length = x.shape[0]
        raw, val = acc[:LANES], acc[LANES:]
        keys_raw[...] = raw
        values[...] = val
        keys, _ = key_norm(raw)
        rate = rates(codes[...], all_frames)
        marks = jnp.broadcast_to(halvings[...].astype(f32).astype(bf16), (16, length))
        ones = jnp.where(causal(length), 1.0, 0.0).astype(bf16)
        counted = jnp.dot(marks, ones, preferred_element_type=f32)[:1]
        at = (lax.broadcasted_iota(jnp.int32, (1, length), 1) + 1).astype(f32)
        prefix = rate * at + log_half * counted
        logs[...] = prefix
        total = counted[:, length - 1 :]
        closing = jnp.exp(rate * float(length) + log_half * total - prefix)
        share = fold(nt(keys * closing, val)).astype(bf16)
        high = jnp.floor(total * (1.0 / COUNT_BASE))
        low = total - high * COUNT_BASE
        top = lax.broadcasted_iota(jnp.int32, (16, 2 * LANES), 0) == 0
        counts = jnp.where(top, high, low).astype(bf16)
        half = LANES // 2
        for z in range(payload.shape[0]):
            payload[z, :half] = share
            payload[z, half:] = counts


def reads_kernel(
    x, wr, keys_raw, values, logs, extra, tutor, reads, scores, local, t0, t1, t2, t3, acc, held
):
    step = pl.program_id(0)

    @pl.when(step == 0)
    def _():
        acc[...] = jnp.zeros_like(acc)

    acc[...] += lax.dot_general(
        wr[...], x[...], (((1,), (1,)), ((), ())), preferred_element_type=f32
    )

    @pl.when(step == STEPS - 1)
    def _():
        length = x.shape[0]
        recept = acc[...]
        reads[...] = recept
        keys, _ = key_norm(keys_raw[...])
        prefix = logs[...]
        val = values[...]
        masked = jnp.where(
            causal(length), tn(keys * jnp.exp(-prefix), recept * jnp.exp(prefix)), 0.0
        )
        scores[...] = masked
        own = jnp.sum(recept * column(extra[...]) * keys, axis=0, keepdims=True)
        local[...] = nn(val, masked) + own * val
        by_frame = tutor[...].astype(f32).T.astype(bf16)
        tiles = GRID["x"] * GRID["core"]
        part = length // tiles
        for i in range(tiles):
            held[i] = fold(by_frame[i * part : (i + 1) * part])
        at = lax.axis_index("x")
        for s, out in enumerate((t0, t1, t2, t3)):
            to = lax.rem(at + s, GRID["x"])
            for c in range(2):
                out[c] = held[to * 2 + c]


def decays(everyone, rate, z, length):
    half = LANES // 2
    total = everyone[z, half : half + 1].astype(f32) * COUNT_BASE + everyone[
        z, half + 1 : half + 2
    ].astype(f32)
    return jnp.exp(rate * float(length) + log_half * total)


def folded_rates(codes_row, all_frames):
    return fold(jnp.broadcast_to(rates(codes_row, all_frames), (LANES, LANES)))


def yields_kernel(all_frames, everyone, local, reads, logs, codes, gain, sent, start, unit, inverse):
    length = local.shape[1]
    mine = lax.axis_index("ctx")
    half = LANES // 2
    rate = folded_rates(codes[...], all_frames)
    state = jnp.zeros((half, 2 * LANES), f32)
    for z in range(everyone.shape[0] - 1):
        longer = decays(everyone, rate, z, length) * state + everyone[z, :half].astype(f32)
        state = jnp.where(z < mine, longer, state)
    begin = unfold(state)
    start[...] = begin
    y = local[...] + tn(begin, reads[...] * jnp.exp(logs[...]))
    centred = y - over_channels(y)
    inv = lax.rsqrt(over_channels(centred * centred) + epsilon)
    inverse[...] = inv
    unit[...] = centred * inv
    normed = (centred * inv * column(gain[...])).T.astype(bf16)
    tiles = GRID["x"] * GRID["core"]
    part = length // tiles
    for i in range(tiles):
        block = fold(normed[i * part : (i + 1) * part])
        for j in range(GRID["y"]):
            sent[j * tiles + i] = block


def spread(blocks):
    cols = []
    for a, b in zip(blocks[::2], blocks[1::2]):
        cols.append(
            jnp.concatenate(
                [
                    jnp.concatenate([a[:, :LANES], b[:, :LANES]], axis=1),
                    jnp.concatenate([a[:, LANES:], b[:, LANES:]], axis=1),
                ],
                axis=0,
            )
        )
    return jnp.concatenate(cols, axis=1)


def by_source(mine, other, x, c):
    step = lax.rem(lax.axis_index("x") - x + GRID["x"], GRID["x"])
    core = lax.axis_index("core")
    return jnp.where(core == c, mine[step, core], other[step, core])


def middle_kernel(
    got, t_mine, t_other, w0, w1, w2, w3, v0, v1, v2, v3, sent, m0, m1, m2, m3, held
):
    at, core = lax.axis_index("x"), lax.axis_index("core")
    tiles = GRID["x"] * GRID["core"]
    rows = GRID["y"]
    group = min(4, rows)
    chunks = []
    for ws, c in (((w0, w1, w2, w3), core), ((v0, v1, v2, v3), 1 - core)):
        for s, w in enumerate(ws):
            x = lax.rem(at - s + GRID["x"], GRID["x"])
            for y in range(0, rows, group):
                chunks.append((w, y, [(y + g) * tiles + x * 2 + c for g in range(group)]))
    acc = None
    for w, y, places in chunks:
        weights = w[y : y + group].reshape(group * LANES, tiles * LANES)
        term = jnp.dot(spread([got[p] for p in places]), weights, preferred_element_type=f32)
        acc = term if acc is None else acc + term
    mixed = acc.astype(bf16)
    for i in range(tiles):
        held[i] = fold(mixed[:, i * LANES : (i + 1) * LANES])
    for s, out in enumerate((m0, m1, m2, m3)):
        to = lax.rem(at + s, GRID["x"])
        for c in range(2):
            out[c] = held[to * 2 + c]
    wanted = spread([by_source(t_mine, t_other, i // 2, i % 2) for i in range(tiles)])
    diff = (mixed.astype(f32) - wanted.astype(f32)).astype(bf16)
    for w, y, places in chunks:
        weights = w[y : y + group].reshape(group * LANES, tiles * LANES)
        grads = lax.dot_general(
            diff, weights, (((1,), (1,)), ((), ())), preferred_element_type=f32
        ).astype(bf16)
        for g, p in enumerate(places):
            sent[p] = fold(grads[:, g * LANES : (g + 1) * LANES])


def back_kernel(got, unit, inverse, gain, reads, logs, payload, sensitivity):
    tiles = GRID["x"] * GRID["core"]
    frames = []
    for i in range(tiles):
        total = got[i].astype(f32)
        for j in range(1, GRID["y"]):
            total = total + got[j * tiles + i].astype(f32)
        frames.append(unfold(total))
    scaled = jnp.concatenate(frames, axis=0).T * column(gain[...])
    each = unit[...]
    grad = inverse[...] * (
        scaled - over_channels(scaled) - each * over_channels(scaled * each)
    )
    sensitivity[...] = grad
    share = fold(nt(reads[...] * jnp.exp(logs[...]), grad)).astype(bf16)
    for z in range(payload.shape[0]):
        payload[z] = share


def window_kernel(
    m_mine, m_other, reads, keys_raw, values, logs, extra, scores, start, sensitivity,
    mixed_out, grad_reads, part_keys, part_values,
):
    length = reads.shape[1]
    tiles = GRID["x"] * GRID["core"]
    mixed_out[...] = (
        jnp.concatenate(
            [
                unfold(by_source(m_mine, m_other, i // 2, i % 2).astype(f32))
                for i in range(tiles)
            ],
            axis=0,
        ).T.astype(bf16)
    )
    recept, val, grad = reads[...], values[...], sensitivity[...]
    keys, _ = key_norm(keys_raw[...])
    prefix = logs[...]
    grow, shrink = jnp.exp(prefix), jnp.exp(-prefix)
    own_weight = column(extra[...])
    twofold = jnp.where(causal(length), tn(val, grad), 0.0)
    progressive = jnp.sum(grad * val, axis=0, keepdims=True) * own_weight
    own = jnp.sum(recept * own_weight * keys, axis=0, keepdims=True)
    grad_reads[...] = (
        grow * (nn(start[...], grad) + nn(keys * shrink, twofold)) + progressive * keys
    ).astype(bf16)
    part_keys[...] = shrink * nt(recept * grow, twofold) + progressive * recept
    part_values[...] = nt(grad, scores[...]) + own * grad


def final_kernel(
    all_frames, later, everyone, part_keys, part_values, keys_raw, values, logs, codes,
    grad_keys, grad_values,
):
    length = keys_raw.shape[1]
    mine = lax.axis_index("ctx")
    half = LANES // 2
    rate = folded_rates(codes[...], all_frames)
    state = jnp.zeros((half, 2 * LANES), f32)
    for z in range(everyone.shape[0] - 1, 0, -1):
        longer = decays(everyone, rate, z, length) * state + later[z].astype(f32)
        state = jnp.where(z > mine, longer, state)
    walking = unfold(state)
    raw = keys_raw[...]
    keys, scale = key_norm(raw)
    prefix = logs[...]
    closing = jnp.exp(prefix[:, length - 1 :] - prefix)
    grad = part_keys[...] + closing * nn(walking, values[...])
    grad_values[...] = (part_values[...] + tn(walking, keys * closing)).astype(bf16)
    grad_keys[...] = (
        0.125 * scale * (grad - scale * scale * raw * over_channels(raw * grad))
    ).astype(bf16)


def call(kernel, outs, args, cost=1 << 23, **more):
    return pl.pallas_call(
        kernel,
        cost_estimate=pl.CostEstimate(flops=1 << 30, transcendentals=0, bytes_accessed=cost),
        out_shape=[jax.ShapeDtypeStruct(shape, kind) for shape, kind in outs],
        **more,
    )(*args)


def exchange(array, axis):
    return lax.all_to_all(array, axis, 0, 0)


def along_x(parts):
    n = GRID["x"]
    return parts[:1] + [
        lax.ppermute(parts[s], "x", [(i, (i + s) % n) for i in range(n)]) for s in range(1, n)
    ]


def swap(array):
    return lax.ppermute(array, "core", [(0, 1), (1, 0)])


def on_device(
    incoming_signals,
    receptor_linear_map,
    lock_linear_map,
    worth_linear_map,
    outbound_linear_map,
    selfward_extra,
    cluster_amplify_level,
    dwindle_powers,
    bisect_indicators,
    tutor_aggregated,
):
    length, width = incoming_signals.shape
    blocks = lax.axis_size("ctx")
    tiles, rows = GRID["x"] * GRID["core"], GRID["y"]
    part = length // tiles
    all_frames = length * blocks
    half = LANES // 2
    head = tuple(GRID)
    flat = (LANES, length)
    block = (part // 2, 2 * LANES)
    barrier = lax.optimization_barrier

    columns = exchange(
        outbound_linear_map.reshape(LANES, rows, tiles * LANES).transpose(1, 0, 2), "y"
    )

    codes = dwindle_powers.reshape(1, LANES)
    extra = selfward_extra.reshape(1, LANES)
    gain = cluster_amplify_level.reshape(1, LANES)
    halvings = bisect_indicators.reshape(1, length)

    depth = width // STEPS
    whole = pl.BlockSpec(memory_space=pltpu.VMEM)
    by_step = [
        pl.BlockSpec((length, depth), lambda k: (0, k)),
        pl.BlockSpec((LANES, depth), lambda k: (0, k)),
    ]
    serial = pltpu.CompilerParams(dimension_semantics=("arbitrary",))
    payload, keys_raw, values, logs = call(
        functools.partial(keys_kernel, all_frames),
        [((blocks, half + 16, 2 * LANES), bf16), (flat, f32), (flat, f32), (flat, f32)],
        (incoming_signals, lock_linear_map.T, worth_linear_map.T, codes, halvings),
        grid=(STEPS,),
        in_specs=[by_step[0], by_step[1], by_step[1], whole, whole],
        out_specs=[whole] * 4,
        scratch_shapes=[pltpu.VMEM((2 * LANES, length), f32)],
        compiler_params=serial,
    )
    reads, scores, local, *tutor = call(
        reads_kernel,
        [(flat, f32), ((length, length), f32), (flat, f32)] + [((2,) + block, bf16)] * GRID["x"],
        (
            incoming_signals, receptor_linear_map.T, keys_raw, values, logs, extra,
            tutor_aggregated.T,
        ),
        grid=(STEPS,),
        in_specs=[by_step[0], by_step[1]] + [whole] * 5,
        out_specs=[whole] * (3 + GRID["x"]),
        scratch_shapes=[pltpu.VMEM(flat, f32), pltpu.VMEM((tiles,) + block, bf16)],
        compiler_params=serial,
    )
    payload, columns, local, *tutor = barrier((payload, columns, local, *tutor))
    everyone = exchange(payload, "ctx")
    w_mine = along_x([columns] * GRID["x"])
    sent, start, unit, inverse = call(
        functools.partial(yields_kernel, all_frames),
        [((rows * tiles,) + block, bf16), ((LANES, LANES), f32), (flat, f32), ((1, length), f32)],
        (everyone, local, reads, logs, codes, gain),
    )
    got = exchange(sent, head)
    w_other = [swap(w) for w in w_mine]
    tutor = jnp.stack(along_x(tutor))
    sent, *mixed = call(
        middle_kernel,
        [((rows * tiles,) + block, bf16)] + [((2,) + block, bf16)] * GRID["x"],
        (got, tutor, swap(tutor), *w_mine, *w_other),
        scratch_shapes=[pltpu.VMEM((tiles,) + block, bf16)],
    )
    got = exchange(sent, head)
    mixed = jnp.stack(along_x(mixed))
    payload, sensitivity = call(
        back_kernel,
        [((blocks, half, 2 * LANES), bf16), (flat, f32)],
        (got, unit, inverse, gain, reads, logs),
    )
    later = exchange(payload, "ctx")
    mixed_out, grad_reads, part_keys, part_values = call(
        window_kernel,
        [(flat, bf16), (flat, bf16), (flat, f32), (flat, f32)],
        (mixed, swap(mixed), reads, keys_raw, values, logs, extra, scores, start, sensitivity),
    )
    grad_keys, grad_values = call(
        functools.partial(final_kernel, all_frames),
        [(flat, bf16), (flat, bf16)],
        (later, everyone, part_keys, part_values, keys_raw, values, logs, codes),
    )
    return (mixed_out.T, grad_reads.T, grad_keys.T, grad_values.T)


def solution(mesh):
    blocks = mesh.shape["ctx"]
    grid = Mesh(mesh.devices.reshape((blocks,) + tuple(GRID.values())), ("ctx",) + tuple(GRID))
    head = tuple(GRID)
    in_specs = (
        P("ctx", None),
        P(None, head),
        P(None, head),
        P(None, head),
        P(head, None),
        P(head),
        P(head),
        P(head),
        P("ctx"),
        P("ctx", head),
    )
    out_specs = (P("ctx", head), P("ctx", head), P("ctx", head), P("ctx", head))
    return jax.shard_map(
        on_device, mesh=grid, in_specs=in_specs, out_specs=out_specs, check_vma=False
    )
```

time: 408 us -> 166 us (0.41)
  the two profiles are of different devices: /device:TPU:16 before, /device:TPU:2 now
where the time goes in v2:
time: 166 us; the launch traced here: 165 us
  starting transfers between devices  97.3 us (59%)
  Pallas kernels  34.8 us (21%)
  waiting for transfers between devices  24.4 us (15%)
  local copies, waits for them, and re-layouts  7.18 us (4%)
    all_to_all x5, starting transfers between devices, exchange(): return lax.all_to_all(array, axis, 0, 0)  52.4 us
    pallas_call x7, Pallas kernels, call(): pl.pallas_call(kernel, cost_estimate=pl.CostEstimate(flops=1 << 30, trans...  34.8 us
    ppermute x9, starting transfers between devices, along_x(): lax.ppermute(parts[s], 'x', [(i, (i + s) % n) for i in range(n)])  32.8 us
    all_to_all x5, waiting for transfers between devices, exchange(): return lax.all_to_all(array, axis, 0, 0)  13.5 us
    ppermute x6, starting transfers between devices, swap(): return lax.ppermute(array, 'core', [(0, 1), (1, 0)])  12.1 us
    ppermute x9, waiting for transfers between devices, along_x(): lax.ppermute(parts[s], 'x', [(i, (i + s) % n) for i in range(n)])  8.4 us
    unnamed x40, local copies, waits for them, and re-layouts  5.27 us
  transfers between devices with their start and end apart: 20, of which 10 were waited for; matrix products, arithmetic and copies ran while one was open for 0% of the time, Pallas kernels for 16%

profile of v2, /device:TPU:2, one launch (start us, length us, event | category | flops | bytes accessed | tf_op | source)
XLA Modules:
  0.0 164.7 jit_solution(2488590182531655629)
XLA Ops:
  0.6 1.9 %copy.17 = bf16[8,8,8,512]{3,2,0,1:T(8,128)(2,1)} copy(bf16[8,8,8,512]{3,2,1,0:T(8,128)(2,1)} %bitcast.29) | data formatting | bytes 1048576 | tf_op jit(solution)/shard_map/reshape | solution.py:368
  2.5 7.1 %all-to-all-start = ((bf16[8,64,512]{2,1,0:T(8,128)(2,1)}), bf16[8,64,512]{2,1,0:T(8,128)(2,1)S(1)}, u32[]{:S(2)}, u32[]{:S(2)}) async-start(bf16[8,64,512]{2,1,0:T(8,128)(2,1)} %bitcast.26), calls=%async_computation | async-start | bytes 1048576 | tf_op jit(solution)/shard_map/all_to_all | solution.py:330
  9.7 7.6 %shard_map.129 = (bf16[12,48,128]{2,1,0:T(8,128)(2,1)}, f32[64,512]{1,0:T(8,128)}, f32[64,512]{1,0:T(8,128)}, f32[64,512]{1,0:T(8,128)}) custom-call(bf16[512,4096]{1,0:T(8,128)(2,1)} %x.3, bf16[64,4096]{1,0:T(8,128)(2,1)} %bitcast.27, bf16[64,4096]{1,0:T(8,128)(2,1)} %bitcast.28, s32[1,64]{1,0:T(1,128)} %bitcast.41, s32[1,512]{1,0:T(1,128)} %bitcast.40), custom_call_target="tpu_custom_call" | custom-call | flops 1073741824 | bytes 8388608 | tf_op jit(solution)/shard_map/pallas_call | solution.py:321
  17.2 8.7 %shard_map.130 = (f32[64,512]{1,0:T(8,128)}, f32[512,512]{1,0:T(8,128)}, f32[64,512]{1,0:T(8,128)}, bf16[2,32,128]{2,1,0:T(8,128)(2,1)}, bf16[2,32,128]{2,1,0:T(...) custom-call(bf16[512,4096]{1,0:T(8,128)(2,1)} %x.3, bf16[64,4096]{1,0:T(8,128)(2,1)} %bitcast.30, ...), custom_call_target="tpu_custom_call" | custom-call | flops 1073741824 | bytes 8388608 | tf_op jit(solution)/shard_map/pallas_call | solution.py:321
  26.0 0.0 copy-start.19
  26.0 0.0 copy-start.18
  26.0 0.0 copy-start.17
  26.0 0.0 copy-start.14
  26.0 1.1 all-to-all-done.w0
  27.1 15.2 %all-to-all-start.1 = ((bf16[12,48,128]{2,1,0:T(8,128)(2,1)}), bf16[12,48,128]{2,1,0:T(8,128)(2,1)S(1)}, u32[]{:S(2)}, u32[]{:S(2)}) async-start(bf16[12,48,128]{2,1,0:T(8,128)(2,1)} %get-tuple-element.48), calls=%async_computation.1 | async-start | bytes 294912 | tf_op jit(solution)/shard_map/all_to_all | solution.py:330
  42.3 2.4 %collective-permute-start.6 = (bf16[8,64,512]{2,1,0:T(8,128)(2,1)S(1)}, bf16[8,64,512]{2,1,0:T(8,128)(2,1)S(1)}, u32[]{:S(2)}, u32[]{:S(2)}) collective-permute-start(bf16[8,64,512]{2,1,0:T(8,128)(2,1)S(1)} %all-to-all-done.w0), channel_id=1, source_target_pairs={{0,6},{2,0},{4,2},{6,4},{1,7},{3,1},{5,3},{7,5},{8,14},{10,8},{12,... | collective-permute-start | bytes 1572872 | tf_op jit(solution)/shard_map/ppermute | solution.py:336
  44.8 4.3 %collective-permute-start.5 = (bf16[8,64,512]{2,1,0:T(8,128)(2,1)S(1)}, bf16[8,64,512]{2,1,0:T(8,128)(2,1)S(1)}, u32[]{:S(2)}, u32[]{:S(2)}) collective-permute-start(bf16[8,64,512]{2,1,0:T(8,128)(2,1)S(1)} %all-to-all-done.w0), channel_id=1, source_target_pairs={{0,4},{2,6},{4,0},{6,2},{1,5},{3,7},{5,1},{7,3},{8,12},{10,14},{12... | collective-permute-start | bytes 1572872 | tf_op jit(solution)/shard_map/ppermute | solution.py:336
  49.1 3.7 %collective-permute-start.4 = (bf16[8,64,512]{2,1,0:T(8,128)(2,1)S(1)}, bf16[8,64,512]{2,1,0:T(8,128)(2,1)S(1)}, u32[]{:S(2)}, u32[]{:S(2)}) collective-permute-start(bf16[8,64,512]{2,1,0:T(8,128)(2,1)S(1)} %all-to-all-done.w0), channel_id=1, source_target_pairs={{0,2},{2,4},{4,6},{6,0},{1,3},{3,5},{5,7},{7,1},{8,10},{10,12},{12... | collective-permute-start | bytes 1572872 | tf_op jit(solution)/shard_map/ppermute | solution.py:336
  52.8 2.5 %all-to-all-done.1.everyone = bf16[12,48,128]{2,1,0:T(8,128)(2,1)S(1)} async-done(((bf16[12,48,128]{2,1,0:T(8,128)(2,1)}), bf16[12,48,128]{2,1,0:T(8,128)(2,1)S(1)}, u32[]{:S(2)}, u32[]{:S(2)}) %all-to-all-start.1) | async-done | bytes 147488 | tf_op jit(solution)/shard_map/all_to_all | solution.py:330
  55.3 0.7 copy-done.10
  56.0 2.7 %shard_map.131 = (bf16[64,32,128]{2,1,0:T(8,128)(2,1)}, f32[64,64]{1,0:T(8,128)}, f32[64,512]{1,0:T(8,128)}, f32[1,512]{1,0:T(1,128)}) custom-call(bf16[12,48,128]{2,1,0:T(8,128)(2,1)} %copy-done.10, f32[64,512]{1,0:T(8,128)} %get-tuple-element.49.local, f32[64,512]{1,0:T(8,128)} %get-tuple-element.50.reads, f32[64,512]{1,0:T(8,128)} %get-tuple-element.42.logs, ...), custom_call_target="tpu_custom_call" | custom-call | flops 1073741824 | bytes 8388608 | tf_op jit(solution)/shard_map/pallas_call | solution.py:321
  58.7 8.9 %all-to-all-start.2 = ((bf16[64,32,128]{2,1,0:T(8,128)(2,1)}), bf16[64,32,128]{2,1,0:T(8,128)(2,1)S(1)}, u32[]{:S(2)}, u32[]{:S(2)}) async-start(bf16[64,32,128]{2,1,0:T(8,128)(2,1)} %get-tuple-element.51), calls=%async_computation.2 | async-start | bytes 1048576 | tf_op jit(solution)/shard_map/all_to_all | solution.py:330
  67.6 2.1 %collective-permute-start.7 = (bf16[8,64,512]{2,1,0:T(8,128)(2,1)S(1)}, bf16[8,64,512]{2,1,0:T(8,128)(2,1)S(1)}, u32[]{:S(2)}, u32[]{:S(2)}) collective-permute-start(bf16[8,64,512]{2,1,0:T(8,128)(2,1)S(1)} %all-to-all-done.w0), channel_id=1, source_target_pairs={{0,1},{1,0},{2,3},{3,2},{4,5},{5,4},{6,7},{7,6},{8,9},{9,8},{10,11... | collective-permute-start | bytes 1572872 | tf_op jit(solution)/shard_map/ppermute | solution.py:341
  69.7 0.0 collective-permute-done.6.w3
  69.7 0.0 copy-start.2
  69.7 2.3 %collective-permute-start.10 = (bf16[8,64,512]{2,1,0:T(8,128)(2,1)S(1)}, bf16[8,64,512]{2,1,0:T(8,128)(2,1)S(1)}, u32[]{:S(2)}, u32[]{:S(2)}) collective-permute-start(bf16[8,64,512]{2,1,0:T(8,128)(2,1)S(1)} %collective-permute-done.6.w3), channel_id=1, source_target_pairs={{0,1},{1,0},{2,3},{3,2},{4,5},{5,4},{6,7},{7,6},{8,9},{9,8},{10,11... | collective-permute-start | bytes 1572872 | tf_op jit(solution)/shard_map/ppermute | solution.py:341
  72.0 0.0 collective-permute-done.5.w2
  72.0 2.1 %collective-permute-start.9 = (bf16[8,64,512]{2,1,0:T(8,128)(2,1)S(1)}, bf16[8,64,512]{2,1,0:T(8,128)(2,1)S(1)}, u32[]{:S(2)}, u32[]{:S(2)}) collective-permute-start(bf16[8,64,512]{2,1,0:T(8,128)(2,1)S(1)} %collective-permute-done.5.w2), channel_id=1, source_target_pairs={{0,1},{1,0},{2,3},{3,2},{4,5},{5,4},{6,7},{7,6},{8,9},{9,8},{10,11... | collective-permute-start | bytes 1572872 | tf_op jit(solution)/shard_map/ppermute | solution.py:341
  74.1 1.1 collective-permute-done.4.w1
  75.1 1.9 %collective-permute-start.8 = (bf16[8,64,512]{2,1,0:T(8,128)(2,1)S(1)}, bf16[8,64,512]{2,1,0:T(8,128)(2,1)}, u32[]{:S(2)}, u32[]{:S(2)}) collective-permute-start(bf16[8,64,512]{2,1,0:T(8,128)(2,1)S(1)} %collective-permute-done.4.w1), channel_id=1, source_target_pairs={{0,1},{1,0},{2,3},{3,2},{4,5},{5,4},{6,7},{7,6},{8,9},{9,8},{10,11... | collective-permute-start | bytes 1572872 | tf_op jit(solution)/shard_map/ppermute | solution.py:341
  77.1 3.0 %collective-permute-start = (bf16[2,32,128]{2,1,0:T(8,128)(2,1)S(1)}, bf16[2,32,128]{2,1,0:T(8,128)(2,1)S(1)}, u32[]{:S(2)}, u32[]{:S(2)}) collective-permute-start(bf16[2,32,128]{2,1,0:T(8,128)(2,1)S(1)} %copy-done.19), channel_id=1, source_target_pairs={{0,2},{2,4},{4,6},{6,0},{1,3},{3,5},{5,7},{7,1},{8,10},{10,12},{12... | collective-permute-start | bytes 49160 | tf_op jit(solution)/shard_map/ppermute | solution.py:336
  80.1 2.7 %collective-permute-done = bf16[2,32,128]{2,1,0:T(8,128)(2,1)S(1)} collective-permute-done((bf16[2,32,128]{2,1,0:T(8,128)(2,1)S(1)}, bf16[2,32,128]{2,1,0:T(8,128)(2,1)S(1)}, u32[]{:S(2)}, u32[]{:S(2)}) %collective-permute-start) | collective-permute-done | bytes 16416 | tf_op jit(solution)/shard_map/ppermute | solution.py:336
  82.7 0.0 copy-done.18
  82.8 3.9 %collective-permute-start.1 = (bf16[2,32,128]{2,1,0:T(8,128)(2,1)S(1)}, bf16[2,32,128]{2,1,0:T(8,128)(2,1)S(1)}, u32[]{:S(2)}, u32[]{:S(2)}) collective-permute-start(bf16[2,32,128]{2,1,0:T(8,128)(2,1)S(1)} %copy-done.18), channel_id=1, source_target_pairs={{0,4},{2,6},{4,0},{6,2},{1,5},{3,7},{5,1},{7,3},{8,12},{10,14},{12... | collective-permute-start | bytes 49160 | tf_op jit(solution)/shard_map/ppermute | solution.py:336
  86.6 3.3 %collective-permute-done.1 = bf16[2,32,128]{2,1,0:T(8,128)(2,1)S(1)} collective-permute-done((bf16[2,32,128]{2,1,0:T(8,128)(2,1)S(1)}, bf16[2,32,128]{2,1,0:T(8,128)(2,1)S(1)}, u32[]{:S(2)}, u32[]{:S(2)}) %collective-permute-start.1) | collective-permute-done | bytes 16416 | tf_op jit(solution)/shard_map/ppermute | solution.py:336
  89.9 5.0 %collective-permute-start.2 = (bf16[2,32,128]{2,1,0:T(8,128)(2,1)S(1)}, bf16[2,32,128]{2,1,0:T(8,128)(2,1)S(1)}, u32[]{:S(2)}, u32[]{:S(2)}) collective-permute-start(bf16[2,32,128]{2,1,0:T(8,128)(2,1)S(1)} %copy-done.17), channel_id=1, source_target_pairs={{0,6},{2,0},{4,2},{6,4},{1,7},{3,1},{5,3},{7,5},{8,14},{10,8},{12,... | collective-permute-start | bytes 49160 | tf_op jit(solution)/shard_map/ppermute | solution.py:336
  94.9 1.4 collective-permute-done.2
  96.3 0.0 copy-done.14
  96.3 0.0 copy-start.9
  96.3 1.9 %collective-permute-start.3 = (bf16[4,2,32,128]{3,2,1,0:T(8,128)(2,1)S(1)}, bf16[4,2,32,128]{3,2,1,0:T(8,128)(2,1)S(1)}, u32[]{:S(2)}, u32[]{:S(2)}) collective-permute-start(bf16[4,2,32,128]{3,2,1,0:T(8,128)(2,1)S(1)} %pad_maximum_fusion.t_mine), channel_id=1, source_target_pairs={{0,1},{1,0},{2,3},{3,2},{4,5},{5,4},{6,7},{7,6},{8,9},{9,8},{10,11... | collective-permute-start | bytes 196616 | tf_op jit(solution)/shard_map/ppermute | solution.py:341
  98.3 1.2 collective-permute-done.3.t_other
  99.5 0.0 collective-permute-done.7.v0
  99.5 0.0 collective-permute-done.10.v3
  99.5 0.0 collective-permute-done.9.v2
  99.5 0.9 copy-done.6
  100.4 0.8 copy-done.7
  101.2 0.0 collective-permute-done.8.v1
  101.2 0.0 all-to-all-done.2.got
  101.2 0.8 copy-done.1
  102.0 5.4 %shard_map.132 = (bf16[64,32,128]{2,1,0:T(8,128)(2,1)}, bf16[2,32,128]{2,1,0:T(8,128)(2,1)}, bf16[2,32,128]{2,1,0:T(8,128)(2,1)}, bf16[2,32,128]{2,1,0:T(8,128)(2,1)}, bf16[2,32,128]{2,1,0:T(8,128)(2,1)}) custom-call(bf16[64,32,128]{2,1,0:T(8,128)(2,1)} %copy-done.1, bf16[4,2,32,128]{3,2,1,0:T(8,128)(2,1)} %copy-done.9, bf16[4,2,32,128]{3,2,1,0:T(8,128)(2,1)} %copy-done.12, ...), custom_call_target="tpu_custom_call" | custom-call | flops 1073741824 | bytes 8388608 | tf_op jit(solution)/shard_map/pallas_call | solution.py:321
  107.5 10.4 %all-to-all-start.3 = ((bf16[64,32,128]{2,1,0:T(8,128)(2,1)}), bf16[64,32,128]{2,1,0:T(8,128)(2,1)S(1)}, u32[]{:S(2)}, u32[]{:S(2)}) async-start(bf16[64,32,128]{2,1,0:T(8,128)(2,1)} %get-tuple-element.63), calls=%async_computation.3 | async-start | bytes 1048576 | tf_op jit(solution)/shard_map/all_to_all | solution.py:330
  117.9 3.4 %collective-permute-start.11 = (bf16[2,32,128]{2,1,0:T(8,128)(2,1)}, bf16[2,32,128]{2,1,0:T(8,128)(2,1)S(1)}, u32[]{:S(2)}, u32[]{:S(2)}) collective-permute-start(bf16[2,32,128]{2,1,0:T(8,128)(2,1)} %get-tuple-element.58), channel_id=1, source_target_pairs={{0,2},{2,4},{4,6},{6,0},{1,3},{3,5},{5,7},{7,1},{8,10},{10,12},{12... | collective-permute-start | bytes 49160 | tf_op jit(solution)/shard_map/ppermute | solution.py:336
  121.3 3.0 %collective-permute-start.12 = (bf16[2,32,128]{2,1,0:T(8,128)(2,1)}, bf16[2,32,128]{2,1,0:T(8,128)(2,1)S(1)}, u32[]{:S(2)}, u32[]{:S(2)}) collective-permute-start(bf16[2,32,128]{2,1,0:T(8,128)(2,1)} %get-tuple-element.59), channel_id=1, source_target_pairs={{0,4},{2,6},{4,0},{6,2},{1,5},{3,7},{5,1},{7,3},{8,12},{10,14},{12... | collective-permute-start | bytes 49160 | tf_op jit(solution)/shard_map/ppermute | solution.py:336
  124.2 4.1 %collective-permute-start.13 = (bf16[2,32,128]{2,1,0:T(8,128)(2,1)}, bf16[2,32,128]{2,1,0:T(8,128)(2,1)S(1)}, u32[]{:S(2)}, u32[]{:S(2)}) collective-permute-start(bf16[2,32,128]{2,1,0:T(8,128)(2,1)} %get-tuple-element.60), channel_id=1, source_target_pairs={{0,6},{2,0},{4,2},{6,4},{1,7},{3,1},{5,3},{7,5},{8,14},{10,8},{12,... | collective-permute-start | bytes 49160 | tf_op jit(solution)/shard_map/ppermute | solution.py:336
  128.3 7.1 %all-to-all-done.3.got = bf16[64,32,128]{2,1,0:T(8,128)(2,1)S(1)} async-done(((bf16[64,32,128]{2,1,0:T(8,128)(2,1)}), bf16[64,32,128]{2,1,0:T(8,128)(2,1)S(1)}, u32[]{:S(2)}, u32[]{:S(2)}) %all-to-all-start.3) | async-done | bytes 524320 | tf_op jit(solution)/shard_map/all_to_all | solution.py:330
  135.4 0.8 copy-done.8
  136.3 2.4 %shard_map.133 = (bf16[12,32,128]{2,1,0:T(8,128)(2,1)}, f32[64,512]{1,0:T(8,128)}) custom-call(bf16[64,32,128]{2,1,0:T(8,128)(2,1)} %copy-done.8, f32[64,512]{1,0:T(8,128)} %get-tuple-element.64.unit, f32[1,512]{1,0:T(1,128)} %get-tuple-element.65.inverse, f32[1,64]{1,0:T(1,128)} %bitcast.47, f32[64,512]{1,0:T(8,128)} %get-tuple-element.50.reads, ...), custom_call_target="tpu_custom_call" | custom-call | flops 1073741824 | bytes 8388608 | tf_op jit(solution)/shard_map/pallas_call | solution.py:321
  138.7 10.9 %all-to-all-start.4 = ((bf16[12,32,128]{2,1,0:T(8,128)(2,1)}), bf16[12,32,128]{2,1,0:T(8,128)(2,1)S(1)}, u32[]{:S(2)}, u32[]{:S(2)}) async-start(bf16[12,32,128]{2,1,0:T(8,128)(2,1)} %get-tuple-element.69), calls=%async_computation.4 | async-start | bytes 196608 | tf_op jit(solution)/shard_map/all_to_all | solution.py:330
  149.6 0.0 collective-permute-done.11
  149.6 0.0 collective-permute-done.12
  149.6 0.0 collective-permute-done.13
  149.6 0.0 copy-start.13
  149.6 1.9 %collective-permute-start.14 = (bf16[4,2,32,128]{3,2,1,0:T(8,128)(2,1)S(1)}, bf16[4,2,32,128]{3,2,1,0:T(8,128)(2,1)S(1)}, u32[]{:S(2)}, u32[]{:S(2)}) collective-permute-start(bf16[4,2,32,128]{3,2,1,0:T(8,128)(2,1)S(1)} %pad_maximum_fusion.1.m_mine), channel_id=1, source_target_pairs={{0,1},{1,0},{2,3},{3,2},{4,5},{5,4},{6,7},{7,6},{8,9},{9,8},{10,11... | collective-permute-start | bytes 196616 | tf_op jit(solution)/shard_map/ppermute | solution.py:341
  151.6 1.2 collective-permute-done.14.m_other
  152.8 0.6 copy-done.16
  153.4 5.4 %shard_map.134 = (bf16[64,512]{1,0:T(8,128)(2,1)}, bf16[64,512]{1,0:T(8,128)(2,1)}, f32[64,512]{1,0:T(8,128)}, f32[64,512]{1,0:T(8,128)}) custom-call(bf16[4,2,32,128]{3,2,1,0:T(8,128)(2,1)} %copy-done.13, bf16[4,2,32,128]{3,2,1,0:T(8,128)(2,1)} %copy-done.16, f32[64,512]{1,0:T(8,128)} %get-tuple-element.50.reads, f32[64,512]{1,0:T(8,128)} %get-tuple-element.40.keys_raw, ...), custom_call_target="tpu_custom_call" | custom-call | flops 1073741824 | bytes 8388608 | tf_op jit(solution)/shard_map/pallas_call | solution.py:321
  158.9 2.8 %all-to-all-done.4.later = bf16[12,32,128]{2,1,0:T(8,128)(2,1)S(1)} async-done(((bf16[12,32,128]{2,1,0:T(8,128)(2,1)}), bf16[12,32,128]{2,1,0:T(8,128)(2,1)S(1)}, u32[]{:S(2)}, u32[]{:S(2)}) %all-to-all-start.4) | async-done | bytes 98336 | tf_op jit(solution)/shard_map/all_to_all | solution.py:330
  161.7 0.6 copy-done.11
  162.3 2.4 %shard_map.135 = (bf16[64,512]{1,0:T(8,128)(2,1)}, bf16[64,512]{1,0:T(8,128)(2,1)}) custom-call(bf16[12,32,128]{2,1,0:T(8,128)(2,1)} %copy-done.11, bf16[12,48,128]{2,1,0:T(8,128)(2,1)} %copy-done.10, f32[64,512]{1,0:T(8,128)} %get-tuple-element.70.part_keys, f32[64,512]{1,0:T(8,128)} %get-tuple-element.71.part_values, ...), custom_call_target="tpu_custom_call" | custom-call | flops 1073741824 | bytes 8388608 | tf_op jit(solution)/shard_map/pallas_call | solution.py:321
  (26 shorter events, 0.1 us)
Async XLA Ops:
  2.5 24.6 %all-to-all-start = ((bf16[8,64,512]{2,1,0:T(8,128)(2,1)}), bf16[8,64,512]{2,1,0:T(8,128)(2,1)S(1)}, u32[]{:S(2)}, u32[]{:S(2)}) async-start(bf16[8,64,512]{2,1,0:T(8,128)(2,1)} %bitcast.26), calls=%async_computation | async-start | bytes 1048576 | tf_op jit(solution)/shard_map/all_to_all | solution.py:330
  26.0 51.1 %copy-start.19 = (bf16[2,32,128]{2,1,0:T(8,128)(2,1)S(1)}, bf16[2,32,128]{2,1,0:T(8,128)(2,1)}, u32[]{:S(2)}) copy-start(bf16[2,32,128]{2,1,0:T(8,128)(2,1)} %get-tuple-element.53) | copy-start | bytes 49156
  26.0 56.8 %copy-start.18 = (bf16[2,32,128]{2,1,0:T(8,128)(2,1)S(1)}, bf16[2,32,128]{2,1,0:T(8,128)(2,1)}, u32[]{:S(2)}) copy-start(bf16[2,32,128]{2,1,0:T(8,128)(2,1)} %get-tuple-element.54) | copy-start | bytes 49156
  26.0 63.9 %copy-start.17 = (bf16[2,32,128]{2,1,0:T(8,128)(2,1)S(1)}, bf16[2,32,128]{2,1,0:T(8,128)(2,1)}, u32[]{:S(2)}) copy-start(bf16[2,32,128]{2,1,0:T(8,128)(2,1)} %get-tuple-element.55) | copy-start | bytes 49156
  26.0 70.3 %copy-start.14 = (bf16[2,32,128]{2,1,0:T(8,128)(2,1)S(1)}, bf16[2,32,128]{2,1,0:T(8,128)(2,1)}, u32[]{:S(2)}) copy-start(bf16[2,32,128]{2,1,0:T(8,128)(2,1)} %get-tuple-element.52) | copy-start | bytes 49156
  27.1 74.0 %copy-start = (bf16[8,64,512]{2,1,0:T(8,128)(2,1)}, bf16[8,64,512]{2,1,0:T(8,128)(2,1)S(1)}, u32[]{:S(2)}) copy-start(bf16[8,64,512]{2,1,0:T(8,128)(2,1)S(1)} %all-to-all-done.w0) | copy-start | bytes 1572868
  27.1 28.2 %all-to-all-start.1 = ((bf16[12,48,128]{2,1,0:T(8,128)(2,1)}), bf16[12,48,128]{2,1,0:T(8,128)(2,1)S(1)}, u32[]{:S(2)}, u32[]{:S(2)}) async-start(bf16[12,48,128]{2,1,0:T(8,128)(2,1)} %get-tuple-element.48), calls=%async_computation.1 | async-start | bytes 294912 | tf_op jit(solution)/shard_map/all_to_all | solution.py:330
  42.3 27.4 %collective-permute-start.6 = (bf16[8,64,512]{2,1,0:T(8,128)(2,1)S(1)}, bf16[8,64,512]{2,1,0:T(8,128)(2,1)S(1)}, u32[]{:S(2)}, u32[]{:S(2)}) collective-permute-start(bf16[8,64,512]{2,1,0:T(8,128)(2,1)S(1)} %all-to-all-done.w0), channel_id=1, source_target_pairs={{0,6},{2,0},{4,2},{6,4},{1,7},{3,1},{5,3},{7,5},{8,14},{10,8},{12,... | collective-permute-start | bytes 1572872 | tf_op jit(solution)/shard_map/ppermute | solution.py:336
  44.8 27.2 %collective-permute-start.5 = (bf16[8,64,512]{2,1,0:T(8,128)(2,1)S(1)}, bf16[8,64,512]{2,1,0:T(8,128)(2,1)S(1)}, u32[]{:S(2)}, u32[]{:S(2)}) collective-permute-start(bf16[8,64,512]{2,1,0:T(8,128)(2,1)S(1)} %all-to-all-done.w0), channel_id=1, source_target_pairs={{0,4},{2,6},{4,0},{6,2},{1,5},{3,7},{5,1},{7,3},{8,12},{10,14},{12... | collective-permute-start | bytes 1572872 | tf_op jit(solution)/shard_map/ppermute | solution.py:336
  49.1 26.0 %collective-permute-start.4 = (bf16[8,64,512]{2,1,0:T(8,128)(2,1)S(1)}, bf16[8,64,512]{2,1,0:T(8,128)(2,1)S(1)}, u32[]{:S(2)}, u32[]{:S(2)}) collective-permute-start(bf16[8,64,512]{2,1,0:T(8,128)(2,1)S(1)} %all-to-all-done.w0), channel_id=1, source_target_pairs={{0,2},{2,4},{4,6},{6,0},{1,3},{3,5},{5,7},{7,1},{8,10},{10,12},{12... | collective-permute-start | bytes 1572872 | tf_op jit(solution)/shard_map/ppermute | solution.py:336
  55.3 0.7 copy-start.10
  58.7 42.5 %all-to-all-start.2 = ((bf16[64,32,128]{2,1,0:T(8,128)(2,1)}), bf16[64,32,128]{2,1,0:T(8,128)(2,1)S(1)}, u32[]{:S(2)}, u32[]{:S(2)}) async-start(bf16[64,32,128]{2,1,0:T(8,128)(2,1)} %get-tuple-element.51), calls=%async_computation.2 | async-start | bytes 1048576 | tf_op jit(solution)/shard_map/all_to_all | solution.py:330
  67.6 31.9 %collective-permute-start.7 = (bf16[8,64,512]{2,1,0:T(8,128)(2,1)S(1)}, bf16[8,64,512]{2,1,0:T(8,128)(2,1)S(1)}, u32[]{:S(2)}, u32[]{:S(2)}) collective-permute-start(bf16[8,64,512]{2,1,0:T(8,128)(2,1)S(1)} %all-to-all-done.w0), channel_id=1, source_target_pairs={{0,1},{1,0},{2,3},{3,2},{4,5},{5,4},{6,7},{7,6},{8,9},{9,8},{10,11... | collective-permute-start | bytes 1572872 | tf_op jit(solution)/shard_map/ppermute | solution.py:341
  69.7 31.5 %copy-start.2 = (bf16[8,64,512]{2,1,0:T(8,128)(2,1)}, bf16[8,64,512]{2,1,0:T(8,128)(2,1)S(1)}, u32[]{:S(2)}) copy-start(bf16[8,64,512]{2,1,0:T(8,128)(2,1)S(1)} %collective-permute-done.6.w3) | copy-start | bytes 1572868
  69.7 29.8 %collective-permute-start.10 = (bf16[8,64,512]{2,1,0:T(8,128)(2,1)S(1)}, bf16[8,64,512]{2,1,0:T(8,128)(2,1)S(1)}, u32[]{:S(2)}, u32[]{:S(2)}) collective-permute-start(bf16[8,64,512]{2,1,0:T(8,128)(2,1)S(1)} %collective-permute-done.6.w3), channel_id=1, source_target_pairs={{0,1},{1,0},{2,3},{3,2},{4,5},{5,4},{6,7},{7,6},{8,9},{9,8},{10,11... | collective-permute-start | bytes 1572872 | tf_op jit(solution)/shard_map/ppermute | solution.py:341
  72.0 29.2 %copy-start.3 = (bf16[8,64,512]{2,1,0:T(8,128)(2,1)}, bf16[8,64,512]{2,1,0:T(8,128)(2,1)S(1)}, u32[]{:S(2)}) copy-start(bf16[8,64,512]{2,1,0:T(8,128)(2,1)S(1)} %collective-permute-done.5.w2) | copy-start | bytes 1572868
  72.0 27.5 %collective-permute-start.9 = (bf16[8,64,512]{2,1,0:T(8,128)(2,1)S(1)}, bf16[8,64,512]{2,1,0:T(8,128)(2,1)S(1)}, u32[]{:S(2)}, u32[]{:S(2)}) collective-permute-start(bf16[8,64,512]{2,1,0:T(8,128)(2,1)S(1)} %collective-permute-done.5.w2), channel_id=1, source_target_pairs={{0,1},{1,0},{2,3},{3,2},{4,5},{5,4},{6,7},{7,6},{8,9},{9,8},{10,11... | collective-permute-start | bytes 1572872 | tf_op jit(solution)/shard_map/ppermute | solution.py:341
  75.1 26.1 %copy-start.4 = (bf16[8,64,512]{2,1,0:T(8,128)(2,1)}, bf16[8,64,512]{2,1,0:T(8,128)(2,1)S(1)}, u32[]{:S(2)}) copy-start(bf16[8,64,512]{2,1,0:T(8,128)(2,1)S(1)} %collective-permute-done.4.w1) | copy-start | bytes 1572868
  75.1 26.0 %collective-permute-start.8 = (bf16[8,64,512]{2,1,0:T(8,128)(2,1)S(1)}, bf16[8,64,512]{2,1,0:T(8,128)(2,1)}, u32[]{:S(2)}, u32[]{:S(2)}) collective-permute-start(bf16[8,64,512]{2,1,0:T(8,128)(2,1)S(1)} %collective-permute-done.4.w1), channel_id=1, source_target_pairs={{0,1},{1,0},{2,3},{3,2},{4,5},{5,4},{6,7},{7,6},{8,9},{9,8},{10,11... | collective-permute-start | bytes 1572872 | tf_op jit(solution)/shard_map/ppermute | solution.py:341
  77.1 5.7 %collective-permute-start = (bf16[2,32,128]{2,1,0:T(8,128)(2,1)S(1)}, bf16[2,32,128]{2,1,0:T(8,128)(2,1)S(1)}, u32[]{:S(2)}, u32[]{:S(2)}) collective-permute-start(bf16[2,32,128]{2,1,0:T(8,128)(2,1)S(1)} %copy-done.19), channel_id=1, source_target_pairs={{0,2},{2,4},{4,6},{6,0},{1,3},{3,5},{5,7},{7,1},{8,10},{10,12},{12... | collective-permute-start | bytes 49160 | tf_op jit(solution)/shard_map/ppermute | solution.py:336
  82.8 7.1 %collective-permute-start.1 = (bf16[2,32,128]{2,1,0:T(8,128)(2,1)S(1)}, bf16[2,32,128]{2,1,0:T(8,128)(2,1)S(1)}, u32[]{:S(2)}, u32[]{:S(2)}) collective-permute-start(bf16[2,32,128]{2,1,0:T(8,128)(2,1)S(1)} %copy-done.18), channel_id=1, source_target_pairs={{0,4},{2,6},{4,0},{6,2},{1,5},{3,7},{5,1},{7,3},{8,12},{10,14},{12... | collective-permute-start | bytes 49160 | tf_op jit(solution)/shard_map/ppermute | solution.py:336
  89.9 6.4 %collective-permute-start.2 = (bf16[2,32,128]{2,1,0:T(8,128)(2,1)S(1)}, bf16[2,32,128]{2,1,0:T(8,128)(2,1)S(1)}, u32[]{:S(2)}, u32[]{:S(2)}) collective-permute-start(bf16[2,32,128]{2,1,0:T(8,128)(2,1)S(1)} %copy-done.17), channel_id=1, source_target_pairs={{0,6},{2,0},{4,2},{6,4},{1,7},{3,1},{5,3},{7,5},{8,14},{10,8},{12,... | collective-permute-start | bytes 49160 | tf_op jit(solution)/shard_map/ppermute | solution.py:336
  96.3 4.9 %copy-start.9 = (bf16[4,2,32,128]{3,2,1,0:T(8,128)(2,1)}, bf16[4,2,32,128]{3,2,1,0:T(8,128)(2,1)S(1)}, u32[]{:S(2)}) copy-start(bf16[4,2,32,128]{3,2,1,0:T(8,128)(2,1)S(1)} %pad_maximum_fusion.t_mine) | copy-start | bytes 196612
  96.3 3.1 %collective-permute-start.3 = (bf16[4,2,32,128]{3,2,1,0:T(8,128)(2,1)S(1)}, bf16[4,2,32,128]{3,2,1,0:T(8,128)(2,1)S(1)}, u32[]{:S(2)}, u32[]{:S(2)}) collective-permute-start(bf16[4,2,32,128]{3,2,1,0:T(8,128)(2,1)S(1)} %pad_maximum_fusion.t_mine), channel_id=1, source_target_pairs={{0,1},{1,0},{2,3},{3,2},{4,5},{5,4},{6,7},{7,6},{8,9},{9,8},{10,11... | collective-permute-start | bytes 196616 | tf_op jit(solution)/shard_map/ppermute | solution.py:341
  99.5 1.7 %copy-start.12 = (bf16[4,2,32,128]{3,2,1,0:T(8,128)(2,1)}, bf16[4,2,32,128]{3,2,1,0:T(8,128)(2,1)S(1)}, u32[]{:S(2)}) copy-start(bf16[4,2,32,128]{3,2,1,0:T(8,128)(2,1)S(1)} %collective-permute-done.3.t_other) | copy-start | bytes 196612
  99.5 1.7 %copy-start.5 = (bf16[8,64,512]{2,1,0:T(8,128)(2,1)}, bf16[8,64,512]{2,1,0:T(8,128)(2,1)S(1)}, u32[]{:S(2)}) copy-start(bf16[8,64,512]{2,1,0:T(8,128)(2,1)S(1)} %collective-permute-done.7.v0) | copy-start | bytes 1572868
  99.5 0.9 copy-start.6
  100.4 0.8 copy-start.7
  101.2 0.8 copy-start.1
  107.5 42.1 %copy-start.15 = (bf16[2,32,128]{2,1,0:T(8,128)(2,1)S(1)}, bf16[2,32,128]{2,1,0:T(8,128)(2,1)}, u32[]{:S(2)}) copy-start(bf16[2,32,128]{2,1,0:T(8,128)(2,1)} %get-tuple-element.57) | copy-start | bytes 49156
  107.5 27.9 %all-to-all-start.3 = ((bf16[64,32,128]{2,1,0:T(8,128)(2,1)}), bf16[64,32,128]{2,1,0:T(8,128)(2,1)S(1)}, u32[]{:S(2)}, u32[]{:S(2)}) async-start(bf16[64,32,128]{2,1,0:T(8,128)(2,1)} %get-tuple-element.63), calls=%async_computation.3 | async-start | bytes 1048576 | tf_op jit(solution)/shard_map/all_to_all | solution.py:330
  117.9 31.7 %collective-permute-start.11 = (bf16[2,32,128]{2,1,0:T(8,128)(2,1)}, bf16[2,32,128]{2,1,0:T(8,128)(2,1)S(1)}, u32[]{:S(2)}, u32[]{:S(2)}) collective-permute-start(bf16[2,32,128]{2,1,0:T(8,128)(2,1)} %get-tuple-element.58), channel_id=1, source_target_pairs={{0,2},{2,4},{4,6},{6,0},{1,3},{3,5},{5,7},{7,1},{8,10},{10,12},{12... | collective-permute-start | bytes 49160 | tf_op jit(solution)/shard_map/ppermute | solution.py:336
  121.3 28.3 %collective-permute-start.12 = (bf16[2,32,128]{2,1,0:T(8,128)(2,1)}, bf16[2,32,128]{2,1,0:T(8,128)(2,1)S(1)}, u32[]{:S(2)}, u32[]{:S(2)}) collective-permute-start(bf16[2,32,128]{2,1,0:T(8,128)(2,1)} %get-tuple-element.59), channel_id=1, source_target_pairs={{0,4},{2,6},{4,0},{6,2},{1,5},{3,7},{5,1},{7,3},{8,12},{10,14},{12... | collective-permute-start | bytes 49160 | tf_op jit(solution)/shard_map/ppermute | solution.py:336
  124.2 25.4 %collective-permute-start.13 = (bf16[2,32,128]{2,1,0:T(8,128)(2,1)}, bf16[2,32,128]{2,1,0:T(8,128)(2,1)S(1)}, u32[]{:S(2)}, u32[]{:S(2)}) collective-permute-start(bf16[2,32,128]{2,1,0:T(8,128)(2,1)} %get-tuple-element.60), channel_id=1, source_target_pairs={{0,6},{2,0},{4,2},{6,4},{1,7},{3,1},{5,3},{7,5},{8,14},{10,8},{12,... | collective-permute-start | bytes 49160 | tf_op jit(solution)/shard_map/ppermute | solution.py:336
  135.4 0.8 copy-start.8
  138.7 22.9 %all-to-all-start.4 = ((bf16[12,32,128]{2,1,0:T(8,128)(2,1)}), bf16[12,32,128]{2,1,0:T(8,128)(2,1)S(1)}, u32[]{:S(2)}, u32[]{:S(2)}) async-start(bf16[12,32,128]{2,1,0:T(8,128)(2,1)} %get-tuple-element.69), calls=%async_computation.4 | async-start | bytes 196608 | tf_op jit(solution)/shard_map/all_to_all | solution.py:330
  149.6 3.2 %copy-start.13 = (bf16[4,2,32,128]{3,2,1,0:T(8,128)(2,1)}, bf16[4,2,32,128]{3,2,1,0:T(8,128)(2,1)S(1)}, u32[]{:S(2)}) copy-start(bf16[4,2,32,128]{3,2,1,0:T(8,128)(2,1)S(1)} %pad_maximum_fusion.1.m_mine) | copy-start | bytes 196612
  149.6 3.1 %collective-permute-start.14 = (bf16[4,2,32,128]{3,2,1,0:T(8,128)(2,1)S(1)}, bf16[4,2,32,128]{3,2,1,0:T(8,128)(2,1)S(1)}, u32[]{:S(2)}, u32[]{:S(2)}) collective-permute-start(bf16[4,2,32,128]{3,2,1,0:T(8,128)(2,1)S(1)} %pad_maximum_fusion.1.m_mine), channel_id=1, source_target_pairs={{0,1},{1,0},{2,3},{3,2},{4,5},{5,4},{6,7},{7,6},{8,9},{9,8},{10,11... | collective-permute-start | bytes 196616 | tf_op jit(solution)/shard_map/ppermute | solution.py:341
  152.8 0.6 copy-start.16
  161.6 0.6 copy-start.11

commit v3 on v2

--- a/solution.py
+++ b/solution.py
@@ -36,6 +36,12 @@
     return nn(a.T, b)
 
 
+def once(a, b, dims):
+    return lax.dot_general(
+        a.astype(bf16), b.astype(bf16), (dims, ((), ())), preferred_element_type=f32
+    )
+
+
 def column(row):
     n = row.shape[1]
     at = lax.broadcasted_iota(jnp.int32, (n, n), 0)
@@ -70,7 +76,10 @@
     return s <= lax.broadcasted_iota(jnp.int32, (length, length), 1)
 
 
-def keys_kernel(all_frames, x, wk, wv, codes, halvings, payload, keys_raw, values, logs, acc):
+def project_kernel(
+    all_frames, x, wr, wk, wv, codes, halvings, extra, tutor,
+    payload, reads, keys_raw, values, logs, scores, local, t0, t1, t2, t3, acc, held,
+):
     step = pl.program_id(0)
 
     @pl.when(step == 0)
@@ -78,8 +87,8 @@
         acc[...] = jnp.zeros_like(acc)
 
     acc[...] += lax.dot_general(
-        jnp.concatenate([wk[...], wv[...]], axis=0),
         x[...],
+        jnp.concatenate([wr[...], wk[...], wv[...]], axis=0),
         (((1,), (1,)), ((), ())),
         preferred_element_type=f32,
     )
@@ -87,13 +96,16 @@
     @pl.when(step == STEPS - 1)
     def _():
         length = x.shape[0]
-        raw, val = acc[:LANES], acc[LANES:]
+        whole = acc[...].T
+        recept, raw, val = whole[:LANES], whole[LANES : 2 * LANES], whole[2 * LANES :]
+        reads[...] = recept
         keys_raw[...] = raw
         values[...] = val
         keys, _ = key_norm(raw)
         rate = rates(codes[...], all_frames)
         marks = jnp.broadcast_to(halvings[...].astype(f32).astype(bf16), (16, length))
-        ones = jnp.where(causal(length), 1.0, 0.0).astype(bf16)
+        mask = causal(length)
+        ones = jnp.where(mask, 1.0, 0.0).astype(bf16)
         counted = jnp.dot(marks, ones, preferred_element_type=f32)[:1]
         at = (lax.broadcasted_iota(jnp.int32, (1, length), 1) + 1).astype(f32)
         prefix = rate * at + log_half * counted
@@ -109,33 +121,8 @@
         for z in range(payload.shape[0]):
             payload[z, :half] = share
             payload[z, half:] = counts
-
-
-def reads_kernel(
-    x, wr, keys_raw, values, logs, extra, tutor, reads, scores, local, t0, t1, t2, t3, acc, held
-):
-    step = pl.program_id(0)
-
-    @pl.when(step == 0)
-    def _():
-        acc[...] = jnp.zeros_like(acc)
-
-    acc[...] += lax.dot_general(
-        wr[...], x[...], (((1,), (1,)), ((), ())), preferred_element_type=f32
-    )
-
-    @pl.when(step == STEPS - 1)
-    def _():
-        length = x.shape[0]
-        recept = acc[...]
-        reads[...] = recept
-        keys, _ = key_norm(keys_raw[...])
-        prefix = logs[...]
-        val = values[...]
-        masked = jnp.where(
-            causal(length), tn(keys * jnp.exp(-prefix), recept * jnp.exp(prefix)), 0.0
-        )
-        scores[...] = masked
+        masked = jnp.where(mask, tn(keys * jnp.exp(-prefix), recept * jnp.exp(prefix)), 0.0)
+        scores[...] = masked.astype(bf16)
         own = jnp.sum(recept * column(extra[...]) * keys, axis=0, keepdims=True)
         local[...] = nn(val, masked) + own * val
         by_frame = tutor[...].astype(f32).T.astype(bf16)
@@ -143,9 +130,9 @@
         part = length // tiles
         for i in range(tiles):
             held[i] = fold(by_frame[i * part : (i + 1) * part])
-        at = lax.axis_index("x")
+        place = lax.axis_index("x")
         for s, out in enumerate((t0, t1, t2, t3)):
-            to = lax.rem(at + s, GRID["x"])
+            to = lax.rem(place + s, GRID["x"])
             for c in range(2):
                 out[c] = held[to * 2 + c]
 
@@ -209,22 +196,28 @@
 
 
 def middle_kernel(
-    got, t_mine, t_other, w0, w1, w2, w3, v0, v1, v2, v3, sent, m0, m1, m2, m3, held
+    got, t_mine, t_other, w0, w1, w2, w3, v0, v1, v2, v3, sent, m0, m1, m2, m3, held, weights, sems
 ):
+    copies = []
+    for n, source in enumerate((w0, v0, w1, v1, w2, v2, w3, v3)):
+        copies.append(pltpu.make_async_copy(source, weights.at[n], sems.at[n]))
+        copies[n].start()
     at, core = lax.axis_index("x"), lax.axis_index("core")
     tiles = GRID["x"] * GRID["core"]
     rows = GRID["y"]
     group = min(4, rows)
     chunks = []
-    for ws, c in (((w0, w1, w2, w3), core), ((v0, v1, v2, v3), 1 - core)):
-        for s, w in enumerate(ws):
-            x = lax.rem(at - s + GRID["x"], GRID["x"])
+    for s in range(GRID["x"]):
+        x = lax.rem(at - s + GRID["x"], GRID["x"])
+        for n, c in ((2 * s, core), (2 * s + 1, 1 - core)):
             for y in range(0, rows, group):
-                chunks.append((w, y, [(y + g) * tiles + x * 2 + c for g in range(group)]))
+                chunks.append((n, y, [(y + g) * tiles + x * 2 + c for g in range(group)]))
     acc = None
-    for w, y, places in chunks:
-        weights = w[y : y + group].reshape(group * LANES, tiles * LANES)
-        term = jnp.dot(spread([got[p] for p in places]), weights, preferred_element_type=f32)
+    for n, y, places in chunks:
+        if y == 0:
+            copies[n].wait()
+        part = weights[n, y : y + group].reshape(group * LANES, tiles * LANES)
+        term = jnp.dot(spread([got[p] for p in places]), part, preferred_element_type=f32)
         acc = term if acc is None else acc + term
     mixed = acc.astype(bf16)
     for i in range(tiles):
@@ -235,10 +228,10 @@
             out[c] = held[to * 2 + c]
     wanted = spread([by_source(t_mine, t_other, i // 2, i % 2) for i in range(tiles)])
     diff = (mixed.astype(f32) - wanted.astype(f32)).astype(bf16)
-    for w, y, places in chunks:
-        weights = w[y : y + group].reshape(group * LANES, tiles * LANES)
+    for n, y, places in chunks:
+        part = weights[n, y : y + group].reshape(group * LANES, tiles * LANES)
         grads = lax.dot_general(
-            diff, weights, (((1,), (1,)), ((), ())), preferred_element_type=f32
+            diff, part, (((1,), (1,)), ((), ())), preferred_element_type=f32
         ).astype(bf16)
         for g, p in enumerate(places):
             sent[p] = fold(grads[:, g * LANES : (g + 1) * LANES])
@@ -283,14 +276,14 @@
     prefix = logs[...]
     grow, shrink = jnp.exp(prefix), jnp.exp(-prefix)
     own_weight = column(extra[...])
-    twofold = jnp.where(causal(length), tn(val, grad), 0.0)
+    twofold = jnp.where(causal(length), once(val.T, grad, ((1,), (0,))), 0.0).astype(bf16)
     progressive = jnp.sum(grad * val, axis=0, keepdims=True) * own_weight
     own = jnp.sum(recept * own_weight * keys, axis=0, keepdims=True)
     grad_reads[...] = (
-        grow * (nn(start[...], grad) + nn(keys * shrink, twofold)) + progressive * keys
+        grow * (nn(start[...], grad) + once(keys * shrink, twofold, ((1,), (0,)))) + progressive * keys
     ).astype(bf16)
-    part_keys[...] = shrink * nt(recept * grow, twofold) + progressive * recept
-    part_values[...] = nt(grad, scores[...]) + own * grad
+    part_keys[...] = shrink * once(recept * grow, twofold, ((1,), (1,))) + progressive * recept
+    part_values[...] = once(grad, scores[...], ((1,), (1,))) + own * grad
 
 
 def final_kernel(
@@ -380,30 +373,27 @@
         pl.BlockSpec((LANES, depth), lambda k: (0, k)),
     ]
     serial = pltpu.CompilerParams(dimension_semantics=("arbitrary",))
-    payload, keys_raw, values, logs = call(
-        functools.partial(keys_kernel, all_frames),
-        [((blocks, half + 16, 2 * LANES), bf16), (flat, f32), (flat, f32), (flat, f32)],
-        (incoming_signals, lock_linear_map.T, worth_linear_map.T, codes, halvings),
-        grid=(STEPS,),
-        in_specs=[by_step[0], by_step[1], by_step[1], whole, whole],
-        out_specs=[whole] * 4,
-        scratch_shapes=[pltpu.VMEM((2 * LANES, length), f32)],
-        compiler_params=serial,
-    )
-    reads, scores, local, *tutor = call(
-        reads_kernel,
-        [(flat, f32), ((length, length), f32), (flat, f32)] + [((2,) + block, bf16)] * GRID["x"],
+    payload, reads, keys_raw, values, logs, scores, local, *tutor = call(
+        functools.partial(project_kernel, all_frames),
+        [
+            ((blocks, half + 16, 2 * LANES), bf16), (flat, f32), (flat, f32), (flat, f32),
+            (flat, f32), ((length, length), bf16), (flat, f32),
+        ]
+        + [((2,) + block, bf16)] * GRID["x"],
         (
-            incoming_signals, receptor_linear_map.T, keys_raw, values, logs, extra,
-            tutor_aggregated.T,
+            incoming_signals, receptor_linear_map.T, lock_linear_map.T, worth_linear_map.T,
+            codes, halvings, extra, tutor_aggregated.T,
         ),
         grid=(STEPS,),
-        in_specs=[by_step[0], by_step[1]] + [whole] * 5,
-        out_specs=[whole] * (3 + GRID["x"]),
-        scratch_shapes=[pltpu.VMEM(flat, f32), pltpu.VMEM((tiles,) + block, bf16)],
+        in_specs=[by_step[0]] + [by_step[1]] * 3 + [whole] * 4,
+        out_specs=[whole] * (7 + GRID["x"]),
+        scratch_shapes=[
+            pltpu.VMEM((length, 3 * LANES), f32), pltpu.VMEM((tiles,) + block, bf16),
+        ],
         compiler_params=serial,
     )
-    payload, columns, local, *tutor = barrier((payload, columns, local, *tutor))
+    tutor = jnp.stack(along_x(tutor))
+    payload, columns, tutor = barrier((payload, columns, tutor))
     everyone = exchange(payload, "ctx")
     w_mine = along_x([columns] * GRID["x"])
     sent, start, unit, inverse = call(
@@ -413,12 +403,16 @@
     )
     got = exchange(sent, head)
     w_other = [swap(w) for w in w_mine]
-    tutor = jnp.stack(along_x(tutor))
     sent, *mixed = call(
         middle_kernel,
         [((rows * tiles,) + block, bf16)] + [((2,) + block, bf16)] * GRID["x"],
         (got, tutor, swap(tutor), *w_mine, *w_other),
-        scratch_shapes=[pltpu.VMEM((tiles,) + block, bf16)],
+        in_specs=[whole] * 3 + [pl.BlockSpec(memory_space=pl.ANY)] * (2 * GRID["x"]),
+        scratch_shapes=[
+            pltpu.VMEM((tiles,) + block, bf16),
+            pltpu.VMEM((2 * GRID["x"], rows, LANES, tiles * LANES), bf16),
+            pltpu.SemaphoreType.DMA((2 * GRID["x"],)),
+        ],
     )
     got = exchange(sent, head)
     mixed = jnp.stack(along_x(mixed))

time: 166 us -> 151 us (0.910)
  Pallas kernels: 34.8 us -> 25.4 us
  starting transfers between devices: 97.3 us -> 92.6 us
  waiting for transfers between devices: 24.4 us -> 22.7 us
    pallas_call x7 -> x6, Pallas kernels: 34.8 us -> 25.4 us  [call(): pl.pallas_call(kernel, cost_estimate=pl.CostEstimate(flops=1 << 30, trans...]
    all_to_all x5, starting transfers between devices: 52.4 us -> 43.7 us  [exchange(): return lax.all_to_all(array, axis, 0, 0)]
    ppermute x9, waiting for transfers between devices: 8.4 us -> 3.91 us  [along_x(): lax.ppermute(parts[s], 'x', [(i, (i + s) % n) for i in range(n)])]
    ppermute x9, starting transfers between devices: 32.8 us -> 36.2 us  [along_x(): lax.ppermute(parts[s], 'x', [(i, (i + s) % n) for i in range(n)])]
    all_to_all x5, waiting for transfers between devices: 13.5 us -> 16.5 us  [exchange(): return lax.all_to_all(array, axis, 0, 0)]
    unnamed x40 -> x32, local copies, waits for them, and re-layouts: 5.27 us -> 5.24 us
  transfers between devices with their start and end apart: 20 -> 20, of which waited for: 10 -> 6; matrix products, arithmetic and copies ran while one was open for 0% -> 0% of each run, Pallas kernels for 16% -> 12%
where the time goes in v3:
time: 151 us; the launch traced here: 150 us
  starting transfers between devices  92.6 us (61%)
  Pallas kernels  25.4 us (17%)
  waiting for transfers between devices  22.7 us (15%)
  local copies, waits for them, and re-layouts  7.16 us (5%)
    all_to_all x5, starting transfers between devices, exchange(): return lax.all_to_all(array, axis, 0, 0)  43.7 us
    ppermute x9, starting transfers between devices, along_x(): lax.ppermute(parts[s], 'x', [(i, (i + s) % n) for i in range(n)])  36.2 us
    pallas_call x6, Pallas kernels, call(): pl.pallas_call(kernel, cost_estimate=pl.CostEstimate(flops=1 << 30, trans...  25.4 us
    all_to_all x5, waiting for transfers between devices, exchange(): return lax.all_to_all(array, axis, 0, 0)  16.5 us
    ppermute x6, starting transfers between devices, swap(): return lax.ppermute(array, 'core', [(0, 1), (1, 0)])  12.6 us
    unnamed x32, local copies, waits for them, and re-layouts  5.24 us
    ppermute x9, waiting for transfers between devices, along_x(): lax.ppermute(parts[s], 'x', [(i, (i + s) % n) for i in range(n)])  3.91 us
  transfers between devices with their start and end apart: 20, of which 6 were waited for; matrix products, arithmetic and copies ran while one was open for 0% of the time, Pallas kernels for 12%

profile of v3, /device:TPU:2, one launch (start us, length us, event | category | flops | bytes accessed | tf_op | source)
XLA Modules:
  0.0 149.7 jit_solution(3950068314399362141)
XLA Ops:
  0.6 1.9 %copy.17 = bf16[8,8,8,512]{3,2,0,1:T(8,128)(2,1)} copy(bf16[8,8,8,512]{3,2,1,0:T(8,128)(2,1)} %bitcast.30) | data formatting | bytes 1048576 | tf_op jit(solution)/shard_map/reshape | solution.py:361
  2.6 7.1 %all-to-all-start = ((bf16[8,64,512]{2,1,0:T(8,128)(2,1)}), bf16[8,64,512]{2,1,0:T(8,128)(2,1)S(1)}, u32[]{:S(2)}, u32[]{:S(2)}) async-start(bf16[8,64,512]{2,1,0:T(8,128)(2,1)} %bitcast.26), calls=%async_computation | async-start | bytes 1048576 | tf_op jit(solution)/shard_map/all_to_all | solution.py:323
  9.7 9.2 %shard_map.129 = (bf16[12,48,128]{2,1,0:T(8,128)(2,1)}, f32[64,512]{1,0:T(8,128)}, f32[64,512]{1,0:T(8,128)}, f32[64,512]{1,0:T(8,128)}, f32[64,512]{1,0:T(8,128...) custom-call(bf16[512,4096]{1,0:T(8,128)(2,1)} %x.1, ...), custom_call_target="tpu_custom_call" | custom-call | flops 1073741824 | bytes 8388608 | tf_op jit(solution)/shard_map/pallas_call | solution.py:314
  18.9 3.4 %collective-permute-start = (bf16[2,32,128]{2,1,0:T(8,128)(2,1)}, bf16[2,32,128]{2,1,0:T(8,128)(2,1)S(1)}, u32[]{:S(2)}, u32[]{:S(2)}) collective-permute-start(bf16[2,32,128]{2,1,0:T(8,128)(2,1)} %get-tuple-element.37), channel_id=1, source_target_pairs={{0,2},{2,4},{4,6},{6,0},{1,3},{3,5},{5,7},{7,1},{8,10},{10,12},{12... | collective-permute-start | bytes 49160 | tf_op jit(solution)/shard_map/ppermute | solution.py:329
  22.3 8.5 %collective-permute-start.1 = (bf16[2,32,128]{2,1,0:T(8,128)(2,1)}, bf16[2,32,128]{2,1,0:T(8,128)(2,1)S(1)}, u32[]{:S(2)}, u32[]{:S(2)}) collective-permute-start(bf16[2,32,128]{2,1,0:T(8,128)(2,1)} %get-tuple-element.38), channel_id=1, source_target_pairs={{0,4},{2,6},{4,0},{6,2},{1,5},{3,7},{5,1},{7,3},{8,12},{10,14},{12... | collective-permute-start | bytes 49160 | tf_op jit(solution)/shard_map/ppermute | solution.py:329
  30.8 1.9 %collective-permute-start.2 = (bf16[2,32,128]{2,1,0:T(8,128)(2,1)}, bf16[2,32,128]{2,1,0:T(8,128)(2,1)S(1)}, u32[]{:S(2)}, u32[]{:S(2)}) collective-permute-start(bf16[2,32,128]{2,1,0:T(8,128)(2,1)} %get-tuple-element.39), channel_id=1, source_target_pairs={{0,6},{2,0},{4,2},{6,4},{1,7},{3,1},{5,3},{7,5},{8,14},{10,8},{12,... | collective-permute-start | bytes 49160 | tf_op jit(solution)/shard_map/ppermute | solution.py:329
  32.7 0.0 collective-permute-done
  32.7 0.0 collective-permute-done.1
  32.7 3.9 %collective-permute-done.2 = bf16[2,32,128]{2,1,0:T(8,128)(2,1)S(1)} collective-permute-done((bf16[2,32,128]{2,1,0:T(8,128)(2,1)}, bf16[2,32,128]{2,1,0:T(8,128)(2,1)S(1)}, u32[]{:S(2)}, u32[]{:S(2)}) %collective-permute-start.2) | collective-permute-done | bytes 16416 | tf_op jit(solution)/shard_map/ppermute | solution.py:329
  36.6 0.7 pad_maximum_fusion.t_mine
  37.3 0.0 copy-start.9
  37.4 0.0 all-to-all-done.w0
  37.4 0.0 copy-start
  37.4 9.7 %all-to-all-start.1 = ((bf16[12,48,128]{2,1,0:T(8,128)(2,1)}), bf16[12,48,128]{2,1,0:T(8,128)(2,1)S(1)}, u32[]{:S(2)}, u32[]{:S(2)}) async-start(bf16[12,48,128]{2,1,0:T(8,128)(2,1)} %get-tuple-element.40), calls=%async_computation.1 | async-start | bytes 294912 | tf_op jit(solution)/shard_map/all_to_all | solution.py:323
  47.1 4.1 %collective-permute-start.6 = (bf16[8,64,512]{2,1,0:T(8,128)(2,1)S(1)}, bf16[8,64,512]{2,1,0:T(8,128)(2,1)S(1)}, u32[]{:S(2)}, u32[]{:S(2)}) collective-permute-start(bf16[8,64,512]{2,1,0:T(8,128)(2,1)S(1)} %all-to-all-done.w0), channel_id=1, source_target_pairs={{0,6},{2,0},{4,2},{6,4},{1,7},{3,1},{5,3},{7,5},{8,14},{10,8},{12,... | collective-permute-start | bytes 1572872 | tf_op jit(solution)/shard_map/ppermute | solution.py:329
  51.2 3.4 %collective-permute-start.5 = (bf16[8,64,512]{2,1,0:T(8,128)(2,1)S(1)}, bf16[8,64,512]{2,1,0:T(8,128)(2,1)S(1)}, u32[]{:S(2)}, u32[]{:S(2)}) collective-permute-start(bf16[8,64,512]{2,1,0:T(8,128)(2,1)S(1)} %all-to-all-done.w0), channel_id=1, source_target_pairs={{0,4},{2,6},{4,0},{6,2},{1,5},{3,7},{5,1},{7,3},{8,12},{10,14},{12... | collective-permute-start | bytes 1572872 | tf_op jit(solution)/shard_map/ppermute | solution.py:329
  54.6 4.5 %collective-permute-start.4 = (bf16[8,64,512]{2,1,0:T(8,128)(2,1)S(1)}, bf16[8,64,512]{2,1,0:T(8,128)(2,1)S(1)}, u32[]{:S(2)}, u32[]{:S(2)}) collective-permute-start(bf16[8,64,512]{2,1,0:T(8,128)(2,1)S(1)} %all-to-all-done.w0), channel_id=1, source_target_pairs={{0,2},{2,4},{4,6},{6,0},{1,3},{3,5},{5,7},{7,1},{8,10},{10,12},{12... | collective-permute-start | bytes 1572872 | tf_op jit(solution)/shard_map/ppermute | solution.py:329
  59.1 0.0 all-to-all-done.1.everyone
  59.1 0.0 copy-start.10
  59.2 0.6 copy-done.10
  59.8 2.7 %shard_map.130 = (bf16[64,32,128]{2,1,0:T(8,128)(2,1)}, f32[64,64]{1,0:T(8,128)}, f32[64,512]{1,0:T(8,128)}, f32[1,512]{1,0:T(1,128)}) custom-call(bf16[12,48,128]{2,1,0:T(8,128)(2,1)} %copy-done.10, f32[64,512]{1,0:T(8,128)} %get-tuple-element.41.local, f32[64,512]{1,0:T(8,128)} %get-tuple-element.42.reads, f32[64,512]{1,0:T(8,128)} %get-tuple-element.43.logs, ...), custom_call_target="tpu_custom_call" | custom-call | flops 1073741824 | bytes 8388608 | tf_op jit(solution)/shard_map/pallas_call | solution.py:314
  62.5 11.8 %all-to-all-start.2 = ((bf16[64,32,128]{2,1,0:T(8,128)(2,1)}), bf16[64,32,128]{2,1,0:T(8,128)(2,1)S(1)}, u32[]{:S(2)}, u32[]{:S(2)}) async-start(bf16[64,32,128]{2,1,0:T(8,128)(2,1)} %get-tuple-element.44), calls=%async_computation.2 | async-start | bytes 1048576 | tf_op jit(solution)/shard_map/all_to_all | solution.py:323
  74.3 2.1 %collective-permute-start.7 = (bf16[8,64,512]{2,1,0:T(8,128)(2,1)S(1)}, bf16[8,64,512]{2,1,0:T(8,128)(2,1)S(1)}, u32[]{:S(2)}, u32[]{:S(2)}) collective-permute-start(bf16[8,64,512]{2,1,0:T(8,128)(2,1)S(1)} %all-to-all-done.w0), channel_id=1, source_target_pairs={{0,1},{1,0},{2,3},{3,2},{4,5},{5,4},{6,7},{7,6},{8,9},{9,8},{10,11... | collective-permute-start | bytes 1572872 | tf_op jit(solution)/shard_map/ppermute | solution.py:334
  76.4 0.0 collective-permute-done.6.w3
  76.4 0.0 copy-start.2
  76.4 2.3 %collective-permute-start.10 = (bf16[8,64,512]{2,1,0:T(8,128)(2,1)S(1)}, bf16[8,64,512]{2,1,0:T(8,128)(2,1)S(1)}, u32[]{:S(2)}, u32[]{:S(2)}) collective-permute-start(bf16[8,64,512]{2,1,0:T(8,128)(2,1)S(1)} %collective-permute-done.6.w3), channel_id=1, source_target_pairs={{0,1},{1,0},{2,3},{3,2},{4,5},{5,4},{6,7},{7,6},{8,9},{9,8},{10,11... | collective-permute-start | bytes 1572872 | tf_op jit(solution)/shard_map/ppermute | solution.py:334
  78.7 0.0 collective-permute-done.5.w2
  78.7 0.0 copy-start.3
  78.7 2.1 %collective-permute-start.9 = (bf16[8,64,512]{2,1,0:T(8,128)(2,1)S(1)}, bf16[8,64,512]{2,1,0:T(8,128)(2,1)S(1)}, u32[]{:S(2)}, u32[]{:S(2)}) collective-permute-start(bf16[8,64,512]{2,1,0:T(8,128)(2,1)S(1)} %collective-permute-done.5.w2), channel_id=1, source_target_pairs={{0,1},{1,0},{2,3},{3,2},{4,5},{5,4},{6,7},{7,6},{8,9},{9,8},{10,11... | collective-permute-start | bytes 1572872 | tf_op jit(solution)/shard_map/ppermute | solution.py:334
  80.8 0.0 collective-permute-done.4.w1
  80.8 0.0 copy-start.4
  80.8 2.3 %collective-permute-start.8 = (bf16[8,64,512]{2,1,0:T(8,128)(2,1)S(1)}, bf16[8,64,512]{2,1,0:T(8,128)(2,1)}, u32[]{:S(2)}, u32[]{:S(2)}) collective-permute-start(bf16[8,64,512]{2,1,0:T(8,128)(2,1)S(1)} %collective-permute-done.4.w1), channel_id=1, source_target_pairs={{0,1},{1,0},{2,3},{3,2},{4,5},{5,4},{6,7},{7,6},{8,9},{9,8},{10,11... | collective-permute-start | bytes 1572872 | tf_op jit(solution)/shard_map/ppermute | solution.py:334
  83.1 2.1 %collective-permute-start.3 = (bf16[4,2,32,128]{3,2,1,0:T(8,128)(2,1)S(1)}, bf16[4,2,32,128]{3,2,1,0:T(8,128)(2,1)S(1)}, u32[]{:S(2)}, u32[]{:S(2)}) collective-permute-start(bf16[4,2,32,128]{3,2,1,0:T(8,128)(2,1)S(1)} %pad_maximum_fusion.t_mine), channel_id=1, source_target_pairs={{0,1},{1,0},{2,3},{3,2},{4,5},{5,4},{6,7},{7,6},{8,9},{9,8},{10,11... | collective-permute-start | bytes 196616 | tf_op jit(solution)/shard_map/ppermute | solution.py:334
  85.1 1.1 collective-permute-done.3.t_other
  86.2 0.0 collective-permute-done.7.v0
  86.2 0.0 collective-permute-done.10.v3
  86.3 0.0 collective-permute-done.9.v2
  86.3 0.8 copy-done.6
  87.1 0.8 copy-done.7
  87.9 0.0 collective-permute-done.8.v1
  87.9 4.0 %all-to-all-done.2.got = bf16[64,32,128]{2,1,0:T(8,128)(2,1)S(1)} async-done(((bf16[64,32,128]{2,1,0:T(8,128)(2,1)}), bf16[64,32,128]{2,1,0:T(8,128)(2,1)S(1)}, u32[]{:S(2)}, u32[]{:S(2)}) %all-to-all-start.2) | async-done | bytes 524320 | tf_op jit(solution)/shard_map/all_to_all | solution.py:323
  91.9 0.0 copy-done
  92.0 0.8 copy-done.1
  92.8 5.7 %shard_map.131 = (bf16[64,32,128]{2,1,0:T(8,128)(2,1)}, bf16[2,32,128]{2,1,0:T(8,128)(2,1)}, bf16[2,32,128]{2,1,0:T(8,128)(2,1)}, bf16[2,32,128]{2,1,0:T(8,128)(2,1)}, bf16[2,32,128]{2,1,0:T(8,128)(2,1)}) custom-call(bf16[64,32,128]{2,1,0:T(8,128)(2,1)} %copy-done.1, bf16[4,2,32,128]{3,2,1,0:T(8,128)(2,1)} %copy-done.9, bf16[4,2,32,128]{3,2,1,0:T(8,128)(2,1)} %copy-done.12, ...), custom_call_target="tpu_custom_call" | custom-call | flops 1073741824 | bytes 8388608 | tf_op jit(solution)/shard_map/pallas_call | solution.py:314
  98.5 0.0 copy-start.14
  98.5 6.3 %all-to-all-start.3 = ((bf16[64,32,128]{2,1,0:T(8,128)(2,1)}), bf16[64,32,128]{2,1,0:T(8,128)(2,1)S(1)}, u32[]{:S(2)}, u32[]{:S(2)}) async-start(bf16[64,32,128]{2,1,0:T(8,128)(2,1)} %get-tuple-element.55), calls=%async_computation.3 | async-start | bytes 1048576 | tf_op jit(solution)/shard_map/all_to_all | solution.py:323
  104.9 3.4 %collective-permute-start.11 = (bf16[2,32,128]{2,1,0:T(8,128)(2,1)}, bf16[2,32,128]{2,1,0:T(8,128)(2,1)S(1)}, u32[]{:S(2)}, u32[]{:S(2)}) collective-permute-start(bf16[2,32,128]{2,1,0:T(8,128)(2,1)} %get-tuple-element.48), channel_id=1, source_target_pairs={{0,2},{2,4},{4,6},{6,0},{1,3},{3,5},{5,7},{7,1},{8,10},{10,12},{12... | collective-permute-start | bytes 49160 | tf_op jit(solution)/shard_map/ppermute | solution.py:329
  108.3 3.0 %collective-permute-start.12 = (bf16[2,32,128]{2,1,0:T(8,128)(2,1)}, bf16[2,32,128]{2,1,0:T(8,128)(2,1)S(1)}, u32[]{:S(2)}, u32[]{:S(2)}) collective-permute-start(bf16[2,32,128]{2,1,0:T(8,128)(2,1)} %get-tuple-element.49), channel_id=1, source_target_pairs={{0,4},{2,6},{4,0},{6,2},{1,5},{3,7},{5,1},{7,3},{8,12},{10,14},{12... | collective-permute-start | bytes 49160 | tf_op jit(solution)/shard_map/ppermute | solution.py:329
  111.2 4.1 %collective-permute-start.13 = (bf16[2,32,128]{2,1,0:T(8,128)(2,1)}, bf16[2,32,128]{2,1,0:T(8,128)(2,1)S(1)}, u32[]{:S(2)}, u32[]{:S(2)}) collective-permute-start(bf16[2,32,128]{2,1,0:T(8,128)(2,1)} %get-tuple-element.50), channel_id=1, source_target_pairs={{0,6},{2,0},{4,2},{6,4},{1,7},{3,1},{5,3},{7,5},{8,14},{10,8},{12,... | collective-permute-start | bytes 49160 | tf_op jit(solution)/shard_map/ppermute | solution.py:329
  115.3 7.1 %all-to-all-done.3.got = bf16[64,32,128]{2,1,0:T(8,128)(2,1)S(1)} async-done(((bf16[64,32,128]{2,1,0:T(8,128)(2,1)}), bf16[64,32,128]{2,1,0:T(8,128)(2,1)S(1)}, u32[]{:S(2)}, u32[]{:S(2)}) %all-to-all-start.3) | async-done | bytes 524320 | tf_op jit(solution)/shard_map/all_to_all | solution.py:323
  122.4 0.8 copy-done.8
  123.3 2.4 %shard_map.132 = (bf16[12,32,128]{2,1,0:T(8,128)(2,1)}, f32[64,512]{1,0:T(8,128)}) custom-call(bf16[64,32,128]{2,1,0:T(8,128)(2,1)} %copy-done.8, f32[64,512]{1,0:T(8,128)} %get-tuple-element.56.unit, f32[1,512]{1,0:T(1,128)} %get-tuple-element.57.inverse, f32[1,64]{1,0:T(1,128)} %bitcast.47, f32[64,512]{1,0:T(8,128)} %get-tuple-element.42.reads, ...), custom_call_target="tpu_custom_call" | custom-call | flops 1073741824 | bytes 8388608 | tf_op jit(solution)/shard_map/pallas_call | solution.py:314
  125.7 8.8 %all-to-all-start.4 = ((bf16[12,32,128]{2,1,0:T(8,128)(2,1)}), bf16[12,32,128]{2,1,0:T(8,128)(2,1)S(1)}, u32[]{:S(2)}, u32[]{:S(2)}) async-start(bf16[12,32,128]{2,1,0:T(8,128)(2,1)} %get-tuple-element.61), calls=%async_computation.4 | async-start | bytes 196608 | tf_op jit(solution)/shard_map/all_to_all | solution.py:323
  134.5 0.0 collective-permute-done.11
  134.5 0.0 collective-permute-done.12
  134.5 0.0 collective-permute-done.13
  134.6 0.0 copy-start.13
  134.6 1.9 %collective-permute-start.14 = (bf16[4,2,32,128]{3,2,1,0:T(8,128)(2,1)S(1)}, bf16[4,2,32,128]{3,2,1,0:T(8,128)(2,1)S(1)}, u32[]{:S(2)}, u32[]{:S(2)}) collective-permute-start(bf16[4,2,32,128]{3,2,1,0:T(8,128)(2,1)S(1)} %pad_maximum_fusion.1.m_mine), channel_id=1, source_target_pairs={{0,1},{1,0},{2,3},{3,2},{4,5},{5,4},{6,7},{7,6},{8,9},{9,8},{10,11... | collective-permute-start | bytes 196616 | tf_op jit(solution)/shard_map/ppermute | solution.py:334
  136.5 1.2 collective-permute-done.14.m_other
  137.7 0.6 copy-done.15
  138.4 2.9 %shard_map.133 = (bf16[64,512]{1,0:T(8,128)(2,1)}, bf16[64,512]{1,0:T(8,128)(2,1)}, f32[64,512]{1,0:T(8,128)}, f32[64,512]{1,0:T(8,128)}) custom-call(bf16[4,2,32,128]{3,2,1,0:T(8,128)(2,1)} %copy-done.13, bf16[4,2,32,128]{3,2,1,0:T(8,128)(2,1)} %copy-done.15, f32[64,512]{1,0:T(8,128)} %get-tuple-element.42.reads, f32[64,512]{1,0:T(8,128)} %get-tuple-element.51.keys_raw, ...), custom_call_target="tpu_custom_call" | custom-call | flops 1073741824 | bytes 8388608 | tf_op jit(solution)/shard_map/pallas_call | solution.py:314
  141.2 5.3 %all-to-all-done.4.later = bf16[12,32,128]{2,1,0:T(8,128)(2,1)S(1)} async-done(((bf16[12,32,128]{2,1,0:T(8,128)(2,1)}), bf16[12,32,128]{2,1,0:T(8,128)(2,1)S(1)}, u32[]{:S(2)}, u32[]{:S(2)}) %all-to-all-start.4) | async-done | bytes 98336 | tf_op jit(solution)/shard_map/all_to_all | solution.py:323
  146.6 0.6 copy-done.11
  147.2 2.4 %shard_map.134 = (bf16[64,512]{1,0:T(8,128)(2,1)}, bf16[64,512]{1,0:T(8,128)(2,1)}) custom-call(bf16[12,32,128]{2,1,0:T(8,128)(2,1)} %copy-done.11, bf16[12,48,128]{2,1,0:T(8,128)(2,1)} %copy-done.10, f32[64,512]{1,0:T(8,128)} %get-tuple-element.62.part_keys, f32[64,512]{1,0:T(8,128)} %get-tuple-element.63.part_values, ...), custom_call_target="tpu_custom_call" | custom-call | flops 1073741824 | bytes 8388608 | tf_op jit(solution)/shard_map/pallas_call | solution.py:314
  (17 shorter events, 0.0 us)
Async XLA Ops:
  2.6 34.8 %all-to-all-start = ((bf16[8,64,512]{2,1,0:T(8,128)(2,1)}), bf16[8,64,512]{2,1,0:T(8,128)(2,1)S(1)}, u32[]{:S(2)}, u32[]{:S(2)}) async-start(bf16[8,64,512]{2,1,0:T(8,128)(2,1)} %bitcast.26), calls=%async_computation | async-start | bytes 1048576 | tf_op jit(solution)/shard_map/all_to_all | solution.py:323
  18.9 13.8 %collective-permute-start = (bf16[2,32,128]{2,1,0:T(8,128)(2,1)}, bf16[2,32,128]{2,1,0:T(8,128)(2,1)S(1)}, u32[]{:S(2)}, u32[]{:S(2)}) collective-permute-start(bf16[2,32,128]{2,1,0:T(8,128)(2,1)} %get-tuple-element.37), channel_id=1, source_target_pairs={{0,2},{2,4},{4,6},{6,0},{1,3},{3,5},{5,7},{7,1},{8,10},{10,12},{12... | collective-permute-start | bytes 49160 | tf_op jit(solution)/shard_map/ppermute | solution.py:329
  22.3 10.4 %collective-permute-start.1 = (bf16[2,32,128]{2,1,0:T(8,128)(2,1)}, bf16[2,32,128]{2,1,0:T(8,128)(2,1)S(1)}, u32[]{:S(2)}, u32[]{:S(2)}) collective-permute-start(bf16[2,32,128]{2,1,0:T(8,128)(2,1)} %get-tuple-element.38), channel_id=1, source_target_pairs={{0,4},{2,6},{4,0},{6,2},{1,5},{3,7},{5,1},{7,3},{8,12},{10,14},{12... | collective-permute-start | bytes 49160 | tf_op jit(solution)/shard_map/ppermute | solution.py:329
  30.8 5.8 %collective-permute-start.2 = (bf16[2,32,128]{2,1,0:T(8,128)(2,1)}, bf16[2,32,128]{2,1,0:T(8,128)(2,1)S(1)}, u32[]{:S(2)}, u32[]{:S(2)}) collective-permute-start(bf16[2,32,128]{2,1,0:T(8,128)(2,1)} %get-tuple-element.39), channel_id=1, source_target_pairs={{0,6},{2,0},{4,2},{6,4},{1,7},{3,1},{5,3},{7,5},{8,14},{10,8},{12,... | collective-permute-start | bytes 49160 | tf_op jit(solution)/shard_map/ppermute | solution.py:329
  37.3 54.5 %copy-start.9 = (bf16[4,2,32,128]{3,2,1,0:T(8,128)(2,1)}, bf16[4,2,32,128]{3,2,1,0:T(8,128)(2,1)S(1)}, u32[]{:S(2)}) copy-start(bf16[4,2,32,128]{3,2,1,0:T(8,128)(2,1)S(1)} %pad_maximum_fusion.t_mine) | copy-start | bytes 196612
  37.4 54.5 %copy-start = (bf16[8,64,512]{2,1,0:T(8,128)(2,1)}, bf16[8,64,512]{2,1,0:T(8,128)(2,1)S(1)}, u32[]{:S(2)}) copy-start(bf16[8,64,512]{2,1,0:T(8,128)(2,1)S(1)} %all-to-all-done.w0) | copy-start | bytes 1572868
  37.4 21.8 %all-to-all-start.1 = ((bf16[12,48,128]{2,1,0:T(8,128)(2,1)}), bf16[12,48,128]{2,1,0:T(8,128)(2,1)S(1)}, u32[]{:S(2)}, u32[]{:S(2)}) async-start(bf16[12,48,128]{2,1,0:T(8,128)(2,1)} %get-tuple-element.40), calls=%async_computation.1 | async-start | bytes 294912 | tf_op jit(solution)/shard_map/all_to_all | solution.py:323
  47.1 29.3 %collective-permute-start.6 = (bf16[8,64,512]{2,1,0:T(8,128)(2,1)S(1)}, bf16[8,64,512]{2,1,0:T(8,128)(2,1)S(1)}, u32[]{:S(2)}, u32[]{:S(2)}) collective-permute-start(bf16[8,64,512]{2,1,0:T(8,128)(2,1)S(1)} %all-to-all-done.w0), channel_id=1, source_target_pairs={{0,6},{2,0},{4,2},{6,4},{1,7},{3,1},{5,3},{7,5},{8,14},{10,8},{12,... | collective-permute-start | bytes 1572872 | tf_op jit(solution)/shard_map/ppermute | solution.py:329
  51.2 27.5 %collective-permute-start.5 = (bf16[8,64,512]{2,1,0:T(8,128)(2,1)S(1)}, bf16[8,64,512]{2,1,0:T(8,128)(2,1)S(1)}, u32[]{:S(2)}, u32[]{:S(2)}) collective-permute-start(bf16[8,64,512]{2,1,0:T(8,128)(2,1)S(1)} %all-to-all-done.w0), channel_id=1, source_target_pairs={{0,4},{2,6},{4,0},{6,2},{1,5},{3,7},{5,1},{7,3},{8,12},{10,14},{12... | collective-permute-start | bytes 1572872 | tf_op jit(solution)/shard_map/ppermute | solution.py:329
  54.6 26.2 %collective-permute-start.4 = (bf16[8,64,512]{2,1,0:T(8,128)(2,1)S(1)}, bf16[8,64,512]{2,1,0:T(8,128)(2,1)S(1)}, u32[]{:S(2)}, u32[]{:S(2)}) collective-permute-start(bf16[8,64,512]{2,1,0:T(8,128)(2,1)S(1)} %all-to-all-done.w0), channel_id=1, source_target_pairs={{0,2},{2,4},{4,6},{6,0},{1,3},{3,5},{5,7},{7,1},{8,10},{10,12},{12... | collective-permute-start | bytes 1572872 | tf_op jit(solution)/shard_map/ppermute | solution.py:329
  59.1 0.7 copy-start.10
  62.5 29.4 %all-to-all-start.2 = ((bf16[64,32,128]{2,1,0:T(8,128)(2,1)}), bf16[64,32,128]{2,1,0:T(8,128)(2,1)S(1)}, u32[]{:S(2)}, u32[]{:S(2)}) async-start(bf16[64,32,128]{2,1,0:T(8,128)(2,1)} %get-tuple-element.44), calls=%async_computation.2 | async-start | bytes 1048576 | tf_op jit(solution)/shard_map/all_to_all | solution.py:323
  74.3 11.9 %collective-permute-start.7 = (bf16[8,64,512]{2,1,0:T(8,128)(2,1)S(1)}, bf16[8,64,512]{2,1,0:T(8,128)(2,1)S(1)}, u32[]{:S(2)}, u32[]{:S(2)}) collective-permute-start(bf16[8,64,512]{2,1,0:T(8,128)(2,1)S(1)} %all-to-all-done.w0), channel_id=1, source_target_pairs={{0,1},{1,0},{2,3},{3,2},{4,5},{5,4},{6,7},{7,6},{8,9},{9,8},{10,11... | collective-permute-start | bytes 1572872 | tf_op jit(solution)/shard_map/ppermute | solution.py:334
  76.4 15.5 %copy-start.2 = (bf16[8,64,512]{2,1,0:T(8,128)(2,1)}, bf16[8,64,512]{2,1,0:T(8,128)(2,1)S(1)}, u32[]{:S(2)}) copy-start(bf16[8,64,512]{2,1,0:T(8,128)(2,1)S(1)} %collective-permute-done.6.w3) | copy-start | bytes 1572868
  76.4 9.8 %collective-permute-start.10 = (bf16[8,64,512]{2,1,0:T(8,128)(2,1)S(1)}, bf16[8,64,512]{2,1,0:T(8,128)(2,1)S(1)}, u32[]{:S(2)}, u32[]{:S(2)}) collective-permute-start(bf16[8,64,512]{2,1,0:T(8,128)(2,1)S(1)} %collective-permute-done.6.w3), channel_id=1, source_target_pairs={{0,1},{1,0},{2,3},{3,2},{4,5},{5,4},{6,7},{7,6},{8,9},{9,8},{10,11... | collective-permute-start | bytes 1572872 | tf_op jit(solution)/shard_map/ppermute | solution.py:334
  78.7 13.2 %copy-start.3 = (bf16[8,64,512]{2,1,0:T(8,128)(2,1)}, bf16[8,64,512]{2,1,0:T(8,128)(2,1)S(1)}, u32[]{:S(2)}) copy-start(bf16[8,64,512]{2,1,0:T(8,128)(2,1)S(1)} %collective-permute-done.5.w2) | copy-start | bytes 1572868
  78.7 7.5 %collective-permute-start.9 = (bf16[8,64,512]{2,1,0:T(8,128)(2,1)S(1)}, bf16[8,64,512]{2,1,0:T(8,128)(2,1)S(1)}, u32[]{:S(2)}, u32[]{:S(2)}) collective-permute-start(bf16[8,64,512]{2,1,0:T(8,128)(2,1)S(1)} %collective-permute-done.5.w2), channel_id=1, source_target_pairs={{0,1},{1,0},{2,3},{3,2},{4,5},{5,4},{6,7},{7,6},{8,9},{9,8},{10,11... | collective-permute-start | bytes 1572872 | tf_op jit(solution)/shard_map/ppermute | solution.py:334
  80.8 11.1 %copy-start.4 = (bf16[8,64,512]{2,1,0:T(8,128)(2,1)}, bf16[8,64,512]{2,1,0:T(8,128)(2,1)S(1)}, u32[]{:S(2)}) copy-start(bf16[8,64,512]{2,1,0:T(8,128)(2,1)S(1)} %collective-permute-done.4.w1) | copy-start | bytes 1572868
  80.8 7.1 %collective-permute-start.8 = (bf16[8,64,512]{2,1,0:T(8,128)(2,1)S(1)}, bf16[8,64,512]{2,1,0:T(8,128)(2,1)}, u32[]{:S(2)}, u32[]{:S(2)}) collective-permute-start(bf16[8,64,512]{2,1,0:T(8,128)(2,1)S(1)} %collective-permute-done.4.w1), channel_id=1, source_target_pairs={{0,1},{1,0},{2,3},{3,2},{4,5},{5,4},{6,7},{7,6},{8,9},{9,8},{10,11... | collective-permute-start | bytes 1572872 | tf_op jit(solution)/shard_map/ppermute | solution.py:334
  83.1 3.1 %collective-permute-start.3 = (bf16[4,2,32,128]{3,2,1,0:T(8,128)(2,1)S(1)}, bf16[4,2,32,128]{3,2,1,0:T(8,128)(2,1)S(1)}, u32[]{:S(2)}, u32[]{:S(2)}) collective-permute-start(bf16[4,2,32,128]{3,2,1,0:T(8,128)(2,1)S(1)} %pad_maximum_fusion.t_mine), channel_id=1, source_target_pairs={{0,1},{1,0},{2,3},{3,2},{4,5},{5,4},{6,7},{7,6},{8,9},{9,8},{10,11... | collective-permute-start | bytes 196616 | tf_op jit(solution)/shard_map/ppermute | solution.py:334
  86.2 5.7 %copy-start.12 = (bf16[4,2,32,128]{3,2,1,0:T(8,128)(2,1)}, bf16[4,2,32,128]{3,2,1,0:T(8,128)(2,1)S(1)}, u32[]{:S(2)}) copy-start(bf16[4,2,32,128]{3,2,1,0:T(8,128)(2,1)S(1)} %collective-permute-done.3.t_other) | copy-start | bytes 196612
  86.2 5.7 %copy-start.5 = (bf16[8,64,512]{2,1,0:T(8,128)(2,1)}, bf16[8,64,512]{2,1,0:T(8,128)(2,1)S(1)}, u32[]{:S(2)}) copy-start(bf16[8,64,512]{2,1,0:T(8,128)(2,1)S(1)} %collective-permute-done.7.v0) | copy-start | bytes 1572868
  86.2 0.8 copy-start.6
  87.1 0.8 copy-start.7
  91.9 0.8 copy-start.1
  98.5 36.0 %copy-start.14 = (bf16[2,32,128]{2,1,0:T(8,128)(2,1)S(1)}, bf16[2,32,128]{2,1,0:T(8,128)(2,1)}, u32[]{:S(2)}) copy-start(bf16[2,32,128]{2,1,0:T(8,128)(2,1)} %get-tuple-element.47) | copy-start | bytes 49156
  98.5 23.9 %all-to-all-start.3 = ((bf16[64,32,128]{2,1,0:T(8,128)(2,1)}), bf16[64,32,128]{2,1,0:T(8,128)(2,1)S(1)}, u32[]{:S(2)}, u32[]{:S(2)}) async-start(bf16[64,32,128]{2,1,0:T(8,128)(2,1)} %get-tuple-element.55), calls=%async_computation.3 | async-start | bytes 1048576 | tf_op jit(solution)/shard_map/all_to_all | solution.py:323
  104.9 29.6 %collective-permute-start.11 = (bf16[2,32,128]{2,1,0:T(8,128)(2,1)}, bf16[2,32,128]{2,1,0:T(8,128)(2,1)S(1)}, u32[]{:S(2)}, u32[]{:S(2)}) collective-permute-start(bf16[2,32,128]{2,1,0:T(8,128)(2,1)} %get-tuple-element.48), channel_id=1, source_target_pairs={{0,2},{2,4},{4,6},{6,0},{1,3},{3,5},{5,7},{7,1},{8,10},{10,12},{12... | collective-permute-start | bytes 49160 | tf_op jit(solution)/shard_map/ppermute | solution.py:329
  108.3 26.3 %collective-permute-start.12 = (bf16[2,32,128]{2,1,0:T(8,128)(2,1)}, bf16[2,32,128]{2,1,0:T(8,128)(2,1)S(1)}, u32[]{:S(2)}, u32[]{:S(2)}) collective-permute-start(bf16[2,32,128]{2,1,0:T(8,128)(2,1)} %get-tuple-element.49), channel_id=1, source_target_pairs={{0,4},{2,6},{4,0},{6,2},{1,5},{3,7},{5,1},{7,3},{8,12},{10,14},{12... | collective-permute-start | bytes 49160 | tf_op jit(solution)/shard_map/ppermute | solution.py:329
  111.2 23.3 %collective-permute-start.13 = (bf16[2,32,128]{2,1,0:T(8,128)(2,1)}, bf16[2,32,128]{2,1,0:T(8,128)(2,1)S(1)}, u32[]{:S(2)}, u32[]{:S(2)}) collective-permute-start(bf16[2,32,128]{2,1,0:T(8,128)(2,1)} %get-tuple-element.50), channel_id=1, source_target_pairs={{0,6},{2,0},{4,2},{6,4},{1,7},{3,1},{5,3},{7,5},{8,14},{10,8},{12,... | collective-permute-start | bytes 49160 | tf_op jit(solution)/shard_map/ppermute | solution.py:329
  122.4 0.8 copy-start.8
  125.7 20.9 %all-to-all-start.4 = ((bf16[12,32,128]{2,1,0:T(8,128)(2,1)}), bf16[12,32,128]{2,1,0:T(8,128)(2,1)S(1)}, u32[]{:S(2)}, u32[]{:S(2)}) async-start(bf16[12,32,128]{2,1,0:T(8,128)(2,1)} %get-tuple-element.61), calls=%async_computation.4 | async-start | bytes 196608 | tf_op jit(solution)/shard_map/all_to_all | solution.py:323
  134.6 3.2 %copy-start.13 = (bf16[4,2,32,128]{3,2,1,0:T(8,128)(2,1)}, bf16[4,2,32,128]{3,2,1,0:T(8,128)(2,1)S(1)}, u32[]{:S(2)}) copy-start(bf16[4,2,32,128]{3,2,1,0:T(8,128)(2,1)S(1)} %pad_maximum_fusion.1.m_mine) | copy-start | bytes 196612
  134.6 3.1 %collective-permute-start.14 = (bf16[4,2,32,128]{3,2,1,0:T(8,128)(2,1)S(1)}, bf16[4,2,32,128]{3,2,1,0:T(8,128)(2,1)S(1)}, u32[]{:S(2)}, u32[]{:S(2)}) collective-permute-start(bf16[4,2,32,128]{3,2,1,0:T(8,128)(2,1)S(1)} %pad_maximum_fusion.1.m_mine), channel_id=1, source_target_pairs={{0,1},{1,0},{2,3},{3,2},{4,5},{5,4},{6,7},{7,6},{8,9},{9,8},{10,11... | collective-permute-start | bytes 196616 | tf_op jit(solution)/shard_map/ppermute | solution.py:334
  137.7 0.6 copy-start.15
  146.6 0.6 copy-start.11

commit v4 on v3

--- a/solution.py
+++ b/solution.py
@@ -10,7 +10,7 @@
 LANES = 64
 CODES = 64
 GRID = {"y": 8, "x": 4, "core": 2}
-STEPS = 8
+STEPS = 4
 COUNT_BASE = 64
 
 epsilon = 1e-05
@@ -20,26 +20,28 @@
 bf16 = jnp.bfloat16
 
 
-def nn(a, b):
-    return lax.dot_general(
-        a, b, (((1,), (0,)), ((), ())), precision=lax.Precision.HIGHEST, preferred_element_type=f32
-    )
-
-
-def nt(a, b):
-    return lax.dot_general(
-        a, b, (((1,), (1,)), ((), ())), precision=lax.Precision.HIGHEST, preferred_element_type=f32
-    )
-
-
-def tn(a, b):
-    return nn(a.T, b)
-
-
 def once(a, b, dims):
     return lax.dot_general(
         a.astype(bf16), b.astype(bf16), (dims, ((), ())), preferred_element_type=f32
     )
+
+
+def split(a):
+    high = a.astype(bf16)
+    return high, (a - high.astype(f32)).astype(bf16)
+
+
+def thrice(a, b):
+    (a_high, a_low), (b_high, b_low) = split(a), split(b)
+    if a.shape[1] <= LANES:
+        return once(
+            jnp.concatenate([a_high, a_high, a_low], axis=1),
+            jnp.concatenate([b_high, b_low, b_high], axis=0),
+            ((1,), (0,)),
+        )
+    both = once(jnp.concatenate([a_high, a_low], axis=0), b_high, ((1,), (0,)))
+    rows = a.shape[0]
+    return both[:rows] + both[rows:] + once(a_high, b_low, ((1,), (0,)))
 
 
 def column(row):
@@ -71,9 +73,9 @@
     return jnp.concatenate([packed[:, :LANES], packed[:, LANES:]], axis=0)
 
 
-def causal(length):
+def earlier(length):
     s = lax.broadcasted_iota(jnp.int32, (length, length), 0)
-    return s <= lax.broadcasted_iota(jnp.int32, (length, length), 1)
+    return s < lax.broadcasted_iota(jnp.int32, (length, length), 1)
 
 
 def project_kernel(
@@ -104,15 +106,15 @@
         keys, _ = key_norm(raw)
         rate = rates(codes[...], all_frames)
         marks = jnp.broadcast_to(halvings[...].astype(f32).astype(bf16), (16, length))
-        mask = causal(length)
+        mask = earlier(length)
         ones = jnp.where(mask, 1.0, 0.0).astype(bf16)
-        counted = jnp.dot(marks, ones, preferred_element_type=f32)[:1]
+        counted = (jnp.dot(marks, ones, preferred_element_type=f32) + marks.astype(f32))[:1]
         at = (lax.broadcasted_iota(jnp.int32, (1, length), 1) + 1).astype(f32)
         prefix = rate * at + log_half * counted
         logs[...] = prefix
         total = counted[:, length - 1 :]
         closing = jnp.exp(rate * float(length) + log_half * total - prefix)
-        share = fold(nt(keys * closing, val)).astype(bf16)
+        share = fold(once(keys * closing, val, ((1,), (1,)))).astype(bf16)
         high = jnp.floor(total * (1.0 / COUNT_BASE))
         low = total - high * COUNT_BASE
         top = lax.broadcasted_iota(jnp.int32, (16, 2 * LANES), 0) == 0
@@ -121,10 +123,12 @@
         for z in range(payload.shape[0]):
             payload[z, :half] = share
             payload[z, half:] = counts
-        masked = jnp.where(mask, tn(keys * jnp.exp(-prefix), recept * jnp.exp(prefix)), 0.0)
+        masked = jnp.where(
+            mask, thrice((keys * jnp.exp(-prefix)).T, recept * jnp.exp(prefix)), 0.0
+        )
         scores[...] = masked.astype(bf16)
-        own = jnp.sum(recept * column(extra[...]) * keys, axis=0, keepdims=True)
-        local[...] = nn(val, masked) + own * val
+        own = jnp.sum(recept * (column(extra[...]) + 1.0) * keys, axis=0, keepdims=True)
+        local[...] = thrice(val, masked) + own * val
         by_frame = tutor[...].astype(f32).T.astype(bf16)
         tiles = GRID["x"] * GRID["core"]
         part = length // tiles
@@ -160,7 +164,7 @@
         state = jnp.where(z < mine, longer, state)
     begin = unfold(state)
     start[...] = begin
-    y = local[...] + tn(begin, reads[...] * jnp.exp(logs[...]))
+    y = local[...] + thrice(begin.T, reads[...] * jnp.exp(logs[...]))
     centred = y - over_channels(y)
     inv = lax.rsqrt(over_channels(centred * centred) + epsilon)
     inverse[...] = inv
@@ -231,10 +235,10 @@
     for n, y, places in chunks:
         part = weights[n, y : y + group].reshape(group * LANES, tiles * LANES)
         grads = lax.dot_general(
-            diff, part, (((1,), (1,)), ((), ())), preferred_element_type=f32
+            part, diff, (((1,), (1,)), ((), ())), preferred_element_type=f32
         ).astype(bf16)
         for g, p in enumerate(places):
-            sent[p] = fold(grads[:, g * LANES : (g + 1) * LANES])
+            sent[p] = fold(grads[g * LANES : (g + 1) * LANES])
 
 
 def back_kernel(got, unit, inverse, gain, reads, logs, payload, sensitivity):
@@ -245,13 +249,13 @@
         for j in range(1, GRID["y"]):
             total = total + got[j * tiles + i].astype(f32)
         frames.append(unfold(total))
-    scaled = jnp.concatenate(frames, axis=0).T * column(gain[...])
+    scaled = jnp.concatenate(frames, axis=1) * column(gain[...])
     each = unit[...]
     grad = inverse[...] * (
         scaled - over_channels(scaled) - each * over_channels(scaled * each)
     )
     sensitivity[...] = grad
-    share = fold(nt(reads[...] * jnp.exp(logs[...]), grad)).astype(bf16)
+    share = fold(once(reads[...] * jnp.exp(logs[...]), grad, ((1,), (1,)))).astype(bf16)
     for z in range(payload.shape[0]):
         payload[z] = share
 
@@ -275,12 +279,12 @@
     keys, _ = key_norm(keys_raw[...])
     prefix = logs[...]
     grow, shrink = jnp.exp(prefix), jnp.exp(-prefix)
-    own_weight = column(extra[...])
-    twofold = jnp.where(causal(length), once(val.T, grad, ((1,), (0,))), 0.0).astype(bf16)
+    own_weight = column(extra[...]) + 1.0
+    twofold = jnp.where(earlier(length), once(val.T, grad, ((1,), (0,))), 0.0).astype(bf16)
     progressive = jnp.sum(grad * val, axis=0, keepdims=True) * own_weight
     own = jnp.sum(recept * own_weight * keys, axis=0, keepdims=True)
     grad_reads[...] = (
-        grow * (nn(start[...], grad) + once(keys * shrink, twofold, ((1,), (0,)))) + progressive * keys
+        grow * (once(start[...], grad, ((1,), (0,))) + once(keys * shrink, twofold, ((1,), (0,)))) + progressive * keys
     ).astype(bf16)
     part_keys[...] = shrink * once(recept * grow, twofold, ((1,), (1,))) + progressive * recept
     part_values[...] = once(grad, scores[...], ((1,), (1,))) + own * grad
@@ -303,20 +307,27 @@
     keys, scale = key_norm(raw)
     prefix = logs[...]
     closing = jnp.exp(prefix[:, length - 1 :] - prefix)
-    grad = part_keys[...] + closing * nn(walking, values[...])
-    grad_values[...] = (part_values[...] + tn(walking, keys * closing)).astype(bf16)
+    grad = part_keys[...] + closing * once(walking, values[...], ((1,), (0,)))
+    grad_values[...] = (part_values[...] + once(walking.T, keys * closing, ((1,), (0,)))).astype(bf16)
     grad_keys[...] = (
         0.125 * scale * (grad - scale * scale * raw * over_channels(raw * grad))
     ).astype(bf16)
 
 
-def call(kernel, outs, args, cost=1 << 23, **more):
+def call(kernel, outs, args, here=(), cost=1 << 23, **more):
     return pl.pallas_call(
         kernel,
         cost_estimate=pl.CostEstimate(flops=1 << 30, transcendentals=0, bytes_accessed=cost),
-        out_shape=[jax.ShapeDtypeStruct(shape, kind) for shape, kind in outs],
+        out_shape=[
+            pltpu.VMEM(shape, kind) if n in here else jax.ShapeDtypeStruct(shape, kind)
+            for n, (shape, kind) in enumerate(outs)
+        ],
         **more,
     )(*args)
+
+
+def near(*arrays):
+    return tuple(pltpu.with_memory_space_constraint(a, pltpu.VMEM) for a in arrays)
 
 
 def exchange(array, axis):
@@ -372,7 +383,6 @@
         pl.BlockSpec((length, depth), lambda k: (0, k)),
         pl.BlockSpec((LANES, depth), lambda k: (0, k)),
     ]
-    serial = pltpu.CompilerParams(dimension_semantics=("arbitrary",))
     payload, reads, keys_raw, values, logs, scores, local, *tutor = call(
         functools.partial(project_kernel, all_frames),
         [
@@ -384,13 +394,13 @@
             incoming_signals, receptor_linear_map.T, lock_linear_map.T, worth_linear_map.T,
             codes, halvings, extra, tutor_aggregated.T,
         ),
+        here=(1, 4, 6),
         grid=(STEPS,),
         in_specs=[by_step[0]] + [by_step[1]] * 3 + [whole] * 4,
         out_specs=[whole] * (7 + GRID["x"]),
         scratch_shapes=[
             pltpu.VMEM((length, 3 * LANES), f32), pltpu.VMEM((tiles,) + block, bf16),
         ],
-        compiler_params=serial,
     )
     tutor = jnp.stack(along_x(tutor))
     payload, columns, tutor = barrier((payload, columns, tutor))
@@ -399,14 +409,15 @@
     sent, start, unit, inverse = call(
         functools.partial(yields_kernel, all_frames),
         [((rows * tiles,) + block, bf16), ((LANES, LANES), f32), (flat, f32), ((1, length), f32)],
-        (everyone, local, reads, logs, codes, gain),
+        near(everyone, local, reads, logs) + (codes, gain),
+        here=(2, 3),
     )
     got = exchange(sent, head)
     w_other = [swap(w) for w in w_mine]
     sent, *mixed = call(
         middle_kernel,
         [((rows * tiles,) + block, bf16)] + [((2,) + block, bf16)] * GRID["x"],
-        (got, tutor, swap(tutor), *w_mine, *w_other),
+        near(got, tutor, swap(tutor)) + (*w_mine, *w_other),
         in_specs=[whole] * 3 + [pl.BlockSpec(memory_space=pl.ANY)] * (2 * GRID["x"]),
         scratch_shapes=[
             pltpu.VMEM((tiles,) + block, bf16),
@@ -419,18 +430,19 @@
     payload, sensitivity = call(
         back_kernel,
         [((blocks, half, 2 * LANES), bf16), (flat, f32)],
-        (got, unit, inverse, gain, reads, logs),
+        near(got, unit, inverse) + (gain,) + near(reads, logs),
     )
     later = exchange(payload, "ctx")
     mixed_out, grad_reads, part_keys, part_values = call(
         window_kernel,
         [(flat, bf16), (flat, bf16), (flat, f32), (flat, f32)],
         (mixed, swap(mixed), reads, keys_raw, values, logs, extra, scores, start, sensitivity),
+        here=(2, 3),
     )
     grad_keys, grad_values = call(
         functools.partial(final_kernel, all_frames),
         [(flat, bf16), (flat, bf16)],
-        (later, everyone, part_keys, part_values, keys_raw, values, logs, codes),
+        near(later, everyone, part_keys, part_values, keys_raw, values, logs) + (codes,),
     )
     return (mixed_out.T, grad_reads.T, grad_keys.T, grad_values.T)
 

time: 151 us -> 145 us (0.960)
  Pallas kernels: 25.4 us -> 19.4 us
  starting transfers between devices: 92.6 us -> 95.7 us
  local copies, waits for them, and re-layouts: 7.16 us -> 4.37 us
    pallas_call x6, Pallas kernels: 25.4 us -> 19.4 us  [call(): pl.pallas_call(kernel, cost_estimate=pl.CostEstimate(flops=1 << 30, trans...]
    all_to_all x5, starting transfers between devices: 43.7 us -> 46.7 us  [exchange(): return lax.all_to_all(array, axis, 0, 0)]
    unnamed x32 -> x26, local copies, waits for them, and re-layouts: 5.24 us -> 2.46 us
  transfers between devices with their start and end apart: 20 -> 20, of which waited for: 6 -> 6; matrix products, arithmetic and copies ran while one was open for 0% -> 1% of each run, Pallas kernels for 12% -> 9%
where the time goes in v4:
time: 145 us; the launch traced here: 144 us
  starting transfers between devices  95.7 us (66%)
  waiting for transfers between devices  22.6 us (16%)
  Pallas kernels  19.4 us (13%)
  local copies, waits for them, and re-layouts  4.37 us (3%)
    all_to_all x5, starting transfers between devices, exchange(): return lax.all_to_all(array, axis, 0, 0)  46.7 us
    ppermute x9, starting transfers between devices, along_x(): lax.ppermute(parts[s], 'x', [(i, (i + s) % n) for i in range(n)])  36.3 us
    pallas_call x6, Pallas kernels, call(): pl.pallas_call(kernel, cost_estimate=pl.CostEstimate(flops=1 << 30, trans...  19.4 us
    all_to_all x5, waiting for transfers between devices, exchange(): return lax.all_to_all(array, axis, 0, 0)  16.4 us
    ppermute x6, starting transfers between devices, swap(): return lax.ppermute(array, 'core', [(0, 1), (1, 0)])  12.6 us
    ppermute x9, waiting for transfers between devices, along_x(): lax.ppermute(parts[s], 'x', [(i, (i + s) % n) for i in range(n)])  3.91 us
  transfers between devices with their start and end apart: 20, of which 6 were waited for; matrix products, arithmetic and copies ran while one was open for 1% of the time, Pallas kernels for 9%

profile of v4, /device:TPU:2, one launch (start us, length us, event | category | flops | bytes accessed | tf_op | source)
XLA Modules:
  0.0 143.8 jit_solution(8911356794101703070)
XLA Ops:
  0.6 1.9 %copy.17 = bf16[8,8,8,512]{3,2,0,1:T(8,128)(2,1)} copy(bf16[8,8,8,512]{3,2,1,0:T(8,128)(2,1)} %bitcast.30) | data formatting | bytes 1048576 | tf_op jit(solution)/shard_map/reshape | solution.py:372
  2.5 7.1 %all-to-all-start = ((bf16[8,64,512]{2,1,0:T(8,128)(2,1)}), bf16[8,64,512]{2,1,0:T(8,128)(2,1)S(1)}, u32[]{:S(2)}, u32[]{:S(2)}) async-start(bf16[8,64,512]{2,1,0:T(8,128)(2,1)} %bitcast.26), calls=%async_computation | async-start | bytes 1048576 | tf_op jit(solution)/shard_map/all_to_all | solution.py:334
  9.6 6.5 %shard_map.129 = (bf16[12,48,128]{2,1,0:T(8,128)(2,1)}, f32[64,512]{1,0:T(8,128)S(1)}, f32[64,512]{1,0:T(8,128)}, f32[64,512]{1,0:T(8,128)}, f32[64,512]{1,0:T(8...) custom-call(bf16[512,4096]{1,0:T(8,128)(2,1)} %x.1, ...), custom_call_target="tpu_custom_call" | custom-call | flops 1073741824 | bytes 8388608 | tf_op jit(solution)/shard_map/pallas_call | solution.py:318
  16.1 0.0 copy-start.2
  16.1 0.0 copy-start.4
  16.1 3.4 %collective-permute-start = (bf16[2,32,128]{2,1,0:T(8,128)(2,1)}, bf16[2,32,128]{2,1,0:T(8,128)(2,1)S(1)}, u32[]{:S(2)}, u32[]{:S(2)}) collective-permute-start(bf16[2,32,128]{2,1,0:T(8,128)(2,1)} %get-tuple-element.37), channel_id=1, source_target_pairs={{0,2},{2,4},{4,6},{6,0},{1,3},{3,5},{5,7},{7,1},{8,10},{10,12},{12... | collective-permute-start | bytes 49160 | tf_op jit(solution)/shard_map/ppermute | solution.py:340
  19.5 8.5 %collective-permute-start.1 = (bf16[2,32,128]{2,1,0:T(8,128)(2,1)}, bf16[2,32,128]{2,1,0:T(8,128)(2,1)S(1)}, u32[]{:S(2)}, u32[]{:S(2)}) collective-permute-start(bf16[2,32,128]{2,1,0:T(8,128)(2,1)} %get-tuple-element.38), channel_id=1, source_target_pairs={{0,4},{2,6},{4,0},{6,2},{1,5},{3,7},{5,1},{7,3},{8,12},{10,14},{12... | collective-permute-start | bytes 49160 | tf_op jit(solution)/shard_map/ppermute | solution.py:340
  28.0 1.9 %collective-permute-start.2 = (bf16[2,32,128]{2,1,0:T(8,128)(2,1)}, bf16[2,32,128]{2,1,0:T(8,128)(2,1)S(1)}, u32[]{:S(2)}, u32[]{:S(2)}) collective-permute-start(bf16[2,32,128]{2,1,0:T(8,128)(2,1)} %get-tuple-element.39), channel_id=1, source_target_pairs={{0,6},{2,0},{4,2},{6,4},{1,7},{3,1},{5,3},{7,5},{8,14},{10,8},{12,... | collective-permute-start | bytes 49160 | tf_op jit(solution)/shard_map/ppermute | solution.py:340
  29.9 0.0 collective-permute-done
  29.9 0.0 collective-permute-done.1
  29.9 3.9 %collective-permute-done.2 = bf16[2,32,128]{2,1,0:T(8,128)(2,1)S(1)} collective-permute-done((bf16[2,32,128]{2,1,0:T(8,128)(2,1)}, bf16[2,32,128]{2,1,0:T(8,128)(2,1)S(1)}, u32[]{:S(2)}, u32[]{:S(2)}) %collective-permute-start.2) | collective-permute-done | bytes 16416 | tf_op jit(solution)/shard_map/ppermute | solution.py:340
  33.8 0.7 pad_maximum_fusion.t_mine
  34.6 0.0 all-to-all-done.w0
  34.6 0.0 copy-start.5
  34.6 9.7 %all-to-all-start.1 = ((bf16[12,48,128]{2,1,0:T(8,128)(2,1)}), bf16[12,48,128]{2,1,0:T(8,128)(2,1)S(1)}, u32[]{:S(2)}, u32[]{:S(2)}) async-start(bf16[12,48,128]{2,1,0:T(8,128)(2,1)} %get-tuple-element.40), calls=%async_computation.1 | async-start | bytes 294912 | tf_op jit(solution)/shard_map/all_to_all | solution.py:334
  44.3 4.1 %collective-permute-start.6 = (bf16[8,64,512]{2,1,0:T(8,128)(2,1)S(1)}, bf16[8,64,512]{2,1,0:T(8,128)(2,1)S(1)}, u32[]{:S(2)}, u32[]{:S(2)}) collective-permute-start(bf16[8,64,512]{2,1,0:T(8,128)(2,1)S(1)} %all-to-all-done.w0), channel_id=1, source_target_pairs={{0,6},{2,0},{4,2},{6,4},{1,7},{3,1},{5,3},{7,5},{8,14},{10,8},{12,... | collective-permute-start | bytes 1572872 | tf_op jit(solution)/shard_map/ppermute | solution.py:340
  48.4 3.4 %collective-permute-start.5 = (bf16[8,64,512]{2,1,0:T(8,128)(2,1)S(1)}, bf16[8,64,512]{2,1,0:T(8,128)(2,1)}, u32[]{:S(2)}, u32[]{:S(2)}) collective-permute-start(bf16[8,64,512]{2,1,0:T(8,128)(2,1)S(1)} %all-to-all-done.w0), channel_id=1, source_target_pairs={{0,4},{2,6},{4,0},{6,2},{1,5},{3,7},{5,1},{7,3},{8,12},{10,14},{12... | collective-permute-start | bytes 1572872 | tf_op jit(solution)/shard_map/ppermute | solution.py:340
  51.8 4.5 %collective-permute-start.4 = (bf16[8,64,512]{2,1,0:T(8,128)(2,1)S(1)}, bf16[8,64,512]{2,1,0:T(8,128)(2,1)}, u32[]{:S(2)}, u32[]{:S(2)}) collective-permute-start(bf16[8,64,512]{2,1,0:T(8,128)(2,1)S(1)} %all-to-all-done.w0), channel_id=1, source_target_pairs={{0,2},{2,4},{4,6},{6,0},{1,3},{3,5},{5,7},{7,1},{8,10},{10,12},{12... | collective-permute-start | bytes 1572872 | tf_op jit(solution)/shard_map/ppermute | solution.py:340
  56.3 0.0 all-to-all-done.1.everyone
  56.3 2.2 %shard_map.130 = (bf16[64,32,128]{2,1,0:T(8,128)(2,1)}, f32[64,64]{1,0:T(8,128)}, f32[64,512]{1,0:T(8,128)S(1)}, f32[1,512]{1,0:T(1,128)S(1)}) custom-call(bf16[12,48,128]{2,1,0:T(8,128)(2,1)S(1)} %all-to-all-done.1.everyone, f32[64,512]{1,0:T(8,128)S(1)} %get-tuple-element.41.local, f32[64,512]{1,0:T(8,128)S(1)} %get-tuple-element.42.reads, ...), custom_call_target="tpu_custom_call" | custom-call | flops 1073741824 | bytes 8388608 | tf_op jit(solution)/shard_map/pallas_call | solution.py:318
  58.6 11.8 %all-to-all-start.2 = ((bf16[64,32,128]{2,1,0:T(8,128)(2,1)}), bf16[64,32,128]{2,1,0:T(8,128)(2,1)S(1)}, u32[]{:S(2)}, u32[]{:S(2)}) async-start(bf16[64,32,128]{2,1,0:T(8,128)(2,1)} %get-tuple-element.44), calls=%async_computation.2 | async-start | bytes 1048576 | tf_op jit(solution)/shard_map/all_to_all | solution.py:334
  70.4 2.1 %collective-permute-start.7 = (bf16[8,64,512]{2,1,0:T(8,128)(2,1)S(1)}, bf16[8,64,512]{2,1,0:T(8,128)(2,1)S(1)}, u32[]{:S(2)}, u32[]{:S(2)}) collective-permute-start(bf16[8,64,512]{2,1,0:T(8,128)(2,1)S(1)} %all-to-all-done.w0), channel_id=1, source_target_pairs={{0,1},{1,0},{2,3},{3,2},{4,5},{5,4},{6,7},{7,6},{8,9},{9,8},{10,11... | collective-permute-start | bytes 1572872 | tf_op jit(solution)/shard_map/ppermute | solution.py:345
  72.5 0.0 collective-permute-done.6.w3
  72.5 0.0 copy-start.6
  72.5 2.3 %collective-permute-start.10 = (bf16[8,64,512]{2,1,0:T(8,128)(2,1)S(1)}, bf16[8,64,512]{2,1,0:T(8,128)(2,1)S(1)}, u32[]{:S(2)}, u32[]{:S(2)}) collective-permute-start(bf16[8,64,512]{2,1,0:T(8,128)(2,1)S(1)} %collective-permute-done.6.w3), channel_id=1, source_target_pairs={{0,1},{1,0},{2,3},{3,2},{4,5},{5,4},{6,7},{7,6},{8,9},{9,8},{10,11... | collective-permute-start | bytes 1572872 | tf_op jit(solution)/shard_map/ppermute | solution.py:345
  74.8 0.0 collective-permute-done.5.w2
  74.8 2.1 %collective-permute-start.9 = (bf16[8,64,512]{2,1,0:T(8,128)(2,1)}, bf16[8,64,512]{2,1,0:T(8,128)(2,1)S(1)}, u32[]{:S(2)}, u32[]{:S(2)}) collective-permute-start(bf16[8,64,512]{2,1,0:T(8,128)(2,1)} %collective-permute-done.5.w2), channel_id=1, source_target_pairs={{0,1},{1,0},{2,3},{3,2},{4,5},{5,4},{6,7},{7,6},{8,9},{9,8},{10,11... | collective-permute-start | bytes 1572872 | tf_op jit(solution)/shard_map/ppermute | solution.py:345
  76.9 0.0 collective-permute-done.4.w1
  76.9 2.3 %collective-permute-start.8 = (bf16[8,64,512]{2,1,0:T(8,128)(2,1)}, bf16[8,64,512]{2,1,0:T(8,128)(2,1)}, u32[]{:S(2)}, u32[]{:S(2)}) collective-permute-start(bf16[8,64,512]{2,1,0:T(8,128)(2,1)} %collective-permute-done.4.w1), channel_id=1, source_target_pairs={{0,1},{1,0},{2,3},{3,2},{4,5},{5,4},{6,7},{7,6},{8,9},{9,8},{10,11... | collective-permute-start | bytes 1572872 | tf_op jit(solution)/shard_map/ppermute | solution.py:345
  79.1 2.1 %collective-permute-start.3 = (bf16[4,2,32,128]{3,2,1,0:T(8,128)(2,1)S(1)}, bf16[4,2,32,128]{3,2,1,0:T(8,128)(2,1)S(1)}, u32[]{:S(2)}, u32[]{:S(2)}) collective-permute-start(bf16[4,2,32,128]{3,2,1,0:T(8,128)(2,1)S(1)} %pad_maximum_fusion.t_mine), channel_id=1, source_target_pairs={{0,1},{1,0},{2,3},{3,2},{4,5},{5,4},{6,7},{7,6},{8,9},{9,8},{10,11... | collective-permute-start | bytes 196616 | tf_op jit(solution)/shard_map/ppermute | solution.py:345
  81.2 1.1 collective-permute-done.3.t_other
  82.3 0.0 collective-permute-done.7.v0
  82.3 0.0 collective-permute-done.10.v3
  82.3 0.0 copy-start.8
  82.3 0.0 collective-permute-done.9.v2
  82.3 0.8 copy-done.7
  83.1 0.2 copy-done.8
  83.3 0.8 copy-done.9
  84.1 0.0 collective-permute-done.8.v1
  84.1 3.9 %all-to-all-done.2.got = bf16[64,32,128]{2,1,0:T(8,128)(2,1)S(1)} async-done(((bf16[64,32,128]{2,1,0:T(8,128)(2,1)}), bf16[64,32,128]{2,1,0:T(8,128)(2,1)S(1)}, u32[]{:S(2)}, u32[]{:S(2)}) %all-to-all-start.2) | async-done | bytes 524320 | tf_op jit(solution)/shard_map/all_to_all | solution.py:334
  88.0 0.0 copy-done.5
  88.0 4.6 %shard_map.131 = (bf16[64,32,128]{2,1,0:T(8,128)(2,1)}, bf16[2,32,128]{2,1,0:T(8,128)(2,1)}, bf16[2,32,128]{2,1,0:T(8,128)(2,1)}, bf16[2,32,128]{2,1,0:T(8,128)(2,1)}, bf16[2,32,128]{2,1,0:T(8,128)(2,1)}) custom-call(bf16[64,32,128]{2,1,0:T(8,128)(2,1)S(1)} %all-to-all-done.2.got, bf16[4,2,32,128]{3,2,1,0:T(8,128)(2,1)S(1)} %pad_maximum_fusion.t_mine, ...), custom_call_target="tpu_custom_call" | custom-call | flops 1073741824 | bytes 8388608 | tf_op jit(solution)/shard_map/pallas_call | solution.py:318
  92.6 0.0 copy-start.11
  92.6 6.6 %all-to-all-start.3 = ((bf16[64,32,128]{2,1,0:T(8,128)(2,1)}), bf16[64,32,128]{2,1,0:T(8,128)(2,1)S(1)}, u32[]{:S(2)}, u32[]{:S(2)}) async-start(bf16[64,32,128]{2,1,0:T(8,128)(2,1)} %get-tuple-element.55), calls=%async_computation.3 | async-start | bytes 1048576 | tf_op jit(solution)/shard_map/all_to_all | solution.py:334
  99.2 0.0 copy-start
  99.3 0.0 copy-start.1
  99.3 3.5 %collective-permute-start.11 = (bf16[2,32,128]{2,1,0:T(8,128)(2,1)}, bf16[2,32,128]{2,1,0:T(8,128)(2,1)S(1)}, u32[]{:S(2)}, u32[]{:S(2)}) collective-permute-start(bf16[2,32,128]{2,1,0:T(8,128)(2,1)} %get-tuple-element.48), channel_id=1, source_target_pairs={{0,2},{2,4},{4,6},{6,0},{1,3},{3,5},{5,7},{7,1},{8,10},{10,12},{12... | collective-permute-start | bytes 49160 | tf_op jit(solution)/shard_map/ppermute | solution.py:340
  102.8 3.0 %collective-permute-start.12 = (bf16[2,32,128]{2,1,0:T(8,128)(2,1)}, bf16[2,32,128]{2,1,0:T(8,128)(2,1)S(1)}, u32[]{:S(2)}, u32[]{:S(2)}) collective-permute-start(bf16[2,32,128]{2,1,0:T(8,128)(2,1)} %get-tuple-element.49), channel_id=1, source_target_pairs={{0,4},{2,6},{4,0},{6,2},{1,5},{3,7},{5,1},{7,3},{8,12},{10,14},{12... | collective-permute-start | bytes 49160 | tf_op jit(solution)/shard_map/ppermute | solution.py:340
  105.8 4.1 %collective-permute-start.13 = (bf16[2,32,128]{2,1,0:T(8,128)(2,1)}, bf16[2,32,128]{2,1,0:T(8,128)(2,1)S(1)}, u32[]{:S(2)}, u32[]{:S(2)}) collective-permute-start(bf16[2,32,128]{2,1,0:T(8,128)(2,1)} %get-tuple-element.50), channel_id=1, source_target_pairs={{0,6},{2,0},{4,2},{6,4},{1,7},{3,1},{5,3},{7,5},{8,14},{10,8},{12,... | collective-permute-start | bytes 49160 | tf_op jit(solution)/shard_map/ppermute | solution.py:340
  109.8 7.0 %all-to-all-done.3.got = bf16[64,32,128]{2,1,0:T(8,128)(2,1)S(1)} async-done(((bf16[64,32,128]{2,1,0:T(8,128)(2,1)}), bf16[64,32,128]{2,1,0:T(8,128)(2,1)S(1)}, u32[]{:S(2)}, u32[]{:S(2)}) %all-to-all-start.3) | async-done | bytes 524320 | tf_op jit(solution)/shard_map/all_to_all | solution.py:334
  116.8 0.0 copy-done.4
  116.8 1.7 %shard_map.132 = (bf16[12,32,128]{2,1,0:T(8,128)(2,1)}, f32[64,512]{1,0:T(8,128)}) custom-call(bf16[64,32,128]{2,1,0:T(8,128)(2,1)S(1)} %all-to-all-done.3.got, f32[64,512]{1,0:T(8,128)S(1)} %get-tuple-element.56.unit, f32[1,512]{1,0:T(1,128)S(1)} %get-tuple-element.57.inverse, f32[1,64]{1,0:T(1,128)} %bitcast.47, f32[64,512]{1,0:T(8,128)S(1)} %get-tuple-element.42.reads, ...), custom_call_target="tpu_custom_call" | custom-call | flops 1073741824 | bytes 8388608 | tf_op jit(solution)/shard_map/pallas_call | solution.py:318
  118.5 11.4 %all-to-all-start.4 = ((bf16[12,32,128]{2,1,0:T(8,128)(2,1)}), bf16[12,32,128]{2,1,0:T(8,128)(2,1)S(1)}, u32[]{:S(2)}, u32[]{:S(2)}) async-start(bf16[12,32,128]{2,1,0:T(8,128)(2,1)} %get-tuple-element.61), calls=%async_computation.4 | async-start | bytes 196608 | tf_op jit(solution)/shard_map/all_to_all | solution.py:334
  130.0 0.0 collective-permute-done.11
  130.0 0.0 collective-permute-done.12
  130.0 0.0 collective-permute-done.13
  130.0 0.0 copy-done.11
  130.0 0.0 copy-start.10
  130.0 1.9 %collective-permute-start.14 = (bf16[4,2,32,128]{3,2,1,0:T(8,128)(2,1)S(1)}, bf16[4,2,32,128]{3,2,1,0:T(8,128)(2,1)S(1)}, u32[]{:S(2)}, u32[]{:S(2)}) collective-permute-start(bf16[4,2,32,128]{3,2,1,0:T(8,128)(2,1)S(1)} %pad_maximum_fusion.1.m_mine), channel_id=1, source_target_pairs={{0,1},{1,0},{2,3},{3,2},{4,5},{5,4},{6,7},{7,6},{8,9},{9,8},{10,11... | collective-permute-start | bytes 196616 | tf_op jit(solution)/shard_map/ppermute | solution.py:345
  132.0 1.2 collective-permute-done.14.m_other
  133.2 0.6 copy-done.12
  133.8 2.7 %shard_map.133 = (bf16[64,512]{1,0:T(8,128)(2,1)}, bf16[64,512]{1,0:T(8,128)(2,1)}, f32[64,512]{1,0:T(8,128)S(1)}, f32[64,512]{1,0:T(8,128)S(1)}) custom-call(bf16[4,2,32,128]{3,2,1,0:T(8,128)(2,1)} %copy-done.10, bf16[4,2,32,128]{3,2,1,0:T(8,128)(2,1)} %copy-done.12, f32[64,512]{1,0:T(8,128)} %copy-done.4, f32[64,512]{1,0:T(8,128)} %get-tuple-element.51.keys_raw, ...), custom_call_target="tpu_custom_call" | custom-call | flops 1073741824 | bytes 8388608 | tf_op jit(solution)/shard_map/pallas_call | solution.py:318
  136.5 5.6 %all-to-all-done.4.later = bf16[12,32,128]{2,1,0:T(8,128)(2,1)S(1)} async-done(((bf16[12,32,128]{2,1,0:T(8,128)(2,1)}), bf16[12,32,128]{2,1,0:T(8,128)(2,1)S(1)}, u32[]{:S(2)}, u32[]{:S(2)}) %all-to-all-start.4) | async-done | bytes 98336 | tf_op jit(solution)/shard_map/all_to_all | solution.py:334
  142.1 1.7 %shard_map.134 = (bf16[64,512]{1,0:T(8,128)(2,1)}, bf16[64,512]{1,0:T(8,128)(2,1)}) custom-call(bf16[12,32,128]{2,1,0:T(8,128)(2,1)S(1)} %all-to-all-done.4.later, bf16[12,48,128]{2,1,0:T(8,128)(2,1)S(1)} %all-to-all-done.1.everyone, f32[64,512]{1,0:T(8,128)S(1)} %get-tuple-element.62.part_keys, f32[64,512]{1,0:T(8,128)S(1)} %get-tuple-element.63.part_values, ...), custom_call_target="tpu_custom_call" | custom-call | flops 1073741824 | bytes 8388608 | tf_op jit(solution)/shard_map/pallas_call | solution.py:318
  (11 shorter events, 0.0 us)
Async XLA Ops:
  2.5 32.0 %all-to-all-start = ((bf16[8,64,512]{2,1,0:T(8,128)(2,1)}), bf16[8,64,512]{2,1,0:T(8,128)(2,1)S(1)}, u32[]{:S(2)}, u32[]{:S(2)}) async-start(bf16[8,64,512]{2,1,0:T(8,128)(2,1)} %bitcast.26), calls=%async_computation | async-start | bytes 1048576 | tf_op jit(solution)/shard_map/all_to_all | solution.py:334
  16.1 100.7 %copy-start.2 = (f32[64,512]{1,0:T(8,128)}, f32[64,512]{1,0:T(8,128)S(1)}, u32[]{:S(2)}) copy-start(f32[64,512]{1,0:T(8,128)S(1)} %get-tuple-element.43.logs) | copy-start | bytes 393220
  16.1 100.7 %copy-start.4 = (f32[64,512]{1,0:T(8,128)}, f32[64,512]{1,0:T(8,128)S(1)}, u32[]{:S(2)}) copy-start(f32[64,512]{1,0:T(8,128)S(1)} %get-tuple-element.42.reads) | copy-start | bytes 393220
  16.1 13.8 %collective-permute-start = (bf16[2,32,128]{2,1,0:T(8,128)(2,1)}, bf16[2,32,128]{2,1,0:T(8,128)(2,1)S(1)}, u32[]{:S(2)}, u32[]{:S(2)}) collective-permute-start(bf16[2,32,128]{2,1,0:T(8,128)(2,1)} %get-tuple-element.37), channel_id=1, source_target_pairs={{0,2},{2,4},{4,6},{6,0},{1,3},{3,5},{5,7},{7,1},{8,10},{10,12},{12... | collective-permute-start | bytes 49160 | tf_op jit(solution)/shard_map/ppermute | solution.py:340
  19.5 10.4 %collective-permute-start.1 = (bf16[2,32,128]{2,1,0:T(8,128)(2,1)}, bf16[2,32,128]{2,1,0:T(8,128)(2,1)S(1)}, u32[]{:S(2)}, u32[]{:S(2)}) collective-permute-start(bf16[2,32,128]{2,1,0:T(8,128)(2,1)} %get-tuple-element.38), channel_id=1, source_target_pairs={{0,4},{2,6},{4,0},{6,2},{1,5},{3,7},{5,1},{7,3},{8,12},{10,14},{12... | collective-permute-start | bytes 49160 | tf_op jit(solution)/shard_map/ppermute | solution.py:340
  28.0 5.8 %collective-permute-start.2 = (bf16[2,32,128]{2,1,0:T(8,128)(2,1)}, bf16[2,32,128]{2,1,0:T(8,128)(2,1)S(1)}, u32[]{:S(2)}, u32[]{:S(2)}) collective-permute-start(bf16[2,32,128]{2,1,0:T(8,128)(2,1)} %get-tuple-element.39), channel_id=1, source_target_pairs={{0,6},{2,0},{4,2},{6,4},{1,7},{3,1},{5,3},{7,5},{8,14},{10,8},{12,... | collective-permute-start | bytes 49160 | tf_op jit(solution)/shard_map/ppermute | solution.py:340
  34.6 53.4 %copy-start.5 = (bf16[8,64,512]{2,1,0:T(8,128)(2,1)}, bf16[8,64,512]{2,1,0:T(8,128)(2,1)S(1)}, u32[]{:S(2)}) copy-start(bf16[8,64,512]{2,1,0:T(8,128)(2,1)S(1)} %all-to-all-done.w0) | copy-start | bytes 1572868
  34.6 21.8 %all-to-all-start.1 = ((bf16[12,48,128]{2,1,0:T(8,128)(2,1)}), bf16[12,48,128]{2,1,0:T(8,128)(2,1)S(1)}, u32[]{:S(2)}, u32[]{:S(2)}) async-start(bf16[12,48,128]{2,1,0:T(8,128)(2,1)} %get-tuple-element.40), calls=%async_computation.1 | async-start | bytes 294912 | tf_op jit(solution)/shard_map/all_to_all | solution.py:334
  44.3 28.2 %collective-permute-start.6 = (bf16[8,64,512]{2,1,0:T(8,128)(2,1)S(1)}, bf16[8,64,512]{2,1,0:T(8,128)(2,1)S(1)}, u32[]{:S(2)}, u32[]{:S(2)}) collective-permute-start(bf16[8,64,512]{2,1,0:T(8,128)(2,1)S(1)} %all-to-all-done.w0), channel_id=1, source_target_pairs={{0,6},{2,0},{4,2},{6,4},{1,7},{3,1},{5,3},{7,5},{8,14},{10,8},{12,... | collective-permute-start | bytes 1572872 | tf_op jit(solution)/shard_map/ppermute | solution.py:340
  48.4 26.4 %collective-permute-start.5 = (bf16[8,64,512]{2,1,0:T(8,128)(2,1)S(1)}, bf16[8,64,512]{2,1,0:T(8,128)(2,1)}, u32[]{:S(2)}, u32[]{:S(2)}) collective-permute-start(bf16[8,64,512]{2,1,0:T(8,128)(2,1)S(1)} %all-to-all-done.w0), channel_id=1, source_target_pairs={{0,4},{2,6},{4,0},{6,2},{1,5},{3,7},{5,1},{7,3},{8,12},{10,14},{12... | collective-permute-start | bytes 1572872 | tf_op jit(solution)/shard_map/ppermute | solution.py:340
  51.8 25.1 %collective-permute-start.4 = (bf16[8,64,512]{2,1,0:T(8,128)(2,1)S(1)}, bf16[8,64,512]{2,1,0:T(8,128)(2,1)}, u32[]{:S(2)}, u32[]{:S(2)}) collective-permute-start(bf16[8,64,512]{2,1,0:T(8,128)(2,1)S(1)} %all-to-all-done.w0), channel_id=1, source_target_pairs={{0,2},{2,4},{4,6},{6,0},{1,3},{3,5},{5,7},{7,1},{8,10},{10,12},{12... | collective-permute-start | bytes 1572872 | tf_op jit(solution)/shard_map/ppermute | solution.py:340
  58.6 29.4 %all-to-all-start.2 = ((bf16[64,32,128]{2,1,0:T(8,128)(2,1)}), bf16[64,32,128]{2,1,0:T(8,128)(2,1)S(1)}, u32[]{:S(2)}, u32[]{:S(2)}) async-start(bf16[64,32,128]{2,1,0:T(8,128)(2,1)} %get-tuple-element.44), calls=%async_computation.2 | async-start | bytes 1048576 | tf_op jit(solution)/shard_map/all_to_all | solution.py:334
  70.4 11.9 %collective-permute-start.7 = (bf16[8,64,512]{2,1,0:T(8,128)(2,1)S(1)}, bf16[8,64,512]{2,1,0:T(8,128)(2,1)S(1)}, u32[]{:S(2)}, u32[]{:S(2)}) collective-permute-start(bf16[8,64,512]{2,1,0:T(8,128)(2,1)S(1)} %all-to-all-done.w0), channel_id=1, source_target_pairs={{0,1},{1,0},{2,3},{3,2},{4,5},{5,4},{6,7},{7,6},{8,9},{9,8},{10,11... | collective-permute-start | bytes 1572872 | tf_op jit(solution)/shard_map/ppermute | solution.py:345
  72.5 15.5 %copy-start.6 = (bf16[8,64,512]{2,1,0:T(8,128)(2,1)}, bf16[8,64,512]{2,1,0:T(8,128)(2,1)S(1)}, u32[]{:S(2)}) copy-start(bf16[8,64,512]{2,1,0:T(8,128)(2,1)S(1)} %collective-permute-done.6.w3) | copy-start | bytes 1572868
  72.5 9.8 %collective-permute-start.10 = (bf16[8,64,512]{2,1,0:T(8,128)(2,1)S(1)}, bf16[8,64,512]{2,1,0:T(8,128)(2,1)S(1)}, u32[]{:S(2)}, u32[]{:S(2)}) collective-permute-start(bf16[8,64,512]{2,1,0:T(8,128)(2,1)S(1)} %collective-permute-done.6.w3), channel_id=1, source_target_pairs={{0,1},{1,0},{2,3},{3,2},{4,5},{5,4},{6,7},{7,6},{8,9},{9,8},{10,11... | collective-permute-start | bytes 1572872 | tf_op jit(solution)/shard_map/ppermute | solution.py:345
  74.8 7.5 %collective-permute-start.9 = (bf16[8,64,512]{2,1,0:T(8,128)(2,1)}, bf16[8,64,512]{2,1,0:T(8,128)(2,1)S(1)}, u32[]{:S(2)}, u32[]{:S(2)}) collective-permute-start(bf16[8,64,512]{2,1,0:T(8,128)(2,1)} %collective-permute-done.5.w2), channel_id=1, source_target_pairs={{0,1},{1,0},{2,3},{3,2},{4,5},{5,4},{6,7},{7,6},{8,9},{9,8},{10,11... | collective-permute-start | bytes 1572872 | tf_op jit(solution)/shard_map/ppermute | solution.py:345
  76.9 7.3 %collective-permute-start.8 = (bf16[8,64,512]{2,1,0:T(8,128)(2,1)}, bf16[8,64,512]{2,1,0:T(8,128)(2,1)}, u32[]{:S(2)}, u32[]{:S(2)}) collective-permute-start(bf16[8,64,512]{2,1,0:T(8,128)(2,1)} %collective-permute-done.4.w1), channel_id=1, source_target_pairs={{0,1},{1,0},{2,3},{3,2},{4,5},{5,4},{6,7},{7,6},{8,9},{9,8},{10,11... | collective-permute-start | bytes 1572872 | tf_op jit(solution)/shard_map/ppermute | solution.py:345
  79.1 3.1 %collective-permute-start.3 = (bf16[4,2,32,128]{3,2,1,0:T(8,128)(2,1)S(1)}, bf16[4,2,32,128]{3,2,1,0:T(8,128)(2,1)S(1)}, u32[]{:S(2)}, u32[]{:S(2)}) collective-permute-start(bf16[4,2,32,128]{3,2,1,0:T(8,128)(2,1)S(1)} %pad_maximum_fusion.t_mine), channel_id=1, source_target_pairs={{0,1},{1,0},{2,3},{3,2},{4,5},{5,4},{6,7},{7,6},{8,9},{9,8},{10,11... | collective-permute-start | bytes 196616 | tf_op jit(solution)/shard_map/ppermute | solution.py:345
  82.3 0.8 copy-start.7
  82.3 1.0 copy-start.8
  83.3 0.8 copy-start.9
  92.6 37.4 %copy-start.11 = (bf16[2,32,128]{2,1,0:T(8,128)(2,1)S(1)}, bf16[2,32,128]{2,1,0:T(8,128)(2,1)}, u32[]{:S(2)}) copy-start(bf16[2,32,128]{2,1,0:T(8,128)(2,1)} %get-tuple-element.47) | copy-start | bytes 49156
  92.6 24.2 %all-to-all-start.3 = ((bf16[64,32,128]{2,1,0:T(8,128)(2,1)}), bf16[64,32,128]{2,1,0:T(8,128)(2,1)S(1)}, u32[]{:S(2)}, u32[]{:S(2)}) async-start(bf16[64,32,128]{2,1,0:T(8,128)(2,1)} %get-tuple-element.55), calls=%async_computation.3 | async-start | bytes 1048576 | tf_op jit(solution)/shard_map/all_to_all | solution.py:334
  99.2 42.8 %copy-start = (f32[64,512]{1,0:T(8,128)S(1)}, f32[64,512]{1,0:T(8,128)}, u32[]{:S(2)}) copy-start(f32[64,512]{1,0:T(8,128)} %get-tuple-element.51.keys_raw) | copy-start | bytes 393220
  99.3 42.8 %copy-start.1 = (f32[64,512]{1,0:T(8,128)S(1)}, f32[64,512]{1,0:T(8,128)}, u32[]{:S(2)}) copy-start(f32[64,512]{1,0:T(8,128)} %get-tuple-element.52.values) | copy-start | bytes 393220
  99.3 30.7 %collective-permute-start.11 = (bf16[2,32,128]{2,1,0:T(8,128)(2,1)}, bf16[2,32,128]{2,1,0:T(8,128)(2,1)S(1)}, u32[]{:S(2)}, u32[]{:S(2)}) collective-permute-start(bf16[2,32,128]{2,1,0:T(8,128)(2,1)} %get-tuple-element.48), channel_id=1, source_target_pairs={{0,2},{2,4},{4,6},{6,0},{1,3},{3,5},{5,7},{7,1},{8,10},{10,12},{12... | collective-permute-start | bytes 49160 | tf_op jit(solution)/shard_map/ppermute | solution.py:340
  102.8 27.2 %collective-permute-start.12 = (bf16[2,32,128]{2,1,0:T(8,128)(2,1)}, bf16[2,32,128]{2,1,0:T(8,128)(2,1)S(1)}, u32[]{:S(2)}, u32[]{:S(2)}) collective-permute-start(bf16[2,32,128]{2,1,0:T(8,128)(2,1)} %get-tuple-element.49), channel_id=1, source_target_pairs={{0,4},{2,6},{4,0},{6,2},{1,5},{3,7},{5,1},{7,3},{8,12},{10,14},{12... | collective-permute-start | bytes 49160 | tf_op jit(solution)/shard_map/ppermute | solution.py:340
  105.8 24.2 %collective-permute-start.13 = (bf16[2,32,128]{2,1,0:T(8,128)(2,1)}, bf16[2,32,128]{2,1,0:T(8,128)(2,1)S(1)}, u32[]{:S(2)}, u32[]{:S(2)}) collective-permute-start(bf16[2,32,128]{2,1,0:T(8,128)(2,1)} %get-tuple-element.50), channel_id=1, source_target_pairs={{0,6},{2,0},{4,2},{6,4},{1,7},{3,1},{5,3},{7,5},{8,14},{10,8},{12,... | collective-permute-start | bytes 49160 | tf_op jit(solution)/shard_map/ppermute | solution.py:340
  118.5 23.5 %copy-start.3 = (f32[64,512]{1,0:T(8,128)S(1)}, f32[64,512]{1,0:T(8,128)}, u32[]{:S(2)}) copy-start(f32[64,512]{1,0:T(8,128)} %copy-done.2) | copy-start | bytes 393220
  118.5 23.5 %all-to-all-start.4 = ((bf16[12,32,128]{2,1,0:T(8,128)(2,1)}), bf16[12,32,128]{2,1,0:T(8,128)(2,1)S(1)}, u32[]{:S(2)}, u32[]{:S(2)}) async-start(bf16[12,32,128]{2,1,0:T(8,128)(2,1)} %get-tuple-element.61), calls=%async_computation.4 | async-start | bytes 196608 | tf_op jit(solution)/shard_map/all_to_all | solution.py:334
  130.0 3.2 %copy-start.10 = (bf16[4,2,32,128]{3,2,1,0:T(8,128)(2,1)}, bf16[4,2,32,128]{3,2,1,0:T(8,128)(2,1)S(1)}, u32[]{:S(2)}) copy-start(bf16[4,2,32,128]{3,2,1,0:T(8,128)(2,1)S(1)} %pad_maximum_fusion.1.m_mine) | copy-start | bytes 196612
  130.0 3.1 %collective-permute-start.14 = (bf16[4,2,32,128]{3,2,1,0:T(8,128)(2,1)S(1)}, bf16[4,2,32,128]{3,2,1,0:T(8,128)(2,1)S(1)}, u32[]{:S(2)}, u32[]{:S(2)}) collective-permute-start(bf16[4,2,32,128]{3,2,1,0:T(8,128)(2,1)S(1)} %pad_maximum_fusion.1.m_mine), channel_id=1, source_target_pairs={{0,1},{1,0},{2,3},{3,2},{4,5},{5,4},{6,7},{7,6},{8,9},{9,8},{10,11... | collective-permute-start | bytes 196616 | tf_op jit(solution)/shard_map/ppermute | solution.py:345
  133.2 0.6 copy-start.12

commit v5 on v4

--- a/solution.py
+++ b/solution.py
@@ -67,6 +67,11 @@
 def fold(square):
     half = square.shape[0] // 2
     return jnp.concatenate([square[:half], square[half:]], axis=1)
+
+
+def beside(block):
+    half = block.shape[0] // 2
+    return jnp.concatenate([block[:half], block[half:]], axis=1)
 
 
 def unfold(packed):
@@ -137,8 +142,7 @@
         place = lax.axis_index("x")
         for s, out in enumerate((t0, t1, t2, t3)):
             to = lax.rem(place + s, GRID["x"])
-            for c in range(2):
-                out[c] = held[to * 2 + c]
+            out[...] = jnp.concatenate([beside(held[to * 2 + c]) for c in range(2)], axis=1)
 
 
 def decays(everyone, rate, z, length):
@@ -193,15 +197,21 @@
     return jnp.concatenate(cols, axis=1)
 
 
+def pack_kernel(columns, t0, t1, t2, t3, p0, p1, p2, p3):
+    rows = columns.shape[0] * columns.shape[1]
+    matrix = columns[...].reshape(rows, columns.shape[2])
+    for out, teacher in ((p0, t0), (p1, t1), (p2, t2), (p3, t3)):
+        out[:rows] = matrix
+        out[rows:] = teacher[...]
+
+
 def by_source(mine, other, x, c):
     step = lax.rem(lax.axis_index("x") - x + GRID["x"], GRID["x"])
     core = lax.axis_index("core")
     return jnp.where(core == c, mine[step, core], other[step, core])
 
 
-def middle_kernel(
-    got, t_mine, t_other, w0, w1, w2, w3, v0, v1, v2, v3, sent, m0, m1, m2, m3, held, weights, sems
-):
+def middle_kernel(got, w0, w1, w2, w3, v0, v1, v2, v3, sent, m0, m1, m2, m3, held, weights, sems):
     copies = []
     for n, source in enumerate((w0, v0, w1, v1, w2, v2, w3, v3)):
         copies.append(pltpu.make_async_copy(source, weights.at[n], sems.at[n]))
@@ -220,7 +230,7 @@
     for n, y, places in chunks:
         if y == 0:
             copies[n].wait()
-        part = weights[n, y : y + group].reshape(group * LANES, tiles * LANES)
+        part = weights[n, y * LANES : (y + group) * LANES]
         term = jnp.dot(spread([got[p] for p in places]), part, preferred_element_type=f32)
         acc = term if acc is None else acc + term
     mixed = acc.astype(bf16)
@@ -230,10 +240,17 @@
         to = lax.rem(at + s, GRID["x"])
         for c in range(2):
             out[c] = held[to * 2 + c]
-    wanted = spread([by_source(t_mine, t_other, i // 2, i % 2) for i in range(tiles)])
+    teachers = []
+    for i in range(tiles):
+        step = lax.rem(at - i // 2 + GRID["x"], GRID["x"])
+        came = weights[2 * step + jnp.where(core == i % 2, 0, 1), rows * LANES :]
+        wide = came.shape[1] // 2
+        mine = jnp.where(core == 0, came[:, :wide], came[:, wide:])
+        teachers.append(jnp.concatenate([mine[:, : wide // 2], mine[:, wide // 2 :]], axis=0))
+    wanted = spread(teachers)
     diff = (mixed.astype(f32) - wanted.astype(f32)).astype(bf16)
     for n, y, places in chunks:
-        part = weights[n, y : y + group].reshape(group * LANES, tiles * LANES)
+        part = weights[n, y * LANES : (y + group) * LANES]
         grads = lax.dot_general(
             part, diff, (((1,), (1,)), ((), ())), preferred_element_type=f32
         ).astype(bf16)
@@ -330,13 +347,17 @@
     return tuple(pltpu.with_memory_space_constraint(a, pltpu.VMEM) for a in arrays)
 
 
+def far(arrays):
+    return [pltpu.with_memory_space_constraint(a, pltpu.HBM) for a in arrays]
+
+
 def exchange(array, axis):
     return lax.all_to_all(array, axis, 0, 0)
 
 
 def along_x(parts):
     n = GRID["x"]
-    return parts[:1] + [
+    return list(parts[:1]) + [
         lax.ppermute(parts[s], "x", [(i, (i + s) % n) for i in range(n)]) for s in range(1, n)
     ]
 
@@ -366,6 +387,7 @@
     head = tuple(GRID)
     flat = (LANES, length)
     block = (part // 2, 2 * LANES)
+    teacher = ((part // 4, 8 * LANES), bf16)
     barrier = lax.optimization_barrier
 
     columns = exchange(
@@ -389,7 +411,7 @@
             ((blocks, half + 16, 2 * LANES), bf16), (flat, f32), (flat, f32), (flat, f32),
             (flat, f32), ((length, length), bf16), (flat, f32),
         ]
-        + [((2,) + block, bf16)] * GRID["x"],
+        + [teacher] * GRID["x"],
         (
             incoming_signals, receptor_linear_map.T, lock_linear_map.T, worth_linear_map.T,
             codes, halvings, extra, tutor_aggregated.T,
@@ -402,10 +424,14 @@
             pltpu.VMEM((length, 3 * LANES), f32), pltpu.VMEM((tiles,) + block, bf16),
         ],
     )
-    tutor = jnp.stack(along_x(tutor))
-    payload, columns, tutor = barrier((payload, columns, tutor))
+    payload, columns, *tutor = barrier((payload, columns, *tutor))
     everyone = exchange(payload, "ctx")
-    w_mine = along_x([columns] * GRID["x"])
+    packed = call(
+        pack_kernel,
+        [((rows * LANES + teacher[0][0], tiles * LANES), bf16)] * GRID["x"],
+        near(columns) + tuple(tutor),
+    )
+    w_mine = far(along_x(packed))
     sent, start, unit, inverse = call(
         functools.partial(yields_kernel, all_frames),
         [((rows * tiles,) + block, bf16), ((LANES, LANES), f32), (flat, f32), ((1, length), f32)],
@@ -413,15 +439,15 @@
         here=(2, 3),
     )
     got = exchange(sent, head)
-    w_other = [swap(w) for w in w_mine]
+    w_other = far([swap(w) for w in w_mine])
     sent, *mixed = call(
         middle_kernel,
         [((rows * tiles,) + block, bf16)] + [((2,) + block, bf16)] * GRID["x"],
-        near(got, tutor, swap(tutor)) + (*w_mine, *w_other),
-        in_specs=[whole] * 3 + [pl.BlockSpec(memory_space=pl.ANY)] * (2 * GRID["x"]),
+        near(got) + (*w_mine, *w_other),
+        in_specs=[whole] + [pl.BlockSpec(memory_space=pl.ANY)] * (2 * GRID["x"]),
         scratch_shapes=[
             pltpu.VMEM((tiles,) + block, bf16),
-            pltpu.VMEM((2 * GRID["x"], rows, LANES, tiles * LANES), bf16),
+            pltpu.VMEM((2 * GRID["x"],) + packed[0].shape, bf16),
             pltpu.SemaphoreType.DMA((2 * GRID["x"],)),
         ],
     )

time: 145 us -> 139 us (0.959)
  starting transfers between devices: 95.7 us -> 73.1 us
  waiting for transfers between devices: 22.6 us -> 38.1 us
  Pallas kernels: 19.4 us -> 21.7 us
    ppermute x9 -> x6, starting transfers between devices: 36.3 us -> 21.2 us  [along_x(): lax.ppermute(parts[s], 'x', [(i, (i + s) % n) for i in range(n)])]
    ppermute x9 -> x6, waiting for transfers between devices: 3.91 us -> 12.8 us  [along_x(): lax.ppermute(parts[s], 'x', [(i, (i + s) % n) for i in range(n)])]
    all_to_all x5, waiting for transfers between devices: 16.4 us -> 23.7 us  [exchange(): return lax.all_to_all(array, axis, 0, 0)]
    all_to_all x5, starting transfers between devices: 46.7 us -> 41.7 us  [exchange(): return lax.all_to_all(array, axis, 0, 0)]
    ppermute x6 -> x5, starting transfers between devices: 12.6 us -> 10.2 us  [swap(): return lax.ppermute(array, 'core', [(0, 1), (1, 0)])]
    pallas_call x6 -> x7, Pallas kernels: 19.4 us -> 21.7 us  [call(): pl.pallas_call(kernel, cost_estimate=pl.CostEstimate(flops=1 << 30, trans...]
  transfers between devices with their start and end apart: 20 -> 16, of which waited for: 6 -> 7; matrix products, arithmetic and copies ran while one was open for 1% -> 0% of each run, Pallas kernels for 9% -> 11%
where the time goes in v5:
time: 139 us; the launch traced here: 138 us
  starting transfers between devices  73.1 us (53%)
  waiting for transfers between devices  38.1 us (27%)
  Pallas kernels  21.7 us (16%)
  local copies, waits for them, and re-layouts  4.32 us (3%)
    all_to_all x5, starting transfers between devices, exchange(): return lax.all_to_all(array, axis, 0, 0)  41.7 us
    all_to_all x5, waiting for transfers between devices, exchange(): return lax.all_to_all(array, axis, 0, 0)  23.7 us
    pallas_call x7, Pallas kernels, call(): pl.pallas_call(kernel, cost_estimate=pl.CostEstimate(flops=1 << 30, trans...  21.7 us
    ppermute x6, starting transfers between devices, along_x(): lax.ppermute(parts[s], 'x', [(i, (i + s) % n) for i in range(n)])  21.2 us
    ppermute x6, waiting for transfers between devices, along_x(): lax.ppermute(parts[s], 'x', [(i, (i + s) % n) for i in range(n)])  12.8 us
    ppermute x5, starting transfers between devices, swap(): return lax.ppermute(array, 'core', [(0, 1), (1, 0)])  10.2 us
  transfers between devices with their start and end apart: 16, of which 7 were waited for; matrix products, arithmetic and copies ran while one was open for 0% of the time, Pallas kernels for 11%

profile of v5, /device:TPU:2, one launch (start us, length us, event | category | flops | bytes accessed | tf_op | source)
XLA Modules:
  0.0 138.2 jit_solution(14642761178215852852)
XLA Ops:
  0.6 1.9 %copy.17 = bf16[8,8,8,512]{3,2,0,1:T(8,128)(2,1)} copy(bf16[8,8,8,512]{3,2,1,0:T(8,128)(2,1)} %bitcast.26) | data formatting | bytes 1048576 | tf_op jit(solution)/shard_map/reshape | solution.py:394
  2.5 7.1 %all-to-all-start = ((bf16[8,64,512]{2,1,0:T(8,128)(2,1)}), bf16[8,64,512]{2,1,0:T(8,128)(2,1)S(1)}, u32[]{:S(2)}, u32[]{:S(2)}) async-start(bf16[8,64,512]{2,1,0:T(8,128)(2,1)} %bitcast.22), calls=%async_computation | async-start | bytes 1048576 | tf_op jit(solution)/shard_map/all_to_all | solution.py:355
  9.6 6.4 %shard_map.129 = (bf16[12,48,128]{2,1,0:T(8,128)(2,1)}, f32[64,512]{1,0:T(8,128)S(1)}, f32[64,512]{1,0:T(8,128)}, f32[64,512]{1,0:T(8,128)}, f32[64,512]{1,0:T(8...) custom-call(bf16[512,4096]{1,0:T(8,128)(2,1)} %x.1, ...), custom_call_target="tpu_custom_call" | custom-call | flops 1073741824 | bytes 8388608 | tf_op jit(solution)/shard_map/pallas_call | solution.py:335
  16.1 0.0 copy-start.2
  16.1 0.0 copy-start.4
  16.1 11.0 %all-to-all-done.columns = bf16[8,64,512]{2,1,0:T(8,128)(2,1)S(1)} async-done(((bf16[8,64,512]{2,1,0:T(8,128)(2,1)}), bf16[8,64,512]{2,1,0:T(8,128)(2,1)S(1)}, u32[]{:S(2)}, u32[]{:S(2)}) %all-to-all-start) | async-done | bytes 524320 | tf_op jit(solution)/shard_map/all_to_all | solution.py:355
  27.1 15.2 %all-to-all-start.1 = ((bf16[12,48,128]{2,1,0:T(8,128)(2,1)}), bf16[12,48,128]{2,1,0:T(8,128)(2,1)S(1)}, u32[]{:S(2)}, u32[]{:S(2)}) async-start(bf16[12,48,128]{2,1,0:T(8,128)(2,1)} %get-tuple-element.47), calls=%async_computation.1 | async-start | bytes 294912 | tf_op jit(solution)/shard_map/all_to_all | solution.py:355
  42.3 2.3 %shard_map.131 = (bf16[528,512]{1,0:T(8,128)(2,1)}, bf16[528,512]{1,0:T(8,128)(2,1)}, bf16[528,512]{1,0:T(8,128)(2,1)}, bf16[528,512]{1,0:T(8,128)(2,1)}) custom-call(bf16[8,64,512]{2,1,0:T(8,128)(2,1)S(1)} %all-to-all-done.columns, bf16[16,512]{1,0:T(8,128)(2,1)} %get-tuple-element.53.t0, bf16[16,512]{1,0:T(8,128)(2,1)} %get-tuple-element.54.t1, ...), custom_call_target="tpu_custom_call" | custom-call | flops 1073741824 | bytes 8388608 | tf_op jit(solution)/shard_map/pallas_call | solution.py:335
  44.6 0.0 copy-start.5
  44.6 3.5 %collective-permute-start = (bf16[528,512]{1,0:T(8,128)(2,1)}, bf16[528,512]{1,0:T(8,128)(2,1)S(1)}, u32[]{:S(2)}, u32[]{:S(2)}) collective-permute-start(bf16[528,512]{1,0:T(8,128)(2,1)} %get-tuple-element.58), channel_id=1, source_target_pairs={{0,2},{2,4},{4,6},{6,0},{1,3},{3,5},{5,7},{7,1},{8,10},{10,12},{12... | collective-permute-start | bytes 1622024 | tf_op jit(solution)/shard_map/ppermute | solution.py:361
  48.1 3.0 %collective-permute-start.1 = (bf16[528,512]{1,0:T(8,128)(2,1)}, bf16[528,512]{1,0:T(8,128)(2,1)}, u32[]{:S(2)}, u32[]{:S(2)}) collective-permute-start(bf16[528,512]{1,0:T(8,128)(2,1)} %get-tuple-element.59), channel_id=1, source_target_pairs={{0,4},{2,6},{4,0},{6,2},{1,5},{3,7},{5,1},{7,3},{8,12},{10,14},{12... | collective-permute-start | bytes 1622024 | tf_op jit(solution)/shard_map/ppermute | solution.py:361
  51.1 4.1 %collective-permute-start.2 = (bf16[528,512]{1,0:T(8,128)(2,1)}, bf16[528,512]{1,0:T(8,128)(2,1)}, u32[]{:S(2)}, u32[]{:S(2)}) collective-permute-start(bf16[528,512]{1,0:T(8,128)(2,1)} %get-tuple-element.60), channel_id=1, source_target_pairs={{0,6},{2,0},{4,2},{6,4},{1,7},{3,1},{5,3},{7,5},{8,14},{10,8},{12,... | collective-permute-start | bytes 1622024 | tf_op jit(solution)/shard_map/ppermute | solution.py:361
  55.2 0.1 all-to-all-done.1.everyone
  55.3 2.2 %shard_map.130 = (bf16[64,32,128]{2,1,0:T(8,128)(2,1)}, f32[64,64]{1,0:T(8,128)}, f32[64,512]{1,0:T(8,128)S(1)}, f32[1,512]{1,0:T(1,128)S(1)}) custom-call(bf16[12,48,128]{2,1,0:T(8,128)(2,1)S(1)} %all-to-all-done.1.everyone, f32[64,512]{1,0:T(8,128)S(1)} %get-tuple-element.48.local, f32[64,512]{1,0:T(8,128)S(1)} %get-tuple-element.49.reads, ...), custom_call_target="tpu_custom_call" | custom-call | flops 1073741824 | bytes 8388608 | tf_op jit(solution)/shard_map/pallas_call | solution.py:335
  57.5 5.4 %all-to-all-start.2 = ((bf16[64,32,128]{2,1,0:T(8,128)(2,1)}), bf16[64,32,128]{2,1,0:T(8,128)(2,1)S(1)}, u32[]{:S(2)}, u32[]{:S(2)}) async-start(bf16[64,32,128]{2,1,0:T(8,128)(2,1)} %get-tuple-element.51), calls=%async_computation.2 | async-start | bytes 1048576 | tf_op jit(solution)/shard_map/all_to_all | solution.py:355
  63.0 0.0 copy-done.5
  63.0 2.1 %collective-permute-start.3 = (bf16[528,512]{1,0:T(8,128)(2,1)S(1)}, bf16[528,512]{1,0:T(8,128)(2,1)S(1)}, u32[]{:S(2)}, u32[]{:S(2)}) collective-permute-start(bf16[528,512]{1,0:T(8,128)(2,1)S(1)} %copy-done.5), channel_id=1, source_target_pairs={{0,1},{1,0},{2,3},{3,2},{4,5},{5,4},{6,7},{7,6},{8,9},{9,8},{10,11... | collective-permute-start | bytes 1622024 | tf_op jit(solution)/shard_map/ppermute | solution.py:366
  65.0 0.0 collective-permute-done.w1
  65.0 0.0 copy-start.6
  65.1 2.3 %collective-permute-start.4 = (bf16[528,512]{1,0:T(8,128)(2,1)S(1)}, bf16[528,512]{1,0:T(8,128)(2,1)S(1)}, u32[]{:S(2)}, u32[]{:S(2)}) collective-permute-start(bf16[528,512]{1,0:T(8,128)(2,1)S(1)} %collective-permute-done.w1), channel_id=1, source_target_pairs={{0,1},{1,0},{2,3},{3,2},{4,5},{5,4},{6,7},{7,6},{8,9},{9,8},{10,11... | collective-permute-start | bytes 1622024 | tf_op jit(solution)/shard_map/ppermute | solution.py:366
  67.3 0.0 collective-permute-done.1.w2
  67.3 2.1 %collective-permute-start.5 = (bf16[528,512]{1,0:T(8,128)(2,1)}, bf16[528,512]{1,0:T(8,128)(2,1)S(1)}, u32[]{:S(2)}, u32[]{:S(2)}) collective-permute-start(bf16[528,512]{1,0:T(8,128)(2,1)} %collective-permute-done.1.w2), channel_id=1, source_target_pairs={{0,1},{1,0},{2,3},{3,2},{4,5},{5,4},{6,7},{7,6},{8,9},{9,8},{10,11... | collective-permute-start | bytes 1622024 | tf_op jit(solution)/shard_map/ppermute | solution.py:366
  69.4 12.8 %collective-permute-done.2.w3 = bf16[528,512]{1,0:T(8,128)(2,1)} collective-permute-done((bf16[528,512]{1,0:T(8,128)(2,1)}, bf16[528,512]{1,0:T(8,128)(2,1)}, u32[]{:S(2)}, u32[]{:S(2)}) %collective-permute-start.2) | collective-permute-done | bytes 540704 | tf_op jit(solution)/shard_map/ppermute | solution.py:361
  82.2 1.9 %collective-permute-start.6 = (bf16[528,512]{1,0:T(8,128)(2,1)}, bf16[528,512]{1,0:T(8,128)(2,1)}, u32[]{:S(2)}, u32[]{:S(2)}) collective-permute-start(bf16[528,512]{1,0:T(8,128)(2,1)} %collective-permute-done.2.w3), channel_id=1, source_target_pairs={{0,1},{1,0},{2,3},{3,2},{4,5},{5,4},{6,7},{7,6},{8,9},{9,8},{10,11... | collective-permute-start | bytes 1622024 | tf_op jit(solution)/shard_map/ppermute | solution.py:366
  84.1 0.0 collective-permute-done.3.v0
  84.1 0.0 copy-start.7
  84.1 0.0 collective-permute-done.4.v1
  84.2 0.0 copy-start.8
  84.2 0.0 collective-permute-done.5.v2
  84.2 0.8 copy-done.7
  84.9 0.2 copy-done.8
  85.1 0.0 copy-start.9
  85.1 0.8 copy-done.9
  85.9 0.4 collective-permute-done.6.v3
  86.4 0.0 all-to-all-done.2.got
  86.4 0.0 copy-done.6
  86.4 4.6 %shard_map.132 = (bf16[64,32,128]{2,1,0:T(8,128)(2,1)}, bf16[2,32,128]{2,1,0:T(8,128)(2,1)}, bf16[2,32,128]{2,1,0:T(8,128)(2,1)}, bf16[2,32,128]{2,1,0:T(8,128)(2,1)}, bf16[2,32,128]{2,1,0:T(8,128)(2,1)}) custom-call(bf16[64,32,128]{2,1,0:T(8,128)(2,1)S(1)} %all-to-all-done.2.got, bf16[528,512]{1,0:T(8,128)(2,1)} %get-tuple-element.57.w0, ...), custom_call_target="tpu_custom_call" | custom-call | flops 1073741824 | bytes 8388608 | tf_op jit(solution)/shard_map/pallas_call | solution.py:335
  91.0 0.0 copy-start.11
  91.0 4.6 %all-to-all-start.3 = ((bf16[64,32,128]{2,1,0:T(8,128)(2,1)}), bf16[64,32,128]{2,1,0:T(8,128)(2,1)S(1)}, u32[]{:S(2)}, u32[]{:S(2)}) async-start(bf16[64,32,128]{2,1,0:T(8,128)(2,1)} %get-tuple-element.69), calls=%async_computation.3 | async-start | bytes 1048576 | tf_op jit(solution)/shard_map/all_to_all | solution.py:355
  95.6 0.0 copy-start
  95.6 0.0 copy-start.1
  95.7 3.5 %collective-permute-start.7 = (bf16[2,32,128]{2,1,0:T(8,128)(2,1)}, bf16[2,32,128]{2,1,0:T(8,128)(2,1)S(1)}, u32[]{:S(2)}, u32[]{:S(2)}) collective-permute-start(bf16[2,32,128]{2,1,0:T(8,128)(2,1)} %get-tuple-element.62), channel_id=1, source_target_pairs={{0,2},{2,4},{4,6},{6,0},{1,3},{3,5},{5,7},{7,1},{8,10},{10,12},{12... | collective-permute-start | bytes 49160 | tf_op jit(solution)/shard_map/ppermute | solution.py:361
  99.2 3.0 %collective-permute-start.8 = (bf16[2,32,128]{2,1,0:T(8,128)(2,1)}, bf16[2,32,128]{2,1,0:T(8,128)(2,1)S(1)}, u32[]{:S(2)}, u32[]{:S(2)}) collective-permute-start(bf16[2,32,128]{2,1,0:T(8,128)(2,1)} %get-tuple-element.63), channel_id=1, source_target_pairs={{0,4},{2,6},{4,0},{6,2},{1,5},{3,7},{5,1},{7,3},{8,12},{10,14},{12... | collective-permute-start | bytes 49160 | tf_op jit(solution)/shard_map/ppermute | solution.py:361
  102.1 4.1 %collective-permute-start.9 = (bf16[2,32,128]{2,1,0:T(8,128)(2,1)}, bf16[2,32,128]{2,1,0:T(8,128)(2,1)S(1)}, u32[]{:S(2)}, u32[]{:S(2)}) collective-permute-start(bf16[2,32,128]{2,1,0:T(8,128)(2,1)} %get-tuple-element.64), channel_id=1, source_target_pairs={{0,6},{2,0},{4,2},{6,4},{1,7},{3,1},{5,3},{7,5},{8,14},{10,8},{12,... | collective-permute-start | bytes 49160 | tf_op jit(solution)/shard_map/ppermute | solution.py:361
  106.2 7.0 %all-to-all-done.3.got = bf16[64,32,128]{2,1,0:T(8,128)(2,1)S(1)} async-done(((bf16[64,32,128]{2,1,0:T(8,128)(2,1)}), bf16[64,32,128]{2,1,0:T(8,128)(2,1)S(1)}, u32[]{:S(2)}, u32[]{:S(2)}) %all-to-all-start.3) | async-done | bytes 524320 | tf_op jit(solution)/shard_map/all_to_all | solution.py:355
  113.2 0.0 copy-done.2
  113.2 0.0 copy-done.4
  113.2 1.7 %shard_map.133 = (bf16[12,32,128]{2,1,0:T(8,128)(2,1)}, f32[64,512]{1,0:T(8,128)}) custom-call(bf16[64,32,128]{2,1,0:T(8,128)(2,1)S(1)} %all-to-all-done.3.got, f32[64,512]{1,0:T(8,128)S(1)} %get-tuple-element.70.unit, f32[1,512]{1,0:T(1,128)S(1)} %get-tuple-element.71.inverse, f32[1,64]{1,0:T(1,128)} %bitcast.39, f32[64,512]{1,0:T(8,128)S(1)} %get-tuple-element.49.reads, ...), custom_call_target="tpu_custom_call" | custom-call | flops 1073741824 | bytes 8388608 | tf_op jit(solution)/shard_map/pallas_call | solution.py:335
  114.9 9.5 %all-to-all-start.4 = ((bf16[12,32,128]{2,1,0:T(8,128)(2,1)}), bf16[12,32,128]{2,1,0:T(8,128)(2,1)S(1)}, u32[]{:S(2)}, u32[]{:S(2)}) async-start(bf16[12,32,128]{2,1,0:T(8,128)(2,1)} %get-tuple-element.75), calls=%async_computation.4 | async-start | bytes 196608 | tf_op jit(solution)/shard_map/all_to_all | solution.py:355
  124.4 0.0 collective-permute-done.7
  124.4 0.0 collective-permute-done.8
  124.4 0.0 collective-permute-done.9
  124.4 0.0 copy-done.11
  124.5 0.0 copy-start.10
  124.5 1.9 %collective-permute-start.10 = (bf16[4,2,32,128]{3,2,1,0:T(8,128)(2,1)S(1)}, bf16[4,2,32,128]{3,2,1,0:T(8,128)(2,1)S(1)}, u32[]{:S(2)}, u32[]{:S(2)}) collective-permute-start(bf16[4,2,32,128]{3,2,1,0:T(8,128)(2,1)S(1)} %pad_maximum_fusion.m_mine), channel_id=1, source_target_pairs={{0,1},{1,0},{2,3},{3,2},{4,5},{5,4},{6,7},{7,6},{8,9},{9,8},{10,11... | collective-permute-start | bytes 196616 | tf_op jit(solution)/shard_map/ppermute | solution.py:366
  126.4 1.2 collective-permute-done.10.m_other
  127.6 0.0 copy-done.10
  127.6 0.6 copy-done.12
  128.3 2.7 %shard_map.134 = (bf16[64,512]{1,0:T(8,128)(2,1)}, bf16[64,512]{1,0:T(8,128)(2,1)}, f32[64,512]{1,0:T(8,128)S(1)}, f32[64,512]{1,0:T(8,128)S(1)}) custom-call(bf16[4,2,32,128]{3,2,1,0:T(8,128)(2,1)} %copy-done.10, bf16[4,2,32,128]{3,2,1,0:T(8,128)(2,1)} %copy-done.12, f32[64,512]{1,0:T(8,128)} %copy-done.4, f32[64,512]{1,0:T(8,128)} %get-tuple-element.65.keys_raw, ...), custom_call_target="tpu_custom_call" | custom-call | flops 1073741824 | bytes 8388608 | tf_op jit(solution)/shard_map/pallas_call | solution.py:335
  130.9 5.6 %all-to-all-done.4.later = bf16[12,32,128]{2,1,0:T(8,128)(2,1)S(1)} async-done(((bf16[12,32,128]{2,1,0:T(8,128)(2,1)}), bf16[12,32,128]{2,1,0:T(8,128)(2,1)S(1)}, u32[]{:S(2)}, u32[]{:S(2)}) %all-to-all-start.4) | async-done | bytes 98336 | tf_op jit(solution)/shard_map/all_to_all | solution.py:355
  136.5 0.0 copy-done
  136.5 0.0 copy-done.1
  136.5 0.0 copy-done.3
  136.5 1.7 %shard_map.135 = (bf16[64,512]{1,0:T(8,128)(2,1)}, bf16[64,512]{1,0:T(8,128)(2,1)}) custom-call(bf16[12,32,128]{2,1,0:T(8,128)(2,1)S(1)} %all-to-all-done.4.later, bf16[12,48,128]{2,1,0:T(8,128)(2,1)S(1)} %all-to-all-done.1.everyone, f32[64,512]{1,0:T(8,128)S(1)} %get-tuple-element.76.part_keys, f32[64,512]{1,0:T(8,128)S(1)} %get-tuple-element.77.part_values, ...), custom_call_target="tpu_custom_call" | custom-call | flops 1073741824 | bytes 8388608 | tf_op jit(solution)/shard_map/pallas_call | solution.py:335
  (3 shorter events, 0.0 us)
Async XLA Ops:
  2.5 24.6 %all-to-all-start = ((bf16[8,64,512]{2,1,0:T(8,128)(2,1)}), bf16[8,64,512]{2,1,0:T(8,128)(2,1)S(1)}, u32[]{:S(2)}, u32[]{:S(2)}) async-start(bf16[8,64,512]{2,1,0:T(8,128)(2,1)} %bitcast.22), calls=%async_computation | async-start | bytes 1048576 | tf_op jit(solution)/shard_map/all_to_all | solution.py:355
  16.1 97.1 %copy-start.2 = (f32[64,512]{1,0:T(8,128)}, f32[64,512]{1,0:T(8,128)S(1)}, u32[]{:S(2)}) copy-start(f32[64,512]{1,0:T(8,128)S(1)} %get-tuple-element.50.logs) | copy-start | bytes 393220
  16.1 97.1 %copy-start.4 = (f32[64,512]{1,0:T(8,128)}, f32[64,512]{1,0:T(8,128)S(1)}, u32[]{:S(2)}) copy-start(f32[64,512]{1,0:T(8,128)S(1)} %get-tuple-element.49.reads) | copy-start | bytes 393220
  27.1 28.2 %all-to-all-start.1 = ((bf16[12,48,128]{2,1,0:T(8,128)(2,1)}), bf16[12,48,128]{2,1,0:T(8,128)(2,1)S(1)}, u32[]{:S(2)}, u32[]{:S(2)}) async-start(bf16[12,48,128]{2,1,0:T(8,128)(2,1)} %get-tuple-element.47), calls=%async_computation.1 | async-start | bytes 294912 | tf_op jit(solution)/shard_map/all_to_all | solution.py:355
  44.6 18.4 %copy-start.5 = (bf16[528,512]{1,0:T(8,128)(2,1)S(1)}, bf16[528,512]{1,0:T(8,128)(2,1)}, u32[]{:S(2)}) copy-start(bf16[528,512]{1,0:T(8,128)(2,1)} %get-tuple-element.57.w0) | copy-start | bytes 1622020
  44.6 20.5 %collective-permute-start = (bf16[528,512]{1,0:T(8,128)(2,1)}, bf16[528,512]{1,0:T(8,128)(2,1)S(1)}, u32[]{:S(2)}, u32[]{:S(2)}) collective-permute-start(bf16[528,512]{1,0:T(8,128)(2,1)} %get-tuple-element.58), channel_id=1, source_target_pairs={{0,2},{2,4},{4,6},{6,0},{1,3},{3,5},{5,7},{7,1},{8,10},{10,12},{12... | collective-permute-start | bytes 1622024 | tf_op jit(solution)/shard_map/ppermute | solution.py:361
  48.1 19.2 %collective-permute-start.1 = (bf16[528,512]{1,0:T(8,128)(2,1)}, bf16[528,512]{1,0:T(8,128)(2,1)}, u32[]{:S(2)}, u32[]{:S(2)}) collective-permute-start(bf16[528,512]{1,0:T(8,128)(2,1)} %get-tuple-element.59), channel_id=1, source_target_pairs={{0,4},{2,6},{4,0},{6,2},{1,5},{3,7},{5,1},{7,3},{8,12},{10,14},{12... | collective-permute-start | bytes 1622024 | tf_op jit(solution)/shard_map/ppermute | solution.py:361
  51.1 31.1 %collective-permute-start.2 = (bf16[528,512]{1,0:T(8,128)(2,1)}, bf16[528,512]{1,0:T(8,128)(2,1)}, u32[]{:S(2)}, u32[]{:S(2)}) collective-permute-start(bf16[528,512]{1,0:T(8,128)(2,1)} %get-tuple-element.60), channel_id=1, source_target_pairs={{0,6},{2,0},{4,2},{6,4},{1,7},{3,1},{5,3},{7,5},{8,14},{10,8},{12,... | collective-permute-start | bytes 1622024 | tf_op jit(solution)/shard_map/ppermute | solution.py:361
  57.5 28.8 %all-to-all-start.2 = ((bf16[64,32,128]{2,1,0:T(8,128)(2,1)}), bf16[64,32,128]{2,1,0:T(8,128)(2,1)S(1)}, u32[]{:S(2)}, u32[]{:S(2)}) async-start(bf16[64,32,128]{2,1,0:T(8,128)(2,1)} %get-tuple-element.51), calls=%async_computation.2 | async-start | bytes 1048576 | tf_op jit(solution)/shard_map/all_to_all | solution.py:355
  63.0 21.2 %collective-permute-start.3 = (bf16[528,512]{1,0:T(8,128)(2,1)S(1)}, bf16[528,512]{1,0:T(8,128)(2,1)S(1)}, u32[]{:S(2)}, u32[]{:S(2)}) collective-permute-start(bf16[528,512]{1,0:T(8,128)(2,1)S(1)} %copy-done.5), channel_id=1, source_target_pairs={{0,1},{1,0},{2,3},{3,2},{4,5},{5,4},{6,7},{7,6},{8,9},{9,8},{10,11... | collective-permute-start | bytes 1622024 | tf_op jit(solution)/shard_map/ppermute | solution.py:366
  65.0 21.3 %copy-start.6 = (bf16[528,512]{1,0:T(8,128)(2,1)}, bf16[528,512]{1,0:T(8,128)(2,1)S(1)}, u32[]{:S(2)}) copy-start(bf16[528,512]{1,0:T(8,128)(2,1)S(1)} %collective-permute-done.w1) | copy-start | bytes 1622020
  65.1 19.1 %collective-permute-start.4 = (bf16[528,512]{1,0:T(8,128)(2,1)S(1)}, bf16[528,512]{1,0:T(8,128)(2,1)S(1)}, u32[]{:S(2)}, u32[]{:S(2)}) collective-permute-start(bf16[528,512]{1,0:T(8,128)(2,1)S(1)} %collective-permute-done.w1), channel_id=1, source_target_pairs={{0,1},{1,0},{2,3},{3,2},{4,5},{5,4},{6,7},{7,6},{8,9},{9,8},{10,11... | collective-permute-start | bytes 1622024 | tf_op jit(solution)/shard_map/ppermute | solution.py:366
  67.3 16.8 %collective-permute-start.5 = (bf16[528,512]{1,0:T(8,128)(2,1)}, bf16[528,512]{1,0:T(8,128)(2,1)S(1)}, u32[]{:S(2)}, u32[]{:S(2)}) collective-permute-start(bf16[528,512]{1,0:T(8,128)(2,1)} %collective-permute-done.1.w2), channel_id=1, source_target_pairs={{0,1},{1,0},{2,3},{3,2},{4,5},{5,4},{6,7},{7,6},{8,9},{9,8},{10,11... | collective-permute-start | bytes 1622024 | tf_op jit(solution)/shard_map/ppermute | solution.py:366
  82.2 4.2 %collective-permute-start.6 = (bf16[528,512]{1,0:T(8,128)(2,1)}, bf16[528,512]{1,0:T(8,128)(2,1)}, u32[]{:S(2)}, u32[]{:S(2)}) collective-permute-start(bf16[528,512]{1,0:T(8,128)(2,1)} %collective-permute-done.2.w3), channel_id=1, source_target_pairs={{0,1},{1,0},{2,3},{3,2},{4,5},{5,4},{6,7},{7,6},{8,9},{9,8},{10,11... | collective-permute-start | bytes 1622024 | tf_op jit(solution)/shard_map/ppermute | solution.py:366
  84.1 0.8 copy-start.7
  84.2 1.0 copy-start.8
  85.1 0.8 copy-start.9
  91.0 33.4 %copy-start.11 = (bf16[2,32,128]{2,1,0:T(8,128)(2,1)S(1)}, bf16[2,32,128]{2,1,0:T(8,128)(2,1)}, u32[]{:S(2)}) copy-start(bf16[2,32,128]{2,1,0:T(8,128)(2,1)} %get-tuple-element.61) | copy-start | bytes 49156
  91.0 22.2 %all-to-all-start.3 = ((bf16[64,32,128]{2,1,0:T(8,128)(2,1)}), bf16[64,32,128]{2,1,0:T(8,128)(2,1)S(1)}, u32[]{:S(2)}, u32[]{:S(2)}) async-start(bf16[64,32,128]{2,1,0:T(8,128)(2,1)} %get-tuple-element.69), calls=%async_computation.3 | async-start | bytes 1048576 | tf_op jit(solution)/shard_map/all_to_all | solution.py:355
  95.6 40.9 %copy-start = (f32[64,512]{1,0:T(8,128)S(1)}, f32[64,512]{1,0:T(8,128)}, u32[]{:S(2)}) copy-start(f32[64,512]{1,0:T(8,128)} %get-tuple-element.65.keys_raw) | copy-start | bytes 393220
  95.6 40.8 %copy-start.1 = (f32[64,512]{1,0:T(8,128)S(1)}, f32[64,512]{1,0:T(8,128)}, u32[]{:S(2)}) copy-start(f32[64,512]{1,0:T(8,128)} %get-tuple-element.66.values) | copy-start | bytes 393220
  95.7 28.8 %collective-permute-start.7 = (bf16[2,32,128]{2,1,0:T(8,128)(2,1)}, bf16[2,32,128]{2,1,0:T(8,128)(2,1)S(1)}, u32[]{:S(2)}, u32[]{:S(2)}) collective-permute-start(bf16[2,32,128]{2,1,0:T(8,128)(2,1)} %get-tuple-element.62), channel_id=1, source_target_pairs={{0,2},{2,4},{4,6},{6,0},{1,3},{3,5},{5,7},{7,1},{8,10},{10,12},{12... | collective-permute-start | bytes 49160 | tf_op jit(solution)/shard_map/ppermute | solution.py:361
  99.2 25.3 %collective-permute-start.8 = (bf16[2,32,128]{2,1,0:T(8,128)(2,1)}, bf16[2,32,128]{2,1,0:T(8,128)(2,1)S(1)}, u32[]{:S(2)}, u32[]{:S(2)}) collective-permute-start(bf16[2,32,128]{2,1,0:T(8,128)(2,1)} %get-tuple-element.63), channel_id=1, source_target_pairs={{0,4},{2,6},{4,0},{6,2},{1,5},{3,7},{5,1},{7,3},{8,12},{10,14},{12... | collective-permute-start | bytes 49160 | tf_op jit(solution)/shard_map/ppermute | solution.py:361
  102.1 22.3 %collective-permute-start.9 = (bf16[2,32,128]{2,1,0:T(8,128)(2,1)}, bf16[2,32,128]{2,1,0:T(8,128)(2,1)S(1)}, u32[]{:S(2)}, u32[]{:S(2)}) collective-permute-start(bf16[2,32,128]{2,1,0:T(8,128)(2,1)} %get-tuple-element.64), channel_id=1, source_target_pairs={{0,6},{2,0},{4,2},{6,4},{1,7},{3,1},{5,3},{7,5},{8,14},{10,8},{12,... | collective-permute-start | bytes 49160 | tf_op jit(solution)/shard_map/ppermute | solution.py:361
  114.9 21.6 %copy-start.3 = (f32[64,512]{1,0:T(8,128)S(1)}, f32[64,512]{1,0:T(8,128)}, u32[]{:S(2)}) copy-start(f32[64,512]{1,0:T(8,128)} %copy-done.2) | copy-start | bytes 393220
  114.9 21.5 %all-to-all-start.4 = ((bf16[12,32,128]{2,1,0:T(8,128)(2,1)}), bf16[12,32,128]{2,1,0:T(8,128)(2,1)S(1)}, u32[]{:S(2)}, u32[]{:S(2)}) async-start(bf16[12,32,128]{2,1,0:T(8,128)(2,1)} %get-tuple-element.75), calls=%async_computation.4 | async-start | bytes 196608 | tf_op jit(solution)/shard_map/all_to_all | solution.py:355
  124.5 3.2 %copy-start.10 = (bf16[4,2,32,128]{3,2,1,0:T(8,128)(2,1)}, bf16[4,2,32,128]{3,2,1,0:T(8,128)(2,1)S(1)}, u32[]{:S(2)}) copy-start(bf16[4,2,32,128]{3,2,1,0:T(8,128)(2,1)S(1)} %pad_maximum_fusion.m_mine) | copy-start | bytes 196612
  124.5 3.1 %collective-permute-start.10 = (bf16[4,2,32,128]{3,2,1,0:T(8,128)(2,1)S(1)}, bf16[4,2,32,128]{3,2,1,0:T(8,128)(2,1)S(1)}, u32[]{:S(2)}, u32[]{:S(2)}) collective-permute-start(bf16[4,2,32,128]{3,2,1,0:T(8,128)(2,1)S(1)} %pad_maximum_fusion.m_mine), channel_id=1, source_target_pairs={{0,1},{1,0},{2,3},{3,2},{4,5},{5,4},{6,7},{7,6},{8,9},{9,8},{10,11... | collective-permute-start | bytes 196616 | tf_op jit(solution)/shard_map/ppermute | solution.py:366
  127.6 0.6 copy-start.12

commit v6 on v5

--- a/solution.py
+++ b/solution.py
@@ -197,12 +197,21 @@
     return jnp.concatenate(cols, axis=1)
 
 
-def pack_kernel(columns, t0, t1, t2, t3, p0, p1, p2, p3):
-    rows = columns.shape[0] * columns.shape[1]
-    matrix = columns[...].reshape(rows, columns.shape[2])
+def pack_kernel(matrix, t0, t1, t2, t3, p0, p1, p2, p3, sems):
+    rows = matrix.shape[0]
+    copies = []
     for out, teacher in ((p0, t0), (p1, t1), (p2, t2), (p3, t3)):
-        out[:rows] = matrix
-        out[rows:] = teacher[...]
+        extra = teacher.shape[0]
+        taken = out.shape[0] - extra
+        for source, target in (
+            (matrix.at[rows - taken :], out.at[:taken]),
+            (teacher, out.at[taken:]),
+        ):
+            copies.append(pltpu.make_async_copy(source, target, sems.at[len(copies)]))
+    for copy in copies:
+        copy.start()
+    for copy in copies:
+        copy.wait()
 
 
 def by_source(mine, other, x, c):
@@ -211,17 +220,24 @@
     return jnp.where(core == c, mine[step, core], other[step, core])
 
 
-def middle_kernel(got, w0, w1, w2, w3, v0, v1, v2, v3, sent, m0, m1, m2, m3, held, weights, sems):
+def middle_kernel(
+    got, w0, w1, w2, w2f, w3, v0, v1, v2, v2f, v3, sent, m0, m1, m2, m3, held, weights, sems
+):
     copies = []
-    for n, source in enumerate((w0, v0, w1, v1, w2, v2, w3, v3)):
-        copies.append(pltpu.make_async_copy(source, weights.at[n], sems.at[n]))
-        copies[n].start()
+    upper = w2f.shape[0]
+    for n, first, source in (
+        (0, 0, w0), (1, 0, v0), (2, 0, w1), (3, 0, v1), (6, 0, w3), (7, 0, v3),
+        (4, upper, w2), (4, 0, w2f), (5, upper, v2), (5, 0, v2f),
+    ):
+        target = weights.at[n, first : first + source.shape[0]]
+        copies.append((n, pltpu.make_async_copy(source, target, sems.at[len(copies)])))
+        copies[-1][1].start()
     at, core = lax.axis_index("x"), lax.axis_index("core")
     tiles = GRID["x"] * GRID["core"]
     rows = GRID["y"]
     group = min(4, rows)
     chunks = []
-    for s in range(GRID["x"]):
+    for s in (0, 1, 3, 2):
         x = lax.rem(at - s + GRID["x"], GRID["x"])
         for n, c in ((2 * s, core), (2 * s + 1, 1 - core)):
             for y in range(0, rows, group):
@@ -229,7 +245,9 @@
     acc = None
     for n, y, places in chunks:
         if y == 0:
-            copies[n].wait()
+            for m, copy in copies:
+                if m == n:
+                    copy.wait()
         part = weights[n, y * LANES : (y + group) * LANES]
         term = jnp.dot(spread([got[p] for p in places]), part, preferred_element_type=f32)
         acc = term if acc is None else acc + term
@@ -347,10 +365,6 @@
     return tuple(pltpu.with_memory_space_constraint(a, pltpu.VMEM) for a in arrays)
 
 
-def far(arrays):
-    return [pltpu.with_memory_space_constraint(a, pltpu.HBM) for a in arrays]
-
-
 def exchange(array, axis):
     return lax.all_to_all(array, axis, 0, 0)
 
@@ -426,12 +440,20 @@
     )
     payload, columns, *tutor = barrier((payload, columns, *tutor))
     everyone = exchange(payload, "ctx")
+    height, upper = rows * LANES, rows * LANES // 2
+    full = ((height + teacher[0][0], tiles * LANES), bf16)
+    lower = ((height - upper + teacher[0][0], tiles * LANES), bf16)
+    anywhere = pl.BlockSpec(memory_space=pl.ANY)
     packed = call(
         pack_kernel,
-        [((rows * LANES + teacher[0][0], tiles * LANES), bf16)] * GRID["x"],
-        near(columns) + tuple(tutor),
-    )
-    w_mine = far(along_x(packed))
+        [full, full, lower, full],
+        near(columns.reshape(height, tiles * LANES)) + tuple(tutor),
+        out_specs=[anywhere] * GRID["x"],
+        scratch_shapes=[pltpu.SemaphoreType.DMA((2 * GRID["x"],))],
+    )
+    w0, w1, w2, w3 = along_x(packed)
+    w2f = lax.ppermute(w3[:upper], "x", [(i, (i + 3) % GRID["x"]) for i in range(GRID["x"])])
+    w_mine = [w0, w1, w2, w2f, w3]
     sent, start, unit, inverse = call(
         functools.partial(yields_kernel, all_frames),
         [((rows * tiles,) + block, bf16), ((LANES, LANES), f32), (flat, f32), ((1, length), f32)],
@@ -439,16 +461,16 @@
         here=(2, 3),
     )
     got = exchange(sent, head)
-    w_other = far([swap(w) for w in w_mine])
+    w_other = [swap(w) for w in w_mine]
     sent, *mixed = call(
         middle_kernel,
         [((rows * tiles,) + block, bf16)] + [((2,) + block, bf16)] * GRID["x"],
         near(got) + (*w_mine, *w_other),
-        in_specs=[whole] + [pl.BlockSpec(memory_space=pl.ANY)] * (2 * GRID["x"]),
+        in_specs=[whole] + [anywhere] * len(w_mine + w_other),
         scratch_shapes=[
             pltpu.VMEM((tiles,) + block, bf16),
             pltpu.VMEM((2 * GRID["x"],) + packed[0].shape, bf16),
-            pltpu.SemaphoreType.DMA((2 * GRID["x"],)),
+            pltpu.SemaphoreType.DMA((len(w_mine + w_other),)),
         ],
     )
     got = exchange(sent, head)

time: 139 us -> 147 us (1.058)
  starting transfers between devices: 73.1 us -> 82 us
    ppermute x6, waiting for transfers between devices: 12.8 us -> 3.32 us  [along_x(): lax.ppermute(parts[s], 'x', [(i, (i + s) % n) for i in range(n)])]
    all_to_all x5, waiting for transfers between devices: 23.7 us -> 28.4 us  [exchange(): return lax.all_to_all(array, axis, 0, 0)]
    all_to_all x5, starting transfers between devices: 41.7 us -> 46.1 us  [exchange(): return lax.all_to_all(array, axis, 0, 0)]
    ppermute x0 -> x1, starting transfers between devices: none -> 3.37 us  [on_device(): lax.ppermute(w3[:upper], 'x', [(i, (i + 3) % GRID['x']) for i in range(GR...]
    ppermute x0 -> x1, waiting for transfers between devices: none -> 3.29 us  [on_device(): lax.ppermute(w3[:upper], 'x', [(i, (i + 3) % GRID['x']) for i in range(GR...]
    ppermute x5 -> x6, starting transfers between devices: 10.2 us -> 12 us  [swap(): return lax.ppermute(array, 'core', [(0, 1), (1, 0)])]
  transfers between devices with their start and end apart: 16 -> 18, of which waited for: 7 -> 8; matrix products, arithmetic and copies ran while one was open for 0% -> 0% of each run, Pallas kernels for 11% -> 10%
where the time goes in v6:
time: 147 us; the launch traced here: 146 us
  starting transfers between devices  82 us (56%)
  waiting for transfers between devices  37.7 us (26%)
  Pallas kernels  21.5 us (15%)
  local copies, waits for them, and re-layouts  3.45 us (2%)
    all_to_all x5, starting transfers between devices, exchange(): return lax.all_to_all(array, axis, 0, 0)  46.1 us
    all_to_all x5, waiting for transfers between devices, exchange(): return lax.all_to_all(array, axis, 0, 0)  28.4 us
    pallas_call x7, Pallas kernels, call(): pl.pallas_call(kernel, cost_estimate=pl.CostEstimate(flops=1 << 30, trans...  21.5 us
    ppermute x6, starting transfers between devices, along_x(): lax.ppermute(parts[s], 'x', [(i, (i + s) % n) for i in range(n)])  20.5 us
    ppermute x6, starting transfers between devices, swap(): return lax.ppermute(array, 'core', [(0, 1), (1, 0)])  12 us
    ppermute x1, starting transfers between devices, on_device(): lax.ppermute(w3[:upper], 'x', [(i, (i + 3) % GRID['x']) for i in range(GR...  3.37 us
    ppermute x6, waiting for transfers between devices, along_x(): lax.ppermute(parts[s], 'x', [(i, (i + s) % n) for i in range(n)])  3.32 us
    ppermute x1, waiting for transfers between devices, on_device(): lax.ppermute(w3[:upper], 'x', [(i, (i + 3) % GRID['x']) for i in range(GR...  3.29 us
  transfers between devices with their start and end apart: 18, of which 8 were waited for; matrix products, arithmetic and copies ran while one was open for 0% of the time, Pallas kernels for 10%

profile of v6, /device:TPU:2, one launch (start us, length us, event | category | flops | bytes accessed | tf_op | source)
XLA Modules:
  0.0 145.7 jit_solution(11470204262533917033)
XLA Ops:
  0.6 1.9 %copy.17 = bf16[8,8,8,512]{3,2,0,1:T(8,128)(2,1)} copy(bf16[8,8,8,512]{3,2,1,0:T(8,128)(2,1)} %bitcast.28) | data formatting | bytes 1048576 | tf_op jit(solution)/shard_map/reshape | solution.py:408
  2.5 7.1 %all-to-all-start = ((bf16[8,64,512]{2,1,0:T(8,128)(2,1)}), bf16[8,64,512]{2,1,0:T(8,128)(2,1)S(1)}, u32[]{:S(2)}, u32[]{:S(2)}) async-start(bf16[8,64,512]{2,1,0:T(8,128)(2,1)} %bitcast.23), calls=%async_computation | async-start | bytes 1048576 | tf_op jit(solution)/shard_map/all_to_all | solution.py:369
  9.6 6.4 %shard_map.129 = (bf16[12,48,128]{2,1,0:T(8,128)(2,1)}, f32[64,512]{1,0:T(8,128)S(1)}, f32[64,512]{1,0:T(8,128)}, f32[64,512]{1,0:T(8,128)}, f32[64,512]{1,0:T(8...) custom-call(bf16[512,4096]{1,0:T(8,128)(2,1)} %x.1, ...), custom_call_target="tpu_custom_call" | custom-call | flops 1073741824 | bytes 8388608 | tf_op jit(solution)/shard_map/pallas_call | solution.py:353
  16.1 0.0 copy-start.4
  16.1 11.0 %all-to-all-done = bf16[8,64,512]{2,1,0:T(8,128)(2,1)S(1)} async-done(((bf16[8,64,512]{2,1,0:T(8,128)(2,1)}), bf16[8,64,512]{2,1,0:T(8,128)(2,1)S(1)}, u32[]{:S(2)}, u32[]{:S(2)}) %all-to-all-start) | async-done | bytes 524320 | tf_op jit(solution)/shard_map/all_to_all | solution.py:369
  27.1 15.2 %all-to-all-start.1 = ((bf16[12,48,128]{2,1,0:T(8,128)(2,1)}), bf16[12,48,128]{2,1,0:T(8,128)(2,1)S(1)}, u32[]{:S(2)}, u32[]{:S(2)}) async-start(bf16[12,48,128]{2,1,0:T(8,128)(2,1)} %get-tuple-element.47), calls=%async_computation.1 | async-start | bytes 294912 | tf_op jit(solution)/shard_map/all_to_all | solution.py:369
  42.3 2.1 %shard_map.131 = (bf16[528,512]{1,0:T(8,128)(2,1)}, bf16[528,512]{1,0:T(8,128)(2,1)}, bf16[272,512]{1,0:T(8,128)(2,1)}, bf16[528,512]{1,0:T(8,128)(2,1)}) custom-call(bf16[512,512]{1,0:T(8,128)(2,1)S(1)} %bitcast.24, bf16[16,512]{1,0:T(8,128)(2,1)} %get-tuple-element.53.t0, bf16[16,512]{1,0:T(8,128)(2,1)} %get-tuple-element.54.t1, ...), custom_call_target="tpu_custom_call" | custom-call | flops 1073741824 | bytes 8388608 | tf_op jit(solution)/shard_map/pallas_call | solution.py:353
  44.4 0.0 copy-start.15
  44.4 0.0 copy-start.6
  44.4 3.5 %collective-permute-start = (bf16[528,512]{1,0:T(8,128)(2,1)}, bf16[528,512]{1,0:T(8,128)(2,1)}, u32[]{:S(2)}, u32[]{:S(2)}) collective-permute-start(bf16[528,512]{1,0:T(8,128)(2,1)} %get-tuple-element.58), channel_id=1, source_target_pairs={{0,2},{2,4},{4,6},{6,0},{1,3},{3,5},{5,7},{7,1},{8,10},{10,12},{12... | collective-permute-start | bytes 1622024 | tf_op jit(solution)/shard_map/ppermute | solution.py:375
  48.0 2.4 %collective-permute-start.2 = (bf16[528,512]{1,0:T(8,128)(2,1)}, bf16[528,512]{1,0:T(8,128)(2,1)S(1)}, u32[]{:S(2)}, u32[]{:S(2)}) collective-permute-start(bf16[528,512]{1,0:T(8,128)(2,1)} %get-tuple-element.60), channel_id=1, source_target_pairs={{0,6},{2,0},{4,2},{6,4},{1,7},{3,1},{5,3},{7,5},{8,14},{10,8},{12,... | collective-permute-start | bytes 1622024 | tf_op jit(solution)/shard_map/ppermute | solution.py:375
  50.4 4.9 %all-to-all-done.1.everyone = bf16[12,48,128]{2,1,0:T(8,128)(2,1)S(1)} async-done(((bf16[12,48,128]{2,1,0:T(8,128)(2,1)}), bf16[12,48,128]{2,1,0:T(8,128)(2,1)S(1)}, u32[]{:S(2)}, u32[]{:S(2)}) %all-to-all-start.1) | async-done | bytes 147488 | tf_op jit(solution)/shard_map/all_to_all | solution.py:369
  55.3 2.2 %shard_map.130 = (bf16[64,32,128]{2,1,0:T(8,128)(2,1)}, f32[64,64]{1,0:T(8,128)}, f32[64,512]{1,0:T(8,128)S(1)}, f32[1,512]{1,0:T(1,128)S(1)}) custom-call(bf16[12,48,128]{2,1,0:T(8,128)(2,1)S(1)} %all-to-all-done.1.everyone, f32[64,512]{1,0:T(8,128)S(1)} %get-tuple-element.48.local, f32[64,512]{1,0:T(8,128)S(1)} %get-tuple-element.49.reads, ...), custom_call_target="tpu_custom_call" | custom-call | flops 1073741824 | bytes 8388608 | tf_op jit(solution)/shard_map/pallas_call | solution.py:353
  57.5 5.4 %all-to-all-start.2 = ((bf16[64,32,128]{2,1,0:T(8,128)(2,1)}), bf16[64,32,128]{2,1,0:T(8,128)(2,1)S(1)}, u32[]{:S(2)}, u32[]{:S(2)}) async-start(bf16[64,32,128]{2,1,0:T(8,128)(2,1)} %get-tuple-element.51), calls=%async_computation.2 | async-start | bytes 1048576 | tf_op jit(solution)/shard_map/all_to_all | solution.py:369
  62.9 0.0 copy-done.15
  62.9 4.0 %collective-permute-start.1 = (bf16[272,512]{1,0:T(8,128)(2,1)S(1)}, bf16[272,512]{1,0:T(8,128)(2,1)S(1)}, u32[]{:S(2)}, u32[]{:S(2)}) collective-permute-start(bf16[272,512]{1,0:T(8,128)(2,1)S(1)} %copy-done.15), channel_id=1, source_target_pairs={{0,4},{2,6},{4,0},{6,2},{1,5},{3,7},{5,1},{7,3},{8,12},{10,14},{12... | collective-permute-start | bytes 835592 | tf_op jit(solution)/shard_map/ppermute | solution.py:375
  66.9 0.0 copy-done.6
  66.9 1.9 %collective-permute-start.4 = (bf16[528,512]{1,0:T(8,128)(2,1)S(1)}, bf16[528,512]{1,0:T(8,128)(2,1)S(1)}, u32[]{:S(2)}, u32[]{:S(2)}) collective-permute-start(bf16[528,512]{1,0:T(8,128)(2,1)S(1)} %copy-done.6), channel_id=1, source_target_pairs={{0,1},{1,0},{2,3},{3,2},{4,5},{5,4},{6,7},{7,6},{8,9},{9,8},{10,11... | collective-permute-start | bytes 1622024 | tf_op jit(solution)/shard_map/ppermute | solution.py:380
  68.9 0.0 collective-permute-done.w1
  68.9 2.4 %collective-permute-start.5 = (bf16[528,512]{1,0:T(8,128)(2,1)}, bf16[528,512]{1,0:T(8,128)(2,1)S(1)}, u32[]{:S(2)}, u32[]{:S(2)}) collective-permute-start(bf16[528,512]{1,0:T(8,128)(2,1)} %collective-permute-done.w1), channel_id=1, source_target_pairs={{0,1},{1,0},{2,3},{3,2},{4,5},{5,4},{6,7},{7,6},{8,9},{9,8},{10,11... | collective-permute-start | bytes 1622024 | tf_op jit(solution)/shard_map/ppermute | solution.py:380
  71.3 0.0 collective-permute-done.2.w3
  71.3 0.0 copy-start.5
  71.3 1.9 %collective-permute-start.8 = (bf16[528,512]{1,0:T(8,128)(2,1)S(1)}, bf16[528,512]{1,0:T(8,128)(2,1)}, u32[]{:S(2)}, u32[]{:S(2)}) collective-permute-start(bf16[528,512]{1,0:T(8,128)(2,1)S(1)} %collective-permute-done.2.w3), channel_id=1, source_target_pairs={{0,1},{1,0},{2,3},{3,2},{4,5},{5,4},{6,7},{7,6},{8,9},{9,8},{10,11... | collective-permute-start | bytes 1622024 | tf_op jit(solution)/shard_map/ppermute | solution.py:380
  73.3 3.4 %collective-permute-start.3 = (bf16[256,512]{1,0:T(8,128)(2,1)S(1)}, bf16[256,512]{1,0:T(8,128)(2,1)S(1)}, u32[]{:S(2)}, u32[]{:S(2)}) collective-permute-start(bf16[256,512]{1,0:T(8,128)(2,1)S(1)} %slice.4), channel_id=1, source_target_pairs={{0,6},{2,0},{4,2},{6,4},{1,7},{3,1},{5,3},{7,5},{8,14},{10,8},{12,... | collective-permute-start | bytes 786440 | tf_op jit(solution)/shard_map/ppermute | solution.py:455
  76.6 3.3 %collective-permute-done.1.w2 = bf16[272,512]{1,0:T(8,128)(2,1)S(1)} collective-permute-done((bf16[272,512]{1,0:T(8,128)(2,1)S(1)}, bf16[272,512]{1,0:T(8,128)(2,1)S(1)}, u32[]{:S(2)}, u32[]{:S(2)}) %collective-permute-start.1) | collective-permute-done | bytes 278560 | tf_op jit(solution)/shard_map/ppermute | solution.py:375
  79.9 1.9 %collective-permute-start.6 = (bf16[272,512]{1,0:T(8,128)(2,1)S(1)}, bf16[272,512]{1,0:T(8,128)(2,1)S(1)}, u32[]{:S(2)}, u32[]{:S(2)}) collective-permute-start(bf16[272,512]{1,0:T(8,128)(2,1)S(1)} %collective-permute-done.1.w2), channel_id=1, source_target_pairs={{0,1},{1,0},{2,3},{3,2},{4,5},{5,4},{6,7},{7,6},{8,9},{9,8},{10,11... | collective-permute-start | bytes 835592 | tf_op jit(solution)/shard_map/ppermute | solution.py:380
  81.9 3.3 %collective-permute-done.3.w2f = bf16[256,512]{1,0:T(8,128)(2,1)S(1)} collective-permute-done((bf16[256,512]{1,0:T(8,128)(2,1)S(1)}, bf16[256,512]{1,0:T(8,128)(2,1)S(1)}, u32[]{:S(2)}, u32[]{:S(2)}) %collective-permute-start.3) | collective-permute-done | bytes 262176 | tf_op jit(solution)/shard_map/ppermute | solution.py:455
  85.2 2.0 %collective-permute-start.7 = (bf16[256,512]{1,0:T(8,128)(2,1)S(1)}, bf16[256,512]{1,0:T(8,128)(2,1)S(1)}, u32[]{:S(2)}, u32[]{:S(2)}) collective-permute-start(bf16[256,512]{1,0:T(8,128)(2,1)S(1)} %collective-permute-done.3.w2f), channel_id=1, source_target_pairs={{0,1},{1,0},{2,3},{3,2},{4,5},{5,4},{6,7},{7,6},{8,9},{9,8},{10,11... | collective-permute-start | bytes 786440 | tf_op jit(solution)/shard_map/ppermute | solution.py:380
  87.1 0.0 collective-permute-done.4.v0
  87.1 0.0 copy-start.7
  87.2 0.0 collective-permute-done.6.v2
  87.2 0.0 copy-start.10
  87.2 1.4 collective-permute-done.7.v2f
  88.6 0.0 collective-permute-done.5.v1
  88.6 0.0 copy-done.7
  88.6 0.0 copy-start.8
  88.6 0.8 copy-done.8
  89.4 0.0 collective-permute-done.8.v3
  89.4 0.0 all-to-all-done.2.got
  89.4 0.0 copy-done.5
  89.5 0.0 copy-done.9
  89.5 0.0 copy-done.11
  89.5 0.0 copy-done.10
  89.5 0.0 copy-done.12
  89.5 4.6 %shard_map.132 = (bf16[64,32,128]{2,1,0:T(8,128)(2,1)}, bf16[2,32,128]{2,1,0:T(8,128)(2,1)}, bf16[2,32,128]{2,1,0:T(8,128)(2,1)}, bf16[2,32,128]{2,1,0:T(8,128)(2,1)}, bf16[2,32,128]{2,1,0:T(8,128)(2,1)}) custom-call(bf16[64,32,128]{2,1,0:T(8,128)(2,1)S(1)} %all-to-all-done.2.got, bf16[528,512]{1,0:T(8,128)(2,1)} %get-tuple-element.57.w0, ...), custom_call_target="tpu_custom_call" | custom-call | flops 1073741824 | bytes 8388608 | tf_op jit(solution)/shard_map/pallas_call | solution.py:353
  94.1 0.0 copy-start.14
  94.1 9.3 %all-to-all-start.3 = ((bf16[64,32,128]{2,1,0:T(8,128)(2,1)}), bf16[64,32,128]{2,1,0:T(8,128)(2,1)S(1)}, u32[]{:S(2)}, u32[]{:S(2)}) async-start(bf16[64,32,128]{2,1,0:T(8,128)(2,1)} %get-tuple-element.69), calls=%async_computation.3 | async-start | bytes 1048576 | tf_op jit(solution)/shard_map/all_to_all | solution.py:369
  103.5 3.5 %collective-permute-start.9 = (bf16[2,32,128]{2,1,0:T(8,128)(2,1)}, bf16[2,32,128]{2,1,0:T(8,128)(2,1)S(1)}, u32[]{:S(2)}, u32[]{:S(2)}) collective-permute-start(bf16[2,32,128]{2,1,0:T(8,128)(2,1)} %get-tuple-element.62), channel_id=1, source_target_pairs={{0,2},{2,4},{4,6},{6,0},{1,3},{3,5},{5,7},{7,1},{8,10},{10,12},{12... | collective-permute-start | bytes 49160 | tf_op jit(solution)/shard_map/ppermute | solution.py:375
  107.0 3.0 %collective-permute-start.10 = (bf16[2,32,128]{2,1,0:T(8,128)(2,1)}, bf16[2,32,128]{2,1,0:T(8,128)(2,1)S(1)}, u32[]{:S(2)}, u32[]{:S(2)}) collective-permute-start(bf16[2,32,128]{2,1,0:T(8,128)(2,1)} %get-tuple-element.63), channel_id=1, source_target_pairs={{0,4},{2,6},{4,0},{6,2},{1,5},{3,7},{5,1},{7,3},{8,12},{10,14},{12... | collective-permute-start | bytes 49160 | tf_op jit(solution)/shard_map/ppermute | solution.py:375
  110.0 4.1 %collective-permute-start.11 = (bf16[2,32,128]{2,1,0:T(8,128)(2,1)}, bf16[2,32,128]{2,1,0:T(8,128)(2,1)S(1)}, u32[]{:S(2)}, u32[]{:S(2)}) collective-permute-start(bf16[2,32,128]{2,1,0:T(8,128)(2,1)} %get-tuple-element.64), channel_id=1, source_target_pairs={{0,6},{2,0},{4,2},{6,4},{1,7},{3,1},{5,3},{7,5},{8,14},{10,8},{12,... | collective-permute-start | bytes 49160 | tf_op jit(solution)/shard_map/ppermute | solution.py:375
  114.0 7.0 %all-to-all-done.3.got = bf16[64,32,128]{2,1,0:T(8,128)(2,1)S(1)} async-done(((bf16[64,32,128]{2,1,0:T(8,128)(2,1)}), bf16[64,32,128]{2,1,0:T(8,128)(2,1)S(1)}, u32[]{:S(2)}, u32[]{:S(2)}) %all-to-all-start.3) | async-done | bytes 524320 | tf_op jit(solution)/shard_map/all_to_all | solution.py:369
  121.0 1.7 %shard_map.133 = (bf16[12,32,128]{2,1,0:T(8,128)(2,1)}, f32[64,512]{1,0:T(8,128)}) custom-call(bf16[64,32,128]{2,1,0:T(8,128)(2,1)S(1)} %all-to-all-done.3.got, f32[64,512]{1,0:T(8,128)S(1)} %get-tuple-element.70.unit, f32[1,512]{1,0:T(1,128)S(1)} %get-tuple-element.71.inverse, f32[1,64]{1,0:T(1,128)} %bitcast.41, f32[64,512]{1,0:T(8,128)S(1)} %get-tuple-element.49.reads, ...), custom_call_target="tpu_custom_call" | custom-call | flops 1073741824 | bytes 8388608 | tf_op jit(solution)/shard_map/pallas_call | solution.py:353
  122.8 9.2 %all-to-all-start.4 = ((bf16[12,32,128]{2,1,0:T(8,128)(2,1)}), bf16[12,32,128]{2,1,0:T(8,128)(2,1)S(1)}, u32[]{:S(2)}, u32[]{:S(2)}) async-start(bf16[12,32,128]{2,1,0:T(8,128)(2,1)} %get-tuple-element.75), calls=%async_computation.4 | async-start | bytes 196608 | tf_op jit(solution)/shard_map/all_to_all | solution.py:369
  131.9 0.0 collective-permute-done.9
  131.9 0.0 collective-permute-done.10
  131.9 0.0 collective-permute-done.11
  132.0 0.0 copy-start.13
  132.0 1.9 %collective-permute-start.12 = (bf16[4,2,32,128]{3,2,1,0:T(8,128)(2,1)S(1)}, bf16[4,2,32,128]{3,2,1,0:T(8,128)(2,1)S(1)}, u32[]{:S(2)}, u32[]{:S(2)}) collective-permute-start(bf16[4,2,32,128]{3,2,1,0:T(8,128)(2,1)S(1)} %pad_maximum_fusion.m_mine), channel_id=1, source_target_pairs={{0,1},{1,0},{2,3},{3,2},{4,5},{5,4},{6,7},{7,6},{8,9},{9,8},{10,11... | collective-permute-start | bytes 196616 | tf_op jit(solution)/shard_map/ppermute | solution.py:380
  133.9 1.2 collective-permute-done.12.m_other
  135.1 0.6 copy-done.16
  135.8 2.7 %shard_map.134 = (bf16[64,512]{1,0:T(8,128)(2,1)}, bf16[64,512]{1,0:T(8,128)(2,1)}, f32[64,512]{1,0:T(8,128)S(1)}, f32[64,512]{1,0:T(8,128)S(1)}) custom-call(bf16[4,2,32,128]{3,2,1,0:T(8,128)(2,1)} %copy-done.13, bf16[4,2,32,128]{3,2,1,0:T(8,128)(2,1)} %copy-done.16, f32[64,512]{1,0:T(8,128)} %copy-done.4, f32[64,512]{1,0:T(8,128)} %get-tuple-element.65.keys_raw, ...), custom_call_target="tpu_custom_call" | custom-call | flops 1073741824 | bytes 8388608 | tf_op jit(solution)/shard_map/pallas_call | solution.py:353
  138.4 5.6 %all-to-all-done.4.later = bf16[12,32,128]{2,1,0:T(8,128)(2,1)S(1)} async-done(((bf16[12,32,128]{2,1,0:T(8,128)(2,1)}), bf16[12,32,128]{2,1,0:T(8,128)(2,1)S(1)}, u32[]{:S(2)}, u32[]{:S(2)}) %all-to-all-start.4) | async-done | bytes 98336 | tf_op jit(solution)/shard_map/all_to_all | solution.py:369
  144.0 0.0 copy-done.1
  144.0 1.7 %shard_map.135 = (bf16[64,512]{1,0:T(8,128)(2,1)}, bf16[64,512]{1,0:T(8,128)(2,1)}) custom-call(bf16[12,32,128]{2,1,0:T(8,128)(2,1)S(1)} %all-to-all-done.4.later, bf16[12,48,128]{2,1,0:T(8,128)(2,1)S(1)} %all-to-all-done.1.everyone, f32[64,512]{1,0:T(8,128)S(1)} %get-tuple-element.76.part_keys, f32[64,512]{1,0:T(8,128)S(1)} %get-tuple-element.77.part_values, ...), custom_call_target="tpu_custom_call" | custom-call | flops 1073741824 | bytes 8388608 | tf_op jit(solution)/shard_map/pallas_call | solution.py:353
  (16 shorter events, 0.1 us)
Async XLA Ops:
  2.5 24.6 %all-to-all-start = ((bf16[8,64,512]{2,1,0:T(8,128)(2,1)}), bf16[8,64,512]{2,1,0:T(8,128)(2,1)S(1)}, u32[]{:S(2)}, u32[]{:S(2)}) async-start(bf16[8,64,512]{2,1,0:T(8,128)(2,1)} %bitcast.23), calls=%async_computation | async-start | bytes 1048576 | tf_op jit(solution)/shard_map/all_to_all | solution.py:369
  16.1 104.9 %copy-start.2 = (f32[64,512]{1,0:T(8,128)}, f32[64,512]{1,0:T(8,128)S(1)}, u32[]{:S(2)}) copy-start(f32[64,512]{1,0:T(8,128)S(1)} %get-tuple-element.50.logs) | copy-start | bytes 393220
  16.1 104.9 %copy-start.4 = (f32[64,512]{1,0:T(8,128)}, f32[64,512]{1,0:T(8,128)S(1)}, u32[]{:S(2)}) copy-start(f32[64,512]{1,0:T(8,128)S(1)} %get-tuple-element.49.reads) | copy-start | bytes 393220
  27.1 28.2 %all-to-all-start.1 = ((bf16[12,48,128]{2,1,0:T(8,128)(2,1)}), bf16[12,48,128]{2,1,0:T(8,128)(2,1)S(1)}, u32[]{:S(2)}, u32[]{:S(2)}) async-start(bf16[12,48,128]{2,1,0:T(8,128)(2,1)} %get-tuple-element.47), calls=%async_computation.1 | async-start | bytes 294912 | tf_op jit(solution)/shard_map/all_to_all | solution.py:369
  44.4 18.5 %copy-start.15 = (bf16[272,512]{1,0:T(8,128)(2,1)S(1)}, bf16[272,512]{1,0:T(8,128)(2,1)}, u32[]{:S(2)}) copy-start(bf16[272,512]{1,0:T(8,128)(2,1)} %get-tuple-element.59) | copy-start | bytes 835588
  44.4 22.5 %copy-start.6 = (bf16[528,512]{1,0:T(8,128)(2,1)S(1)}, bf16[528,512]{1,0:T(8,128)(2,1)}, u32[]{:S(2)}) copy-start(bf16[528,512]{1,0:T(8,128)(2,1)} %get-tuple-element.57.w0) | copy-start | bytes 1622020
  44.4 24.4 %collective-permute-start = (bf16[528,512]{1,0:T(8,128)(2,1)}, bf16[528,512]{1,0:T(8,128)(2,1)}, u32[]{:S(2)}, u32[]{:S(2)}) collective-permute-start(bf16[528,512]{1,0:T(8,128)(2,1)} %get-tuple-element.58), channel_id=1, source_target_pairs={{0,2},{2,4},{4,6},{6,0},{1,3},{3,5},{5,7},{7,1},{8,10},{10,12},{12... | collective-permute-start | bytes 1622024 | tf_op jit(solution)/shard_map/ppermute | solution.py:375
  48.0 23.3 %collective-permute-start.2 = (bf16[528,512]{1,0:T(8,128)(2,1)}, bf16[528,512]{1,0:T(8,128)(2,1)S(1)}, u32[]{:S(2)}, u32[]{:S(2)}) collective-permute-start(bf16[528,512]{1,0:T(8,128)(2,1)} %get-tuple-element.60), channel_id=1, source_target_pairs={{0,6},{2,0},{4,2},{6,4},{1,7},{3,1},{5,3},{7,5},{8,14},{10,8},{12,... | collective-permute-start | bytes 1622024 | tf_op jit(solution)/shard_map/ppermute | solution.py:375
  57.5 31.9 %all-to-all-start.2 = ((bf16[64,32,128]{2,1,0:T(8,128)(2,1)}), bf16[64,32,128]{2,1,0:T(8,128)(2,1)S(1)}, u32[]{:S(2)}, u32[]{:S(2)}) async-start(bf16[64,32,128]{2,1,0:T(8,128)(2,1)} %get-tuple-element.51), calls=%async_computation.2 | async-start | bytes 1048576 | tf_op jit(solution)/shard_map/all_to_all | solution.py:369
  62.9 17.0 %collective-permute-start.1 = (bf16[272,512]{1,0:T(8,128)(2,1)S(1)}, bf16[272,512]{1,0:T(8,128)(2,1)S(1)}, u32[]{:S(2)}, u32[]{:S(2)}) collective-permute-start(bf16[272,512]{1,0:T(8,128)(2,1)S(1)} %copy-done.15), channel_id=1, source_target_pairs={{0,4},{2,6},{4,0},{6,2},{1,5},{3,7},{5,1},{7,3},{8,12},{10,14},{12... | collective-permute-start | bytes 835592 | tf_op jit(solution)/shard_map/ppermute | solution.py:375
  66.9 20.2 %collective-permute-start.4 = (bf16[528,512]{1,0:T(8,128)(2,1)S(1)}, bf16[528,512]{1,0:T(8,128)(2,1)S(1)}, u32[]{:S(2)}, u32[]{:S(2)}) collective-permute-start(bf16[528,512]{1,0:T(8,128)(2,1)S(1)} %copy-done.6), channel_id=1, source_target_pairs={{0,1},{1,0},{2,3},{3,2},{4,5},{5,4},{6,7},{7,6},{8,9},{9,8},{10,11... | collective-permute-start | bytes 1622024 | tf_op jit(solution)/shard_map/ppermute | solution.py:380
  68.9 19.7 %collective-permute-start.5 = (bf16[528,512]{1,0:T(8,128)(2,1)}, bf16[528,512]{1,0:T(8,128)(2,1)S(1)}, u32[]{:S(2)}, u32[]{:S(2)}) collective-permute-start(bf16[528,512]{1,0:T(8,128)(2,1)} %collective-permute-done.w1), channel_id=1, source_target_pairs={{0,1},{1,0},{2,3},{3,2},{4,5},{5,4},{6,7},{7,6},{8,9},{9,8},{10,11... | collective-permute-start | bytes 1622024 | tf_op jit(solution)/shard_map/ppermute | solution.py:380
  71.3 18.2 %copy-start.5 = (bf16[528,512]{1,0:T(8,128)(2,1)}, bf16[528,512]{1,0:T(8,128)(2,1)S(1)}, u32[]{:S(2)}) copy-start(bf16[528,512]{1,0:T(8,128)(2,1)S(1)} %collective-permute-done.2.w3) | copy-start | bytes 1622020
  71.3 18.1 %collective-permute-start.8 = (bf16[528,512]{1,0:T(8,128)(2,1)S(1)}, bf16[528,512]{1,0:T(8,128)(2,1)}, u32[]{:S(2)}, u32[]{:S(2)}) collective-permute-start(bf16[528,512]{1,0:T(8,128)(2,1)S(1)} %collective-permute-done.2.w3), channel_id=1, source_target_pairs={{0,1},{1,0},{2,3},{3,2},{4,5},{5,4},{6,7},{7,6},{8,9},{9,8},{10,11... | collective-permute-start | bytes 1622024 | tf_op jit(solution)/shard_map/ppermute | solution.py:380
  73.3 11.9 %collective-permute-start.3 = (bf16[256,512]{1,0:T(8,128)(2,1)S(1)}, bf16[256,512]{1,0:T(8,128)(2,1)S(1)}, u32[]{:S(2)}, u32[]{:S(2)}) collective-permute-start(bf16[256,512]{1,0:T(8,128)(2,1)S(1)} %slice.4), channel_id=1, source_target_pairs={{0,6},{2,0},{4,2},{6,4},{1,7},{3,1},{5,3},{7,5},{8,14},{10,8},{12,... | collective-permute-start | bytes 786440 | tf_op jit(solution)/shard_map/ppermute | solution.py:455
  79.9 9.5 %copy-start.9 = (bf16[272,512]{1,0:T(8,128)(2,1)}, bf16[272,512]{1,0:T(8,128)(2,1)S(1)}, u32[]{:S(2)}) copy-start(bf16[272,512]{1,0:T(8,128)(2,1)S(1)} %collective-permute-done.1.w2) | copy-start | bytes 835588
  79.9 7.2 %collective-permute-start.6 = (bf16[272,512]{1,0:T(8,128)(2,1)S(1)}, bf16[272,512]{1,0:T(8,128)(2,1)S(1)}, u32[]{:S(2)}, u32[]{:S(2)}) collective-permute-start(bf16[272,512]{1,0:T(8,128)(2,1)S(1)} %collective-permute-done.1.w2), channel_id=1, source_target_pairs={{0,1},{1,0},{2,3},{3,2},{4,5},{5,4},{6,7},{7,6},{8,9},{9,8},{10,11... | collective-permute-start | bytes 835592 | tf_op jit(solution)/shard_map/ppermute | solution.py:380
  85.2 4.3 %copy-start.11 = (bf16[256,512]{1,0:T(8,128)(2,1)}, bf16[256,512]{1,0:T(8,128)(2,1)S(1)}, u32[]{:S(2)}) copy-start(bf16[256,512]{1,0:T(8,128)(2,1)S(1)} %collective-permute-done.3.w2f) | copy-start | bytes 786436
  85.2 3.4 %collective-permute-start.7 = (bf16[256,512]{1,0:T(8,128)(2,1)S(1)}, bf16[256,512]{1,0:T(8,128)(2,1)S(1)}, u32[]{:S(2)}, u32[]{:S(2)}) collective-permute-start(bf16[256,512]{1,0:T(8,128)(2,1)S(1)} %collective-permute-done.3.w2f), channel_id=1, source_target_pairs={{0,1},{1,0},{2,3},{3,2},{4,5},{5,4},{6,7},{7,6},{8,9},{9,8},{10,11... | collective-permute-start | bytes 786440 | tf_op jit(solution)/shard_map/ppermute | solution.py:380
  87.1 1.4 copy-start.7
  87.2 2.3 %copy-start.10 = (bf16[272,512]{1,0:T(8,128)(2,1)}, bf16[272,512]{1,0:T(8,128)(2,1)S(1)}, u32[]{:S(2)}) copy-start(bf16[272,512]{1,0:T(8,128)(2,1)S(1)} %collective-permute-done.6.v2) | copy-start | bytes 835588
  88.6 0.9 copy-start.12
  88.6 0.9 copy-start.8
  94.1 37.8 %copy-start.14 = (bf16[2,32,128]{2,1,0:T(8,128)(2,1)S(1)}, bf16[2,32,128]{2,1,0:T(8,128)(2,1)}, u32[]{:S(2)}) copy-start(bf16[2,32,128]{2,1,0:T(8,128)(2,1)} %get-tuple-element.61) | copy-start | bytes 49156
  94.1 26.9 %all-to-all-start.3 = ((bf16[64,32,128]{2,1,0:T(8,128)(2,1)}), bf16[64,32,128]{2,1,0:T(8,128)(2,1)S(1)}, u32[]{:S(2)}, u32[]{:S(2)}) async-start(bf16[64,32,128]{2,1,0:T(8,128)(2,1)} %get-tuple-element.69), calls=%async_computation.3 | async-start | bytes 1048576 | tf_op jit(solution)/shard_map/all_to_all | solution.py:369
  103.4 40.6 %copy-start = (f32[64,512]{1,0:T(8,128)S(1)}, f32[64,512]{1,0:T(8,128)}, u32[]{:S(2)}) copy-start(f32[64,512]{1,0:T(8,128)} %get-tuple-element.65.keys_raw) | copy-start | bytes 393220
  103.5 40.5 %copy-start.1 = (f32[64,512]{1,0:T(8,128)S(1)}, f32[64,512]{1,0:T(8,128)}, u32[]{:S(2)}) copy-start(f32[64,512]{1,0:T(8,128)} %get-tuple-element.66.values) | copy-start | bytes 393220
  103.5 28.5 %collective-permute-start.9 = (bf16[2,32,128]{2,1,0:T(8,128)(2,1)}, bf16[2,32,128]{2,1,0:T(8,128)(2,1)S(1)}, u32[]{:S(2)}, u32[]{:S(2)}) collective-permute-start(bf16[2,32,128]{2,1,0:T(8,128)(2,1)} %get-tuple-element.62), channel_id=1, source_target_pairs={{0,2},{2,4},{4,6},{6,0},{1,3},{3,5},{5,7},{7,1},{8,10},{10,12},{12... | collective-permute-start | bytes 49160 | tf_op jit(solution)/shard_map/ppermute | solution.py:375
  107.0 25.0 %collective-permute-start.10 = (bf16[2,32,128]{2,1,0:T(8,128)(2,1)}, bf16[2,32,128]{2,1,0:T(8,128)(2,1)S(1)}, u32[]{:S(2)}, u32[]{:S(2)}) collective-permute-start(bf16[2,32,128]{2,1,0:T(8,128)(2,1)} %get-tuple-element.63), channel_id=1, source_target_pairs={{0,4},{2,6},{4,0},{6,2},{1,5},{3,7},{5,1},{7,3},{8,12},{10,14},{12... | collective-permute-start | bytes 49160 | tf_op jit(solution)/shard_map/ppermute | solution.py:375
  110.0 22.0 %collective-permute-start.11 = (bf16[2,32,128]{2,1,0:T(8,128)(2,1)}, bf16[2,32,128]{2,1,0:T(8,128)(2,1)S(1)}, u32[]{:S(2)}, u32[]{:S(2)}) collective-permute-start(bf16[2,32,128]{2,1,0:T(8,128)(2,1)} %get-tuple-element.64), channel_id=1, source_target_pairs={{0,6},{2,0},{4,2},{6,4},{1,7},{3,1},{5,3},{7,5},{8,14},{10,8},{12,... | collective-permute-start | bytes 49160 | tf_op jit(solution)/shard_map/ppermute | solution.py:375
  122.8 21.2 %copy-start.3 = (f32[64,512]{1,0:T(8,128)S(1)}, f32[64,512]{1,0:T(8,128)}, u32[]{:S(2)}) copy-start(f32[64,512]{1,0:T(8,128)} %copy-done.2) | copy-start | bytes 393220
  122.8 21.2 %all-to-all-start.4 = ((bf16[12,32,128]{2,1,0:T(8,128)(2,1)}), bf16[12,32,128]{2,1,0:T(8,128)(2,1)S(1)}, u32[]{:S(2)}, u32[]{:S(2)}) async-start(bf16[12,32,128]{2,1,0:T(8,128)(2,1)} %get-tuple-element.75), calls=%async_computation.4 | async-start | bytes 196608 | tf_op jit(solution)/shard_map/all_to_all | solution.py:369
  132.0 3.2 %copy-start.13 = (bf16[4,2,32,128]{3,2,1,0:T(8,128)(2,1)}, bf16[4,2,32,128]{3,2,1,0:T(8,128)(2,1)S(1)}, u32[]{:S(2)}) copy-start(bf16[4,2,32,128]{3,2,1,0:T(8,128)(2,1)S(1)} %pad_maximum_fusion.m_mine) | copy-start | bytes 196612
  132.0 3.1 %collective-permute-start.12 = (bf16[4,2,32,128]{3,2,1,0:T(8,128)(2,1)S(1)}, bf16[4,2,32,128]{3,2,1,0:T(8,128)(2,1)S(1)}, u32[]{:S(2)}, u32[]{:S(2)}) collective-permute-start(bf16[4,2,32,128]{3,2,1,0:T(8,128)(2,1)S(1)} %pad_maximum_fusion.m_mine), channel_id=1, source_target_pairs={{0,1},{1,0},{2,3},{3,2},{4,5},{5,4},{6,7},{7,6},{8,9},{9,8},{10,11... | collective-permute-start | bytes 196616 | tf_op jit(solution)/shard_map/ppermute | solution.py:380
  135.1 0.6 copy-start.16

commit v7 on v5

--- a/solution.py
+++ b/solution.py
@@ -211,7 +211,7 @@
     return jnp.where(core == c, mine[step, core], other[step, core])
 
 
-def middle_kernel(got, w0, w1, w2, w3, v0, v1, v2, v3, sent, m0, m1, m2, m3, held, weights, sems):
+def middle_kernel(got, w0, w1, w3, w2, v0, v1, v3, v2, sent, m0, m1, m2, m3, held, weights, sems):
     copies = []
     for n, source in enumerate((w0, v0, w1, v1, w2, v2, w3, v3)):
         copies.append(pltpu.make_async_copy(source, weights.at[n], sems.at[n]))
@@ -221,7 +221,7 @@
     rows = GRID["y"]
     group = min(4, rows)
     chunks = []
-    for s in range(GRID["x"]):
+    for s in (0, 1, 3, 2):
         x = lax.rem(at - s + GRID["x"], GRID["x"])
         for n, c in ((2 * s, core), (2 * s + 1, 1 - core)):
             for y in range(0, rows, group):
@@ -347,19 +347,16 @@
     return tuple(pltpu.with_memory_space_constraint(a, pltpu.VMEM) for a in arrays)
 
 
-def far(arrays):
-    return [pltpu.with_memory_space_constraint(a, pltpu.HBM) for a in arrays]
-
-
 def exchange(array, axis):
     return lax.all_to_all(array, axis, 0, 0)
 
 
 def along_x(parts):
     n = GRID["x"]
-    return list(parts[:1]) + [
-        lax.ppermute(parts[s], "x", [(i, (i + s) % n) for i in range(n)]) for s in range(1, n)
-    ]
+    came = {
+        s: lax.ppermute(parts[s], "x", [(i, (i + s) % n) for i in range(n)]) for s in (1, 3, 2)
+    }
+    return [parts[0], came[1], came[2], came[3]]
 
 
 def swap(array):
@@ -431,7 +428,7 @@
         [((rows * LANES + teacher[0][0], tiles * LANES), bf16)] * GRID["x"],
         near(columns) + tuple(tutor),
     )
-    w_mine = far(along_x(packed))
+    w_mine = along_x(packed)
     sent, start, unit, inverse = call(
         functools.partial(yields_kernel, all_frames),
         [((rows * tiles,) + block, bf16), ((LANES, LANES), f32), (flat, f32), ((1, length), f32)],
@@ -439,12 +436,17 @@
         here=(2, 3),
     )
     got = exchange(sent, head)
-    w_other = far([swap(w) for w in w_mine])
+    other = {s: swap(w_mine[s]) for s in (0, 1, 3, 2)}
+    w_other = [other[s] for s in (0, 1, 3, 2)]
+    w_mine = [w_mine[s] for s in (0, 1, 3, 2)]
     sent, *mixed = call(
         middle_kernel,
         [((rows * tiles,) + block, bf16)] + [((2,) + block, bf16)] * GRID["x"],
-        near(got) + (*w_mine, *w_other),
-        in_specs=[whole] + [pl.BlockSpec(memory_space=pl.ANY)] * (2 * GRID["x"]),
+        near(got) + (*w_mine,) + near(w_other[0]) + (*w_other[1:],),
+        in_specs=[whole]
+        + [pl.BlockSpec(memory_space=pl.ANY)] * GRID["x"]
+        + [whole]
+        + [pl.BlockSpec(memory_space=pl.ANY)] * (GRID["x"] - 1),
         scratch_shapes=[
             pltpu.VMEM((tiles,) + block, bf16),
             pltpu.VMEM((2 * GRID["x"],) + packed[0].shape, bf16),

time: 139 us -> 141 us (1.014)
    all_to_all x5, starting transfers between devices: 41.7 us -> 43.6 us  [exchange(): return lax.all_to_all(array, axis, 0, 0)]
where the time goes in v7:
time: 141 us; the launch traced here: 139 us
  starting transfers between devices  74.3 us (53%)
  waiting for transfers between devices  38.1 us (27%)
  Pallas kernels  21.8 us (15%)
  local copies, waits for them, and re-layouts  4.16 us (3%)
    all_to_all x5, starting transfers between devices, exchange(): return lax.all_to_all(array, axis, 0, 0)  43.6 us
    all_to_all x5, waiting for transfers between devices, exchange(): return lax.all_to_all(array, axis, 0, 0)  24.3 us
    pallas_call x7, Pallas kernels, call(): pl.pallas_call(kernel, cost_estimate=pl.CostEstimate(flops=1 << 30, trans...  21.8 us
    ppermute x6, starting transfers between devices, along_x(): lax.ppermute(parts[s], 'x', [(i, (i + s) % n) for i in range(n)])  20.6 us
    ppermute x6, waiting for transfers between devices, along_x(): lax.ppermute(parts[s], 'x', [(i, (i + s) % n) for i in range(n)])  12.1 us
    ppermute x5, starting transfers between devices, swap(): return lax.ppermute(array, 'core', [(0, 1), (1, 0)])  10.2 us
  transfers between devices with their start and end apart: 16, of which 7 were waited for; matrix products, arithmetic and copies ran while one was open for 0% of the time, Pallas kernels for 11%

profile of v7, /device:TPU:2, one launch (start us, length us, event | category | flops | bytes accessed | tf_op | source)
XLA Modules:
  0.0 139.4 jit_solution(4716199329252831906)
XLA Ops:
  0.6 1.9 %copy.17 = bf16[8,8,8,512]{3,2,0,1:T(8,128)(2,1)} copy(bf16[8,8,8,512]{3,2,1,0:T(8,128)(2,1)} %bitcast.26) | data formatting | bytes 1048576 | tf_op jit(solution)/shard_map/reshape | solution.py:391
  2.5 7.1 %all-to-all-start = ((bf16[8,64,512]{2,1,0:T(8,128)(2,1)}), bf16[8,64,512]{2,1,0:T(8,128)(2,1)S(1)}, u32[]{:S(2)}, u32[]{:S(2)}) async-start(bf16[8,64,512]{2,1,0:T(8,128)(2,1)} %bitcast.22), calls=%async_computation | async-start | bytes 1048576 | tf_op jit(solution)/shard_map/all_to_all | solution.py:351
  9.6 6.5 %shard_map.129 = (bf16[12,48,128]{2,1,0:T(8,128)(2,1)}, f32[64,512]{1,0:T(8,128)S(1)}, f32[64,512]{1,0:T(8,128)}, f32[64,512]{1,0:T(8,128)}, f32[64,512]{1,0:T(8...) custom-call(bf16[512,4096]{1,0:T(8,128)(2,1)} %x.1, ...), custom_call_target="tpu_custom_call" | custom-call | flops 1073741824 | bytes 8388608 | tf_op jit(solution)/shard_map/pallas_call | solution.py:335
  16.1 0.0 copy-start.2
  16.1 0.0 copy-start.4
  16.1 11.0 %all-to-all-done.columns = bf16[8,64,512]{2,1,0:T(8,128)(2,1)S(1)} async-done(((bf16[8,64,512]{2,1,0:T(8,128)(2,1)}), bf16[8,64,512]{2,1,0:T(8,128)(2,1)S(1)}, u32[]{:S(2)}, u32[]{:S(2)}) %all-to-all-start) | async-done | bytes 524320 | tf_op jit(solution)/shard_map/all_to_all | solution.py:351
  27.1 15.2 %all-to-all-start.1 = ((bf16[12,48,128]{2,1,0:T(8,128)(2,1)}), bf16[12,48,128]{2,1,0:T(8,128)(2,1)S(1)}, u32[]{:S(2)}, u32[]{:S(2)}) async-start(bf16[12,48,128]{2,1,0:T(8,128)(2,1)} %get-tuple-element.47), calls=%async_computation.1 | async-start | bytes 294912 | tf_op jit(solution)/shard_map/all_to_all | solution.py:351
  42.3 2.3 %shard_map.131 = (bf16[528,512]{1,0:T(8,128)(2,1)}, bf16[528,512]{1,0:T(8,128)(2,1)}, bf16[528,512]{1,0:T(8,128)(2,1)}, bf16[528,512]{1,0:T(8,128)(2,1)}) custom-call(bf16[8,64,512]{2,1,0:T(8,128)(2,1)S(1)} %all-to-all-done.columns, bf16[16,512]{1,0:T(8,128)(2,1)} %get-tuple-element.53.t0, bf16[16,512]{1,0:T(8,128)(2,1)} %get-tuple-element.54.t1, ...), custom_call_target="tpu_custom_call" | custom-call | flops 1073741824 | bytes 8388608 | tf_op jit(solution)/shard_map/pallas_call | solution.py:335
  44.6 0.0 copy-start.5
  44.6 3.5 %collective-permute-start = (bf16[528,512]{1,0:T(8,128)(2,1)}, bf16[528,512]{1,0:T(8,128)(2,1)S(1)}, u32[]{:S(2)}, u32[]{:S(2)}) collective-permute-start(bf16[528,512]{1,0:T(8,128)(2,1)} %get-tuple-element.58), channel_id=1, source_target_pairs={{0,2},{2,4},{4,6},{6,0},{1,3},{3,5},{5,7},{7,1},{8,10},{10,12},{12... | collective-permute-start | bytes 1622024 | tf_op jit(solution)/shard_map/ppermute | solution.py:357
  48.1 2.4 %collective-permute-start.1 = (bf16[528,512]{1,0:T(8,128)(2,1)}, bf16[528,512]{1,0:T(8,128)(2,1)}, u32[]{:S(2)}, u32[]{:S(2)}) collective-permute-start(bf16[528,512]{1,0:T(8,128)(2,1)} %get-tuple-element.59), channel_id=1, source_target_pairs={{0,6},{2,0},{4,2},{6,4},{1,7},{3,1},{5,3},{7,5},{8,14},{10,8},{12,... | collective-permute-start | bytes 1622024 | tf_op jit(solution)/shard_map/ppermute | solution.py:357
  50.5 4.0 %collective-permute-start.2 = (bf16[528,512]{1,0:T(8,128)(2,1)}, bf16[528,512]{1,0:T(8,128)(2,1)}, u32[]{:S(2)}, u32[]{:S(2)}) collective-permute-start(bf16[528,512]{1,0:T(8,128)(2,1)} %get-tuple-element.60), channel_id=1, source_target_pairs={{0,4},{2,6},{4,0},{6,2},{1,5},{3,7},{5,1},{7,3},{8,12},{10,14},{12... | collective-permute-start | bytes 1622024 | tf_op jit(solution)/shard_map/ppermute | solution.py:357
  54.6 0.7 all-to-all-done.1.everyone
  55.3 2.2 %shard_map.130 = (bf16[64,32,128]{2,1,0:T(8,128)(2,1)}, f32[64,64]{1,0:T(8,128)}, f32[64,512]{1,0:T(8,128)S(1)}, f32[1,512]{1,0:T(1,128)S(1)}) custom-call(bf16[12,48,128]{2,1,0:T(8,128)(2,1)S(1)} %all-to-all-done.1.everyone, f32[64,512]{1,0:T(8,128)S(1)} %get-tuple-element.48.local, f32[64,512]{1,0:T(8,128)S(1)} %get-tuple-element.49.reads, ...), custom_call_target="tpu_custom_call" | custom-call | flops 1073741824 | bytes 8388608 | tf_op jit(solution)/shard_map/pallas_call | solution.py:335
  57.5 5.4 %all-to-all-start.2 = ((bf16[64,32,128]{2,1,0:T(8,128)(2,1)}), bf16[64,32,128]{2,1,0:T(8,128)(2,1)S(1)}, u32[]{:S(2)}, u32[]{:S(2)}) async-start(bf16[64,32,128]{2,1,0:T(8,128)(2,1)} %get-tuple-element.51), calls=%async_computation.2 | async-start | bytes 1048576 | tf_op jit(solution)/shard_map/all_to_all | solution.py:351
  62.9 0.0 copy-done.5
  62.9 2.1 %collective-permute-start.3 = (bf16[528,512]{1,0:T(8,128)(2,1)S(1)}, bf16[528,512]{1,0:T(8,128)(2,1)S(1)}, u32[]{:S(2)}, u32[]{:S(2)}) collective-permute-start(bf16[528,512]{1,0:T(8,128)(2,1)S(1)} %copy-done.5), channel_id=1, source_target_pairs={{0,1},{1,0},{2,3},{3,2},{4,5},{5,4},{6,7},{7,6},{8,9},{9,8},{10,11... | collective-permute-start | bytes 1622024 | tf_op jit(solution)/shard_map/ppermute | solution.py:363
  65.0 0.0 collective-permute-done.w1
  65.0 0.0 copy-start.6
  65.0 2.3 %collective-permute-start.4 = (bf16[528,512]{1,0:T(8,128)(2,1)S(1)}, bf16[528,512]{1,0:T(8,128)(2,1)S(1)}, u32[]{:S(2)}, u32[]{:S(2)}) collective-permute-start(bf16[528,512]{1,0:T(8,128)(2,1)S(1)} %collective-permute-done.w1), channel_id=1, source_target_pairs={{0,1},{1,0},{2,3},{3,2},{4,5},{5,4},{6,7},{7,6},{8,9},{9,8},{10,11... | collective-permute-start | bytes 1622024 | tf_op jit(solution)/shard_map/ppermute | solution.py:363
  67.3 0.0 collective-permute-done.1.w3
  67.3 2.1 %collective-permute-start.5 = (bf16[528,512]{1,0:T(8,128)(2,1)}, bf16[528,512]{1,0:T(8,128)(2,1)S(1)}, u32[]{:S(2)}, u32[]{:S(2)}) collective-permute-start(bf16[528,512]{1,0:T(8,128)(2,1)} %collective-permute-done.1.w3), channel_id=1, source_target_pairs={{0,1},{1,0},{2,3},{3,2},{4,5},{5,4},{6,7},{7,6},{8,9},{9,8},{10,11... | collective-permute-start | bytes 1622024 | tf_op jit(solution)/shard_map/ppermute | solution.py:363
  69.4 12.1 %collective-permute-done.2.w2 = bf16[528,512]{1,0:T(8,128)(2,1)} collective-permute-done((bf16[528,512]{1,0:T(8,128)(2,1)}, bf16[528,512]{1,0:T(8,128)(2,1)}, u32[]{:S(2)}, u32[]{:S(2)}) %collective-permute-start.2) | collective-permute-done | bytes 540704 | tf_op jit(solution)/shard_map/ppermute | solution.py:357
  81.4 1.9 %collective-permute-start.6 = (bf16[528,512]{1,0:T(8,128)(2,1)}, bf16[528,512]{1,0:T(8,128)(2,1)}, u32[]{:S(2)}, u32[]{:S(2)}) collective-permute-start(bf16[528,512]{1,0:T(8,128)(2,1)} %collective-permute-done.2.w2), channel_id=1, source_target_pairs={{0,1},{1,0},{2,3},{3,2},{4,5},{5,4},{6,7},{7,6},{8,9},{9,8},{10,11... | collective-permute-start | bytes 1622024 | tf_op jit(solution)/shard_map/ppermute | solution.py:363
  83.3 0.0 collective-permute-done.3.v0
  83.3 0.0 collective-permute-done.4.v1
  83.4 0.0 copy-start.7
  83.4 0.0 collective-permute-done.5.v3
  83.4 0.8 copy-done.7
  84.2 0.0 copy-start.8
  84.2 0.8 copy-done.8
  85.0 0.6 collective-permute-done.6.v2
  85.6 0.0 all-to-all-done.2.got
  85.6 0.0 copy-done.6
  85.6 4.7 %shard_map.132 = (bf16[64,32,128]{2,1,0:T(8,128)(2,1)}, bf16[2,32,128]{2,1,0:T(8,128)(2,1)}, bf16[2,32,128]{2,1,0:T(8,128)(2,1)}, bf16[2,32,128]{2,1,0:T(8,128)(2,1)}, bf16[2,32,128]{2,1,0:T(8,128)(2,1)}) custom-call(bf16[64,32,128]{2,1,0:T(8,128)(2,1)S(1)} %all-to-all-done.2.got, bf16[528,512]{1,0:T(8,128)(2,1)} %get-tuple-element.57.w0, ...), custom_call_target="tpu_custom_call" | custom-call | flops 1073741824 | bytes 8388608 | tf_op jit(solution)/shard_map/pallas_call | solution.py:335
  90.3 0.0 copy-start.10
  90.3 6.7 %all-to-all-start.3 = ((bf16[64,32,128]{2,1,0:T(8,128)(2,1)}), bf16[64,32,128]{2,1,0:T(8,128)(2,1)S(1)}, u32[]{:S(2)}, u32[]{:S(2)}) async-start(bf16[64,32,128]{2,1,0:T(8,128)(2,1)} %get-tuple-element.69), calls=%async_computation.3 | async-start | bytes 1048576 | tf_op jit(solution)/shard_map/all_to_all | solution.py:351
  97.0 0.0 copy-start
  97.0 0.0 copy-start.1
  97.1 3.5 %collective-permute-start.7 = (bf16[2,32,128]{2,1,0:T(8,128)(2,1)}, bf16[2,32,128]{2,1,0:T(8,128)(2,1)S(1)}, u32[]{:S(2)}, u32[]{:S(2)}) collective-permute-start(bf16[2,32,128]{2,1,0:T(8,128)(2,1)} %get-tuple-element.62), channel_id=1, source_target_pairs={{0,2},{2,4},{4,6},{6,0},{1,3},{3,5},{5,7},{7,1},{8,10},{10,12},{12... | collective-permute-start | bytes 49160 | tf_op jit(solution)/shard_map/ppermute | solution.py:357
  100.6 3.0 %collective-permute-start.8 = (bf16[2,32,128]{2,1,0:T(8,128)(2,1)}, bf16[2,32,128]{2,1,0:T(8,128)(2,1)S(1)}, u32[]{:S(2)}, u32[]{:S(2)}) collective-permute-start(bf16[2,32,128]{2,1,0:T(8,128)(2,1)} %get-tuple-element.63), channel_id=1, source_target_pairs={{0,4},{2,6},{4,0},{6,2},{1,5},{3,7},{5,1},{7,3},{8,12},{10,14},{12... | collective-permute-start | bytes 49160 | tf_op jit(solution)/shard_map/ppermute | solution.py:357
  103.5 4.1 %collective-permute-start.9 = (bf16[2,32,128]{2,1,0:T(8,128)(2,1)}, bf16[2,32,128]{2,1,0:T(8,128)(2,1)S(1)}, u32[]{:S(2)}, u32[]{:S(2)}) collective-permute-start(bf16[2,32,128]{2,1,0:T(8,128)(2,1)} %get-tuple-element.64), channel_id=1, source_target_pairs={{0,6},{2,0},{4,2},{6,4},{1,7},{3,1},{5,3},{7,5},{8,14},{10,8},{12,... | collective-permute-start | bytes 49160 | tf_op jit(solution)/shard_map/ppermute | solution.py:357
  107.6 7.0 %all-to-all-done.3.got = bf16[64,32,128]{2,1,0:T(8,128)(2,1)S(1)} async-done(((bf16[64,32,128]{2,1,0:T(8,128)(2,1)}), bf16[64,32,128]{2,1,0:T(8,128)(2,1)S(1)}, u32[]{:S(2)}, u32[]{:S(2)}) %all-to-all-start.3) | async-done | bytes 524320 | tf_op jit(solution)/shard_map/all_to_all | solution.py:351
  114.6 0.0 copy-done.2
  114.6 0.0 copy-done.4
  114.6 1.7 %shard_map.133 = (bf16[12,32,128]{2,1,0:T(8,128)(2,1)}, f32[64,512]{1,0:T(8,128)}) custom-call(bf16[64,32,128]{2,1,0:T(8,128)(2,1)S(1)} %all-to-all-done.3.got, f32[64,512]{1,0:T(8,128)S(1)} %get-tuple-element.70.unit, f32[1,512]{1,0:T(1,128)S(1)} %get-tuple-element.71.inverse, f32[1,64]{1,0:T(1,128)} %bitcast.39, f32[64,512]{1,0:T(8,128)S(1)} %get-tuple-element.49.reads, ...), custom_call_target="tpu_custom_call" | custom-call | flops 1073741824 | bytes 8388608 | tf_op jit(solution)/shard_map/pallas_call | solution.py:335
  116.3 0.0 copy-start.3
  116.3 9.2 %all-to-all-start.4 = ((bf16[12,32,128]{2,1,0:T(8,128)(2,1)}), bf16[12,32,128]{2,1,0:T(8,128)(2,1)S(1)}, u32[]{:S(2)}, u32[]{:S(2)}) async-start(bf16[12,32,128]{2,1,0:T(8,128)(2,1)} %get-tuple-element.75), calls=%async_computation.4 | async-start | bytes 196608 | tf_op jit(solution)/shard_map/all_to_all | solution.py:351
  125.6 0.0 collective-permute-done.7
  125.6 0.0 collective-permute-done.8
  125.6 0.0 collective-permute-done.9
  125.6 0.0 copy-done.10
  125.7 0.0 copy-start.9
  125.7 1.9 %collective-permute-start.10 = (bf16[4,2,32,128]{3,2,1,0:T(8,128)(2,1)S(1)}, bf16[4,2,32,128]{3,2,1,0:T(8,128)(2,1)S(1)}, u32[]{:S(2)}, u32[]{:S(2)}) collective-permute-start(bf16[4,2,32,128]{3,2,1,0:T(8,128)(2,1)S(1)} %pad_maximum_fusion.m_mine), channel_id=1, source_target_pairs={{0,1},{1,0},{2,3},{3,2},{4,5},{5,4},{6,7},{7,6},{8,9},{9,8},{10,11... | collective-permute-start | bytes 196616 | tf_op jit(solution)/shard_map/ppermute | solution.py:363
  127.6 1.2 collective-permute-done.10.m_other
  128.8 0.0 copy-start.11
  128.8 0.0 copy-done.9
  128.8 0.6 copy-done.11
  129.4 2.7 %shard_map.134 = (bf16[64,512]{1,0:T(8,128)(2,1)}, bf16[64,512]{1,0:T(8,128)(2,1)}, f32[64,512]{1,0:T(8,128)S(1)}, f32[64,512]{1,0:T(8,128)S(1)}) custom-call(bf16[4,2,32,128]{3,2,1,0:T(8,128)(2,1)} %copy-done.9, bf16[4,2,32,128]{3,2,1,0:T(8,128)(2,1)} %copy-done.11, f32[64,512]{1,0:T(8,128)} %copy-done.4, f32[64,512]{1,0:T(8,128)} %get-tuple-element.65.keys_raw, ...), custom_call_target="tpu_custom_call" | custom-call | flops 1073741824 | bytes 8388608 | tf_op jit(solution)/shard_map/pallas_call | solution.py:335
  132.1 5.6 %all-to-all-done.4.later = bf16[12,32,128]{2,1,0:T(8,128)(2,1)S(1)} async-done(((bf16[12,32,128]{2,1,0:T(8,128)(2,1)}), bf16[12,32,128]{2,1,0:T(8,128)(2,1)S(1)}, u32[]{:S(2)}, u32[]{:S(2)}) %all-to-all-start.4) | async-done | bytes 98336 | tf_op jit(solution)/shard_map/all_to_all | solution.py:351
  137.7 0.0 copy-done
  137.7 0.0 copy-done.1
  137.7 0.0 copy-done.3
  137.7 1.7 %shard_map.135 = (bf16[64,512]{1,0:T(8,128)(2,1)}, bf16[64,512]{1,0:T(8,128)(2,1)}) custom-call(bf16[12,32,128]{2,1,0:T(8,128)(2,1)S(1)} %all-to-all-done.4.later, bf16[12,48,128]{2,1,0:T(8,128)(2,1)S(1)} %all-to-all-done.1.everyone, f32[64,512]{1,0:T(8,128)S(1)} %get-tuple-element.76.part_keys, f32[64,512]{1,0:T(8,128)S(1)} %get-tuple-element.77.part_values, ...), custom_call_target="tpu_custom_call" | custom-call | flops 1073741824 | bytes 8388608 | tf_op jit(solution)/shard_map/pallas_call | solution.py:335
  (1 shorter events, 0.0 us)
Async XLA Ops:
  2.5 24.6 %all-to-all-start = ((bf16[8,64,512]{2,1,0:T(8,128)(2,1)}), bf16[8,64,512]{2,1,0:T(8,128)(2,1)S(1)}, u32[]{:S(2)}, u32[]{:S(2)}) async-start(bf16[8,64,512]{2,1,0:T(8,128)(2,1)} %bitcast.22), calls=%async_computation | async-start | bytes 1048576 | tf_op jit(solution)/shard_map/all_to_all | solution.py:351
  16.1 98.5 %copy-start.2 = (f32[64,512]{1,0:T(8,128)}, f32[64,512]{1,0:T(8,128)S(1)}, u32[]{:S(2)}) copy-start(f32[64,512]{1,0:T(8,128)S(1)} %get-tuple-element.50.logs) | copy-start | bytes 393220
  16.1 98.5 %copy-start.4 = (f32[64,512]{1,0:T(8,128)}, f32[64,512]{1,0:T(8,128)S(1)}, u32[]{:S(2)}) copy-start(f32[64,512]{1,0:T(8,128)S(1)} %get-tuple-element.49.reads) | copy-start | bytes 393220
  27.1 28.2 %all-to-all-start.1 = ((bf16[12,48,128]{2,1,0:T(8,128)(2,1)}), bf16[12,48,128]{2,1,0:T(8,128)(2,1)S(1)}, u32[]{:S(2)}, u32[]{:S(2)}) async-start(bf16[12,48,128]{2,1,0:T(8,128)(2,1)} %get-tuple-element.47), calls=%async_computation.1 | async-start | bytes 294912 | tf_op jit(solution)/shard_map/all_to_all | solution.py:351
  44.6 18.4 %copy-start.5 = (bf16[528,512]{1,0:T(8,128)(2,1)S(1)}, bf16[528,512]{1,0:T(8,128)(2,1)}, u32[]{:S(2)}) copy-start(bf16[528,512]{1,0:T(8,128)(2,1)} %get-tuple-element.57.w0) | copy-start | bytes 1622020
  44.6 20.4 %collective-permute-start = (bf16[528,512]{1,0:T(8,128)(2,1)}, bf16[528,512]{1,0:T(8,128)(2,1)S(1)}, u32[]{:S(2)}, u32[]{:S(2)}) collective-permute-start(bf16[528,512]{1,0:T(8,128)(2,1)} %get-tuple-element.58), channel_id=1, source_target_pairs={{0,2},{2,4},{4,6},{6,0},{1,3},{3,5},{5,7},{7,1},{8,10},{10,12},{12... | collective-permute-start | bytes 1622024 | tf_op jit(solution)/shard_map/ppermute | solution.py:357
  48.1 19.2 %collective-permute-start.1 = (bf16[528,512]{1,0:T(8,128)(2,1)}, bf16[528,512]{1,0:T(8,128)(2,1)}, u32[]{:S(2)}, u32[]{:S(2)}) collective-permute-start(bf16[528,512]{1,0:T(8,128)(2,1)} %get-tuple-element.59), channel_id=1, source_target_pairs={{0,6},{2,0},{4,2},{6,4},{1,7},{3,1},{5,3},{7,5},{8,14},{10,8},{12,... | collective-permute-start | bytes 1622024 | tf_op jit(solution)/shard_map/ppermute | solution.py:357
  50.5 30.9 %collective-permute-start.2 = (bf16[528,512]{1,0:T(8,128)(2,1)}, bf16[528,512]{1,0:T(8,128)(2,1)}, u32[]{:S(2)}, u32[]{:S(2)}) collective-permute-start(bf16[528,512]{1,0:T(8,128)(2,1)} %get-tuple-element.60), channel_id=1, source_target_pairs={{0,4},{2,6},{4,0},{6,2},{1,5},{3,7},{5,1},{7,3},{8,12},{10,14},{12... | collective-permute-start | bytes 1622024 | tf_op jit(solution)/shard_map/ppermute | solution.py:357
  57.5 28.1 %all-to-all-start.2 = ((bf16[64,32,128]{2,1,0:T(8,128)(2,1)}), bf16[64,32,128]{2,1,0:T(8,128)(2,1)S(1)}, u32[]{:S(2)}, u32[]{:S(2)}) async-start(bf16[64,32,128]{2,1,0:T(8,128)(2,1)} %get-tuple-element.51), calls=%async_computation.2 | async-start | bytes 1048576 | tf_op jit(solution)/shard_map/all_to_all | solution.py:351
  62.9 20.4 %collective-permute-start.3 = (bf16[528,512]{1,0:T(8,128)(2,1)S(1)}, bf16[528,512]{1,0:T(8,128)(2,1)S(1)}, u32[]{:S(2)}, u32[]{:S(2)}) collective-permute-start(bf16[528,512]{1,0:T(8,128)(2,1)S(1)} %copy-done.5), channel_id=1, source_target_pairs={{0,1},{1,0},{2,3},{3,2},{4,5},{5,4},{6,7},{7,6},{8,9},{9,8},{10,11... | collective-permute-start | bytes 1622024 | tf_op jit(solution)/shard_map/ppermute | solution.py:363
  65.0 20.6 %copy-start.6 = (bf16[528,512]{1,0:T(8,128)(2,1)}, bf16[528,512]{1,0:T(8,128)(2,1)S(1)}, u32[]{:S(2)}) copy-start(bf16[528,512]{1,0:T(8,128)(2,1)S(1)} %collective-permute-done.w1) | copy-start | bytes 1622020
  65.0 18.3 %collective-permute-start.4 = (bf16[528,512]{1,0:T(8,128)(2,1)S(1)}, bf16[528,512]{1,0:T(8,128)(2,1)S(1)}, u32[]{:S(2)}, u32[]{:S(2)}) collective-permute-start(bf16[528,512]{1,0:T(8,128)(2,1)S(1)} %collective-permute-done.w1), channel_id=1, source_target_pairs={{0,1},{1,0},{2,3},{3,2},{4,5},{5,4},{6,7},{7,6},{8,9},{9,8},{10,11... | collective-permute-start | bytes 1622024 | tf_op jit(solution)/shard_map/ppermute | solution.py:363
  67.3 16.1 %collective-permute-start.5 = (bf16[528,512]{1,0:T(8,128)(2,1)}, bf16[528,512]{1,0:T(8,128)(2,1)S(1)}, u32[]{:S(2)}, u32[]{:S(2)}) collective-permute-start(bf16[528,512]{1,0:T(8,128)(2,1)} %collective-permute-done.1.w3), channel_id=1, source_target_pairs={{0,1},{1,0},{2,3},{3,2},{4,5},{5,4},{6,7},{7,6},{8,9},{9,8},{10,11... | collective-permute-start | bytes 1622024 | tf_op jit(solution)/shard_map/ppermute | solution.py:363
  81.4 4.2 %collective-permute-start.6 = (bf16[528,512]{1,0:T(8,128)(2,1)}, bf16[528,512]{1,0:T(8,128)(2,1)}, u32[]{:S(2)}, u32[]{:S(2)}) collective-permute-start(bf16[528,512]{1,0:T(8,128)(2,1)} %collective-permute-done.2.w2), channel_id=1, source_target_pairs={{0,1},{1,0},{2,3},{3,2},{4,5},{5,4},{6,7},{7,6},{8,9},{9,8},{10,11... | collective-permute-start | bytes 1622024 | tf_op jit(solution)/shard_map/ppermute | solution.py:363
  83.4 0.8 copy-start.7
  84.2 0.8 copy-start.8
  90.3 35.3 %copy-start.10 = (bf16[2,32,128]{2,1,0:T(8,128)(2,1)S(1)}, bf16[2,32,128]{2,1,0:T(8,128)(2,1)}, u32[]{:S(2)}) copy-start(bf16[2,32,128]{2,1,0:T(8,128)(2,1)} %get-tuple-element.61) | copy-start | bytes 49156
  90.3 24.2 %all-to-all-start.3 = ((bf16[64,32,128]{2,1,0:T(8,128)(2,1)}), bf16[64,32,128]{2,1,0:T(8,128)(2,1)S(1)}, u32[]{:S(2)}, u32[]{:S(2)}) async-start(bf16[64,32,128]{2,1,0:T(8,128)(2,1)} %get-tuple-element.69), calls=%async_computation.3 | async-start | bytes 1048576 | tf_op jit(solution)/shard_map/all_to_all | solution.py:351
  97.0 40.6 %copy-start = (f32[64,512]{1,0:T(8,128)S(1)}, f32[64,512]{1,0:T(8,128)}, u32[]{:S(2)}) copy-start(f32[64,512]{1,0:T(8,128)} %get-tuple-element.65.keys_raw) | copy-start | bytes 393220
  97.0 40.6 %copy-start.1 = (f32[64,512]{1,0:T(8,128)S(1)}, f32[64,512]{1,0:T(8,128)}, u32[]{:S(2)}) copy-start(f32[64,512]{1,0:T(8,128)} %get-tuple-element.66.values) | copy-start | bytes 393220
  97.1 28.5 %collective-permute-start.7 = (bf16[2,32,128]{2,1,0:T(8,128)(2,1)}, bf16[2,32,128]{2,1,0:T(8,128)(2,1)S(1)}, u32[]{:S(2)}, u32[]{:S(2)}) collective-permute-start(bf16[2,32,128]{2,1,0:T(8,128)(2,1)} %get-tuple-element.62), channel_id=1, source_target_pairs={{0,2},{2,4},{4,6},{6,0},{1,3},{3,5},{5,7},{7,1},{8,10},{10,12},{12... | collective-permute-start | bytes 49160 | tf_op jit(solution)/shard_map/ppermute | solution.py:357
  100.6 25.0 %collective-permute-start.8 = (bf16[2,32,128]{2,1,0:T(8,128)(2,1)}, bf16[2,32,128]{2,1,0:T(8,128)(2,1)S(1)}, u32[]{:S(2)}, u32[]{:S(2)}) collective-permute-start(bf16[2,32,128]{2,1,0:T(8,128)(2,1)} %get-tuple-element.63), channel_id=1, source_target_pairs={{0,4},{2,6},{4,0},{6,2},{1,5},{3,7},{5,1},{7,3},{8,12},{10,14},{12... | collective-permute-start | bytes 49160 | tf_op jit(solution)/shard_map/ppermute | solution.py:357
  103.5 22.1 %collective-permute-start.9 = (bf16[2,32,128]{2,1,0:T(8,128)(2,1)}, bf16[2,32,128]{2,1,0:T(8,128)(2,1)S(1)}, u32[]{:S(2)}, u32[]{:S(2)}) collective-permute-start(bf16[2,32,128]{2,1,0:T(8,128)(2,1)} %get-tuple-element.64), channel_id=1, source_target_pairs={{0,6},{2,0},{4,2},{6,4},{1,7},{3,1},{5,3},{7,5},{8,14},{10,8},{12,... | collective-permute-start | bytes 49160 | tf_op jit(solution)/shard_map/ppermute | solution.py:357
  116.3 21.3 %copy-start.3 = (f32[64,512]{1,0:T(8,128)S(1)}, f32[64,512]{1,0:T(8,128)}, u32[]{:S(2)}) copy-start(f32[64,512]{1,0:T(8,128)} %copy-done.2) | copy-start | bytes 393220
  116.3 21.3 %all-to-all-start.4 = ((bf16[12,32,128]{2,1,0:T(8,128)(2,1)}), bf16[12,32,128]{2,1,0:T(8,128)(2,1)S(1)}, u32[]{:S(2)}, u32[]{:S(2)}) async-start(bf16[12,32,128]{2,1,0:T(8,128)(2,1)} %get-tuple-element.75), calls=%async_computation.4 | async-start | bytes 196608 | tf_op jit(solution)/shard_map/all_to_all | solution.py:351
  125.7 3.2 %copy-start.9 = (bf16[4,2,32,128]{3,2,1,0:T(8,128)(2,1)}, bf16[4,2,32,128]{3,2,1,0:T(8,128)(2,1)S(1)}, u32[]{:S(2)}) copy-start(bf16[4,2,32,128]{3,2,1,0:T(8,128)(2,1)S(1)} %pad_maximum_fusion.m_mine) | copy-start | bytes 196612
  125.7 3.1 %collective-permute-start.10 = (bf16[4,2,32,128]{3,2,1,0:T(8,128)(2,1)S(1)}, bf16[4,2,32,128]{3,2,1,0:T(8,128)(2,1)S(1)}, u32[]{:S(2)}, u32[]{:S(2)}) collective-permute-start(bf16[4,2,32,128]{3,2,1,0:T(8,128)(2,1)S(1)} %pad_maximum_fusion.m_mine), channel_id=1, source_target_pairs={{0,1},{1,0},{2,3},{3,2},{4,5},{5,4},{6,7},{7,6},{8,9},{9,8},{10,11... | collective-permute-start | bytes 196616 | tf_op jit(solution)/shard_map/ppermute | solution.py:363
  128.8 0.6 copy-start.11

commit v8 on v7

--- a/solution.py
+++ b/solution.py
@@ -211,7 +211,7 @@
     return jnp.where(core == c, mine[step, core], other[step, core])
 
 
-def middle_kernel(got, w0, w1, w3, w2, v0, v1, v3, v2, sent, m0, m1, m2, m3, held, weights, sems):
+def middle_kernel(got, w0, w3, w2, w1, v0, v3, v2, v1, sent, m0, m1, m2, m3, held, weights, sems):
     copies = []
     for n, source in enumerate((w0, v0, w1, v1, w2, v2, w3, v3)):
         copies.append(pltpu.make_async_copy(source, weights.at[n], sems.at[n]))
@@ -221,7 +221,7 @@
     rows = GRID["y"]
     group = min(4, rows)
     chunks = []
-    for s in (0, 1, 3, 2):
+    for s in (0, 3, 2, 1):
         x = lax.rem(at - s + GRID["x"], GRID["x"])
         for n, c in ((2 * s, core), (2 * s + 1, 1 - core)):
             for y in range(0, rows, group):
@@ -354,7 +354,7 @@
 def along_x(parts):
     n = GRID["x"]
     came = {
-        s: lax.ppermute(parts[s], "x", [(i, (i + s) % n) for i in range(n)]) for s in (1, 3, 2)
+        s: lax.ppermute(parts[s], "x", [(i, (i + s) % n) for i in range(n)]) for s in (3, 2, 1)
     }
     return [parts[0], came[1], came[2], came[3]]
 
@@ -436,9 +436,9 @@
         here=(2, 3),
     )
     got = exchange(sent, head)
-    other = {s: swap(w_mine[s]) for s in (0, 1, 3, 2)}
-    w_other = [other[s] for s in (0, 1, 3, 2)]
-    w_mine = [w_mine[s] for s in (0, 1, 3, 2)]
+    other = {s: swap(w_mine[s]) for s in (0, 3, 2, 1)}
+    w_other = [other[s] for s in (0, 3, 2, 1)]
+    w_mine = [w_mine[s] for s in (0, 3, 2, 1)]
     sent, *mixed = call(
         middle_kernel,
         [((rows * tiles,) + block, bf16)] + [((2,) + block, bf16)] * GRID["x"],

time: 141 us -> 141 us (level)
  transfers between devices with their start and end apart: 16 -> 16, of which waited for: 7 -> 8; matrix products, arithmetic and copies ran while one was open for 0% -> 0% of each run, Pallas kernels for 11% -> 11%
where the time goes in v8:
time: 141 us; the launch traced here: 140 us
  starting transfers between devices  75.4 us (53%)
  waiting for transfers between devices  37.7 us (27%)
  Pallas kernels  22.1 us (16%)
  local copies, waits for them, and re-layouts  4.16 us (3%)
    all_to_all x5, starting transfers between devices, exchange(): return lax.all_to_all(array, axis, 0, 0)  44.1 us
    all_to_all x5, waiting for transfers between devices, exchange(): return lax.all_to_all(array, axis, 0, 0)  23.7 us
    pallas_call x7, Pallas kernels, call(): pl.pallas_call(kernel, cost_estimate=pl.CostEstimate(flops=1 << 30, trans...  22.1 us
    ppermute x6, starting transfers between devices, along_x(): lax.ppermute(parts[s], 'x', [(i, (i + s) % n) for i in range(n)])  21.2 us
    ppermute x6, waiting for transfers between devices, along_x(): lax.ppermute(parts[s], 'x', [(i, (i + s) % n) for i in range(n)])  12.2 us
    ppermute x5, starting transfers between devices, swap(): return lax.ppermute(array, 'core', [(0, 1), (1, 0)])  10.1 us
  transfers between devices with their start and end apart: 16, of which 8 were waited for; matrix products, arithmetic and copies ran while one was open for 0% of the time, Pallas kernels for 11%

profile of v8, /device:TPU:2, one launch (start us, length us, event | category | flops | bytes accessed | tf_op | source)
XLA Modules:
  0.0 140.2 jit_solution(16208894838824611806)
XLA Ops:
  0.6 1.9 %copy.17 = bf16[8,8,8,512]{3,2,0,1:T(8,128)(2,1)} copy(bf16[8,8,8,512]{3,2,1,0:T(8,128)(2,1)} %bitcast.26) | data formatting | bytes 1048576 | tf_op jit(solution)/shard_map/reshape | solution.py:391
  2.5 7.1 %all-to-all-start = ((bf16[8,64,512]{2,1,0:T(8,128)(2,1)}), bf16[8,64,512]{2,1,0:T(8,128)(2,1)S(1)}, u32[]{:S(2)}, u32[]{:S(2)}) async-start(bf16[8,64,512]{2,1,0:T(8,128)(2,1)} %bitcast.22), calls=%async_computation | async-start | bytes 1048576 | tf_op jit(solution)/shard_map/all_to_all | solution.py:351
  9.6 6.5 %shard_map.129 = (bf16[12,48,128]{2,1,0:T(8,128)(2,1)}, f32[64,512]{1,0:T(8,128)S(1)}, f32[64,512]{1,0:T(8,128)}, f32[64,512]{1,0:T(8,128)}, f32[64,512]{1,0:T(8...) custom-call(bf16[512,4096]{1,0:T(8,128)(2,1)} %x.1, ...), custom_call_target="tpu_custom_call" | custom-call | flops 1073741824 | bytes 8388608 | tf_op jit(solution)/shard_map/pallas_call | solution.py:335
  16.1 0.0 copy-start.2
  16.1 0.0 copy-start.4
  16.1 11.0 %all-to-all-done.columns = bf16[8,64,512]{2,1,0:T(8,128)(2,1)S(1)} async-done(((bf16[8,64,512]{2,1,0:T(8,128)(2,1)}), bf16[8,64,512]{2,1,0:T(8,128)(2,1)S(1)}, u32[]{:S(2)}, u32[]{:S(2)}) %all-to-all-start) | async-done | bytes 524320 | tf_op jit(solution)/shard_map/all_to_all | solution.py:351
  27.1 15.2 %all-to-all-start.1 = ((bf16[12,48,128]{2,1,0:T(8,128)(2,1)}), bf16[12,48,128]{2,1,0:T(8,128)(2,1)S(1)}, u32[]{:S(2)}, u32[]{:S(2)}) async-start(bf16[12,48,128]{2,1,0:T(8,128)(2,1)} %get-tuple-element.47), calls=%async_computation.1 | async-start | bytes 294912 | tf_op jit(solution)/shard_map/all_to_all | solution.py:351
  42.3 2.2 %shard_map.131 = (bf16[528,512]{1,0:T(8,128)(2,1)}, bf16[528,512]{1,0:T(8,128)(2,1)}, bf16[528,512]{1,0:T(8,128)(2,1)}, bf16[528,512]{1,0:T(8,128)(2,1)}) custom-call(bf16[8,64,512]{2,1,0:T(8,128)(2,1)S(1)} %all-to-all-done.columns, bf16[16,512]{1,0:T(8,128)(2,1)} %get-tuple-element.53.t0, bf16[16,512]{1,0:T(8,128)(2,1)} %get-tuple-element.54.t1, ...), custom_call_target="tpu_custom_call" | custom-call | flops 1073741824 | bytes 8388608 | tf_op jit(solution)/shard_map/pallas_call | solution.py:335
  44.5 0.0 copy-start.5
  44.5 2.6 %collective-permute-start = (bf16[528,512]{1,0:T(8,128)(2,1)}, bf16[528,512]{1,0:T(8,128)(2,1)S(1)}, u32[]{:S(2)}, u32[]{:S(2)}) collective-permute-start(bf16[528,512]{1,0:T(8,128)(2,1)} %get-tuple-element.58), channel_id=1, source_target_pairs={{0,6},{2,0},{4,2},{6,4},{1,7},{3,1},{5,3},{7,5},{8,14},{10,8},{12,... | collective-permute-start | bytes 1622024 | tf_op jit(solution)/shard_map/ppermute | solution.py:357
  47.1 4.3 %collective-permute-start.1 = (bf16[528,512]{1,0:T(8,128)(2,1)}, bf16[528,512]{1,0:T(8,128)(2,1)}, u32[]{:S(2)}, u32[]{:S(2)}) collective-permute-start(bf16[528,512]{1,0:T(8,128)(2,1)} %get-tuple-element.59), channel_id=1, source_target_pairs={{0,4},{2,6},{4,0},{6,2},{1,5},{3,7},{5,1},{7,3},{8,12},{10,14},{12... | collective-permute-start | bytes 1622024 | tf_op jit(solution)/shard_map/ppermute | solution.py:357
  51.4 3.7 %collective-permute-start.2 = (bf16[528,512]{1,0:T(8,128)(2,1)}, bf16[528,512]{1,0:T(8,128)(2,1)}, u32[]{:S(2)}, u32[]{:S(2)}) collective-permute-start(bf16[528,512]{1,0:T(8,128)(2,1)} %get-tuple-element.60), channel_id=1, source_target_pairs={{0,2},{2,4},{4,6},{6,0},{1,3},{3,5},{5,7},{7,1},{8,10},{10,12},{12... | collective-permute-start | bytes 1622024 | tf_op jit(solution)/shard_map/ppermute | solution.py:357
  55.1 0.1 all-to-all-done.1.everyone
  55.3 2.2 %shard_map.130 = (bf16[64,32,128]{2,1,0:T(8,128)(2,1)}, f32[64,64]{1,0:T(8,128)}, f32[64,512]{1,0:T(8,128)S(1)}, f32[1,512]{1,0:T(1,128)S(1)}) custom-call(bf16[12,48,128]{2,1,0:T(8,128)(2,1)S(1)} %all-to-all-done.1.everyone, f32[64,512]{1,0:T(8,128)S(1)} %get-tuple-element.48.local, f32[64,512]{1,0:T(8,128)S(1)} %get-tuple-element.49.reads, ...), custom_call_target="tpu_custom_call" | custom-call | flops 1073741824 | bytes 8388608 | tf_op jit(solution)/shard_map/pallas_call | solution.py:335
  57.5 5.4 %all-to-all-start.2 = ((bf16[64,32,128]{2,1,0:T(8,128)(2,1)}), bf16[64,32,128]{2,1,0:T(8,128)(2,1)S(1)}, u32[]{:S(2)}, u32[]{:S(2)}) async-start(bf16[64,32,128]{2,1,0:T(8,128)(2,1)} %get-tuple-element.51), calls=%async_computation.2 | async-start | bytes 1048576 | tf_op jit(solution)/shard_map/all_to_all | solution.py:351
  62.9 0.0 copy-done.5
  62.9 2.1 %collective-permute-start.3 = (bf16[528,512]{1,0:T(8,128)(2,1)S(1)}, bf16[528,512]{1,0:T(8,128)(2,1)S(1)}, u32[]{:S(2)}, u32[]{:S(2)}) collective-permute-start(bf16[528,512]{1,0:T(8,128)(2,1)S(1)} %copy-done.5), channel_id=1, source_target_pairs={{0,1},{1,0},{2,3},{3,2},{4,5},{5,4},{6,7},{7,6},{8,9},{9,8},{10,11... | collective-permute-start | bytes 1622024 | tf_op jit(solution)/shard_map/ppermute | solution.py:363
  65.0 0.0 collective-permute-done.w3
  65.0 0.0 copy-start.6
  65.0 2.3 %collective-permute-start.4 = (bf16[528,512]{1,0:T(8,128)(2,1)S(1)}, bf16[528,512]{1,0:T(8,128)(2,1)S(1)}, u32[]{:S(2)}, u32[]{:S(2)}) collective-permute-start(bf16[528,512]{1,0:T(8,128)(2,1)S(1)} %collective-permute-done.w3), channel_id=1, source_target_pairs={{0,1},{1,0},{2,3},{3,2},{4,5},{5,4},{6,7},{7,6},{8,9},{9,8},{10,11... | collective-permute-start | bytes 1622024 | tf_op jit(solution)/shard_map/ppermute | solution.py:363
  67.3 11.0 %collective-permute-done.1.w2 = bf16[528,512]{1,0:T(8,128)(2,1)} collective-permute-done((bf16[528,512]{1,0:T(8,128)(2,1)}, bf16[528,512]{1,0:T(8,128)(2,1)}, u32[]{:S(2)}, u32[]{:S(2)}) %collective-permute-start.1) | collective-permute-done | bytes 540704 | tf_op jit(solution)/shard_map/ppermute | solution.py:357
  78.3 1.9 %collective-permute-start.5 = (bf16[528,512]{1,0:T(8,128)(2,1)}, bf16[528,512]{1,0:T(8,128)(2,1)S(1)}, u32[]{:S(2)}, u32[]{:S(2)}) collective-permute-start(bf16[528,512]{1,0:T(8,128)(2,1)} %collective-permute-done.1.w2), channel_id=1, source_target_pairs={{0,1},{1,0},{2,3},{3,2},{4,5},{5,4},{6,7},{7,6},{8,9},{9,8},{10,11... | collective-permute-start | bytes 1622024 | tf_op jit(solution)/shard_map/ppermute | solution.py:363
  80.2 1.2 collective-permute-done.2.w1
  81.4 1.9 %collective-permute-start.6 = (bf16[528,512]{1,0:T(8,128)(2,1)}, bf16[528,512]{1,0:T(8,128)(2,1)}, u32[]{:S(2)}, u32[]{:S(2)}) collective-permute-start(bf16[528,512]{1,0:T(8,128)(2,1)} %collective-permute-done.2.w1), channel_id=1, source_target_pairs={{0,1},{1,0},{2,3},{3,2},{4,5},{5,4},{6,7},{7,6},{8,9},{9,8},{10,11... | collective-permute-start | bytes 1622024 | tf_op jit(solution)/shard_map/ppermute | solution.py:363
  83.3 0.0 collective-permute-done.3.v0
  83.3 0.0 collective-permute-done.4.v3
  83.3 0.0 copy-start.7
  83.3 0.0 collective-permute-done.5.v2
  83.3 0.8 copy-done.7
  84.1 0.0 copy-start.8
  84.1 0.8 copy-done.8
  84.9 0.6 collective-permute-done.6.v1
  85.5 0.0 all-to-all-done.2.got
  85.5 0.0 copy-done.6
  85.5 5.0 %shard_map.132 = (bf16[64,32,128]{2,1,0:T(8,128)(2,1)}, bf16[2,32,128]{2,1,0:T(8,128)(2,1)}, bf16[2,32,128]{2,1,0:T(8,128)(2,1)}, bf16[2,32,128]{2,1,0:T(8,128)(2,1)}, bf16[2,32,128]{2,1,0:T(8,128)(2,1)}) custom-call(bf16[64,32,128]{2,1,0:T(8,128)(2,1)S(1)} %all-to-all-done.2.got, bf16[528,512]{1,0:T(8,128)(2,1)} %get-tuple-element.57.w0, ...), custom_call_target="tpu_custom_call" | custom-call | flops 1073741824 | bytes 8388608 | tf_op jit(solution)/shard_map/pallas_call | solution.py:335
  90.6 0.0 copy-start.10
  90.6 7.0 %all-to-all-start.3 = ((bf16[64,32,128]{2,1,0:T(8,128)(2,1)}), bf16[64,32,128]{2,1,0:T(8,128)(2,1)S(1)}, u32[]{:S(2)}, u32[]{:S(2)}) async-start(bf16[64,32,128]{2,1,0:T(8,128)(2,1)} %get-tuple-element.69), calls=%async_computation.3 | async-start | bytes 1048576 | tf_op jit(solution)/shard_map/all_to_all | solution.py:351
  97.6 0.0 copy-start
  97.6 0.0 copy-start.1
  97.6 3.5 %collective-permute-start.7 = (bf16[2,32,128]{2,1,0:T(8,128)(2,1)}, bf16[2,32,128]{2,1,0:T(8,128)(2,1)S(1)}, u32[]{:S(2)}, u32[]{:S(2)}) collective-permute-start(bf16[2,32,128]{2,1,0:T(8,128)(2,1)} %get-tuple-element.62), channel_id=1, source_target_pairs={{0,2},{2,4},{4,6},{6,0},{1,3},{3,5},{5,7},{7,1},{8,10},{10,12},{12... | collective-permute-start | bytes 49160 | tf_op jit(solution)/shard_map/ppermute | solution.py:357
  101.2 3.0 %collective-permute-start.8 = (bf16[2,32,128]{2,1,0:T(8,128)(2,1)}, bf16[2,32,128]{2,1,0:T(8,128)(2,1)S(1)}, u32[]{:S(2)}, u32[]{:S(2)}) collective-permute-start(bf16[2,32,128]{2,1,0:T(8,128)(2,1)} %get-tuple-element.63), channel_id=1, source_target_pairs={{0,4},{2,6},{4,0},{6,2},{1,5},{3,7},{5,1},{7,3},{8,12},{10,14},{12... | collective-permute-start | bytes 49160 | tf_op jit(solution)/shard_map/ppermute | solution.py:357
  104.1 4.1 %collective-permute-start.9 = (bf16[2,32,128]{2,1,0:T(8,128)(2,1)}, bf16[2,32,128]{2,1,0:T(8,128)(2,1)S(1)}, u32[]{:S(2)}, u32[]{:S(2)}) collective-permute-start(bf16[2,32,128]{2,1,0:T(8,128)(2,1)} %get-tuple-element.64), channel_id=1, source_target_pairs={{0,6},{2,0},{4,2},{6,4},{1,7},{3,1},{5,3},{7,5},{8,14},{10,8},{12,... | collective-permute-start | bytes 49160 | tf_op jit(solution)/shard_map/ppermute | solution.py:357
  108.2 7.0 %all-to-all-done.3.got = bf16[64,32,128]{2,1,0:T(8,128)(2,1)S(1)} async-done(((bf16[64,32,128]{2,1,0:T(8,128)(2,1)}), bf16[64,32,128]{2,1,0:T(8,128)(2,1)S(1)}, u32[]{:S(2)}, u32[]{:S(2)}) %all-to-all-start.3) | async-done | bytes 524320 | tf_op jit(solution)/shard_map/all_to_all | solution.py:351
  115.2 0.0 copy-done.2
  115.2 0.0 copy-done.4
  115.2 1.7 %shard_map.133 = (bf16[12,32,128]{2,1,0:T(8,128)(2,1)}, f32[64,512]{1,0:T(8,128)}) custom-call(bf16[64,32,128]{2,1,0:T(8,128)(2,1)S(1)} %all-to-all-done.3.got, f32[64,512]{1,0:T(8,128)S(1)} %get-tuple-element.70.unit, f32[1,512]{1,0:T(1,128)S(1)} %get-tuple-element.71.inverse, f32[1,64]{1,0:T(1,128)} %bitcast.39, f32[64,512]{1,0:T(8,128)S(1)} %get-tuple-element.49.reads, ...), custom_call_target="tpu_custom_call" | custom-call | flops 1073741824 | bytes 8388608 | tf_op jit(solution)/shard_map/pallas_call | solution.py:335
  116.9 0.0 copy-start.3
  116.9 9.5 %all-to-all-start.4 = ((bf16[12,32,128]{2,1,0:T(8,128)(2,1)}), bf16[12,32,128]{2,1,0:T(8,128)(2,1)S(1)}, u32[]{:S(2)}, u32[]{:S(2)}) async-start(bf16[12,32,128]{2,1,0:T(8,128)(2,1)} %get-tuple-element.75), calls=%async_computation.4 | async-start | bytes 196608 | tf_op jit(solution)/shard_map/all_to_all | solution.py:351
  126.4 0.0 collective-permute-done.7
  126.4 0.0 collective-permute-done.8
  126.4 0.0 collective-permute-done.9
  126.4 0.0 copy-done.10
  126.5 0.0 copy-start.9
  126.5 1.9 %collective-permute-start.10 = (bf16[4,2,32,128]{3,2,1,0:T(8,128)(2,1)S(1)}, bf16[4,2,32,128]{3,2,1,0:T(8,128)(2,1)S(1)}, u32[]{:S(2)}, u32[]{:S(2)}) collective-permute-start(bf16[4,2,32,128]{3,2,1,0:T(8,128)(2,1)S(1)} %pad_maximum_fusion.m_mine), channel_id=1, source_target_pairs={{0,1},{1,0},{2,3},{3,2},{4,5},{5,4},{6,7},{7,6},{8,9},{9,8},{10,11... | collective-permute-start | bytes 196616 | tf_op jit(solution)/shard_map/ppermute | solution.py:363
  128.4 1.2 collective-permute-done.10.m_other
  129.6 0.0 copy-start.11
  129.6 0.0 copy-done.9
  129.6 0.6 copy-done.11
  130.2 2.7 %shard_map.134 = (bf16[64,512]{1,0:T(8,128)(2,1)}, bf16[64,512]{1,0:T(8,128)(2,1)}, f32[64,512]{1,0:T(8,128)S(1)}, f32[64,512]{1,0:T(8,128)S(1)}) custom-call(bf16[4,2,32,128]{3,2,1,0:T(8,128)(2,1)} %copy-done.9, bf16[4,2,32,128]{3,2,1,0:T(8,128)(2,1)} %copy-done.11, f32[64,512]{1,0:T(8,128)} %copy-done.4, f32[64,512]{1,0:T(8,128)} %get-tuple-element.65.keys_raw, ...), custom_call_target="tpu_custom_call" | custom-call | flops 1073741824 | bytes 8388608 | tf_op jit(solution)/shard_map/pallas_call | solution.py:335
  132.9 5.6 %all-to-all-done.4.later = bf16[12,32,128]{2,1,0:T(8,128)(2,1)S(1)} async-done(((bf16[12,32,128]{2,1,0:T(8,128)(2,1)}), bf16[12,32,128]{2,1,0:T(8,128)(2,1)S(1)}, u32[]{:S(2)}, u32[]{:S(2)}) %all-to-all-start.4) | async-done | bytes 98336 | tf_op jit(solution)/shard_map/all_to_all | solution.py:351
  138.5 0.0 copy-done
  138.5 0.0 copy-done.1
  138.5 0.0 copy-done.3
  138.5 1.7 %shard_map.135 = (bf16[64,512]{1,0:T(8,128)(2,1)}, bf16[64,512]{1,0:T(8,128)(2,1)}) custom-call(bf16[12,32,128]{2,1,0:T(8,128)(2,1)S(1)} %all-to-all-done.4.later, bf16[12,48,128]{2,1,0:T(8,128)(2,1)S(1)} %all-to-all-done.1.everyone, f32[64,512]{1,0:T(8,128)S(1)} %get-tuple-element.76.part_keys, f32[64,512]{1,0:T(8,128)S(1)} %get-tuple-element.77.part_values, ...), custom_call_target="tpu_custom_call" | custom-call | flops 1073741824 | bytes 8388608 | tf_op jit(solution)/shard_map/pallas_call | solution.py:335
  (1 shorter events, 0.0 us)
Async XLA Ops:
  2.5 24.6 %all-to-all-start = ((bf16[8,64,512]{2,1,0:T(8,128)(2,1)}), bf16[8,64,512]{2,1,0:T(8,128)(2,1)S(1)}, u32[]{:S(2)}, u32[]{:S(2)}) async-start(bf16[8,64,512]{2,1,0:T(8,128)(2,1)} %bitcast.22), calls=%async_computation | async-start | bytes 1048576 | tf_op jit(solution)/shard_map/all_to_all | solution.py:351
  16.1 99.1 %copy-start.2 = (f32[64,512]{1,0:T(8,128)}, f32[64,512]{1,0:T(8,128)S(1)}, u32[]{:S(2)}) copy-start(f32[64,512]{1,0:T(8,128)S(1)} %get-tuple-element.50.logs) | copy-start | bytes 393220
  16.1 99.1 %copy-start.4 = (f32[64,512]{1,0:T(8,128)}, f32[64,512]{1,0:T(8,128)S(1)}, u32[]{:S(2)}) copy-start(f32[64,512]{1,0:T(8,128)S(1)} %get-tuple-element.49.reads) | copy-start | bytes 393220
  27.1 28.2 %all-to-all-start.1 = ((bf16[12,48,128]{2,1,0:T(8,128)(2,1)}), bf16[12,48,128]{2,1,0:T(8,128)(2,1)S(1)}, u32[]{:S(2)}, u32[]{:S(2)}) async-start(bf16[12,48,128]{2,1,0:T(8,128)(2,1)} %get-tuple-element.47), calls=%async_computation.1 | async-start | bytes 294912 | tf_op jit(solution)/shard_map/all_to_all | solution.py:351
  44.5 18.4 %copy-start.5 = (bf16[528,512]{1,0:T(8,128)(2,1)S(1)}, bf16[528,512]{1,0:T(8,128)(2,1)}, u32[]{:S(2)}) copy-start(bf16[528,512]{1,0:T(8,128)(2,1)} %get-tuple-element.57.w0) | copy-start | bytes 1622020
  44.5 20.5 %collective-permute-start = (bf16[528,512]{1,0:T(8,128)(2,1)}, bf16[528,512]{1,0:T(8,128)(2,1)S(1)}, u32[]{:S(2)}, u32[]{:S(2)}) collective-permute-start(bf16[528,512]{1,0:T(8,128)(2,1)} %get-tuple-element.58), channel_id=1, source_target_pairs={{0,6},{2,0},{4,2},{6,4},{1,7},{3,1},{5,3},{7,5},{8,14},{10,8},{12,... | collective-permute-start | bytes 1622024 | tf_op jit(solution)/shard_map/ppermute | solution.py:357
  47.1 31.2 %collective-permute-start.1 = (bf16[528,512]{1,0:T(8,128)(2,1)}, bf16[528,512]{1,0:T(8,128)(2,1)}, u32[]{:S(2)}, u32[]{:S(2)}) collective-permute-start(bf16[528,512]{1,0:T(8,128)(2,1)} %get-tuple-element.59), channel_id=1, source_target_pairs={{0,4},{2,6},{4,0},{6,2},{1,5},{3,7},{5,1},{7,3},{8,12},{10,14},{12... | collective-permute-start | bytes 1622024 | tf_op jit(solution)/shard_map/ppermute | solution.py:357
  51.4 29.9 %collective-permute-start.2 = (bf16[528,512]{1,0:T(8,128)(2,1)}, bf16[528,512]{1,0:T(8,128)(2,1)}, u32[]{:S(2)}, u32[]{:S(2)}) collective-permute-start(bf16[528,512]{1,0:T(8,128)(2,1)} %get-tuple-element.60), channel_id=1, source_target_pairs={{0,2},{2,4},{4,6},{6,0},{1,3},{3,5},{5,7},{7,1},{8,10},{10,12},{12... | collective-permute-start | bytes 1622024 | tf_op jit(solution)/shard_map/ppermute | solution.py:357
  57.5 28.0 %all-to-all-start.2 = ((bf16[64,32,128]{2,1,0:T(8,128)(2,1)}), bf16[64,32,128]{2,1,0:T(8,128)(2,1)S(1)}, u32[]{:S(2)}, u32[]{:S(2)}) async-start(bf16[64,32,128]{2,1,0:T(8,128)(2,1)} %get-tuple-element.51), calls=%async_computation.2 | async-start | bytes 1048576 | tf_op jit(solution)/shard_map/all_to_all | solution.py:351
  62.9 20.4 %collective-permute-start.3 = (bf16[528,512]{1,0:T(8,128)(2,1)S(1)}, bf16[528,512]{1,0:T(8,128)(2,1)S(1)}, u32[]{:S(2)}, u32[]{:S(2)}) collective-permute-start(bf16[528,512]{1,0:T(8,128)(2,1)S(1)} %copy-done.5), channel_id=1, source_target_pairs={{0,1},{1,0},{2,3},{3,2},{4,5},{5,4},{6,7},{7,6},{8,9},{9,8},{10,11... | collective-permute-start | bytes 1622024 | tf_op jit(solution)/shard_map/ppermute | solution.py:363
  65.0 20.5 %copy-start.6 = (bf16[528,512]{1,0:T(8,128)(2,1)}, bf16[528,512]{1,0:T(8,128)(2,1)S(1)}, u32[]{:S(2)}) copy-start(bf16[528,512]{1,0:T(8,128)(2,1)S(1)} %collective-permute-done.w3) | copy-start | bytes 1622020
  65.0 18.3 %collective-permute-start.4 = (bf16[528,512]{1,0:T(8,128)(2,1)S(1)}, bf16[528,512]{1,0:T(8,128)(2,1)S(1)}, u32[]{:S(2)}, u32[]{:S(2)}) collective-permute-start(bf16[528,512]{1,0:T(8,128)(2,1)S(1)} %collective-permute-done.w3), channel_id=1, source_target_pairs={{0,1},{1,0},{2,3},{3,2},{4,5},{5,4},{6,7},{7,6},{8,9},{9,8},{10,11... | collective-permute-start | bytes 1622024 | tf_op jit(solution)/shard_map/ppermute | solution.py:363
  78.3 5.1 %collective-permute-start.5 = (bf16[528,512]{1,0:T(8,128)(2,1)}, bf16[528,512]{1,0:T(8,128)(2,1)S(1)}, u32[]{:S(2)}, u32[]{:S(2)}) collective-permute-start(bf16[528,512]{1,0:T(8,128)(2,1)} %collective-permute-done.1.w2), channel_id=1, source_target_pairs={{0,1},{1,0},{2,3},{3,2},{4,5},{5,4},{6,7},{7,6},{8,9},{9,8},{10,11... | collective-permute-start | bytes 1622024 | tf_op jit(solution)/shard_map/ppermute | solution.py:363
  81.4 4.2 %collective-permute-start.6 = (bf16[528,512]{1,0:T(8,128)(2,1)}, bf16[528,512]{1,0:T(8,128)(2,1)}, u32[]{:S(2)}, u32[]{:S(2)}) collective-permute-start(bf16[528,512]{1,0:T(8,128)(2,1)} %collective-permute-done.2.w1), channel_id=1, source_target_pairs={{0,1},{1,0},{2,3},{3,2},{4,5},{5,4},{6,7},{7,6},{8,9},{9,8},{10,11... | collective-permute-start | bytes 1622024 | tf_op jit(solution)/shard_map/ppermute | solution.py:363
  83.3 0.8 copy-start.7
  84.1 0.8 copy-start.8
  90.6 35.9 %copy-start.10 = (bf16[2,32,128]{2,1,0:T(8,128)(2,1)S(1)}, bf16[2,32,128]{2,1,0:T(8,128)(2,1)}, u32[]{:S(2)}) copy-start(bf16[2,32,128]{2,1,0:T(8,128)(2,1)} %get-tuple-element.61) | copy-start | bytes 49156
  90.6 24.6 %all-to-all-start.3 = ((bf16[64,32,128]{2,1,0:T(8,128)(2,1)}), bf16[64,32,128]{2,1,0:T(8,128)(2,1)S(1)}, u32[]{:S(2)}, u32[]{:S(2)}) async-start(bf16[64,32,128]{2,1,0:T(8,128)(2,1)} %get-tuple-element.69), calls=%async_computation.3 | async-start | bytes 1048576 | tf_op jit(solution)/shard_map/all_to_all | solution.py:351
  97.6 40.8 %copy-start = (f32[64,512]{1,0:T(8,128)S(1)}, f32[64,512]{1,0:T(8,128)}, u32[]{:S(2)}) copy-start(f32[64,512]{1,0:T(8,128)} %get-tuple-element.65.keys_raw) | copy-start | bytes 393220
  97.6 40.8 %copy-start.1 = (f32[64,512]{1,0:T(8,128)S(1)}, f32[64,512]{1,0:T(8,128)}, u32[]{:S(2)}) copy-start(f32[64,512]{1,0:T(8,128)} %get-tuple-element.66.values) | copy-start | bytes 393220
  97.6 28.8 %collective-permute-start.7 = (bf16[2,32,128]{2,1,0:T(8,128)(2,1)}, bf16[2,32,128]{2,1,0:T(8,128)(2,1)S(1)}, u32[]{:S(2)}, u32[]{:S(2)}) collective-permute-start(bf16[2,32,128]{2,1,0:T(8,128)(2,1)} %get-tuple-element.62), channel_id=1, source_target_pairs={{0,2},{2,4},{4,6},{6,0},{1,3},{3,5},{5,7},{7,1},{8,10},{10,12},{12... | collective-permute-start | bytes 49160 | tf_op jit(solution)/shard_map/ppermute | solution.py:357
  101.2 25.3 %collective-permute-start.8 = (bf16[2,32,128]{2,1,0:T(8,128)(2,1)}, bf16[2,32,128]{2,1,0:T(8,128)(2,1)S(1)}, u32[]{:S(2)}, u32[]{:S(2)}) collective-permute-start(bf16[2,32,128]{2,1,0:T(8,128)(2,1)} %get-tuple-element.63), channel_id=1, source_target_pairs={{0,4},{2,6},{4,0},{6,2},{1,5},{3,7},{5,1},{7,3},{8,12},{10,14},{12... | collective-permute-start | bytes 49160 | tf_op jit(solution)/shard_map/ppermute | solution.py:357
  104.1 22.3 %collective-permute-start.9 = (bf16[2,32,128]{2,1,0:T(8,128)(2,1)}, bf16[2,32,128]{2,1,0:T(8,128)(2,1)S(1)}, u32[]{:S(2)}, u32[]{:S(2)}) collective-permute-start(bf16[2,32,128]{2,1,0:T(8,128)(2,1)} %get-tuple-element.64), channel_id=1, source_target_pairs={{0,6},{2,0},{4,2},{6,4},{1,7},{3,1},{5,3},{7,5},{8,14},{10,8},{12,... | collective-permute-start | bytes 49160 | tf_op jit(solution)/shard_map/ppermute | solution.py:357
  116.9 21.6 %copy-start.3 = (f32[64,512]{1,0:T(8,128)S(1)}, f32[64,512]{1,0:T(8,128)}, u32[]{:S(2)}) copy-start(f32[64,512]{1,0:T(8,128)} %copy-done.2) | copy-start | bytes 393220
  116.9 21.5 %all-to-all-start.4 = ((bf16[12,32,128]{2,1,0:T(8,128)(2,1)}), bf16[12,32,128]{2,1,0:T(8,128)(2,1)S(1)}, u32[]{:S(2)}, u32[]{:S(2)}) async-start(bf16[12,32,128]{2,1,0:T(8,128)(2,1)} %get-tuple-element.75), calls=%async_computation.4 | async-start | bytes 196608 | tf_op jit(solution)/shard_map/all_to_all | solution.py:351
  126.5 3.2 %copy-start.9 = (bf16[4,2,32,128]{3,2,1,0:T(8,128)(2,1)}, bf16[4,2,32,128]{3,2,1,0:T(8,128)(2,1)S(1)}, u32[]{:S(2)}) copy-start(bf16[4,2,32,128]{3,2,1,0:T(8,128)(2,1)S(1)} %pad_maximum_fusion.m_mine) | copy-start | bytes 196612
  126.5 3.1 %collective-permute-start.10 = (bf16[4,2,32,128]{3,2,1,0:T(8,128)(2,1)S(1)}, bf16[4,2,32,128]{3,2,1,0:T(8,128)(2,1)S(1)}, u32[]{:S(2)}, u32[]{:S(2)}) collective-permute-start(bf16[4,2,32,128]{3,2,1,0:T(8,128)(2,1)S(1)} %pad_maximum_fusion.m_mine), channel_id=1, source_target_pairs={{0,1},{1,0},{2,3},{3,2},{4,5},{5,4},{6,7},{7,6},{8,9},{9,8},{10,11... | collective-permute-start | bytes 196616 | tf_op jit(solution)/shard_map/ppermute | solution.py:363
  129.6 0.6 copy-start.11

commit v9 on v8

--- a/solution.py
+++ b/solution.py
@@ -211,7 +211,7 @@
     return jnp.where(core == c, mine[step, core], other[step, core])
 
 
-def middle_kernel(got, w0, w3, w2, w1, v0, v3, v2, v1, sent, m0, m1, m2, m3, held, weights, sems):
+def middle_kernel(got, w0, w1, w2, w3, v0, v1, v2, v3, sent, m0, m1, m2, m3, held, weights, sems):
     copies = []
     for n, source in enumerate((w0, v0, w1, v1, w2, v2, w3, v3)):
         copies.append(pltpu.make_async_copy(source, weights.at[n], sems.at[n]))
@@ -221,7 +221,7 @@
     rows = GRID["y"]
     group = min(4, rows)
     chunks = []
-    for s in (0, 3, 2, 1):
+    for s in (0, 1, 2, 3):
         x = lax.rem(at - s + GRID["x"], GRID["x"])
         for n, c in ((2 * s, core), (2 * s + 1, 1 - core)):
             for y in range(0, rows, group):
@@ -354,7 +354,7 @@
 def along_x(parts):
     n = GRID["x"]
     came = {
-        s: lax.ppermute(parts[s], "x", [(i, (i + s) % n) for i in range(n)]) for s in (3, 2, 1)
+        s: lax.ppermute(parts[s], "x", [(i, (i + s) % n) for i in range(n)]) for s in (1, 2, 3)
     }
     return [parts[0], came[1], came[2], came[3]]
 
@@ -436,9 +436,9 @@
         here=(2, 3),
     )
     got = exchange(sent, head)
-    other = {s: swap(w_mine[s]) for s in (0, 3, 2, 1)}
-    w_other = [other[s] for s in (0, 3, 2, 1)]
-    w_mine = [w_mine[s] for s in (0, 3, 2, 1)]
+    other = {s: swap(w_mine[s]) for s in (0, 1, 2, 3)}
+    w_other = [other[s] for s in (0, 1, 2, 3)]
+    w_mine = [w_mine[s] for s in (0, 1, 2, 3)]
     sent, *mixed = call(
         middle_kernel,
         [((rows * tiles,) + block, bf16)] + [((2,) + block, bf16)] * GRID["x"],

time: 141 us -> 139 us (0.986)
  starting transfers between devices: 75.4 us -> 73.1 us
    all_to_all x5, starting transfers between devices: 44.1 us -> 41.7 us  [exchange(): return lax.all_to_all(array, axis, 0, 0)]
  transfers between devices with their start and end apart: 16 -> 16, of which waited for: 8 -> 7; matrix products, arithmetic and copies ran while one was open for 0% -> 0% of each run, Pallas kernels for 11% -> 11%
where the time goes in v9:
time: 139 us; the launch traced here: 138 us
  starting transfers between devices  73.1 us (53%)
  waiting for transfers between devices  38.3 us (28%)
  Pallas kernels  21.5 us (15%)
  local copies, waits for them, and re-layouts  4.16 us (3%)
    all_to_all x5, starting transfers between devices, exchange(): return lax.all_to_all(array, axis, 0, 0)  41.7 us
    all_to_all x5, waiting for transfers between devices, exchange(): return lax.all_to_all(array, axis, 0, 0)  23.6 us
    pallas_call x7, Pallas kernels, call(): pl.pallas_call(kernel, cost_estimate=pl.CostEstimate(flops=1 << 30, trans...  21.5 us
    ppermute x6, starting transfers between devices, along_x(): lax.ppermute(parts[s], 'x', [(i, (i + s) % n) for i in range(n)])  21.2 us
    ppermute x6, waiting for transfers between devices, along_x(): lax.ppermute(parts[s], 'x', [(i, (i + s) % n) for i in range(n)])  12.8 us
    ppermute x5, starting transfers between devices, swap(): return lax.ppermute(array, 'core', [(0, 1), (1, 0)])  10.2 us
  transfers between devices with their start and end apart: 16, of which 7 were waited for; matrix products, arithmetic and copies ran while one was open for 0% of the time, Pallas kernels for 11%

profile of v9, /device:TPU:2, one launch (start us, length us, event | category | flops | bytes accessed | tf_op | source)
XLA Modules:
  0.0 138.0 jit_solution(963299543304474948)
XLA Ops:
  0.6 1.9 %copy.17 = bf16[8,8,8,512]{3,2,0,1:T(8,128)(2,1)} copy(bf16[8,8,8,512]{3,2,1,0:T(8,128)(2,1)} %bitcast.26) | data formatting | bytes 1048576 | tf_op jit(solution)/shard_map/reshape | solution.py:391
  2.5 7.1 %all-to-all-start = ((bf16[8,64,512]{2,1,0:T(8,128)(2,1)}), bf16[8,64,512]{2,1,0:T(8,128)(2,1)S(1)}, u32[]{:S(2)}, u32[]{:S(2)}) async-start(bf16[8,64,512]{2,1,0:T(8,128)(2,1)} %bitcast.22), calls=%async_computation | async-start | bytes 1048576 | tf_op jit(solution)/shard_map/all_to_all | solution.py:351
  9.6 6.5 %shard_map.129 = (bf16[12,48,128]{2,1,0:T(8,128)(2,1)}, f32[64,512]{1,0:T(8,128)S(1)}, f32[64,512]{1,0:T(8,128)}, f32[64,512]{1,0:T(8,128)}, f32[64,512]{1,0:T(8...) custom-call(bf16[512,4096]{1,0:T(8,128)(2,1)} %x.1, ...), custom_call_target="tpu_custom_call" | custom-call | flops 1073741824 | bytes 8388608 | tf_op jit(solution)/shard_map/pallas_call | solution.py:335
  16.1 0.0 copy-start.2
  16.1 0.0 copy-start.4
  16.1 11.0 %all-to-all-done.columns = bf16[8,64,512]{2,1,0:T(8,128)(2,1)S(1)} async-done(((bf16[8,64,512]{2,1,0:T(8,128)(2,1)}), bf16[8,64,512]{2,1,0:T(8,128)(2,1)S(1)}, u32[]{:S(2)}, u32[]{:S(2)}) %all-to-all-start) | async-done | bytes 524320 | tf_op jit(solution)/shard_map/all_to_all | solution.py:351
  27.1 15.2 %all-to-all-start.1 = ((bf16[12,48,128]{2,1,0:T(8,128)(2,1)}), bf16[12,48,128]{2,1,0:T(8,128)(2,1)S(1)}, u32[]{:S(2)}, u32[]{:S(2)}) async-start(bf16[12,48,128]{2,1,0:T(8,128)(2,1)} %get-tuple-element.47), calls=%async_computation.1 | async-start | bytes 294912 | tf_op jit(solution)/shard_map/all_to_all | solution.py:351
  42.3 2.3 %shard_map.131 = (bf16[528,512]{1,0:T(8,128)(2,1)}, bf16[528,512]{1,0:T(8,128)(2,1)}, bf16[528,512]{1,0:T(8,128)(2,1)}, bf16[528,512]{1,0:T(8,128)(2,1)}) custom-call(bf16[8,64,512]{2,1,0:T(8,128)(2,1)S(1)} %all-to-all-done.columns, bf16[16,512]{1,0:T(8,128)(2,1)} %get-tuple-element.53.t0, bf16[16,512]{1,0:T(8,128)(2,1)} %get-tuple-element.54.t1, ...), custom_call_target="tpu_custom_call" | custom-call | flops 1073741824 | bytes 8388608 | tf_op jit(solution)/shard_map/pallas_call | solution.py:335
  44.6 0.0 copy-start.5
  44.6 3.5 %collective-permute-start = (bf16[528,512]{1,0:T(8,128)(2,1)}, bf16[528,512]{1,0:T(8,128)(2,1)S(1)}, u32[]{:S(2)}, u32[]{:S(2)}) collective-permute-start(bf16[528,512]{1,0:T(8,128)(2,1)} %get-tuple-element.58), channel_id=1, source_target_pairs={{0,2},{2,4},{4,6},{6,0},{1,3},{3,5},{5,7},{7,1},{8,10},{10,12},{12... | collective-permute-start | bytes 1622024 | tf_op jit(solution)/shard_map/ppermute | solution.py:357
  48.1 3.0 %collective-permute-start.1 = (bf16[528,512]{1,0:T(8,128)(2,1)}, bf16[528,512]{1,0:T(8,128)(2,1)}, u32[]{:S(2)}, u32[]{:S(2)}) collective-permute-start(bf16[528,512]{1,0:T(8,128)(2,1)} %get-tuple-element.59), channel_id=1, source_target_pairs={{0,4},{2,6},{4,0},{6,2},{1,5},{3,7},{5,1},{7,3},{8,12},{10,14},{12... | collective-permute-start | bytes 1622024 | tf_op jit(solution)/shard_map/ppermute | solution.py:357
  51.1 4.1 %collective-permute-start.2 = (bf16[528,512]{1,0:T(8,128)(2,1)}, bf16[528,512]{1,0:T(8,128)(2,1)}, u32[]{:S(2)}, u32[]{:S(2)}) collective-permute-start(bf16[528,512]{1,0:T(8,128)(2,1)} %get-tuple-element.60), channel_id=1, source_target_pairs={{0,6},{2,0},{4,2},{6,4},{1,7},{3,1},{5,3},{7,5},{8,14},{10,8},{12,... | collective-permute-start | bytes 1622024 | tf_op jit(solution)/shard_map/ppermute | solution.py:357
  55.2 0.1 all-to-all-done.1.everyone
  55.3 2.2 %shard_map.130 = (bf16[64,32,128]{2,1,0:T(8,128)(2,1)}, f32[64,64]{1,0:T(8,128)}, f32[64,512]{1,0:T(8,128)S(1)}, f32[1,512]{1,0:T(1,128)S(1)}) custom-call(bf16[12,48,128]{2,1,0:T(8,128)(2,1)S(1)} %all-to-all-done.1.everyone, f32[64,512]{1,0:T(8,128)S(1)} %get-tuple-element.48.local, f32[64,512]{1,0:T(8,128)S(1)} %get-tuple-element.49.reads, ...), custom_call_target="tpu_custom_call" | custom-call | flops 1073741824 | bytes 8388608 | tf_op jit(solution)/shard_map/pallas_call | solution.py:335
  57.5 5.4 %all-to-all-start.2 = ((bf16[64,32,128]{2,1,0:T(8,128)(2,1)}), bf16[64,32,128]{2,1,0:T(8,128)(2,1)S(1)}, u32[]{:S(2)}, u32[]{:S(2)}) async-start(bf16[64,32,128]{2,1,0:T(8,128)(2,1)} %get-tuple-element.51), calls=%async_computation.2 | async-start | bytes 1048576 | tf_op jit(solution)/shard_map/all_to_all | solution.py:351
  62.9 0.0 copy-done.5
  62.9 2.1 %collective-permute-start.3 = (bf16[528,512]{1,0:T(8,128)(2,1)S(1)}, bf16[528,512]{1,0:T(8,128)(2,1)S(1)}, u32[]{:S(2)}, u32[]{:S(2)}) collective-permute-start(bf16[528,512]{1,0:T(8,128)(2,1)S(1)} %copy-done.5), channel_id=1, source_target_pairs={{0,1},{1,0},{2,3},{3,2},{4,5},{5,4},{6,7},{7,6},{8,9},{9,8},{10,11... | collective-permute-start | bytes 1622024 | tf_op jit(solution)/shard_map/ppermute | solution.py:363
  65.0 0.0 collective-permute-done.w1
  65.0 0.0 copy-start.6
  65.0 2.3 %collective-permute-start.4 = (bf16[528,512]{1,0:T(8,128)(2,1)S(1)}, bf16[528,512]{1,0:T(8,128)(2,1)S(1)}, u32[]{:S(2)}, u32[]{:S(2)}) collective-permute-start(bf16[528,512]{1,0:T(8,128)(2,1)S(1)} %collective-permute-done.w1), channel_id=1, source_target_pairs={{0,1},{1,0},{2,3},{3,2},{4,5},{5,4},{6,7},{7,6},{8,9},{9,8},{10,11... | collective-permute-start | bytes 1622024 | tf_op jit(solution)/shard_map/ppermute | solution.py:363
  67.3 0.0 collective-permute-done.1.w2
  67.3 2.1 %collective-permute-start.5 = (bf16[528,512]{1,0:T(8,128)(2,1)}, bf16[528,512]{1,0:T(8,128)(2,1)S(1)}, u32[]{:S(2)}, u32[]{:S(2)}) collective-permute-start(bf16[528,512]{1,0:T(8,128)(2,1)} %collective-permute-done.1.w2), channel_id=1, source_target_pairs={{0,1},{1,0},{2,3},{3,2},{4,5},{5,4},{6,7},{7,6},{8,9},{9,8},{10,11... | collective-permute-start | bytes 1622024 | tf_op jit(solution)/shard_map/ppermute | solution.py:363
  69.4 12.8 %collective-permute-done.2.w3 = bf16[528,512]{1,0:T(8,128)(2,1)} collective-permute-done((bf16[528,512]{1,0:T(8,128)(2,1)}, bf16[528,512]{1,0:T(8,128)(2,1)}, u32[]{:S(2)}, u32[]{:S(2)}) %collective-permute-start.2) | collective-permute-done | bytes 540704 | tf_op jit(solution)/shard_map/ppermute | solution.py:357
  82.2 1.9 %collective-permute-start.6 = (bf16[528,512]{1,0:T(8,128)(2,1)}, bf16[528,512]{1,0:T(8,128)(2,1)}, u32[]{:S(2)}, u32[]{:S(2)}) collective-permute-start(bf16[528,512]{1,0:T(8,128)(2,1)} %collective-permute-done.2.w3), channel_id=1, source_target_pairs={{0,1},{1,0},{2,3},{3,2},{4,5},{5,4},{6,7},{7,6},{8,9},{9,8},{10,11... | collective-permute-start | bytes 1622024 | tf_op jit(solution)/shard_map/ppermute | solution.py:363
  84.1 0.0 collective-permute-done.3.v0
  84.1 0.0 collective-permute-done.4.v1
  84.1 0.0 copy-start.7
  84.2 0.0 collective-permute-done.5.v2
  84.2 0.8 copy-done.7
  85.0 0.0 copy-start.8
  85.0 0.8 copy-done.8
  85.8 0.6 collective-permute-done.6.v3
  86.4 0.0 all-to-all-done.2.got
  86.4 0.0 copy-done.6
  86.4 4.5 %shard_map.132 = (bf16[64,32,128]{2,1,0:T(8,128)(2,1)}, bf16[2,32,128]{2,1,0:T(8,128)(2,1)}, bf16[2,32,128]{2,1,0:T(8,128)(2,1)}, bf16[2,32,128]{2,1,0:T(8,128)(2,1)}, bf16[2,32,128]{2,1,0:T(8,128)(2,1)}) custom-call(bf16[64,32,128]{2,1,0:T(8,128)(2,1)S(1)} %all-to-all-done.2.got, bf16[528,512]{1,0:T(8,128)(2,1)} %get-tuple-element.57.w0, ...), custom_call_target="tpu_custom_call" | custom-call | flops 1073741824 | bytes 8388608 | tf_op jit(solution)/shard_map/pallas_call | solution.py:335
  90.8 0.0 copy-start.10
  90.9 4.6 %all-to-all-start.3 = ((bf16[64,32,128]{2,1,0:T(8,128)(2,1)}), bf16[64,32,128]{2,1,0:T(8,128)(2,1)S(1)}, u32[]{:S(2)}, u32[]{:S(2)}) async-start(bf16[64,32,128]{2,1,0:T(8,128)(2,1)} %get-tuple-element.69), calls=%async_computation.3 | async-start | bytes 1048576 | tf_op jit(solution)/shard_map/all_to_all | solution.py:351
  95.5 0.0 copy-start
  95.5 0.0 copy-start.1
  95.5 3.5 %collective-permute-start.7 = (bf16[2,32,128]{2,1,0:T(8,128)(2,1)}, bf16[2,32,128]{2,1,0:T(8,128)(2,1)S(1)}, u32[]{:S(2)}, u32[]{:S(2)}) collective-permute-start(bf16[2,32,128]{2,1,0:T(8,128)(2,1)} %get-tuple-element.62), channel_id=1, source_target_pairs={{0,2},{2,4},{4,6},{6,0},{1,3},{3,5},{5,7},{7,1},{8,10},{10,12},{12... | collective-permute-start | bytes 49160 | tf_op jit(solution)/shard_map/ppermute | solution.py:357
  99.0 3.0 %collective-permute-start.8 = (bf16[2,32,128]{2,1,0:T(8,128)(2,1)}, bf16[2,32,128]{2,1,0:T(8,128)(2,1)S(1)}, u32[]{:S(2)}, u32[]{:S(2)}) collective-permute-start(bf16[2,32,128]{2,1,0:T(8,128)(2,1)} %get-tuple-element.63), channel_id=1, source_target_pairs={{0,4},{2,6},{4,0},{6,2},{1,5},{3,7},{5,1},{7,3},{8,12},{10,14},{12... | collective-permute-start | bytes 49160 | tf_op jit(solution)/shard_map/ppermute | solution.py:357
  102.0 4.1 %collective-permute-start.9 = (bf16[2,32,128]{2,1,0:T(8,128)(2,1)}, bf16[2,32,128]{2,1,0:T(8,128)(2,1)S(1)}, u32[]{:S(2)}, u32[]{:S(2)}) collective-permute-start(bf16[2,32,128]{2,1,0:T(8,128)(2,1)} %get-tuple-element.64), channel_id=1, source_target_pairs={{0,6},{2,0},{4,2},{6,4},{1,7},{3,1},{5,3},{7,5},{8,14},{10,8},{12,... | collective-permute-start | bytes 49160 | tf_op jit(solution)/shard_map/ppermute | solution.py:357
  106.1 7.0 %all-to-all-done.3.got = bf16[64,32,128]{2,1,0:T(8,128)(2,1)S(1)} async-done(((bf16[64,32,128]{2,1,0:T(8,128)(2,1)}), bf16[64,32,128]{2,1,0:T(8,128)(2,1)S(1)}, u32[]{:S(2)}, u32[]{:S(2)}) %all-to-all-start.3) | async-done | bytes 524320 | tf_op jit(solution)/shard_map/all_to_all | solution.py:351
  113.0 0.0 copy-done.2
  113.0 0.0 copy-done.4
  113.0 1.7 %shard_map.133 = (bf16[12,32,128]{2,1,0:T(8,128)(2,1)}, f32[64,512]{1,0:T(8,128)}) custom-call(bf16[64,32,128]{2,1,0:T(8,128)(2,1)S(1)} %all-to-all-done.3.got, f32[64,512]{1,0:T(8,128)S(1)} %get-tuple-element.70.unit, f32[1,512]{1,0:T(1,128)S(1)} %get-tuple-element.71.inverse, f32[1,64]{1,0:T(1,128)} %bitcast.39, f32[64,512]{1,0:T(8,128)S(1)} %get-tuple-element.49.reads, ...), custom_call_target="tpu_custom_call" | custom-call | flops 1073741824 | bytes 8388608 | tf_op jit(solution)/shard_map/pallas_call | solution.py:335
  114.8 0.0 copy-start.3
  114.8 9.5 %all-to-all-start.4 = ((bf16[12,32,128]{2,1,0:T(8,128)(2,1)}), bf16[12,32,128]{2,1,0:T(8,128)(2,1)S(1)}, u32[]{:S(2)}, u32[]{:S(2)}) async-start(bf16[12,32,128]{2,1,0:T(8,128)(2,1)} %get-tuple-element.75), calls=%async_computation.4 | async-start | bytes 196608 | tf_op jit(solution)/shard_map/all_to_all | solution.py:351
  124.2 0.0 collective-permute-done.7
  124.2 0.0 collective-permute-done.8
  124.3 0.0 collective-permute-done.9
  124.3 0.0 copy-done.10
  124.3 0.0 copy-start.9
  124.3 1.9 %collective-permute-start.10 = (bf16[4,2,32,128]{3,2,1,0:T(8,128)(2,1)S(1)}, bf16[4,2,32,128]{3,2,1,0:T(8,128)(2,1)S(1)}, u32[]{:S(2)}, u32[]{:S(2)}) collective-permute-start(bf16[4,2,32,128]{3,2,1,0:T(8,128)(2,1)S(1)} %pad_maximum_fusion.m_mine), channel_id=1, source_target_pairs={{0,1},{1,0},{2,3},{3,2},{4,5},{5,4},{6,7},{7,6},{8,9},{9,8},{10,11... | collective-permute-start | bytes 196616 | tf_op jit(solution)/shard_map/ppermute | solution.py:363
  126.2 1.2 collective-permute-done.10.m_other
  127.5 0.0 copy-start.11
  127.5 0.0 copy-done.9
  127.5 0.6 copy-done.11
  128.1 2.7 %shard_map.134 = (bf16[64,512]{1,0:T(8,128)(2,1)}, bf16[64,512]{1,0:T(8,128)(2,1)}, f32[64,512]{1,0:T(8,128)S(1)}, f32[64,512]{1,0:T(8,128)S(1)}) custom-call(bf16[4,2,32,128]{3,2,1,0:T(8,128)(2,1)} %copy-done.9, bf16[4,2,32,128]{3,2,1,0:T(8,128)(2,1)} %copy-done.11, f32[64,512]{1,0:T(8,128)} %copy-done.4, f32[64,512]{1,0:T(8,128)} %get-tuple-element.65.keys_raw, ...), custom_call_target="tpu_custom_call" | custom-call | flops 1073741824 | bytes 8388608 | tf_op jit(solution)/shard_map/pallas_call | solution.py:335
  130.8 5.6 %all-to-all-done.4.later = bf16[12,32,128]{2,1,0:T(8,128)(2,1)S(1)} async-done(((bf16[12,32,128]{2,1,0:T(8,128)(2,1)}), bf16[12,32,128]{2,1,0:T(8,128)(2,1)S(1)}, u32[]{:S(2)}, u32[]{:S(2)}) %all-to-all-start.4) | async-done | bytes 98336 | tf_op jit(solution)/shard_map/all_to_all | solution.py:351
  136.3 0.0 copy-done
  136.3 0.0 copy-done.1
  136.3 0.0 copy-done.3
  136.3 1.7 %shard_map.135 = (bf16[64,512]{1,0:T(8,128)(2,1)}, bf16[64,512]{1,0:T(8,128)(2,1)}) custom-call(bf16[12,32,128]{2,1,0:T(8,128)(2,1)S(1)} %all-to-all-done.4.later, bf16[12,48,128]{2,1,0:T(8,128)(2,1)S(1)} %all-to-all-done.1.everyone, f32[64,512]{1,0:T(8,128)S(1)} %get-tuple-element.76.part_keys, f32[64,512]{1,0:T(8,128)S(1)} %get-tuple-element.77.part_values, ...), custom_call_target="tpu_custom_call" | custom-call | flops 1073741824 | bytes 8388608 | tf_op jit(solution)/shard_map/pallas_call | solution.py:335
  (1 shorter events, 0.0 us)
Async XLA Ops:
  2.5 24.6 %all-to-all-start = ((bf16[8,64,512]{2,1,0:T(8,128)(2,1)}), bf16[8,64,512]{2,1,0:T(8,128)(2,1)S(1)}, u32[]{:S(2)}, u32[]{:S(2)}) async-start(bf16[8,64,512]{2,1,0:T(8,128)(2,1)} %bitcast.22), calls=%async_computation | async-start | bytes 1048576 | tf_op jit(solution)/shard_map/all_to_all | solution.py:351
  16.1 97.0 %copy-start.2 = (f32[64,512]{1,0:T(8,128)}, f32[64,512]{1,0:T(8,128)S(1)}, u32[]{:S(2)}) copy-start(f32[64,512]{1,0:T(8,128)S(1)} %get-tuple-element.50.logs) | copy-start | bytes 393220
  16.1 96.9 %copy-start.4 = (f32[64,512]{1,0:T(8,128)}, f32[64,512]{1,0:T(8,128)S(1)}, u32[]{:S(2)}) copy-start(f32[64,512]{1,0:T(8,128)S(1)} %get-tuple-element.49.reads) | copy-start | bytes 393220
  27.1 28.2 %all-to-all-start.1 = ((bf16[12,48,128]{2,1,0:T(8,128)(2,1)}), bf16[12,48,128]{2,1,0:T(8,128)(2,1)S(1)}, u32[]{:S(2)}, u32[]{:S(2)}) async-start(bf16[12,48,128]{2,1,0:T(8,128)(2,1)} %get-tuple-element.47), calls=%async_computation.1 | async-start | bytes 294912 | tf_op jit(solution)/shard_map/all_to_all | solution.py:351
  44.6 18.4 %copy-start.5 = (bf16[528,512]{1,0:T(8,128)(2,1)S(1)}, bf16[528,512]{1,0:T(8,128)(2,1)}, u32[]{:S(2)}) copy-start(bf16[528,512]{1,0:T(8,128)(2,1)} %get-tuple-element.57.w0) | copy-start | bytes 1622020
  44.6 20.4 %collective-permute-start = (bf16[528,512]{1,0:T(8,128)(2,1)}, bf16[528,512]{1,0:T(8,128)(2,1)S(1)}, u32[]{:S(2)}, u32[]{:S(2)}) collective-permute-start(bf16[528,512]{1,0:T(8,128)(2,1)} %get-tuple-element.58), channel_id=1, source_target_pairs={{0,2},{2,4},{4,6},{6,0},{1,3},{3,5},{5,7},{7,1},{8,10},{10,12},{12... | collective-permute-start | bytes 1622024 | tf_op jit(solution)/shard_map/ppermute | solution.py:357
  48.1 19.2 %collective-permute-start.1 = (bf16[528,512]{1,0:T(8,128)(2,1)}, bf16[528,512]{1,0:T(8,128)(2,1)}, u32[]{:S(2)}, u32[]{:S(2)}) collective-permute-start(bf16[528,512]{1,0:T(8,128)(2,1)} %get-tuple-element.59), channel_id=1, source_target_pairs={{0,4},{2,6},{4,0},{6,2},{1,5},{3,7},{5,1},{7,3},{8,12},{10,14},{12... | collective-permute-start | bytes 1622024 | tf_op jit(solution)/shard_map/ppermute | solution.py:357
  51.1 31.1 %collective-permute-start.2 = (bf16[528,512]{1,0:T(8,128)(2,1)}, bf16[528,512]{1,0:T(8,128)(2,1)}, u32[]{:S(2)}, u32[]{:S(2)}) collective-permute-start(bf16[528,512]{1,0:T(8,128)(2,1)} %get-tuple-element.60), channel_id=1, source_target_pairs={{0,6},{2,0},{4,2},{6,4},{1,7},{3,1},{5,3},{7,5},{8,14},{10,8},{12,... | collective-permute-start | bytes 1622024 | tf_op jit(solution)/shard_map/ppermute | solution.py:357
  57.5 28.9 %all-to-all-start.2 = ((bf16[64,32,128]{2,1,0:T(8,128)(2,1)}), bf16[64,32,128]{2,1,0:T(8,128)(2,1)S(1)}, u32[]{:S(2)}, u32[]{:S(2)}) async-start(bf16[64,32,128]{2,1,0:T(8,128)(2,1)} %get-tuple-element.51), calls=%async_computation.2 | async-start | bytes 1048576 | tf_op jit(solution)/shard_map/all_to_all | solution.py:351
  62.9 21.2 %collective-permute-start.3 = (bf16[528,512]{1,0:T(8,128)(2,1)S(1)}, bf16[528,512]{1,0:T(8,128)(2,1)S(1)}, u32[]{:S(2)}, u32[]{:S(2)}) collective-permute-start(bf16[528,512]{1,0:T(8,128)(2,1)S(1)} %copy-done.5), channel_id=1, source_target_pairs={{0,1},{1,0},{2,3},{3,2},{4,5},{5,4},{6,7},{7,6},{8,9},{9,8},{10,11... | collective-permute-start | bytes 1622024 | tf_op jit(solution)/shard_map/ppermute | solution.py:363
  65.0 21.4 %copy-start.6 = (bf16[528,512]{1,0:T(8,128)(2,1)}, bf16[528,512]{1,0:T(8,128)(2,1)S(1)}, u32[]{:S(2)}) copy-start(bf16[528,512]{1,0:T(8,128)(2,1)S(1)} %collective-permute-done.w1) | copy-start | bytes 1622020
  65.0 19.1 %collective-permute-start.4 = (bf16[528,512]{1,0:T(8,128)(2,1)S(1)}, bf16[528,512]{1,0:T(8,128)(2,1)S(1)}, u32[]{:S(2)}, u32[]{:S(2)}) collective-permute-start(bf16[528,512]{1,0:T(8,128)(2,1)S(1)} %collective-permute-done.w1), channel_id=1, source_target_pairs={{0,1},{1,0},{2,3},{3,2},{4,5},{5,4},{6,7},{7,6},{8,9},{9,8},{10,11... | collective-permute-start | bytes 1622024 | tf_op jit(solution)/shard_map/ppermute | solution.py:363
  67.3 16.9 %collective-permute-start.5 = (bf16[528,512]{1,0:T(8,128)(2,1)}, bf16[528,512]{1,0:T(8,128)(2,1)S(1)}, u32[]{:S(2)}, u32[]{:S(2)}) collective-permute-start(bf16[528,512]{1,0:T(8,128)(2,1)} %collective-permute-done.1.w2), channel_id=1, source_target_pairs={{0,1},{1,0},{2,3},{3,2},{4,5},{5,4},{6,7},{7,6},{8,9},{9,8},{10,11... | collective-permute-start | bytes 1622024 | tf_op jit(solution)/shard_map/ppermute | solution.py:363
  82.2 4.2 %collective-permute-start.6 = (bf16[528,512]{1,0:T(8,128)(2,1)}, bf16[528,512]{1,0:T(8,128)(2,1)}, u32[]{:S(2)}, u32[]{:S(2)}) collective-permute-start(bf16[528,512]{1,0:T(8,128)(2,1)} %collective-permute-done.2.w3), channel_id=1, source_target_pairs={{0,1},{1,0},{2,3},{3,2},{4,5},{5,4},{6,7},{7,6},{8,9},{9,8},{10,11... | collective-permute-start | bytes 1622024 | tf_op jit(solution)/shard_map/ppermute | solution.py:363
  84.1 0.8 copy-start.7
  85.0 0.8 copy-start.8
  90.8 33.4 %copy-start.10 = (bf16[2,32,128]{2,1,0:T(8,128)(2,1)S(1)}, bf16[2,32,128]{2,1,0:T(8,128)(2,1)}, u32[]{:S(2)}) copy-start(bf16[2,32,128]{2,1,0:T(8,128)(2,1)} %get-tuple-element.61) | copy-start | bytes 49156
  90.9 22.2 %all-to-all-start.3 = ((bf16[64,32,128]{2,1,0:T(8,128)(2,1)}), bf16[64,32,128]{2,1,0:T(8,128)(2,1)S(1)}, u32[]{:S(2)}, u32[]{:S(2)}) async-start(bf16[64,32,128]{2,1,0:T(8,128)(2,1)} %get-tuple-element.69), calls=%async_computation.3 | async-start | bytes 1048576 | tf_op jit(solution)/shard_map/all_to_all | solution.py:351
  95.5 40.9 %copy-start = (f32[64,512]{1,0:T(8,128)S(1)}, f32[64,512]{1,0:T(8,128)}, u32[]{:S(2)}) copy-start(f32[64,512]{1,0:T(8,128)} %get-tuple-element.65.keys_raw) | copy-start | bytes 393220
  95.5 40.8 %copy-start.1 = (f32[64,512]{1,0:T(8,128)S(1)}, f32[64,512]{1,0:T(8,128)}, u32[]{:S(2)}) copy-start(f32[64,512]{1,0:T(8,128)} %get-tuple-element.66.values) | copy-start | bytes 393220
  95.5 28.8 %collective-permute-start.7 = (bf16[2,32,128]{2,1,0:T(8,128)(2,1)}, bf16[2,32,128]{2,1,0:T(8,128)(2,1)S(1)}, u32[]{:S(2)}, u32[]{:S(2)}) collective-permute-start(bf16[2,32,128]{2,1,0:T(8,128)(2,1)} %get-tuple-element.62), channel_id=1, source_target_pairs={{0,2},{2,4},{4,6},{6,0},{1,3},{3,5},{5,7},{7,1},{8,10},{10,12},{12... | collective-permute-start | bytes 49160 | tf_op jit(solution)/shard_map/ppermute | solution.py:357
  99.0 25.3 %collective-permute-start.8 = (bf16[2,32,128]{2,1,0:T(8,128)(2,1)}, bf16[2,32,128]{2,1,0:T(8,128)(2,1)S(1)}, u32[]{:S(2)}, u32[]{:S(2)}) collective-permute-start(bf16[2,32,128]{2,1,0:T(8,128)(2,1)} %get-tuple-element.63), channel_id=1, source_target_pairs={{0,4},{2,6},{4,0},{6,2},{1,5},{3,7},{5,1},{7,3},{8,12},{10,14},{12... | collective-permute-start | bytes 49160 | tf_op jit(solution)/shard_map/ppermute | solution.py:357
  102.0 22.3 %collective-permute-start.9 = (bf16[2,32,128]{2,1,0:T(8,128)(2,1)}, bf16[2,32,128]{2,1,0:T(8,128)(2,1)S(1)}, u32[]{:S(2)}, u32[]{:S(2)}) collective-permute-start(bf16[2,32,128]{2,1,0:T(8,128)(2,1)} %get-tuple-element.64), channel_id=1, source_target_pairs={{0,6},{2,0},{4,2},{6,4},{1,7},{3,1},{5,3},{7,5},{8,14},{10,8},{12,... | collective-permute-start | bytes 49160 | tf_op jit(solution)/shard_map/ppermute | solution.py:357
  114.8 21.6 %copy-start.3 = (f32[64,512]{1,0:T(8,128)S(1)}, f32[64,512]{1,0:T(8,128)}, u32[]{:S(2)}) copy-start(f32[64,512]{1,0:T(8,128)} %copy-done.2) | copy-start | bytes 393220
  114.8 21.5 %all-to-all-start.4 = ((bf16[12,32,128]{2,1,0:T(8,128)(2,1)}), bf16[12,32,128]{2,1,0:T(8,128)(2,1)S(1)}, u32[]{:S(2)}, u32[]{:S(2)}) async-start(bf16[12,32,128]{2,1,0:T(8,128)(2,1)} %get-tuple-element.75), calls=%async_computation.4 | async-start | bytes 196608 | tf_op jit(solution)/shard_map/all_to_all | solution.py:351
  124.3 3.2 %copy-start.9 = (bf16[4,2,32,128]{3,2,1,0:T(8,128)(2,1)}, bf16[4,2,32,128]{3,2,1,0:T(8,128)(2,1)S(1)}, u32[]{:S(2)}) copy-start(bf16[4,2,32,128]{3,2,1,0:T(8,128)(2,1)S(1)} %pad_maximum_fusion.m_mine) | copy-start | bytes 196612
  124.3 3.1 %collective-permute-start.10 = (bf16[4,2,32,128]{3,2,1,0:T(8,128)(2,1)S(1)}, bf16[4,2,32,128]{3,2,1,0:T(8,128)(2,1)S(1)}, u32[]{:S(2)}, u32[]{:S(2)}) collective-permute-start(bf16[4,2,32,128]{3,2,1,0:T(8,128)(2,1)S(1)} %pad_maximum_fusion.m_mine), channel_id=1, source_target_pairs={{0,1},{1,0},{2,3},{3,2},{4,5},{5,4},{6,7},{7,6},{8,9},{9,8},{10,11... | collective-permute-start | bytes 196616 | tf_op jit(solution)/shard_map/ppermute | solution.py:363
  127.5 0.6 copy-start.11
